TPU v7x, 32 devices: a whole 2x2x4 slice. The times are simulated.
32 devices in a mesh: ctx: 8 (over z, x), fsdp: 4 (over y, core).
Axes of the slice: x: 2, y: 2, z: 4, core: 2. Of those that a mesh axis runs over, the one named last changes fastest.
Arguments:
- block_in: bfloat16 [4, 2048, 1024], P('fsdp', 'ctx'), may hold values from -6 to 6
- out_grad: bfloat16 [4, 2048, 1024], P('fsdp', 'ctx'), may hold values from -6 to 6
- w_query: bfloat16 [1024, 1024], P('fsdp'), may hold values from -0.1875 to 0.1875
- w_key: bfloat16 [1024, 1024], P('fsdp'), may hold values from -0.1875 to 0.1875
- w_value: bfloat16 [1024, 1024], P('fsdp'), may hold values from -0.1875 to 0.1875
- w_out: bfloat16 [1024, 1024], P('fsdp'), may hold values from -0.1875 to 0.1875
- norm_one: float32 [1024], replicated, may hold values from 0.25 to 1.75
- norm_two: float32 [1024], replicated, may hold values from 0.25 to 1.75
- w_gate: bfloat16 [1024, 2816], P('fsdp'), may hold values from -0.1875 to 0.1875
- w_up: bfloat16 [1024, 2816], P('fsdp'), may hold values from -0.1875 to 0.1875
- w_down: bfloat16 [2816, 1024], P('fsdp'), may hold values from -0.109375 to 0.109375
- norm_three: float32 [1024], replicated, may hold values from 0.25 to 1.75
- norm_four: float32 [1024], replicated, may hold values from 0.25 to 1.75
- prompt_len: int32 [4], replicated, may hold values from 512 to 1024, as said below
- cont_len: int32 [4, 2], replicated, may hold values from 257 to 512, as said below
- group_ids: int32 [4], replicated, may hold values from 0 to 3, each once
- cont_ids: int32 [4, 2], replicated, may hold values from 0 to 1, each once within a row
Outputs:
- block_out: bfloat16 [4, 2048, 1024], P('fsdp', 'ctx')
- in_grad: float32 [4, 2048, 1024], P('fsdp', 'ctx')
- grad_query: float32 [1024, 1024], P('fsdp')
- grad_key: float32 [1024, 1024], P('fsdp')
- grad_value: float32 [1024, 1024], P('fsdp')
- grad_out: float32 [1024, 1024], P('fsdp')
- grad_norm_one: float32 [1024], replicated
- grad_norm_two: float32 [1024], replicated
- grad_gate: float32 [1024, 2816], P('fsdp')
- grad_up: float32 [1024, 2816], P('fsdp')
- grad_down: float32 [2816, 1024], P('fsdp')
- grad_norm_three: float32 [1024], replicated
- grad_norm_four: float32 [1024], replicated
Inputs may be any that keep to these rules, and one draw needn't show every extreme that they name: `prompt_len`: in every draw some group's prompt has exactly 1024 tokens. `cont_len`: every group has a continuation of exactly 512 tokens. `group_ids`: A permutation of the groups. `cont_ids`: each row is a permutation of the continuation numbers.
All inputs are finite; a program needn't handle non-finite values.
Results may differ from a plain program's by a relative error of at most 0.023.
Values may be sent and summed in bfloat16 or wider, within the bound.
No kernel may reach another device: no remote copies, remote signals or barrier semaphores. Data moves between devices by JAX's collectives and lax.ppermute only.
A program may use at most 192 MiB of HBM per device.

v0:
```python
import math

import jax
import jax.numpy as jnp
from jax import lax
from jax.sharding import PartitionSpec as P

HEAD = 128
P_DEV = 128
CONT = 512


eps_norm = 1e-06
rope_base = 50000.0
masked_out = -1e30


def rms_norm(values, gain_vec):
    inverse = lax.rsqrt(jnp.mean(values * values, axis=-1, keepdims=True) + eps_norm)
    return (values * inverse * gain_vec, inverse)


def norm_back(values, inverse, gain_vec, upstream):
    weighted = upstream * gain_vec
    inner_mean = jnp.mean(values * weighted, axis=-1, keepdims=True)
    value_grad = inverse * weighted - values * inverse * inverse * inverse * inner_mean
    return (value_grad, jnp.sum(upstream * values * inverse, axis=0))


def rotate(values, position, turn_sign):
    seq_len = values.shape[0]
    half_size = HEAD // 2
    split_heads = values.reshape(seq_len, -1, HEAD)
    frequencies = rope_base ** (-2.0 * jnp.arange(half_size, dtype=jnp.float32) / HEAD)
    angles = position.astype(jnp.float32)[:, None] * frequencies[None, :]
    cosine = jnp.concatenate([jnp.cos(angles), jnp.cos(angles)], axis=-1)[:, None, :]
    sine_part = turn_sign * jnp.concatenate([jnp.sin(angles), jnp.sin(angles)], axis=-1)[:, None, :]
    turned = jnp.concatenate([-split_heads[..., half_size:], split_heads[..., :half_size]], axis=-1)
    return (split_heads * cosine + turned * sine_part).reshape(seq_len, -1)


def token_info(slot_index, prompt, prompt_size, slot_lens):
    in_cont = slot_index >= prompt
    rel_index = jnp.maximum(slot_index - prompt, 0)
    slot_of = jnp.where(in_cont, rel_index // CONT, -1)
    offset = rel_index % CONT
    slot_range = jnp.arange(slot_lens.shape[0], dtype=jnp.int32)
    slot_len = jnp.sum(
        jnp.where(slot_of[:, None] == slot_range[None, :], slot_lens[None, :], 0), axis=1
    )
    token_valid = jnp.where(in_cont, offset < slot_len, slot_index < prompt_size)
    position = jnp.where(in_cont, prompt_size + offset, slot_index)
    return (token_valid, slot_of, position)


def cross_dot(operand, partner):
    return lax.dot_general(
        operand, partner, (((0,), (0,)), ((), ())), preferred_element_type=jnp.float32
    )


def back_dot(operand, partner):
    return lax.dot_general(
        operand, partner, (((1,), (1,)), ((), ())), preferred_element_type=jnp.float32
    )


def keep_same(state):
    return state


def shards(
    block_in,
    out_grad,
    w_query,
    w_key,
    w_value,
    w_out,
    norm_one,
    norm_two,
    w_gate,
    w_up,
    w_down,
    norm_three,
    norm_four,
    prompt_len,
    cont_len,
    group_ids,
    cont_ids,
):
    local_rows = block_in.shape[1]
    model_width = block_in.shape[2]
    ff_width = w_gate.shape[1]
    ctx_size = lax.axis_size("ctx")
    group_rows = local_rows * ctx_size
    prompt = P_DEV * ctx_size
    head_count = model_width // HEAD
    score_scale = 1.0 / math.sqrt(HEAD)
    row_index = lax.axis_index("fsdp")
    groups = group_ids.shape[0]
    slot_count = cont_ids.shape[1]
    group_range = jnp.arange(groups, dtype=jnp.int32)
    own_group = jnp.sum(jnp.where(group_range == row_index, group_ids, 0))
    own_prompt = jnp.sum(jnp.where(group_range == own_group, prompt_len, 0))
    own_lens = jnp.sum(jnp.where((group_range == own_group)[:, None], cont_len, 0), axis=0)
    own_ids = jnp.sum(jnp.where((group_range == row_index)[:, None], cont_ids, 0), axis=0)
    slot_range = jnp.arange(slot_count, dtype=jnp.int32)
    slot_lens = jnp.sum(
        jnp.where(own_ids[:, None] == slot_range[None, :], own_lens[None, :], 0), axis=1
    )
    query_index = lax.axis_index("ctx") * local_rows + jnp.arange(local_rows, dtype=jnp.int32)
    key_index = jnp.arange(group_rows, dtype=jnp.int32)
    query_valid, query_slot, position = token_info(query_index, prompt, own_prompt, slot_lens)
    key_valid, key_slot, unused_pos = token_info(key_index, prompt, own_prompt, slot_lens)
    tokens = block_in[0].astype(jnp.float32)
    full_query, full_key, full_value, full_out = (
        lax.all_gather(w_query, "fsdp", axis=0, tiled=True),
        lax.all_gather(w_key, "fsdp", axis=0, tiled=True),
        lax.all_gather(w_value, "fsdp", axis=0, tiled=True),
        lax.all_gather(w_out, "fsdp", axis=0, tiled=True),
    )
    normed_full, inverse_one = rms_norm(tokens, norm_one)
    normed = normed_full.astype(jnp.bfloat16)
    queries = rotate(
        jnp.dot(normed, full_query, preferred_element_type=jnp.float32), position, 1.0
    ).astype(jnp.bfloat16)
    keys_local = rotate(
        jnp.dot(normed, full_key, preferred_element_type=jnp.float32), position, 1.0
    ).astype(jnp.bfloat16)
    values_local = jnp.dot(normed, full_value, preferred_element_type=jnp.float32).astype(
        jnp.bfloat16
    )
    all_keys, all_values = (
        lax.all_gather(keys_local, "ctx", axis=0, tiled=True),
        lax.all_gather(values_local, "ctx", axis=0, tiled=True),
    )
    key_block = math.gcd(group_rows, 512)
    block_count = group_rows // key_block
    blocks_in = (
        all_keys.reshape(block_count, key_block, head_count, HEAD),
        all_values.reshape(block_count, key_block, head_count, HEAD),
        key_valid.reshape(block_count, key_block),
        key_slot.reshape(block_count, key_block),
        key_index.reshape(block_count, key_block),
    )
    query_heads = queries.reshape(local_rows, head_count, HEAD)

    def mask_of(inputs):
        key_ids = inputs[4]
        return (
            query_valid[:, None]
            & inputs[2][None, :]
            & (key_ids[None, :] <= query_index[:, None])
            & ((key_ids[None, :] < prompt) | (inputs[3][None, :] == query_slot[:, None]))
        )

    def raw_scores(inputs):
        return (
            jnp.einsum("qhd,khd->hqk", query_heads, inputs[0], preferred_element_type=jnp.float32)
            * score_scale
        )

    def running(state_in, inputs):
        allowed = mask_of(inputs)

        def running_visit(state):
            row_top, exp_total = state
            scores = jnp.where(allowed[None], raw_scores(inputs), masked_out)
            new_top = jnp.maximum(row_top, jnp.max(scores, axis=-1, keepdims=True))
            exp_total = exp_total * jnp.exp(row_top - new_top) + jnp.sum(
                jnp.where(allowed[None], jnp.exp(scores - new_top), 0.0), axis=-1, keepdims=True
            )
            return (new_top, exp_total)

        return (lax.cond(jnp.any(allowed), running_visit, keep_same, state_in), None)

    start_top = jnp.full((head_count, local_rows, 1), -jnp.inf, jnp.float32)
    start_total = jnp.zeros((head_count, local_rows, 1), jnp.float32)
    (row_top, exp_total), unused = lax.scan(running, (start_top, start_total), blocks_in)
    has_keys = exp_total > 0.0
    log_total = jnp.where(has_keys, row_top + jnp.log(jnp.where(has_keys, exp_total, 1.0)), 0.0)

    def probs_of(inputs, allowed):
        return jnp.where(allowed[None], jnp.exp(raw_scores(inputs) - log_total), 0.0)

    def mix_step(accumulated, inputs):
        allowed = mask_of(inputs)

        def mix_visit(total):
            attn_probs = probs_of(inputs, allowed).astype(jnp.bfloat16)
            return total + jnp.einsum(
                "hqk,khd->qhd", attn_probs, inputs[1], preferred_element_type=jnp.float32
            )

        return (lax.cond(jnp.any(allowed), mix_visit, keep_same, accumulated), None)

    mixture, unused = lax.scan(
        mix_step, jnp.zeros((local_rows, head_count, HEAD), jnp.float32), blocks_in
    )
    valid_col = query_valid[:, None].astype(jnp.float32)
    attended = (mixture.reshape(local_rows, model_width) * valid_col).astype(jnp.bfloat16)
    branch = jnp.dot(attended, full_out, preferred_element_type=jnp.float32)
    branch_normed, inverse_two = rms_norm(branch, norm_two)
    middle = tokens + branch_normed
    full_gate, full_up, full_down = (
        lax.all_gather(w_gate, "fsdp", axis=0, tiled=True),
        lax.all_gather(w_up, "fsdp", axis=0, tiled=True),
        lax.all_gather(w_down, "fsdp", axis=0, tiled=True),
    )
    ff_normed, inverse_three = rms_norm(middle, norm_three)
    ff_input = ff_normed.astype(jnp.bfloat16)
    gate_pre = jnp.dot(ff_input, full_gate, preferred_element_type=jnp.float32)
    upward = jnp.dot(ff_input, full_up, preferred_element_type=jnp.float32)
    gate_sig = jax.nn.sigmoid(gate_pre)
    swish_out = gate_pre * gate_sig
    hidden = (swish_out * upward).astype(jnp.bfloat16)
    ff_out = jnp.dot(hidden, full_down, preferred_element_type=jnp.float32)
    out_normed, inverse_four = rms_norm(ff_out, norm_four)
    result = middle + out_normed
    upstream = out_grad[0].astype(jnp.float32)
    ff_out_full, grad_norm_four = norm_back(ff_out, inverse_four, norm_four, upstream)
    ff_out_grad = ff_out_full.astype(jnp.bfloat16)
    hidden_grad = back_dot(ff_out_grad, full_down)
    up_grad = (hidden_grad * swish_out).astype(jnp.bfloat16)
    gate_grad = (hidden_grad * upward * gate_sig * (1.0 + gate_pre * (1.0 - gate_sig))).astype(
        jnp.bfloat16
    )
    ff_in_grad = back_dot(gate_grad, full_gate) + back_dot(up_grad, full_up)
    middle_part, grad_norm_three = norm_back(middle, inverse_three, norm_three, ff_in_grad)
    middle_grad = upstream + middle_part
    branch_full, grad_norm_two = norm_back(branch, inverse_two, norm_two, middle_grad)
    branch_grad = branch_full.astype(jnp.bfloat16)
    attended_grad = back_dot(branch_grad, full_out).astype(jnp.bfloat16) * valid_col.astype(
        jnp.bfloat16
    )
    grad_heads = attended_grad.reshape(local_rows, head_count, HEAD)

    def delta_step(accumulated, inputs):
        allowed = mask_of(inputs)

        def delta_visit(total):
            attn_probs = probs_of(inputs, allowed)
            prob_grad = jnp.einsum(
                "qhd,khd->hqk", grad_heads, inputs[1], preferred_element_type=jnp.float32
            )
            return total + jnp.sum(attn_probs * prob_grad, axis=-1, keepdims=True)

        return (lax.cond(jnp.any(allowed), delta_visit, keep_same, accumulated), None)

    row_delta, unused = lax.scan(
        delta_step, jnp.zeros((head_count, local_rows, 1), jnp.float32), blocks_in
    )
    zero_part = jnp.zeros((key_block, head_count, HEAD), jnp.float32)

    def grad_step(accumulated, inputs):
        allowed = mask_of(inputs)

        def grad_visit(total):
            attn_probs = probs_of(inputs, allowed)
            prob_grad = jnp.einsum(
                "qhd,khd->hqk", grad_heads, inputs[1], preferred_element_type=jnp.float32
            )
            score_grad = (attn_probs * (prob_grad - row_delta)).astype(jnp.bfloat16)
            total = total + jnp.einsum(
                "hqk,khd->qhd", score_grad, inputs[0], preferred_element_type=jnp.float32
            )
            key_part = jnp.einsum(
                "hqk,qhd->khd", score_grad, query_heads, preferred_element_type=jnp.float32
            )
            value_part = jnp.einsum(
                "hqk,qhd->khd",
                attn_probs.astype(jnp.bfloat16),
                grad_heads,
                preferred_element_type=jnp.float32,
            )
            return (total, (key_part, value_part))

        def skip(total):
            return (total, (zero_part, zero_part))

        return lax.cond(jnp.any(allowed), grad_visit, skip, accumulated)

    query_acc, (key_parts, value_parts) = lax.scan(
        grad_step, jnp.zeros((local_rows, head_count, HEAD), jnp.float32), blocks_in
    )
    key_terms = key_parts.reshape(group_rows, model_width) * score_scale
    value_terms = value_parts.reshape(group_rows, model_width)
    key_sum, value_sum = (
        lax.psum_scatter(
            key_terms.astype(jnp.bfloat16), "ctx", scatter_dimension=0, tiled=True
        ).astype(jnp.float32),
        lax.psum_scatter(
            value_terms.astype(jnp.bfloat16), "ctx", scatter_dimension=0, tiled=True
        ).astype(jnp.float32),
    )
    query_grad = rotate(
        query_acc.reshape(local_rows, model_width) * score_scale, position, -1.0
    ).astype(jnp.bfloat16)
    key_grad = rotate(key_sum, position, -1.0).astype(jnp.bfloat16)
    value_grad = value_sum.astype(jnp.bfloat16)
    normed_grad = (
        back_dot(query_grad, full_query)
        + back_dot(key_grad, full_key)
        + back_dot(value_grad, full_value)
    )
    input_part, grad_norm_one = norm_back(tokens, inverse_one, norm_one, normed_grad)
    input_grad = middle_grad + input_part
    wide_pairs = (
        (normed, query_grad),
        (normed, key_grad),
        (normed, value_grad),
        (attended, branch_grad),
        (ff_input, gate_grad),
        (ff_input, up_grad),
    )

    def wide_term(selector):
        return jnp.concatenate(
            [cross_dot(selector(operand), partner) for operand, partner in wide_pairs], axis=1
        )

    wide_local = lax.psum_scatter(
        wide_term(lambda operand: operand).astype(jnp.bfloat16),
        "fsdp",
        scatter_dimension=0,
        tiled=True,
    )
    ff_local = lax.psum_scatter(
        cross_dot((lambda operand: operand)(hidden), ff_out_grad).astype(jnp.bfloat16),
        "fsdp",
        scatter_dimension=0,
        tiled=True,
    )
    wide_sum, ff_sum = (
        lax.psum(wide_local, "ctx").astype(jnp.float32),
        lax.psum(ff_local, "ctx").astype(jnp.float32),
    )
    gain_sums = lax.psum(
        jnp.stack([grad_norm_one, grad_norm_two, grad_norm_three, grad_norm_four]), ("ctx", "fsdp")
    )
    edge_two = 2 * model_width
    edge_three = 3 * model_width
    edge_four = 4 * model_width
    edge_five = 4 * model_width + ff_width
    return (
        result.astype(jnp.bfloat16)[None],
        input_grad[None],
        wide_sum[:, :model_width],
        wide_sum[:, model_width:edge_two],
        wide_sum[:, edge_two:edge_three],
        wide_sum[:, edge_three:edge_four],
        gain_sums[0],
        gain_sums[1],
        wide_sum[:, edge_four:edge_five],
        wide_sum[:, edge_five:],
        ff_sum,
        gain_sums[2],
        gain_sums[3],
    )


def solution(mesh):
    return jax.shard_map(
        shards,
        mesh=mesh,
        in_specs=(
            P("fsdp", "ctx", None),
            P("fsdp", "ctx", None),
            P("fsdp", None),
            P("fsdp", None),
            P("fsdp", None),
            P("fsdp", None),
            P(),
            P(),
            P("fsdp", None),
            P("fsdp", None),
            P("fsdp", None),
            P(),
            P(),
            P(),
            P(),
            P(),
            P(),
        ),
        out_specs=(
            P("fsdp", "ctx", None),
            P("fsdp", "ctx", None),
            P("fsdp", None),
            P("fsdp", None),
            P("fsdp", None),
            P("fsdp", None),
            P(),
            P(),
            P("fsdp", None),
            P("fsdp", None),
            P("fsdp", None),
            P(),
            P(),
        ),
        check_vma=False,
    )
```

profile of v0, /device:TPU:0, one launch (start us, length us, event | category | flops | bytes accessed | tf_op | source)
XLA Modules:
  0.0 1122.9 jit_solution(17604052558741267211)
XLA Ops:
  16.3 18.6 %all-gather.14.cloned.1.call-done = bf16[1024,1024]{1,0:T(8,128)(2,1)} async-done(((bf16[256,1024]{1,0:T(8,128)(2,1)}), bf16[1024,1024]{1,0:T(8,128)(2,1)}) %all-gather.14.cloned.1.call-update) | async-done | bytes 2097168 | tf_op jit(solution)/shard_map/all_gather | solution.py:117
  34.9 2.9 copy.85
  37.8 21.3 %all-gather.10.cloned.1.call-done = bf16[1024,1024]{1,0:T(8,128)(2,1)} async-done(((bf16[256,1024]{1,0:T(8,128)(2,1)}), bf16[1024,1024]{1,0:T(8,128)(2,1)}) %all-gather.10.cloned.1.call-update) | async-done | bytes 2097168 | tf_op jit(solution)/shard_map/all_gather | solution.py:118
  59.1 3.9 copy.83
  63.8 2.4 fusion.106
  67.9 15.3 %all-gather.16.cloned.1.call-done = bf16[1024,1024]{1,0:T(8,128)(2,1)} async-done(((bf16[256,1024]{1,0:T(8,128)(2,1)}), bf16[1024,1024]{1,0:T(8,128)(2,1)}) %all-gather.16.cloned.1.call-update) | async-done | bytes 2097168 | tf_op jit(solution)/shard_map/all_gather | solution.py:119
  83.3 3.1 convolution_convert_fusion.6
  92.4 66.9 %all-gather.12.cloned.1.call-done = bf16[2048,1024]{1,0:T(8,128)(2,1)} async-done(((bf16[256,1024]{1,0:T(8,128)(2,1)}), bf16[2048,1024]{1,0:T(8,128)(2,1)}) %all-gather.12.cloned.1.call-update) | async-done | bytes 4194320 | tf_op jit(solution)/shard_map/all_gather | solution.py:134
  159.2 3.3 copy.128
  162.5 3.0 copy.88
  165.5 68.0 %all-gather.18.cloned.1.call-done = bf16[2048,1024]{1,0:T(8,128)(2,1)} async-done(((bf16[256,1024]{1,0:T(8,128)(2,1)}), bf16[2048,1024]{1,0:T(8,128)(2,1)}) %all-gather.18.cloned.1.call-update) | async-done | bytes 4194320 | tf_op jit(solution)/shard_map/all_gather | solution.py:135
  233.5 3.3 copy.129
  236.8 2.9 copy.90
  239.7 10.0 while.63
  241.3 3.1 conditional.16
  241.4 2.0 fusion.16
  249.8 10.7 while.64
  251.5 3.6 conditional.17
  251.5 3.6 fusion.24
  263.2 2.8 multiply_reduce_fusion.6
  267.4 33.4 %all-gather.22.cloned.1.call-done = bf16[1024,2816]{1,0:T(8,128)(2,1)} async-done(((bf16[256,2816]{1,0:T(8,128)(2,1)}), bf16[1024,2816]{1,0:T(8,128)(2,1)}) %all-gather.22.cloned.1.call-update) | async-done | bytes 5767184 | tf_op jit(solution)/shard_map/all_gather | solution.py:206
  300.8 6.0 fusion.145
  306.8 39.0 %all-gather.24.cloned.1.call-done = bf16[1024,2816]{1,0:T(8,128)(2,1)} async-done(((bf16[256,2816]{1,0:T(8,128)(2,1)}), bf16[1024,2816]{1,0:T(8,128)(2,1)}) %all-gather.24.cloned.1.call-update) | async-done | bytes 5767184 | tf_op jit(solution)/shard_map/all_gather | solution.py:207
  345.8 7.4 multiply_convert_fusion.3
  353.2 37.6 %all-gather.26.cloned.1.call-done = bf16[2816,1024]{1,0:T(8,128)(2,1)} async-done(((bf16[704,1024]{1,0:T(8,128)(2,1)}), bf16[2816,1024]{1,0:T(8,128)(2,1)}) %all-gather.26.cloned.1.call-update) | async-done | bytes 5767184 | tf_op jit(solution)/shard_map/all_gather | solution.py:208
  390.8 5.0 multiply_reduce_fusion.4
  398.1 6.0 multiply_convert_fusion.1
  410.5 11.4 %while.65 = (s32[]{:T(128)}, f32[8,256,1]{1,2,0:T(1,128)S(1)}, pred[256]{0:T(512)(128)(4,1)S(1)}, pred[4,512]{1,0:T(4,128)(4,1)S(1)}, s32[4,512]{1,0:T(4,128)S(1...) while((s32[]{:T(128)}, f32[8,256,1]{1,2,0:T(1,128)S(1)}, ...), condition=%wide.region_31.32_spmd.clone.clone, body=%wide.region_26.31_spmd.clone.clone.sunk | while | flops 543035136 | bytes 11857887 | solution.py:250
  412.2 4.5 conditional.18
  414.2 2.5 fusion.35
  423.0 38.1 %while.66 = (s32[]{:T(128)}, f32[256,8,128]{2,0,1:T(8,128)}, f32[4,512,8,128]{3,1,2,0:T(8,128)}, bf16[4,512,8,128]{3,1,2,0:T(8,128)(2,1)}, pred[256]{0:T(512)(12...) while((s32[]{:T(128)}, f32[256,8,128]{2,0,1:T(8,128)}, ...), condition=%wide.region_36.37_spmd.clone.clone, body=%wide.region_32.36_spmd.clone.clone.sunk | while | flops 1353846528 | bytes 89568512 | solution.py:283
  424.6 9.4 conditional.19
  424.7 2.1 fusion.57
  426.8 2.6 fusion.43
  429.4 2.4 fusion.54
  437.3 2.1 copy-done.17
  444.5 2.1 copy-done.17
  451.7 2.1 copy-done.17
  458.9 2.1 copy-done.17
  461.1 4.6 multiply_convert_fusion
  465.7 2.7 copy.104
  468.4 3.2 copy.136
  471.7 4.9 copy.108
  476.6 3.1 copy.135
  481.1 4.2 convolution_convert_fusion
  487.9 3.1 convolution_convert_fusion.2
  491.1 4.2 copy.112
  496.4 90.5 %reduce-scatter.5.cloned.1.call-done = bf16[256,1024]{1,0:T(8,128)(2,1)} async-done(((bf16[2048,1024]{1,0:T(8,128)(2,1)}), bf16[256,1024]{1,0:T(8,128)(2,1)}) %reduce-scatter.5.cloned.1.call-update) | async-done | bytes 524304 | tf_op jit(solution)/shard_map/reduce_scatter | solution.py:289
  591.2 2.1 convolution_convert_fusion.1
  593.3 2.9 copy.109
  596.2 1.9 add_convert_fusion
  598.9 2.2 convolution_convert_fusion.4
  601.1 3.9 copy.110
  605.0 73.9 %reduce-scatter.7.cloned.1.call-done = bf16[256,1024]{1,0:T(8,128)(2,1)} async-done(((bf16[2048,1024]{1,0:T(8,128)(2,1)}), bf16[256,1024]{1,0:T(8,128)(2,1)}) %reduce-scatter.7.cloned.1.call-update) | async-done | bytes 524304 | tf_op jit(solution)/shard_map/reduce_scatter | solution.py:292
  678.9 3.2 convolution_convert_fusion.3
  682.1 3.9 copy.111
  693.5 4.2 convert_dynamic-update-slice_fusion.1
  697.7 4.5 convert_dynamic-update-slice_fusion
  702.2 33.7 %reduce-scatter.11.cloned.1.call-done = bf16[704,1024]{1,0:T(8,128)(2,1)} async-done(((bf16[2816,1024]{1,0:T(8,128)(2,1)}), bf16[704,1024]{1,0:T(8,128)(2,1)}) %reduce-scatter.11.cloned.1.call-update) | async-done | bytes 1441808 | tf_op jit(solution)/shard_map/reduce_scatter | solution.py:328
  735.9 149.1 %reduce-scatter.9.cloned.1.call-done = bf16[256,9728]{1,0:T(8,128)(2,1)} async-done(((bf16[1024,9728]{1,0:T(8,128)(2,1)}), bf16[256,9728]{1,0:T(8,128)(2,1)}) %reduce-scatter.9.cloned.1.call-update) | async-done | bytes 4980752 | tf_op jit(solution)/shard_map/reduce_scatter | solution.py:322
  889.7 43.4 %psum.22 = f32[4,1024]{1,0:T(4,128)S(1)} all-reduce(f32[4,1024]{1,0:T(4,128)S(1)} %pad_maximum_fusion.2), channel_id=1, replica_groups=mesh['ctx'=8,'fsdp'=4] {'ctx','fsdp'}, use_global_device_ids=true, to_apply=%region_46.47 | all-reduce | flops 4096 | bytes 32768 | tf_op jit(solution)/shard_map/psum | solution.py:338
  935.0 172.4 %all-reduce.3.cloned.1.call-done = (bf16[256,9728]{1,0:T(8,128)(2,1)}, bf16[704,1024]{1,0:T(8,128)(2,1)}) async-done(((bf16[256,9728]{1,0:T(8,128)(2,1)}, bf16[704,1024]{1,0:T(8,128)(2,1)}), (bf16[256,9728]{1,0:T(8,128)(2,1)}, bf16[704,1024]{1,0:T(8,128)(2,1)})) %all-reduce.3.cloned.1.call-update) | async-done | bytes 6422544 | tf_op jit(solution)/shard_map/psum | solution.py:335
  1107.4 3.9 fusion.143
  1111.3 2.9 fusion.142
  (334 shorter events, 93.5 us)
Async XLA Ops:
  7.2 27.7 %all-gather.14.cloned.1.call-start = ((), (), s32[]{:S(2)}) async-start(), calls=%async_computation.6 | async-start | bytes 2621440 | tf_op jit(solution)/shard_map/all_gather | solution.py:117
  7.9 51.2 %all-gather.10.cloned.1.call-start = ((), (), s32[]{:S(2)}) async-start(), calls=%async_computation.4 | async-start | bytes 2621440 | tf_op jit(solution)/shard_map/all_gather | solution.py:118
  8.7 74.6 %all-gather.16.cloned.1.call-start = ((), (), s32[]{:S(2)}) async-start(), calls=%async_computation.7 | async-start | bytes 2621440 | tf_op jit(solution)/shard_map/all_gather | solution.py:119
  9.4 149.9 %all-gather.12.cloned.1.call-start = ((), (), s32[]{:S(2)}) async-start(), calls=%async_computation.5 | async-start | bytes 4718592 | tf_op jit(solution)/shard_map/all_gather | solution.py:134
  15.0 51.4 %copy-start.26 = (f32[256,128]{0,1:T(8,128)}, f32[256,128]{0,1:T(8,128)S(1)}, u32[]{:S(2)}) copy-start(f32[256,128]{0,1:T(8,128)S(1)} %get-tuple-element.1103) | copy-start | bytes 393220
  16.3 67.0 %copy-start.37 = (f32[256]{0:T(256)}, f32[256]{0:T(256)S(1)}, u32[]{:S(2)}) copy-start(f32[256]{0:T(256)S(1)} %add_rsqrt_fusion.3) | copy-start | bytes 3076
  34.9 28.1 %copy-start.3 = (bf16[1,256,1024]{2,1,0:T(8,128)(2,1)S(1)}, bf16[1,256,1024]{2,1,0:T(8,128)(2,1)}, u32[]{:S(2)}) copy-start(bf16[1,256,1024]{2,1,0:T(8,128)(2,1)} %param.33) | copy-start | bytes 1572868
  34.9 28.1 %copy-start.35 = (f32[1024]{0:T(1024)S(1)}, f32[1024]{0:T(1024)}, u32[]{:S(2)}) copy-start(f32[1024]{0:T(1024)} %param.39) | copy-start | bytes 12292
  67.9 22.3 %copy-start.43 = (s32[4,2]{0,1:T(2,128)S(1)}, s32[4,2]{0,1:T(2,128)}, u32[]{:S(2)}) copy-start(s32[4,2]{0,1:T(2,128)} %param.47) | copy-start | bytes 100
  67.9 22.3 %copy-start.44 = (s32[4,2]{0,1:T(2,128)S(1)}, s32[4,2]{0,1:T(2,128)}, u32[]{:S(2)}) copy-start(s32[4,2]{0,1:T(2,128)} %param.49) | copy-start | bytes 100
  67.9 165.6 %all-gather.18.cloned.1.call-start = ((), (), s32[]{:S(2)}) async-start(), calls=%async_computation.8 | async-start | bytes 4718592 | tf_op jit(solution)/shard_map/all_gather | solution.py:135
  86.4 176.7 %all-gather.20.cloned.1.call-start = ((), (), s32[]{:S(2)}) async-start(), calls=%async_computation.9 | async-start | bytes 2621440 | tf_op jit(solution)/shard_map/all_gather | solution.py:120
  87.0 213.8 %all-gather.22.cloned.1.call-start = ((), (), s32[]{:S(2)}) async-start(), calls=%async_computation.10 | async-start | bytes 7208960 | tf_op jit(solution)/shard_map/all_gather | solution.py:206
  87.8 258.0 %all-gather.24.cloned.1.call-start = ((), (), s32[]{:S(2)}) async-start(), calls=%async_computation.11 | async-start | bytes 7208960 | tf_op jit(solution)/shard_map/all_gather | solution.py:207
  88.5 302.3 %all-gather.26.cloned.1.call-start = ((), (), s32[]{:S(2)}) async-start(), calls=%async_computation.12 | async-start | bytes 7208960 | tf_op jit(solution)/shard_map/all_gather | solution.py:208
  89.3 497.7 %reduce-scatter.5.cloned.1.call-start = ((), (), s32[]{:S(2)}) async-start(), calls=%async_computation.13 | async-start | bytes 4718592 | tf_op jit(solution)/shard_map/reduce_scatter | solution.py:289
  260.5 5.5 copy-start.39
  261.8 4.6 copy-start.40
  263.2 2.9 copy-start.14
  390.8 7.3 slice-start.4
  390.8 5.0 copy-start.12
  390.8 5.0 copy-start.42
  390.8 7.3 slice-start.5
  396.8 7.4 slice-start
  396.8 9.1 slice-start.2
  398.1 6.1 copy-start.23
  398.1 6.1 slice-start.1
  398.1 7.8 slice-start.3
  424.7 4.7 copy-start.32
  426.8 2.6 copy-start
  431.8 2.3 copy-start.1
  434.1 2.9 copy-start.16
  435.6 3.8 copy-start.31
  437.3 2.1 copy-start.17
  441.3 2.9 copy-start.16
  442.8 3.8 copy-start.31
  444.5 2.1 copy-start.17
  448.5 2.9 copy-start.16
  450.1 3.7 copy-start.31
  455.7 2.9 copy-start.16
  457.3 3.7 copy-start.31
  471.6 207.3 %reduce-scatter.7.cloned.1.call-start = ((), (), s32[]{:S(2)}) async-start(), calls=%async_computation.14 | async-start | bytes 4718592 | tf_op jit(solution)/shard_map/reduce_scatter | solution.py:292
  479.6 256.3 %reduce-scatter.11.cloned.1.call-start = ((), (), s32[]{:S(2)}) async-start(), calls=%async_computation.16 | async-start | bytes 7208960 | tf_op jit(solution)/shard_map/reduce_scatter | solution.py:328
  485.3 2.3 copy-start.2
  485.3 2.6 copy-start.15
  485.3 399.7 %reduce-scatter.9.cloned.1.call-start = ((), (), s32[]{:S(2)}) async-start(), calls=%async_computation.15 | async-start | bytes 24903680 | tf_op jit(solution)/shard_map/reduce_scatter | solution.py:322
  495.2 93.1 %copy-start.28 = (f32[256,128]{0,1:T(8,128)S(1)}, f32[256,128]{0,1:T(8,128)}, u32[]{:S(2)}) copy-start(f32[256,128]{0,1:T(8,128)} %get-tuple-element.1104) | copy-start | bytes 393220
  495.2 93.1 %copy-start.29 = (f32[256,128]{0,1:T(8,128)S(1)}, f32[256,128]{0,1:T(8,128)}, u32[]{:S(2)}) copy-start(f32[256,128]{0,1:T(8,128)} %get-tuple-element.1102) | copy-start | bytes 393220
  588.2 3.0 copy-start.36
  588.2 3.0 copy-start.38
  686.0 2.5 copy-start.10
  686.0 4.1 copy-start.11
  688.5 3.3 copy-start.9
  690.2 3.3 copy-start.34
  690.2 3.3 copy-start.48
  693.5 4.2 copy-start.46
  702.2 182.9 %copy-start.7 = (bf16[1024,1024]{1,0:T(8,128)(2,1)S(1)}, bf16[1024,1024]{1,0:T(8,128)(2,1)}, u32[]{:S(2)}) copy-start(bf16[1024,1024]{1,0:T(8,128)(2,1)} %all-gather.14.cloned.1.call-done) | copy-start | bytes 6291460
  702.2 405.2 %all-reduce.3.cloned.1.call-start = ((), (), s32[]{:S(2)}) async-start(), calls=%async_computation.17 | async-start | bytes 12845056 | tf_op jit(solution)/shard_map/psum | solution.py:335
  885.1 3.5 copy-start.19
  885.1 3.5 copy-start.21
  886.7 3.0 copy-start.41
  886.7 47.0 %copy-start.6 = (f32[256,1024]{1,0:T(8,128)S(1)}, f32[256,1024]{1,0:T(8,128)}, u32[]{:S(2)}) copy-start(f32[256,1024]{1,0:T(8,128)} %copy-done.5) | copy-start | bytes 3145732
  1107.4 3.9 copy-start.4
  1111.3 2.9 copy-start.25
  (17 other events, 25.3 us)
Sparse Core Ops, SparseCore 0:
  9.6 25.2 all-gather.13
  36.5 22.5 all-gather.9
  60.6 22.5 all-gather.15
  85.8 73.3 all-gather.11
  161.8 71.6 all-gather.17
  234.9 20.8 all-gather.19
  257.4 43.3 all-gather.21
  302.4 43.3 all-gather.23
  347.4 43.3 all-gather.25
  471.7 115.1 reduce-scatter.4
  591.0 87.8 reduce-scatter.6
  681.3 54.5 reduce-scatter.10
  738.7 146.2 reduce-scatter.8
  888.9 218.4 all-reduce.2
where the time goes:
time: 1130 us; the launch traced here: 1120 us
  waiting for transfers between devices  824 us (73%)
  local copies, waits for them, and re-layouts  97.8 us (9%)
  matrix products  83.8 us (7%)
  other arithmetic  46.4 us (4%)
  blocking collectives  43.4 us (4%)
  between operations  15 us (1%)
  loops' own time  11.6 us (1%)
    psum x1, waiting for transfers between devices, shards(): lax.psum(wide_local, 'ctx').astype(jnp.float32)  172 us
    reduce_scatter x1, waiting for transfers between devices, shards(): lax.psum_scatter(wide_term(lambda operand: operand).astype(jnp.bfloat16),...  149 us
    reduce_scatter x1, waiting for transfers between devices, shards(): lax.psum_scatter(key_terms.astype(jnp.bfloat16), 'ctx', scatter_dimension...  90.5 us
    reduce_scatter x1, waiting for transfers between devices, shards(): lax.psum_scatter(value_terms.astype(jnp.bfloat16), 'ctx', scatter_dimensi...  73.9 us
    all_gather x1, waiting for transfers between devices, shards(): lax.all_gather(values_local, 'ctx', axis=0, tiled=True)  68 us
    all_gather x1, waiting for transfers between devices, shards(): lax.all_gather(keys_local, 'ctx', axis=0, tiled=True)  66.9 us
    psum x1, blocking collectives, shards(): lax.psum(jnp.stack([grad_norm_one, grad_norm_two, grad_norm_three, grad_n...  43.4 us
    all_gather x1, waiting for transfers between devices, shards(): lax.all_gather(w_up, 'fsdp', axis=0, tiled=True)  39 us
  transfers between devices with their start and end apart: 14, of which 13 were waited for; matrix products, arithmetic and copies ran while one was open for 12% of the time, Pallas kernels for 0%

commit v1 on v0

--- a/solution.py
+++ b/solution.py
@@ -1,19 +1,24 @@
+import functools
 import math
 
 import jax
 import jax.numpy as jnp
 from jax import lax
+from jax.experimental import pallas as pl
+from jax.experimental.pallas import tpu as pltpu
 from jax.sharding import PartitionSpec as P
 
 HEAD = 128
 P_DEV = 128
 CONT = 512
-
+LOG2E = 1.4426950408889634
 
 eps_norm = 1e-06
 rope_base = 50000.0
 masked_out = -1e30
 
+bf16 = jnp.bfloat16
+f32 = jnp.float32
 
 def rms_norm(values, gain_vec):
     inverse = lax.rsqrt(jnp.mean(values * values, axis=-1, keepdims=True) + eps_norm)
@@ -359,43 +364,724 @@
     )
 
 
+IN_SPECS = (
+    (P("fsdp", "ctx", None),) * 2
+    + (P("fsdp", None),) * 4
+    + (P(), P())
+    + (P("fsdp", None),) * 3
+    + (P(),) * 6
+)
+OUT_SPECS = (
+    (P("fsdp", "ctx", None),) * 2
+    + (P("fsdp", None),) * 4
+    + (P(), P())
+    + (P("fsdp", None),) * 3
+    + (P(), P())
+)
+
+
+REL = (0, 2, 1, 3)
+MIB = 1 << 20
+
+
+def core_swap(values):
+    return lax.ppermute(values, "fsdp", [(i, i ^ 1) for i in range(4)])
+
+
+def y_swap(values):
+    return lax.ppermute(values, "fsdp", [(i, i ^ 2) for i in range(4)])
+
+
+def gather_rows(own):
+    across = y_swap(own)
+    beside = core_swap(own)
+    corner = core_swap(across)
+    return jnp.stack([own, across, beside, corner])
+
+
+def exchange_sums(keep, send):
+    received = core_swap(send)
+    onward = (keep[1].astype(f32) + received[1].astype(f32)).astype(bf16)
+    return keep, received, y_swap(onward)
+
+
+def params(limit_mib, *semantics):
+    return pltpu.CompilerParams(
+        dimension_semantics=semantics or None, vmem_limit_bytes=limit_mib * MIB
+    )
+
+
+def whole(shape):
+    return pl.BlockSpec(shape, lambda *_: (0,) * len(shape))
+
+
+def place(shape):
+    return pl.BlockSpec((1,) + shape, lambda t: (t,) + (0,) * len(shape))
+
+
+def first_place(shape):
+    return pl.BlockSpec((1,) + shape, lambda *_: (0,) * (1 + len(shape)))
+
+
+def kept(shape):
+    return pl.BlockSpec((1,) + shape, lambda t: (jnp.minimum(t, 1),) + (0,) * len(shape))
+
+
+def sent(shape):
+    return pl.BlockSpec((1,) + shape, lambda t: (jnp.maximum(t - 2, 0),) + (0,) * len(shape))
+
+
+def put_partial(step, partial, keep_ref, send_ref):
+    rounded = partial.astype(bf16)
+
+    @pl.when(step < 2)
+    def _():
+        keep_ref[0] = rounded
+
+    @pl.when(step >= 2)
+    def _():
+        send_ref[0] = rounded
+
+
+def dot_nn(a, b):
+    return lax.dot_general(a, b, (((1,), (0,)), ((), ())), preferred_element_type=f32)
+
+
+def dot_nt(a, b):
+    return lax.dot_general(a, b, (((1,), (1,)), ((), ())), preferred_element_type=f32)
+
+
+def dot_tn(a, b):
+    return lax.dot_general(a, b, (((0,), (0,)), ((), ())), preferred_element_type=f32)
+
+
+def inverse_rms(values):
+    return lax.rsqrt(jnp.mean(values * values, axis=-1, keepdims=True) + eps_norm)
+
+
+def turn(values, cosine, sine):
+    return values * cosine + pltpu.roll(values, HEAD // 2, 1) * sine
+
+
+def project_kernel(x_ref, gain_ref, w_ref, cos_ref, sin_ref, out_ref):
+    x = x_ref[0].astype(f32)
+    normed = (x * inverse_rms(x) * gain_ref[...]).astype(bf16)
+    product = dot_nn(normed, w_ref[...])
+    heads = out_ref.shape[0]
+    for kind in range(3):
+        for head in range(heads):
+            start = (kind * heads + head) * HEAD
+            part = product[:, start : start + HEAD]
+            if kind < 2:
+                part = turn(part, cos_ref[0], sin_ref[0])
+            out_ref[head, kind] = part.astype(bf16)
+
+
+def key_span(chunk, prompt_chunks, cont_chunks):
+    in_cont = chunk >= prompt_chunks
+    first = jnp.where(
+        in_cont, prompt_chunks + (chunk - prompt_chunks) // cont_chunks * cont_chunks, 0
+    )
+    return first, jnp.where(in_cont, prompt_chunks, 0)
+
+
+def attend_kernel(
+    prompt_chunks, cont_chunks, info_ref, qkv_ref, out_ref, exact_ref, lse_ref
+):
+    chunk = pl.program_id(0)
+    rows = qkv_ref.shape[2]
+    scale = LOG2E / math.sqrt(HEAD)
+    query = qkv_ref[chunk, 0]
+    prompt_size = info_ref[0]
+    first, ahead = key_span(chunk, prompt_chunks, cont_chunks)
+    key_place = lax.broadcasted_iota(jnp.int32, (rows, rows), 0)
+    query_place = lax.broadcasted_iota(jnp.int32, (rows, rows), 1)
+
+    def visit(key_chunk, bias, state):
+        top, total, mixed = state
+        scores = dot_nt(qkv_ref[key_chunk, 1], query) * scale + bias
+        new_top = jnp.maximum(top, jnp.max(scores, axis=0, keepdims=True))
+        weights = jnp.exp2(scores - new_top)
+        shrink = jnp.exp2(top - new_top)
+        total = total * shrink + jnp.sum(weights, axis=0, keepdims=True)
+        mixed = mixed * shrink + dot_tn(qkv_ref[key_chunk, 2], weights.astype(bf16))
+        return new_top, total, mixed
+
+    def prompt_visit(key_chunk, state):
+        bias = jnp.where(key_chunk * rows + key_place < prompt_size, 0.0, masked_out)
+        return visit(key_chunk, bias, state)
+
+    def own_visit(key_chunk, state):
+        return visit(key_chunk, 0.0, state)
+
+    state = (
+        jnp.full((1, rows), -1e38, f32),
+        jnp.zeros((1, rows), f32),
+        jnp.zeros((HEAD, rows), f32),
+    )
+    state = visit(chunk, jnp.where(key_place <= query_place, 0.0, masked_out), state)
+    state = lax.fori_loop(0, ahead, prompt_visit, state)
+    top, total, mixed = lax.fori_loop(first, chunk, own_visit, state)
+    slot = jnp.maximum(chunk - prompt_chunks, 0) // cont_chunks
+    start = jnp.where(
+        chunk < prompt_chunks,
+        chunk,
+        jnp.maximum(chunk - prompt_chunks, 0) % cont_chunks,
+    )
+    limit = jnp.where(chunk < prompt_chunks, prompt_size, info_ref[1 + slot])
+    valid = start * rows + lax.broadcasted_iota(jnp.int32, (1, rows), 1) < limit
+    mixed = jnp.where(valid, mixed / total, 0.0)
+    settled = mixed.T
+    out_ref[chunk] = settled.astype(bf16)
+    exact_ref[chunk] = settled
+    lse_ref[chunk] = top + jnp.log2(total)
+
+
+def attend_back_kernel(
+    prompt_chunks,
+    cont_chunks,
+    info_ref,
+    qkv_ref,
+    grad_ref,
+    exact_ref,
+    lse_ref,
+    cos_ref,
+    sin_ref,
+    out_ref,
+    key_sum,
+    value_sum,
+):
+    chunk = pl.program_id(0)
+    chunks = pl.num_programs(0)
+    rows = qkv_ref.shape[2]
+    scale = LOG2E / math.sqrt(HEAD)
+    query = qkv_ref[chunk, 0]
+    prompt_size = info_ref[0]
+    first, ahead = key_span(chunk, prompt_chunks, cont_chunks)
+    key_place = lax.broadcasted_iota(jnp.int32, (rows, rows), 0)
+    query_place = lax.broadcasted_iota(jnp.int32, (rows, rows), 1)
+    slot = jnp.maximum(chunk - prompt_chunks, 0) // cont_chunks
+    start = jnp.where(
+        chunk < prompt_chunks,
+        chunk,
+        jnp.maximum(chunk - prompt_chunks, 0) % cont_chunks,
+    )
+    limit = jnp.where(chunk < prompt_chunks, prompt_size, info_ref[1 + slot])
+    valid = start * rows + lax.broadcasted_iota(jnp.int32, (rows, 1), 0) < limit
+    grad_full = jnp.where(valid, grad_ref[chunk].astype(f32), 0.0)
+    grad = grad_full.astype(bf16)
+    delta = jnp.sum((grad_full * exact_ref[chunk]).T, axis=0, keepdims=True)
+    log_total = lse_ref[chunk]
+
+    @pl.when(chunk == 0)
+    def _():
+        key_sum[...] = jnp.zeros_like(key_sum)
+        value_sum[...] = jnp.zeros_like(value_sum)
+
+    def visit(key_chunk, bias, query_sum):
+        key = qkv_ref[key_chunk, 1]
+        scores = dot_nt(key, query) * scale + bias
+        weights = jnp.exp2(scores - log_total)
+        weight_grad = dot_nt(qkv_ref[key_chunk, 2], grad)
+        score_grad = (weights * (weight_grad - delta)).astype(bf16)
+        value_sum[key_chunk] += dot_nn(weights.astype(bf16), grad)
+        key_sum[key_chunk] += dot_nn(score_grad, query)
+        return query_sum + dot_tn(key, score_grad)
+
+    def prompt_visit(key_chunk, query_sum):
+        bias = jnp.where(key_chunk * rows + key_place < prompt_size, 0.0, masked_out)
+        return visit(key_chunk, bias, query_sum)
+
+    def own_visit(key_chunk, query_sum):
+        return visit(key_chunk, 0.0, query_sum)
+
+    query_sum = visit(
+        chunk,
+        jnp.where(key_place <= query_place, 0.0, masked_out),
+        jnp.zeros((HEAD, rows), f32),
+    )
+    query_sum = lax.fori_loop(0, ahead, prompt_visit, query_sum)
+    query_sum = lax.fori_loop(first, chunk, own_visit, query_sum)
+    back = 1.0 / math.sqrt(HEAD)
+    out_ref[chunk, 0] = turn(query_sum.T * back, cos_ref[chunk], -sin_ref[chunk]).astype(bf16)
+
+    @pl.when(chunk == chunks - 1)
+    def _():
+        @pl.loop(0, chunks)
+        def _(key_chunk):
+            out_ref[key_chunk, 1] = turn(
+                key_sum[key_chunk] * back, cos_ref[key_chunk], -sin_ref[key_chunk]
+            ).astype(bf16)
+            out_ref[key_chunk, 2] = value_sum[key_chunk].astype(bf16)
+
+
+def mix_out_kernel(heads_ref, w_ref, keep_ref, send_ref):
+    step = pl.program_id(0)
+    both = jnp.concatenate([heads_ref[j] for j in range(heads_ref.shape[0])], axis=1)
+    put_partial(step, dot_nn(both, w_ref[...]), keep_ref, send_ref)
+
+
+def middle_kernel(
+    keep_ref, received_ref, across_ref, x_ref, two_ref, three_ref, branch_ref, middle_ref, input_ref
+):
+    branch = (
+        keep_ref[0].astype(f32) + received_ref[0].astype(f32) + across_ref[...].astype(f32)
+    )
+    middle = x_ref[...].astype(f32) + branch * inverse_rms(branch) * two_ref[...]
+    branch_ref[...] = branch
+    middle_ref[...] = middle
+    input_ref[...] = (middle * inverse_rms(middle) * three_ref[...]).astype(bf16)
+
+
+def ff_kernel(x_ref, gate_ref, up_ref, down_ref, keep_ref, send_ref, slope_ref, swish_ref, hidden_ref):
+    step = pl.program_id(0)
+    x = x_ref[0]
+    gate = dot_nn(x, gate_ref[...])
+    upward = dot_nn(x, up_ref[...])
+    sigma = 1.0 / (1.0 + jnp.exp(-gate))
+    swish = gate * sigma
+    hidden = (swish * upward).astype(bf16)
+    slope_ref[0] = (upward * sigma * (1.0 + gate * (1.0 - sigma))).astype(bf16)
+    swish_ref[0] = swish.astype(bf16)
+    hidden_ref[0] = hidden
+    put_partial(step, dot_nn(hidden, down_ref[...]), keep_ref, send_ref)
+
+
+def norm_back_parts(values, gain, upstream):
+    inverse = inverse_rms(values)
+    weighted = upstream * gain
+    inner = jnp.mean(values * weighted, axis=-1, keepdims=True)
+    value_grad = inverse * weighted - values * (inverse * inverse * inverse * inner)
+    return value_grad, jnp.sum(upstream * values * inverse, axis=0, keepdims=True)
+
+
+def turnaround_kernel(
+    keep_ref, received_ref, across_ref, middle_ref, grad_ref, four_ref, out_ref, back_ref, gain_ref
+):
+    ff_out = keep_ref[0].astype(f32) + received_ref[0].astype(f32) + across_ref[...].astype(f32)
+    out_ref[...] = (middle_ref[...] + ff_out * inverse_rms(ff_out) * four_ref[...]).astype(bf16)
+    value_grad, gain = norm_back_parts(ff_out, four_ref[...], grad_ref[...].astype(f32))
+    back_ref[...] = value_grad.astype(bf16)
+    gain_ref[...] = gain
+
+
+def ff_back_kernel(
+    grad_ref, gate_ref, up_ref, down_ref, slope_ref, swish_ref, keep_ref, send_ref, gate_grad_ref, up_grad_ref
+):
+    step = pl.program_id(0)
+    hidden_grad = dot_nt(grad_ref[0], down_ref[...])
+    gate_grad = (hidden_grad * slope_ref[0].astype(f32)).astype(bf16)
+    up_grad = (hidden_grad * swish_ref[0].astype(f32)).astype(bf16)
+    gate_grad_ref[0] = gate_grad
+    up_grad_ref[0] = up_grad
+    partial = dot_nt(gate_grad, gate_ref[...]) + dot_nt(up_grad, up_ref[...])
+    put_partial(step, partial, keep_ref, send_ref)
+
+
+def branch_back_kernel(
+    keep_ref,
+    received_ref,
+    across_ref,
+    middle_ref,
+    branch_ref,
+    grad_ref,
+    two_ref,
+    three_ref,
+    middle_grad_ref,
+    branch_grad_ref,
+    gain_two_ref,
+    gain_three_ref,
+):
+    input_grad = keep_ref[0].astype(f32) + received_ref[0].astype(f32) + across_ref[...].astype(f32)
+    middle_part, gain_three_ref[...] = norm_back_parts(middle_ref[...], three_ref[...], input_grad)
+    middle_grad = grad_ref[...].astype(f32) + middle_part
+    middle_grad_ref[...] = middle_grad
+    branch_grad, gain_two_ref[...] = norm_back_parts(branch_ref[...], two_ref[...], middle_grad)
+    branch_grad_ref[...] = branch_grad.astype(bf16)
+
+
+def heads_back_kernel(grad_ref, w_ref, out_ref):
+    both = dot_nt(grad_ref[0], w_ref[...]).astype(bf16)
+    for head in range(out_ref.shape[0]):
+        out_ref[head] = both[:, head * HEAD : (head + 1) * HEAD]
+
+
+def project_back_kernel(
+    pieces_ref, x_ref, gain_ref, w_ref, keep_ref, send_ref, grad_ref, total
+):
+    step = pl.program_id(0)
+    heads = pieces_ref.shape[0]
+    pieces = jnp.concatenate(
+        [pieces_ref[head, kind] for kind in range(3) for head in range(heads)], axis=1
+    )
+    put_partial(step, dot_nt(pieces, w_ref[...]), keep_ref, send_ref)
+    x = x_ref[0].astype(f32)
+    normed = (x * inverse_rms(x) * gain_ref[...]).astype(bf16)
+    term = dot_tn(normed, pieces)
+
+    @pl.when(step == 0)
+    def _():
+        total[...] = term
+
+    @pl.when(step > 0)
+    def _():
+        total[...] += term
+
+    @pl.when(step == pl.num_programs(0) - 1)
+    def _():
+        grad_ref[...] = total[...].astype(bf16)
+
+
+def input_back_kernel(
+    keep_ref, received_ref, across_ref, x_ref, middle_grad_ref, one_ref, out_ref, gain_ref
+):
+    normed_grad = keep_ref[0].astype(f32) + received_ref[0].astype(f32) + across_ref[...].astype(f32)
+    part, gain_ref[...] = norm_back_parts(x_ref[...].astype(f32), one_ref[...], normed_grad)
+    out_ref[...] = middle_grad_ref[...] + part
+
+
+def shaped(*shape, kind=bf16):
+    return jax.ShapeDtypeStruct(shape, kind)
+
+
+def rope_tables(position):
+    half = HEAD // 2
+    frequencies = rope_base ** (-2.0 * jnp.arange(half, dtype=f32) / HEAD)
+    angles = position.astype(f32)[..., None] * frequencies
+    cosine, sine = jnp.cos(angles), jnp.sin(angles)
+    return (
+        jnp.concatenate([cosine, cosine], axis=-1),
+        jnp.concatenate([-sine, sine], axis=-1),
+    )
+
+
+def cross_dot_low(operand, partner):
+    return lax.dot_general(
+        operand, partner, (((0,), (0,)), ((), ())), preferred_element_type=f32
+    ).astype(bf16)
+
+
+def pair_shards(
+    block_in,
+    out_grad,
+    w_query,
+    w_key,
+    w_value,
+    w_out,
+    norm_one,
+    norm_two,
+    w_gate,
+    w_up,
+    w_down,
+    norm_three,
+    norm_four,
+    prompt_len,
+    cont_len,
+    group_ids,
+    cont_ids,
+):
+    rows, width = block_in.shape[1:]
+    ctx_size = lax.axis_size("ctx")
+    heads = width // HEAD // 4
+    prompt = P_DEV * ctx_size
+    prompt_chunks, cont_chunks = prompt // rows, CONT // rows
+    ff_part = w_down.shape[0]
+    ff_width = w_gate.shape[1]
+    my_row = lax.axis_index("fsdp")
+    my_chunk = lax.axis_index("ctx")
+    groups, slots = cont_ids.shape
+
+    row_of = my_row ^ jnp.array(REL, jnp.int32)
+    group_range = jnp.arange(groups, dtype=jnp.int32)
+    slot_range = jnp.arange(slots, dtype=jnp.int32)
+    pick_row = row_of[:, None] == group_range[None, :]
+    group_of = jnp.sum(jnp.where(pick_row, group_ids[None, :], 0), axis=1)
+    pick_group = group_of[:, None] == group_range[None, :]
+    prompt_of = jnp.sum(jnp.where(pick_group, prompt_len[None, :], 0), axis=1)
+    lens_of = jnp.sum(jnp.where(pick_group[:, :, None], cont_len[None], 0), axis=1)
+    ids_of = jnp.sum(jnp.where(pick_row[:, :, None], cont_ids[None], 0), axis=1)
+    slot_lens = jnp.sum(
+        jnp.where(ids_of[:, :, None] == slot_range, lens_of[:, None, :], 0), axis=2
+    )
+    pick_pair = jnp.arange(4, dtype=jnp.int32) == my_chunk // heads
+    pair_prompt = jnp.sum(jnp.where(pick_pair, prompt_of, 0))
+    pair_lens = jnp.sum(jnp.where(pick_pair[:, None], slot_lens, 0), axis=0)
+    info = jnp.concatenate([pair_prompt[None], pair_lens])
+
+    def positions(slot, prompt_size):
+        return jnp.where(slot >= prompt, prompt_size + (slot - prompt) % CONT, slot)
+
+    own_slots = my_chunk * rows + jnp.arange(rows, dtype=jnp.int32)
+    cos_own, sin_own = rope_tables(positions(own_slots[None, :], prompt_of[:, None]))
+    all_slots = jnp.arange(rows * ctx_size, dtype=jnp.int32).reshape(ctx_size, rows)
+    cos_all, sin_all = rope_tables(positions(all_slots, pair_prompt))
+
+    gain_one, gain_two, gain_three, gain_four = (
+        gain[None, :] for gain in (norm_one, norm_two, norm_three, norm_four)
+    )
+    x_own, grad_own = block_in[0], out_grad[0]
+
+    x_all = gather_rows(x_own)
+    part = heads * HEAD
+    wide = jnp.stack(
+        [w.reshape(rows, 4, part) for w in (w_query, w_key, w_value)], axis=2
+    ).transpose(1, 0, 2, 3)
+    w_qkv = lax.all_to_all(
+        wide.reshape(4, rows, 3 * part), "fsdp", 0, 0, tiled=True
+    ).reshape(width, 3 * part)
+    w_pair = lax.all_to_all(
+        jnp.stack([w.reshape(w.shape[0], 4, ff_part).transpose(1, 0, 2) for w in (w_gate, w_up)], axis=1),
+        "fsdp",
+        0,
+        0,
+        tiled=True,
+    )
+    gate_part = w_pair[:, 0].reshape(width, ff_part)
+    up_part = w_pair[:, 1].reshape(width, ff_part)
+
+    piece = (heads, 3, rows, HEAD)
+    qkv = pl.pallas_call(
+        project_kernel,
+        name="project",
+        grid=(4,),
+        in_specs=[
+            place((rows, width)),
+            whole((1, width)),
+            whole((width, 3 * part)),
+            place((rows, HEAD)),
+            place((rows, HEAD)),
+        ],
+        out_specs=pl.BlockSpec(piece, lambda t: (t, 0, 0, 0)),
+        out_shape=shaped(4 * heads, 3, rows, HEAD),
+        compiler_params=params(24, "arbitrary"),
+    )(x_all, gain_one, w_qkv, cos_own, sin_own)
+    qkv = lax.all_to_all(qkv, "ctx", 0, 0, tiled=True)
+
+    smem = pl.BlockSpec(memory_space=pltpu.SMEM)
+    qkv_shape, head_shape = (ctx_size, 3, rows, HEAD), (ctx_size, rows, HEAD)
+    mixed, exact, log_total = pl.pallas_call(
+        functools.partial(attend_kernel, prompt_chunks, cont_chunks),
+        name="attend",
+        grid=(ctx_size,),
+        in_specs=[smem, whole(qkv_shape)],
+        out_specs=[whole(head_shape), whole(head_shape), whole((ctx_size, 1, rows))],
+        out_shape=[
+            shaped(*head_shape),
+            shaped(*head_shape, kind=f32),
+            shaped(ctx_size, 1, rows, kind=f32),
+        ],
+        compiler_params=params(32, "arbitrary"),
+    )(info, qkv)
+    attended = lax.all_to_all(mixed, "ctx", 0, 0, tiled=True)
+
+    pair_spec = pl.BlockSpec((heads, rows, HEAD), lambda t: (t, 0, 0))
+    two = shaped(2, rows, width)
+    keep, send = pl.pallas_call(
+        mix_out_kernel,
+        name="mix_out",
+        grid=(4,),
+        in_specs=[pair_spec, whole((part, width))],
+        out_specs=[kept((rows, width)), sent((rows, width))],
+        out_shape=[two, two],
+        compiler_params=params(16, "arbitrary"),
+    )(attended, w_out)
+
+    row_spec, gain_spec = whole((rows, width)), whole((1, width))
+    sum_specs = [first_place((rows, width)), first_place((rows, width)), row_spec]
+    full_row, low_row, gain_row = (
+        shaped(rows, width, kind=f32),
+        shaped(rows, width),
+        shaped(1, width, kind=f32),
+    )
+    branch, middle, ff_input = pl.pallas_call(
+        middle_kernel,
+        name="middle",
+        grid=(1,),
+        in_specs=sum_specs + [row_spec, gain_spec, gain_spec],
+        out_specs=[row_spec] * 3,
+        out_shape=[full_row, full_row, low_row],
+        compiler_params=params(24),
+    )(*exchange_sums(keep, send), x_own, gain_two, gain_three)
+    ff_all = gather_rows(ff_input)
+
+    ff_rows = shaped(4, rows, ff_part)
+    keep, send, slope, swish, hidden = pl.pallas_call(
+        ff_kernel,
+        name="ff",
+        grid=(4,),
+        in_specs=[
+            place((rows, width)),
+            whole((width, ff_part)),
+            whole((width, ff_part)),
+            whole((ff_part, width)),
+        ],
+        out_specs=[kept((rows, width)), sent((rows, width))] + [place((rows, ff_part))] * 3,
+        out_shape=[two, two, ff_rows, ff_rows, ff_rows],
+        compiler_params=params(40, "arbitrary"),
+    )(ff_all, gate_part, up_part, w_down)
+
+    block_out, ff_grad, part_four = pl.pallas_call(
+        turnaround_kernel,
+        name="turnaround",
+        grid=(1,),
+        in_specs=sum_specs + [row_spec, row_spec, gain_spec],
+        out_specs=[row_spec, row_spec, gain_spec],
+        out_shape=[low_row, low_row, gain_row],
+        compiler_params=params(24),
+    )(*exchange_sums(keep, send), middle, grad_own, gain_four)
+
+    ff_grad_all = gather_rows(ff_grad)
+    keep, send, gate_grad, up_grad = pl.pallas_call(
+        ff_back_kernel,
+        name="ff_back",
+        grid=(4,),
+        in_specs=[
+            place((rows, width)),
+            whole((width, ff_part)),
+            whole((width, ff_part)),
+            whole((ff_part, width)),
+            place((rows, ff_part)),
+            place((rows, ff_part)),
+        ],
+        out_specs=[kept((rows, width)), sent((rows, width))] + [place((rows, ff_part))] * 2,
+        out_shape=[two, two, ff_rows, ff_rows],
+        compiler_params=params(40, "arbitrary"),
+    )(ff_grad_all, gate_part, up_part, w_down, slope, swish)
+
+    tokens = 4 * rows
+    flat_input = ff_all.reshape(tokens, width)
+    down_term = cross_dot_low(
+        hidden.reshape(tokens, ff_part), ff_grad_all.reshape(tokens, width)
+    )
+    pair_term = jnp.stack(
+        [
+            cross_dot_low(flat_input, grad.reshape(tokens, ff_part)).reshape(4, rows, ff_part)
+            for grad in (gate_grad, up_grad)
+        ],
+        axis=1,
+    )
+    pair_term = lax.all_to_all(pair_term, "fsdp", 0, 0, tiled=True)
+    pair_term = pair_term.transpose(1, 2, 0, 3).reshape(2, rows, ff_width)
+
+    middle_grad, branch_grad, part_two, part_three = pl.pallas_call(
+        branch_back_kernel,
+        name="branch_back",
+        grid=(1,),
+        in_specs=sum_specs + [row_spec, row_spec, row_spec, gain_spec, gain_spec],
+        out_specs=[row_spec, row_spec, gain_spec, gain_spec],
+        out_shape=[full_row, low_row, gain_row, gain_row],
+        compiler_params=params(24),
+    )(*exchange_sums(keep, send), middle, branch, grad_own, gain_two, gain_three)
+    branch_grad_all = gather_rows(branch_grad)
+
+    attended_grad = pl.pallas_call(
+        heads_back_kernel,
+        name="heads_back",
+        grid=(4,),
+        in_specs=[place((rows, width)), whole((part, width))],
+        out_specs=pair_spec,
+        out_shape=shaped(4 * heads, rows, HEAD),
+        compiler_params=params(16, "arbitrary"),
+    )(branch_grad_all, w_out)
+    attended_grad = lax.all_to_all(attended_grad, "ctx", 0, 0, tiled=True)
+    out_term = cross_dot_low(
+        attended.reshape(4, heads, rows, HEAD).transpose(0, 2, 1, 3).reshape(tokens, part),
+        branch_grad_all.reshape(tokens, width),
+    )
+
+    pieces = pl.pallas_call(
+        functools.partial(attend_back_kernel, prompt_chunks, cont_chunks),
+        name="attend_back",
+        grid=(ctx_size,),
+        in_specs=[
+            smem,
+            whole(qkv_shape),
+            whole(head_shape),
+            whole(head_shape),
+            whole((ctx_size, 1, rows)),
+            whole(head_shape),
+            whole(head_shape),
+        ],
+        out_specs=whole(qkv_shape),
+        out_shape=shaped(*qkv_shape),
+        scratch_shapes=[pltpu.VMEM(head_shape, f32), pltpu.VMEM(head_shape, f32)],
+        compiler_params=params(40, "arbitrary"),
+    )(info, qkv, attended_grad, exact, log_total, cos_all, sin_all)
+    pieces = lax.all_to_all(pieces, "ctx", 0, 0, tiled=True)
+
+    keep, send, qkv_term = pl.pallas_call(
+        project_back_kernel,
+        name="project_back",
+        grid=(4,),
+        in_specs=[
+            pl.BlockSpec(piece, lambda t: (t, 0, 0, 0)),
+            place((rows, width)),
+            gain_spec,
+            whole((width, 3 * part)),
+        ],
+        out_specs=[kept((rows, width)), sent((rows, width)), whole((width, 3 * part))],
+        out_shape=[two, two, shaped(width, 3 * part)],
+        scratch_shapes=[pltpu.VMEM((width, 3 * part), f32)],
+        compiler_params=params(32, "arbitrary"),
+    )(pieces, x_all, gain_one, w_qkv)
+
+    in_grad, part_one = pl.pallas_call(
+        input_back_kernel,
+        name="input_back",
+        grid=(1,),
+        in_specs=sum_specs + [row_spec, row_spec, gain_spec],
+        out_specs=[row_spec, gain_spec],
+        out_shape=[full_row, gain_row],
+        compiler_params=params(24),
+    )(*exchange_sums(keep, send), x_own, middle_grad, gain_one)
+
+    qkv_term = lax.all_to_all(qkv_term.reshape(4, rows, 3 * part), "fsdp", 0, 0, tiled=True)
+    ff_sums = lax.psum((pair_term, down_term, out_term), "ctx")
+    qkv_sum = lax.psum(qkv_term, "ctx")
+    qkv_sum = (
+        qkv_sum.reshape(4, rows, 3, part).transpose(2, 1, 0, 3).reshape(3, rows, width).astype(f32)
+    )
+    gain_sums = lax.psum(
+        jnp.concatenate([part_one, part_two, part_three, part_four]), ("ctx", "fsdp")
+    )
+    return (
+        block_out[None],
+        in_grad[None],
+        qkv_sum[0],
+        qkv_sum[1],
+        qkv_sum[2],
+        ff_sums[2].astype(f32),
+        gain_sums[0],
+        gain_sums[1],
+        ff_sums[0][0].astype(f32),
+        ff_sums[0][1].astype(f32),
+        ff_sums[1].astype(f32),
+        gain_sums[2],
+        gain_sums[3],
+    )
+
+
 def solution(mesh):
-    return jax.shard_map(
-        shards,
-        mesh=mesh,
-        in_specs=(
-            P("fsdp", "ctx", None),
-            P("fsdp", "ctx", None),
-            P("fsdp", None),
-            P("fsdp", None),
-            P("fsdp", None),
-            P("fsdp", None),
-            P(),
-            P(),
-            P("fsdp", None),
-            P("fsdp", None),
-            P("fsdp", None),
-            P(),
-            P(),
-            P(),
-            P(),
-            P(),
-            P(),
-        ),
-        out_specs=(
-            P("fsdp", "ctx", None),
-            P("fsdp", "ctx", None),
-            P("fsdp", None),
-            P("fsdp", None),
-            P("fsdp", None),
-            P("fsdp", None),
-            P(),
-            P(),
-            P("fsdp", None),
-            P("fsdp", None),
-            P("fsdp", None),
-            P(),
-            P(),
-        ),
-        check_vma=False,
-    )
+    fsdp, ctx = mesh.shape["fsdp"], mesh.shape["ctx"]
+
+    def step(*args):
+        width, groups = args[0].shape[2], args[0].shape[0]
+        heads = width // HEAD
+        rows = args[0].shape[1] // ctx
+        paired = (
+            fsdp == 4
+            and groups == fsdp
+            and heads == ctx
+            and CONT % rows == 0
+            and (P_DEV * ctx) % rows == 0
+            and width // fsdp == rows
+        )
+        return jax.shard_map(
+            pair_shards if paired else shards,
+            mesh=mesh,
+            in_specs=IN_SPECS,
+            out_specs=OUT_SPECS,
+            check_vma=False,
+        )(*args)
+
+    return step

time: 1130 us -> 701 us (0.62)
  waiting for transfers between devices: 824 us -> 388 us
  Pallas kernels: 0 us -> 71.8 us
  matrix products: 83.8 us -> 15.4 us
  starting transfers between devices: 0.73 us -> 43.8 us
  local copies, waits for them, and re-layouts: 97.8 us -> 70 us
  other arithmetic: 46.4 us -> 30.4 us
  blocking collectives: 43.4 us -> 58.6 us
  loops' own time: 11.6 us -> 0 us
    reduce_scatter x4 -> x0, waiting for transfers between devices: 347 us -> none  [the longest x1 149 us: shards(): lax.psum_scatter(wide_term(lambda operand: operand).astype(jnp.bfloat16),...]
    all_gather x9 -> x0, waiting for transfers between devices: 300 us -> none  [the longest x1 68 us: shards(): lax.all_gather(values_local, 'ctx', axis=0, tiled=True)]
    ppermute x0 -> x20, waiting for transfers between devices: none -> 136 us  [the longest x8 124 us: y_swap(): return lax.ppermute(values, 'fsdp', [(i, i ^ 2) for i in range(4)])]
    all_to_all x0 -> x7, waiting for transfers between devices: none -> 95 us  [the longest x1 34.9 us: pair_shards(): qkv = lax.all_to_all(qkv, 'ctx', 0, 0, tiled=True)]
    pallas_call x0 -> x12, Pallas kernels: none -> 71.8 us  [the longest x1 18.2 us: pair_shards(): pl.pallas_call(functools.partial(attend_back_kernel, prompt_chunks, cont_...]
    dot_general x30 -> x4, matrix products: 83.8 us -> 15.4 us  [cross_dot_low(): lax.dot_general(operand, partner, (((0,), (0,)), ((), ())), preferred_ele...]
    all_to_all x0 -> x7, starting transfers between devices: none -> 33.8 us  [the longest x1 6.16 us: pair_shards(): qkv = lax.all_to_all(qkv, 'ctx', 0, 0, tiled=True)]
    all_to_all x0 -> x1, blocking collectives: none -> 18.1 us  [pair_shards(): attended = lax.all_to_all(mixed, 'ctx', 0, 0, tiled=True)]
  transfers between devices with their start and end apart: 14 -> 28, of which waited for: 13 -> 20; matrix products, arithmetic and copies ran while one was open for 12% -> 10% of each run, Pallas kernels for 0% -> 2%
where the time goes in v1:
time: 701 us; the launch traced here: 693 us
  waiting for transfers between devices  388 us (55%)
  Pallas kernels  71.8 us (10%)
  local copies, waits for them, and re-layouts  70 us (10%)
  blocking collectives  58.6 us (8%)
  starting transfers between devices  43.8 us (6%)
  other arithmetic  30.4 us (4%)
  matrix products  15.4 us (2%)
  between operations  14.9 us (2%)
    psum x1, waiting for transfers between devices, pair_shards(): qkv_sum = lax.psum(qkv_term, 'ctx')  157 us
    ppermute x8, waiting for transfers between devices, y_swap(): return lax.ppermute(values, 'fsdp', [(i, i ^ 2) for i in range(4)])  124 us
    psum x1, blocking collectives, pair_shards(): lax.psum(jnp.concatenate([part_one, part_two, part_three, part_four]), ('...  40.5 us
    unnamed x124, local copies, waits for them, and re-layouts  38.8 us
    all_to_all x1, waiting for transfers between devices, pair_shards(): qkv = lax.all_to_all(qkv, 'ctx', 0, 0, tiled=True)  34.9 us
    pallas_call x1, Pallas kernels, pair_shards(): pl.pallas_call(functools.partial(attend_back_kernel, prompt_chunks, cont_...  18.2 us
    all_to_all x1, blocking collectives, pair_shards(): attended = lax.all_to_all(mixed, 'ctx', 0, 0, tiled=True)  18.1 us
    all_to_all x1, waiting for transfers between devices, pair_shards(): pair_term = lax.all_to_all(pair_term, 'fsdp', 0, 0, tiled=True)  17.5 us
  transfers between devices with their start and end apart: 28, of which 20 were waited for; matrix products, arithmetic and copies ran while one was open for 10% of the time, Pallas kernels for 2%

profile of v1, /device:TPU:0, one launch (start us, length us, event | category | flops | bytes accessed | tf_op | source)
XLA Modules:
  0.0 693.0 jit_solution(1456884347267850181)
XLA Ops:
  7.2 3.0 collective-permute-start
  14.3 4.5 all-to-all-start
  19.3 3.6 collective-permute-done
  22.9 1.9 fusion.9
  28.3 11.0 %all-to-all-done = bf16[4,256,768]{1,2,0:T(8,128)(2,1)} async-done(((bf16[4,256,768]{1,2,0:T(8,128)(2,1)}), bf16[4,256,768]{1,2,0:T(8,128)(2,1)}, u32[]{:S(2)}, u32[]{:S(2)}) %all-to-all-start) | async-done | bytes 1572896 | tf_op jit(solution)/shard_map/all_to_all | solution.py:829
  39.3 2.6 copy.90
  44.3 3.0 project.1
  48.5 6.2 all-to-all-start.1
  56.5 34.9 %all-to-all-done.1.qkv_ref = bf16[8,3,256,128]{3,2,1,0:T(8,128)(2,1)S(1)} async-done(((bf16[8,3,256,128]{3,2,1,0:T(8,128)(2,1)}), bf16[8,3,256,128]{3,2,1,0:T(8,128)(2,1)S(1)}, u32[]{:S(2)}, u32[]{:S(2)}) %all-to-all-start.1) | async-done | bytes 1572896 | tf_op jit(solution)/shard_map/all_to_all | solution.py:858
  91.4 15.5 %attend.1 = (bf16[8,256,128]{2,1,0:T(8,128)(2,1)S(1)}, f32[8,256,128]{2,1,0:T(8,128)S(1)}, f32[8,1,256]{2,1,0:T(1,128)S(1)}) custom-call(s32[3]{0:T(128)S(1)} %pad_add_fusion.info_ref, bf16[8,3,256,128]{3,2,1,0:T(8,128)(2,1)S(1)} %all-to-all-done.1.qkv_ref), custom_call_target="tpu_custom_call" | custom-call | tf_op jit(solution)/shard_map/attend/pallas_call | solution.py:862
  106.9 18.1 %all_to_all.40.heads_ref = bf16[8,256,128]{2,1,0:T(8,128)(2,1)S(1)} all-to-all(bf16[8,256,128]{2,1,0:T(8,128)(2,1)S(1)} %get-tuple-element.42), channel_id=1, replica_groups=mesh['ctx'=8,'fsdp'=4] {'ctx'}, dimensions={0} | all-to-all | bytes 1048576 | tf_op jit(solution)/shard_map/all_to_all | solution.py:875
  125.0 2.2 mix_out.1
  129.1 2.5 copy.91
  131.6 2.5 copy.92
  134.1 2.1 pad_maximum_fusion
  136.2 1.8 copy.93
  138.0 5.2 all-to-all-start.3
  144.5 2.1 collective-permute-start.4
  146.6 42.0 %collective-permute-done.4.across_ref = bf16[256,1024]{1,0:T(8,128)(2,1)S(1)} collective-permute-done((bf16[256,1024]{1,0:T(8,128)(2,1)S(1)}, bf16[256,1024]{1,0:T(8,128)(2,1)S(1)}, u32[]{:S(2)}, u32[]{:S(2)}) %collective-permute-start.4) | collective-permute-done | bytes 524320 | tf_op jit(solution)/shard_map/ppermute | solution.py:392
  188.6 2.4 middle.1
  193.3 13.4 %collective-permute-done.5 = bf16[256,1024]{1,0:T(8,128)(2,1)} collective-permute-done((bf16[256,1024]{1,0:T(8,128)(2,1)}, bf16[256,1024]{1,0:T(8,128)(2,1)}, u32[]{:S(2)}, u32[]{:S(2)}) %collective-permute-start.5) | collective-permute-done | bytes 524320 | tf_op jit(solution)/shard_map/ppermute | solution.py:392
  206.7 3.1 fusion.16
  210.4 1.7 copy.95
  212.2 1.9 pad_maximum_fusion.3.x_ref
  214.2 6.0 ff.1
  220.7 2.3 collective-permute-done.8.received_ref
  224.0 13.5 %collective-permute-done.9.across_ref = bf16[256,1024]{1,0:T(8,128)(2,1)S(1)} collective-permute-done((bf16[256,1024]{1,0:T(8,128)(2,1)S(1)}, bf16[256,1024]{1,0:T(8,128)(2,1)S(1)}, u32[]{:S(2)}, u32[]{:S(2)}) %collective-permute-start.9) | collective-permute-done | bytes 524320 | tf_op jit(solution)/shard_map/ppermute | solution.py:392
  239.7 12.7 %collective-permute-done.10 = bf16[256,1024]{1,0:T(8,128)(2,1)S(1)} collective-permute-done((bf16[256,1024]{1,0:T(8,128)(2,1)S(1)}, bf16[256,1024]{1,0:T(8,128)(2,1)S(1)}, u32[]{:S(2)}, u32[]{:S(2)}) %collective-permute-start.10) | collective-permute-done | bytes 524320 | tf_op jit(solution)/shard_map/ppermute | solution.py:392
  252.4 1.9 collective-permute-done.12
  255.9 9.9 %ff_back.1 = (bf16[2,256,1024]{2,1,0:T(8,128)(2,1)S(1)}, bf16[2,256,1024]{2,1,0:T(8,128)(2,1)S(1)}, bf16[4,256,704]{2,1,0:T(8,128)(2,1)S(1)}, bf16[4,256,704]{2,1,0:T(8,128)(2,1)S(1)}) custom-call(bf16[4,256,1024]{2,1,0:T(8,128)(2,1)} %pad_maximum_fusion.4.grad_ref, bf16[1024,704]{1,0:T(8,128)(2,1)S(1)} %bitcast.99, bf16[1024,704]{1,0:T(8,128)(2,1)S(1)} %bitcast.101, ...), custom_call_target="tpu_custom_call" | custom-call | tf_op jit(solution)/shard_map/ff_back/pallas_call | solution.py:934
  266.0 2.5 collective-permute-done.13.received_ref
  269.4 13.3 %collective-permute-done.14.across_ref = bf16[256,1024]{1,0:T(8,128)(2,1)S(1)} collective-permute-done((bf16[256,1024]{1,0:T(8,128)(2,1)S(1)}, bf16[256,1024]{1,0:T(8,128)(2,1)S(1)}, u32[]{:S(2)}, u32[]{:S(2)}) %collective-permute-start.14) | collective-permute-done | bytes 524320 | tf_op jit(solution)/shard_map/ppermute | solution.py:392
  284.6 12.4 %collective-permute-done.15 = bf16[256,1024]{1,0:T(8,128)(2,1)S(1)} collective-permute-done((bf16[256,1024]{1,0:T(8,128)(2,1)S(1)}, bf16[256,1024]{1,0:T(8,128)(2,1)S(1)}, u32[]{:S(2)}, u32[]{:S(2)}) %collective-permute-start.15) | collective-permute-done | bytes 524320 | tf_op jit(solution)/shard_map/ppermute | solution.py:392
  297.1 1.9 collective-permute-done.17
  300.0 2.3 heads_back.1
  302.4 4.3 all-to-all-start.4
  307.4 3.7 fusion.8
  312.7 9.1 %all-to-all-done.4.grad_ref = bf16[8,256,128]{2,1,0:T(8,128)(2,1)} async-done(((bf16[8,256,128]{2,1,0:T(8,128)(2,1)}), bf16[8,256,128]{2,1,0:T(8,128)(2,1)}, u32[]{:S(2)}, u32[]{:S(2)}) %all-to-all-start.4) | async-done | bytes 524320 | tf_op jit(solution)/shard_map/all_to_all | solution.py:986
  325.6 18.2 %attend_back.1 = bf16[8,3,256,128]{3,2,1,0:T(8,128)(2,1)S(1)} custom-call(s32[3]{0:T(128)S(1)} %pad_add_fusion.info_ref, bf16[8,3,256,128]{3,2,1,0:T(8,128)(2,1)S(1)} %copy-done.3, bf16[8,256,128]{2,1,0:T(8,128)(2,1)} %all-to-all-done.4.grad_ref, f32[8,256,128]{2,1,0:T(8,128)S(1)} %copy-done.30, f32[8,1,256]{2,1,0:T(1,128)S(1)} %get-tuple-element.58.lse_ref, ...), custom_call_target="tpu_custom_call" | custom-call | tf_op jit(solution)/shard_map/attend_back/pallas_call | solution.py:992
  345.0 4.5 all-to-all-start.5
  349.6 4.9 bitcast_convert_fusion.2
  354.5 4.0 stack_reshape.18
  358.5 2.8 copy.100
  361.3 4.3 bitcast_convert_fusion.1
  365.6 4.0 stack_reshape.19
  369.6 1.7 copy.101
  371.4 1.8 pad_maximum_fusion.1
  373.2 13.0 %all-to-all-done.5.pieces_ref = bf16[8,3,256,128]{3,2,1,0:T(8,128)(2,1)} async-done(((bf16[8,3,256,128]{3,2,1,0:T(8,128)(2,1)}), bf16[8,3,256,128]{3,2,1,0:T(8,128)(2,1)}, u32[]{:S(2)}, u32[]{:S(2)}) %all-to-all-start.5) | async-done | bytes 1572896 | tf_op jit(solution)/shard_map/all_to_all | solution.py:1010
  386.2 4.7 all-to-all-start.7
  393.9 8.0 %project_back.1 = (bf16[2,256,1024]{2,1,0:T(8,128)(2,1)S(1)}, bf16[2,256,1024]{2,1,0:T(8,128)(2,1)S(1)}, bf16[1024,768]{1,0:T(8,128)(2,1)S(1)}) custom-call(bf16[8,3,256,128]{3,2,1,0:T(8,128)(2,1)} %all-to-all-done.5.pieces_ref, bf16[4,256,1024]{2,1,0:T(8,128)(2,1)S(1)} %copy-done.1, f32[1,1024]{1,0:T(1,128)S(1)} %bitcast.116, bf16[1024,768]{1,0:T(8,128)(2,1)S(1)} %bitcast.103), custom_call_target="tpu_custom_call" | custom-call | tf_op jit(solution)/shard_map/project_back/pallas_call | solution.py:1012
  405.0 2.6 copy.96
  407.6 17.5 %all-to-all-done.7 = bf16[4,2,256,704]{2,3,1,0:T(8,128)(2,1)} async-done(((bf16[4,2,256,704]{2,3,1,0:T(8,128)(2,1)}), bf16[4,2,256,704]{2,3,1,0:T(8,128)(2,1)}, u32[]{:S(2)}, u32[]{:S(2)}) %all-to-all-start.7) | async-done | bytes 2883616 | tf_op jit(solution)/shard_map/all_to_all | solution.py:963
  425.1 4.4 all-to-all-start.6
  430.3 4.6 bitcast_convert_fusion
  435.0 3.6 copy.102
  440.1 9.5 %all-to-all-done.6 = bf16[4,256,768]{1,2,0:T(8,128)(2,1)} async-done(((bf16[4,256,768]{1,2,0:T(8,128)(2,1)}), bf16[4,256,768]{1,2,0:T(8,128)(2,1)}, u32[]{:S(2)}, u32[]{:S(2)}) %all-to-all-start.6) | async-done | bytes 1572896 | tf_op jit(solution)/shard_map/all_to_all | solution.py:1038
  450.8 2.7 collective-permute-done.18.received_ref
  454.1 13.6 %collective-permute-done.19.across_ref = bf16[256,1024]{1,0:T(8,128)(2,1)S(1)} collective-permute-done((bf16[256,1024]{1,0:T(8,128)(2,1)S(1)}, bf16[256,1024]{1,0:T(8,128)(2,1)S(1)}, u32[]{:S(2)}, u32[]{:S(2)}) %collective-permute-start.19) | collective-permute-done | bytes 524320 | tf_op jit(solution)/shard_map/ppermute | solution.py:392
  469.4 40.5 %psum.37 = f32[4,1024]{1,0:T(4,128)S(1)} all-reduce(f32[4,1024]{1,0:T(4,128)S(1)} %pad_maximum_fusion.11), channel_id=1, replica_groups=mesh['ctx'=8,'fsdp'=4] {'ctx','fsdp'}, use_global_device_ids=true, to_apply=%region_9.10 | all-reduce | flops 4096 | bytes 32768 | tf_op jit(solution)/shard_map/psum | solution.py:1044
  510.5 157.3 %all-reduce.3.cloned.1.call-done = (bf16[3,256,4,256]{1,3,0,2:T(8,128)(2,1)}, bf16[256,1024]{1,0:T(8,128)(2,1)}, bf16[2,256,2816]{1,2,0:T(8,128)(2,1)}, bf16[704,1024]{1,0:T(8,128)(2,1)}) async-done(((bf16[3,256,4,256]{1,3,0,2:T(8,128)(2,1)}, bf16[256,1024]{1,0:T(8,128)(2,1)}, bf16[2,256,2816]{1,2,0:T(8,128)(2,1)}, bf16[704,1024]{1,0:T(8,128)(2,1)}), (bf16[3,256,4,256]{1,3,0,2:T(8,128)(2,1)}, ...) | async-done | bytes 6422544 | tf_op jit(solution)/shard_map/psum | solution.py:1040
  667.8 3.8 fusion
  671.6 3.4 copy.107
  675.0 2.2 copy.108
  682.8 1.9 convert_element_type.140
  (185 shorter events, 55.6 us)
Async XLA Ops:
  7.2 5.5 copy-start.46
  7.2 15.7 %collective-permute-start = (bf16[256,1024]{1,0:T(8,128)(2,1)}, bf16[256,1024]{1,0:T(8,128)(2,1)S(1)}, u32[]{:S(2)}, u32[]{:S(2)}) collective-permute-start(bf16[256,1024]{1,0:T(8,128)(2,1)} %bitcast.105), channel_id=1, source_target_pairs={{0,2},{1,3},{2,0},{3,1},{4,6},{5,7},{6,4},{7,5},{8,10},{9,11},{10,... | collective-permute-start | bytes 1572872 | tf_op jit(solution)/shard_map/ppermute | solution.py:392
  10.2 15.8 %collective-permute-start.1 = (bf16[256,1024]{1,0:T(8,128)(2,1)}, bf16[256,1024]{1,0:T(8,128)(2,1)S(1)}, u32[]{:S(2)}, u32[]{:S(2)}) collective-permute-start(bf16[256,1024]{1,0:T(8,128)(2,1)} %bitcast.106), channel_id=1, source_target_pairs={{0,1},{1,0},{2,3},{3,2},{4,5},{5,4},{6,7},{7,6},{8,9},{9,8},{10,11... | collective-permute-start | bytes 1572872 | tf_op jit(solution)/shard_map/ppermute | solution.py:388
  14.3 4.5 copy-start.56
  14.3 4.5 copy-start.54
  14.3 4.8 copy-start.55
  14.3 25.1 %all-to-all-start = ((bf16[4,256,768]{1,2,0:T(8,128)(2,1)}), bf16[4,256,768]{1,2,0:T(8,128)(2,1)}, u32[]{:S(2)}, u32[]{:S(2)}) async-start(bf16[4,256,768]{1,2,0:T(8,128)(2,1)} %bitcast.10), calls=%async_computation | async-start | bytes 3145728 | tf_op jit(solution)/shard_map/all_to_all | solution.py:829
  22.9 3.1 copy-start.50
  22.9 3.2 collective-permute-start.2
  22.9 3.9 copy-start.11
  28.3 19.1 %copy-start = (bf16[4,256,1024]{2,1,0:T(8,128)(2,1)}, bf16[4,256,1024]{2,1,0:T(8,128)(2,1)S(1)}, u32[]{:S(2)}) copy-start(bf16[4,256,1024]{2,1,0:T(8,128)(2,1)S(1)} %pad_maximum_fusion.2.x_ref) | copy-start | bytes 6291460
  28.3 13.6 %copy-start.33 = (f32[1024]{0:T(1024)S(1)}, f32[1024]{0:T(1024)}, u32[]{:S(2)}) copy-start(f32[1024]{0:T(1024)} %param.24) | copy-start | bytes 12292
  48.5 7.0 %copy-start.52 = (s32[4,2]{0,1:T(2,128)S(1)}, s32[4,2]{0,1:T(2,128)}, u32[]{:S(2)}) copy-start(s32[4,2]{0,1:T(2,128)} %param.32) | copy-start | bytes 100
  48.5 7.0 %copy-start.53 = (s32[4,2]{0,1:T(2,128)S(1)}, s32[4,2]{0,1:T(2,128)}, u32[]{:S(2)}) copy-start(s32[4,2]{0,1:T(2,128)} %param.34) | copy-start | bytes 100
  48.5 42.9 %all-to-all-start.1 = ((bf16[8,3,256,128]{3,2,1,0:T(8,128)(2,1)}), bf16[8,3,256,128]{3,2,1,0:T(8,128)(2,1)S(1)}, u32[]{:S(2)}, u32[]{:S(2)}) async-start(bf16[8,3,256,128]{3,2,1,0:T(8,128)(2,1)} %copy-done.6), calls=%async_computation.1 | async-start | bytes 3145728 | tf_op jit(solution)/shard_map/all_to_all | solution.py:858
  54.7 70.4 %copy-start.21 = (bf16[256,1024]{1,0:T(8,128)(2,1)S(1)}, bf16[256,1024]{1,0:T(8,128)(2,1)}, u32[]{:S(2)}) copy-start(bf16[256,1024]{1,0:T(8,128)(2,1)} %w_ref.3) | copy-start | bytes 1572868
  91.4 40.2 %copy-start.2 = (bf16[8,3,256,128]{3,2,1,0:T(8,128)(2,1)}, bf16[8,3,256,128]{3,2,1,0:T(8,128)(2,1)S(1)}, u32[]{:S(2)}) copy-start(bf16[8,3,256,128]{3,2,1,0:T(8,128)(2,1)S(1)} %all-to-all-done.1.qkv_ref) | copy-start | bytes 4718596
  106.9 20.4 %copy-start.29 = (f32[8,256,128]{2,1,0:T(8,128)}, f32[8,256,128]{2,1,0:T(8,128)S(1)}, u32[]{:S(2)}) copy-start(f32[8,256,128]{2,1,0:T(8,128)S(1)} %get-tuple-element.57.exact_ref) | copy-start | bytes 3145732
  129.1 14.2 %collective-permute-start.3 = (bf16[2,256,1024]{2,1,0:T(8,128)(2,1)}, bf16[2,256,1024]{2,1,0:T(8,128)(2,1)}, u32[]{:S(2)}, u32[]{:S(2)}) collective-permute-start(bf16[2,256,1024]{2,1,0:T(8,128)(2,1)} %get-tuple-element.44), channel_id=1, source_target_pairs={{0,1},{1,0},{2,3},{3,2},{4,5},{5,4},{6,7},{7,6},{8,9},{9,8},{10,11... | collective-permute-start | bytes 3145736 | tf_op jit(solution)/shard_map/ppermute | solution.py:388
  138.0 5.3 copy-start.19
  138.0 50.6 %copy-start.34 = (f32[1024]{0:T(1024)S(1)}, f32[1024]{0:T(1024)}, u32[]{:S(2)}) copy-start(f32[1024]{0:T(1024)} %param.25) | copy-start | bytes 12292
  138.0 50.6 %copy-start.35 = (f32[1024]{0:T(1024)S(1)}, f32[1024]{0:T(1024)}, u32[]{:S(2)}) copy-start(f32[1024]{0:T(1024)} %param.29) | copy-start | bytes 12292
  138.0 68.7 %all-to-all-start.3 = ((bf16[4,2,256,704]{2,3,1,0:T(8,128)(2,1)}), bf16[4,2,256,704]{2,3,1,0:T(8,128)(2,1)}, u32[]{:S(2)}, u32[]{:S(2)}) async-start(bf16[4,2,256,704]{2,3,1,0:T(8,128)(2,1)} %copy.93), calls=%async_computation.3 | async-start | bytes 5767168 | tf_op jit(solution)/shard_map/all_to_all | solution.py:832
  144.5 44.0 %collective-permute-start.4 = (bf16[256,1024]{1,0:T(8,128)(2,1)S(1)}, bf16[256,1024]{1,0:T(8,128)(2,1)S(1)}, u32[]{:S(2)}, u32[]{:S(2)}) collective-permute-start(bf16[256,1024]{1,0:T(8,128)(2,1)S(1)} %fusion.2), channel_id=1, source_target_pairs={{0,2},{1,3},{2,0},{3,1},{4,6},{5,7},{6,4},{7,5},{8,10},{9,11},{10,... | collective-permute-start | bytes 1572872 | tf_op jit(solution)/shard_map/ppermute | solution.py:392
  192.9 13.8 %collective-permute-start.5 = (bf16[256,1024]{1,0:T(8,128)(2,1)}, bf16[256,1024]{1,0:T(8,128)(2,1)}, u32[]{:S(2)}, u32[]{:S(2)}) collective-permute-start(bf16[256,1024]{1,0:T(8,128)(2,1)} %get-tuple-element.45), channel_id=1, source_target_pairs={{0,2},{1,3},{2,0},{3,1},{4,6},{5,7},{6,4},{7,5},{8,10},{9,11},{10,... | collective-permute-start | bytes 1572872 | tf_op jit(solution)/shard_map/ppermute | solution.py:392
  193.3 18.9 %collective-permute-start.6 = (bf16[256,1024]{1,0:T(8,128)(2,1)}, bf16[256,1024]{1,0:T(8,128)(2,1)}, u32[]{:S(2)}, u32[]{:S(2)}) collective-permute-start(bf16[256,1024]{1,0:T(8,128)(2,1)} %get-tuple-element.45), channel_id=1, source_target_pairs={{0,1},{1,0},{2,3},{3,2},{4,5},{5,4},{6,7},{7,6},{8,9},{9,8},{10,11... | collective-permute-start | bytes 1572872 | tf_op jit(solution)/shard_map/ppermute | solution.py:388
  206.7 5.5 collective-permute-start.7
  212.2 2.0 copy-start.8
  214.2 23.3 %copy-start.20 = (bf16[1,256,1024]{2,1,0:T(8,128)(2,1)S(1)}, bf16[1,256,1024]{2,1,0:T(8,128)(2,1)}, u32[]{:S(2)}) copy-start(bf16[1,256,1024]{2,1,0:T(8,128)(2,1)} %param.19) | copy-start | bytes 1572868
  214.2 23.3 %copy-start.36 = (f32[1024]{0:T(1024)S(1)}, f32[1024]{0:T(1024)}, u32[]{:S(2)}) copy-start(f32[1024]{0:T(1024)} %param.30) | copy-start | bytes 12292
  220.1 2.9 copy-start.37
  220.1 17.3 %copy-start.14 = (f32[256,1024]{1,0:T(8,128)S(1)}, f32[256,1024]{1,0:T(8,128)}, u32[]{:S(2)}) copy-start(f32[256,1024]{1,0:T(8,128)} %copy-done.13) | copy-start | bytes 3145732
  220.1 2.9 collective-permute-start.8
  223.2 14.3 %collective-permute-start.9 = (bf16[256,1024]{1,0:T(8,128)(2,1)S(1)}, bf16[256,1024]{1,0:T(8,128)(2,1)S(1)}, u32[]{:S(2)}, u32[]{:S(2)}) collective-permute-start(bf16[256,1024]{1,0:T(8,128)(2,1)S(1)} %fusion.3), channel_id=1, source_target_pairs={{0,2},{1,3},{2,0},{3,1},{4,6},{5,7},{6,4},{7,5},{8,10},{9,11},{10,... | collective-permute-start | bytes 1572872 | tf_op jit(solution)/shard_map/ppermute | solution.py:392
  239.0 16.9 %copy-start.31 = (bf16[256,1024]{1,0:T(8,128)(2,1)}, bf16[256,1024]{1,0:T(8,128)(2,1)S(1)}, u32[]{:S(2)}) copy-start(bf16[256,1024]{1,0:T(8,128)(2,1)S(1)} %get-tuple-element.50) | copy-start | bytes 1572868
  239.0 13.4 %collective-permute-start.10 = (bf16[256,1024]{1,0:T(8,128)(2,1)S(1)}, bf16[256,1024]{1,0:T(8,128)(2,1)S(1)}, u32[]{:S(2)}, u32[]{:S(2)}) collective-permute-start(bf16[256,1024]{1,0:T(8,128)(2,1)S(1)} %get-tuple-element.50), channel_id=1, source_target_pairs={{0,2},{1,3},{2,0},{3,1},{4,6},{5,7},{6,4},{7,5},{8,10},{9,11},{10,... | collective-permute-start | bytes 1572872 | tf_op jit(solution)/shard_map/ppermute | solution.py:392
  239.7 12.7 %collective-permute-start.11 = (bf16[256,1024]{1,0:T(8,128)(2,1)S(1)}, bf16[256,1024]{1,0:T(8,128)(2,1)S(1)}, u32[]{:S(2)}, u32[]{:S(2)}) collective-permute-start(bf16[256,1024]{1,0:T(8,128)(2,1)S(1)} %get-tuple-element.50), channel_id=1, source_target_pairs={{0,1},{1,0},{2,3},{3,2},{4,5},{5,4},{6,7},{7,6},{8,9},{9,8},{10,11... | collective-permute-start | bytes 1572872 | tf_op jit(solution)/shard_map/ppermute | solution.py:388
  252.3 3.5 copy-start.47
  252.3 1.9 collective-permute-start.12
  252.4 3.5 copy-start.48
  265.7 18.1 %copy-start.38 = (bf16[4,256,704]{2,1,0:T(8,128)(2,1)}, bf16[4,256,704]{2,1,0:T(8,128)(2,1)S(1)}, u32[]{:S(2)}) copy-start(bf16[4,256,704]{2,1,0:T(8,128)(2,1)S(1)} %get-tuple-element.69) | copy-start | bytes 4325380
  265.7 18.1 %copy-start.40 = (bf16[4,256,704]{2,1,0:T(8,128)(2,1)}, bf16[4,256,704]{2,1,0:T(8,128)(2,1)S(1)}, u32[]{:S(2)}) copy-start(bf16[4,256,704]{2,1,0:T(8,128)(2,1)S(1)} %get-tuple-element.68) | copy-start | bytes 4325380
  265.7 17.0 %copy-start.28 = (f32[256,1024]{1,0:T(8,128)S(1)}, f32[256,1024]{1,0:T(8,128)}, u32[]{:S(2)}) copy-start(f32[256,1024]{1,0:T(8,128)} %copy-done.27) | copy-start | bytes 3145732
  265.8 2.7 collective-permute-start.13
  268.7 14.0 %collective-permute-start.14 = (bf16[256,1024]{1,0:T(8,128)(2,1)S(1)}, bf16[256,1024]{1,0:T(8,128)(2,1)S(1)}, u32[]{:S(2)}, u32[]{:S(2)}) collective-permute-start(bf16[256,1024]{1,0:T(8,128)(2,1)S(1)} %fusion.4), channel_id=1, source_target_pairs={{0,2},{1,3},{2,0},{3,1},{4,6},{5,7},{6,4},{7,5},{8,10},{9,11},{10,... | collective-permute-start | bytes 1572872 | tf_op jit(solution)/shard_map/ppermute | solution.py:392
  283.9 15.4 %copy-start.25 = (f32[256,1024]{1,0:T(8,128)}, f32[256,1024]{1,0:T(8,128)S(1)}, u32[]{:S(2)}) copy-start(f32[256,1024]{1,0:T(8,128)S(1)} %get-tuple-element.61.middle_grad_ref) | copy-start | bytes 3145732
  283.9 13.2 %collective-permute-start.15 = (bf16[256,1024]{1,0:T(8,128)(2,1)S(1)}, bf16[256,1024]{1,0:T(8,128)(2,1)S(1)}, u32[]{:S(2)}, u32[]{:S(2)}) collective-permute-start(bf16[256,1024]{1,0:T(8,128)(2,1)S(1)} %get-tuple-element.56), channel_id=1, source_target_pairs={{0,2},{1,3},{2,0},{3,1},{4,6},{5,7},{6,4},{7,5},{8,10},{9,11},{10,... | collective-permute-start | bytes 1572872 | tf_op jit(solution)/shard_map/ppermute | solution.py:392
  284.6 12.4 %collective-permute-start.16 = (bf16[256,1024]{1,0:T(8,128)(2,1)S(1)}, bf16[256,1024]{1,0:T(8,128)(2,1)S(1)}, u32[]{:S(2)}, u32[]{:S(2)}) collective-permute-start(bf16[256,1024]{1,0:T(8,128)(2,1)S(1)} %get-tuple-element.56), channel_id=1, source_target_pairs={{0,1},{1,0},{2,3},{3,2},{4,5},{5,4},{6,7},{7,6},{8,9},{9,8},{10,11... | collective-permute-start | bytes 1572872 | tf_op jit(solution)/shard_map/ppermute | solution.py:388
  297.1 1.9 collective-permute-start.17
  302.4 19.4 %all-to-all-start.4 = ((bf16[8,256,128]{2,1,0:T(8,128)(2,1)}), bf16[8,256,128]{2,1,0:T(8,128)(2,1)}, u32[]{:S(2)}, u32[]{:S(2)}) async-start(bf16[8,256,128]{2,1,0:T(8,128)(2,1)} %heads_back.1), calls=%async_computation.4 | async-start | bytes 1048576 | tf_op jit(solution)/shard_map/all_to_all | solution.py:986
  345.0 41.2 %all-to-all-start.5 = ((bf16[8,3,256,128]{3,2,1,0:T(8,128)(2,1)}), bf16[8,3,256,128]{3,2,1,0:T(8,128)(2,1)}, u32[]{:S(2)}, u32[]{:S(2)}) async-start(bf16[8,3,256,128]{3,2,1,0:T(8,128)(2,1)} %copy-done.7), calls=%async_computation.5 | async-start | bytes 3145728 | tf_op jit(solution)/shard_map/all_to_all | solution.py:1010
  358.5 2.8 copy-start.39
  386.2 38.9 %all-to-all-start.7 = ((bf16[4,2,256,704]{2,3,1,0:T(8,128)(2,1)}), bf16[4,2,256,704]{2,3,1,0:T(8,128)(2,1)}, u32[]{:S(2)}, u32[]{:S(2)}) async-start(bf16[4,2,256,704]{2,3,1,0:T(8,128)(2,1)} %pad_maximum_fusion.1), calls=%async_computation.7 | async-start | bytes 5767168 | tf_op jit(solution)/shard_map/all_to_all | solution.py:963
  407.6 22.1 %copy-start.10 = (bf16[8,256,128]{2,1,0:T(8,128)(2,1)S(1)}, bf16[8,256,128]{2,1,0:T(8,128)(2,1)}, u32[]{:S(2)}) copy-start(bf16[8,256,128]{2,1,0:T(8,128)(2,1)} %copy-done.9) | copy-start | bytes 1572868
  407.6 22.7 %copy-start.32 = (bf16[256,1024]{1,0:T(8,128)(2,1)S(1)}, bf16[256,1024]{1,0:T(8,128)(2,1)}, u32[]{:S(2)}) copy-start(bf16[256,1024]{1,0:T(8,128)(2,1)} %copy-done.31) | copy-start | bytes 1572868
  425.1 24.5 %all-to-all-start.6 = ((bf16[4,256,768]{1,2,0:T(8,128)(2,1)}), bf16[4,256,768]{1,2,0:T(8,128)(2,1)}, u32[]{:S(2)}, u32[]{:S(2)}) async-start(bf16[4,256,768]{1,2,0:T(8,128)(2,1)} %copy.96), calls=%async_computation.6 | async-start | bytes 3145728 | tf_op jit(solution)/shard_map/all_to_all | solution.py:1038
  429.5 238.3 %all-reduce.3.cloned.1.call-start = ((), (), s32[]{:S(2)}) async-start(), calls=%async_computation.8 | async-start | bytes 12845056 | tf_op jit(solution)/shard_map/psum | solution.py:1040
  449.6 3.9 copy-start.17
  449.6 18.1 %copy-start.12 = (bf16[1,256,1024]{2,1,0:T(8,128)(2,1)S(1)}, bf16[1,256,1024]{2,1,0:T(8,128)(2,1)}, u32[]{:S(2)}) copy-start(bf16[1,256,1024]{2,1,0:T(8,128)(2,1)} %param.18) | copy-start | bytes 1572868
  449.6 18.1 %copy-start.26 = (f32[256,1024]{1,0:T(8,128)S(1)}, f32[256,1024]{1,0:T(8,128)}, u32[]{:S(2)}) copy-start(f32[256,1024]{1,0:T(8,128)} %copy-done.25) | copy-start | bytes 3145732
  450.8 2.7 collective-permute-start.18
  453.7 14.0 %collective-permute-start.19 = (bf16[256,1024]{1,0:T(8,128)(2,1)S(1)}, bf16[256,1024]{1,0:T(8,128)(2,1)S(1)}, u32[]{:S(2)}, u32[]{:S(2)}) collective-permute-start(bf16[256,1024]{1,0:T(8,128)(2,1)S(1)} %fusion.5), channel_id=1, source_target_pairs={{0,2},{1,3},{2,0},{3,1},{4,6},{5,7},{6,4},{7,5},{8,10},{9,11},{10,... | collective-permute-start | bytes 1572872 | tf_op jit(solution)/shard_map/ppermute | solution.py:392
  680.2 2.6 copy-start.44
  682.8 1.9 copy-start.45
  (21 other events, 24.9 us)
Sparse Core Ops, SparseCore 0:
  449.8 218.0 all-reduce.2

commit v2 on v1

--- a/solution.py
+++ b/solution.py
@@ -380,8 +380,8 @@
 )
 
 
-REL = (0, 2, 1, 3)
 MIB = 1 << 20
+PLACES = 4
 
 
 def core_swap(values):
@@ -392,17 +392,27 @@
     return lax.ppermute(values, "fsdp", [(i, i ^ 2) for i in range(4)])
 
 
-def gather_rows(own):
+def ctx_swap(values, bit):
+    size = lax.axis_size("ctx")
+    return lax.ppermute(values, "ctx", [(i, i ^ bit) for i in range(size)])
+
+
+def z_shift(values):
+    size = lax.axis_size("ctx")
+    return lax.ppermute(values, "ctx", [(i, (i + 2) % size) for i in range(size)])
+
+
+def tie(*values):
+    return lax.optimization_barrier(values)
+
+
+def after(value, *others):
+    return lax.optimization_barrier((value, others))[0]
+
+
+def far_rows(own):
     across = y_swap(own)
-    beside = core_swap(own)
-    corner = core_swap(across)
-    return jnp.stack([own, across, beside, corner])
-
-
-def exchange_sums(keep, send):
-    received = core_swap(send)
-    onward = (keep[1].astype(f32) + received[1].astype(f32)).astype(bf16)
-    return keep, received, y_swap(onward)
+    return across, core_swap(across)
 
 
 def params(limit_mib, *semantics):
@@ -411,36 +421,15 @@
     )
 
 
+def cost(microseconds):
+    return pl.CostEstimate(flops=int(microseconds * 3e8), bytes_accessed=0, transcendentals=0)
+
+
 def whole(shape):
     return pl.BlockSpec(shape, lambda *_: (0,) * len(shape))
 
 
-def place(shape):
-    return pl.BlockSpec((1,) + shape, lambda t: (t,) + (0,) * len(shape))
-
-
-def first_place(shape):
-    return pl.BlockSpec((1,) + shape, lambda *_: (0,) * (1 + len(shape)))
-
-
-def kept(shape):
-    return pl.BlockSpec((1,) + shape, lambda t: (jnp.minimum(t, 1),) + (0,) * len(shape))
-
-
-def sent(shape):
-    return pl.BlockSpec((1,) + shape, lambda t: (jnp.maximum(t - 2, 0),) + (0,) * len(shape))
-
-
-def put_partial(step, partial, keep_ref, send_ref):
-    rounded = partial.astype(bf16)
-
-    @pl.when(step < 2)
-    def _():
-        keep_ref[0] = rounded
-
-    @pl.when(step >= 2)
-    def _():
-        send_ref[0] = rounded
+SMEM = pl.BlockSpec(memory_space=pltpu.SMEM)
 
 
 def dot_nn(a, b):
@@ -463,10 +452,70 @@
     return values * cosine + pltpu.roll(values, HEAD // 2, 1) * sine
 
 
-def project_kernel(x_ref, gain_ref, w_ref, cos_ref, sin_ref, out_ref):
-    x = x_ref[0].astype(f32)
-    normed = (x * inverse_rms(x) * gain_ref[...]).astype(bf16)
-    product = dot_nn(normed, w_ref[...])
+def choose(step, refs, target):
+    for index, ref in enumerate(refs):
+
+        @pl.when(step == index)
+        def _(ref=ref):
+            target[...] = ref[...]
+
+
+def columns_of(me_ref, place, rows):
+    return pl.ds(pl.multiple_of((me_ref[0] ^ place) * rows, rows), rows)
+
+
+def split_qkv_kernel(me_ref, q_ref, k_ref, v_ref, *out_refs):
+    part = out_refs[0].shape[1] // 3
+    for place, out_ref in enumerate(out_refs):
+        for kind, ref in enumerate((q_ref, k_ref, v_ref)):
+            out_ref[:, kind * part : (kind + 1) * part] = ref[:, columns_of(me_ref, place, part)]
+
+
+def pair_columns(half):
+    main = half // HEAD * HEAD
+    rest = half - main
+    return (
+        (0, 0, 0, main),
+        (1, 0, main, main),
+        (0, main, 2 * main, rest),
+        (1, main, 2 * main + rest, rest),
+    )
+
+
+def split_ff_kernel(
+    me_ref, gate_ref, up_ref, down_ref, own_ref, own_sent, beside_ref, beside_sent, down_sent
+):
+    half = own_ref.shape[-1] // 2
+    for me in range(PLACES):
+
+        @pl.when(me_ref[0] == me)
+        def _(me=me):
+            for place in range(PLACES):
+                target = own_ref if place % 2 == 0 else beside_ref
+                for kind, start, where, size in pair_columns(half):
+                    first = (me ^ place) * half + start
+                    target[place // 2, :, where : where + size] = (gate_ref, up_ref)[kind][
+                        :, first : first + size
+                    ]
+
+    side = me_ref[1] % 2
+    own_sent[...] = own_ref[1 - side]
+    beside_sent[...] = beside_ref[1 - side]
+    columns = down_sent.shape[1]
+    down_sent[...] = down_ref[:, pl.ds(pl.multiple_of(side * columns, columns), columns)]
+
+
+def project_kernel(
+    me_ref, x0, x1, x2, x3, gain_ref, w0, w1, w2, w3, cos_ref, sin_ref, out_ref, x_scr, normed_scr
+):
+    choose(pl.program_id(0), (x0, x1, x2, x3), x_scr)
+    x = x_scr[...].astype(f32)
+    normed_scr[...] = (x * inverse_rms(x) * gain_ref[...]).astype(bf16)
+    rows = w0.shape[0]
+    product = sum(
+        dot_nn(normed_scr[:, columns_of(me_ref, place, rows)], w[...])
+        for place, w in enumerate((w0, w1, w2, w3))
+    )
     heads = out_ref.shape[0]
     for kind in range(3):
         for head in range(heads):
@@ -477,12 +526,15 @@
             out_ref[head, kind] = part.astype(bf16)
 
 
-def key_span(chunk, prompt_chunks, cont_chunks):
+def chunk_facts(chunk, rows, prompt_chunks, cont_chunks, info_ref):
+    beyond = jnp.maximum(chunk - prompt_chunks, 0)
     in_cont = chunk >= prompt_chunks
-    first = jnp.where(
-        in_cont, prompt_chunks + (chunk - prompt_chunks) // cont_chunks * cont_chunks, 0
-    )
-    return first, jnp.where(in_cont, prompt_chunks, 0)
+    slot = beyond // cont_chunks
+    first = jnp.where(in_cont, prompt_chunks + slot * cont_chunks, 0)
+    ahead = jnp.where(in_cont, prompt_chunks, 0)
+    start = jnp.where(in_cont, beyond % cont_chunks, chunk) * rows
+    limit = jnp.where(in_cont, info_ref[1 + slot], info_ref[0])
+    return first, ahead, start, limit
 
 
 def attend_kernel(
@@ -492,8 +544,7 @@
     rows = qkv_ref.shape[2]
     scale = LOG2E / math.sqrt(HEAD)
     query = qkv_ref[chunk, 0]
-    prompt_size = info_ref[0]
-    first, ahead = key_span(chunk, prompt_chunks, cont_chunks)
+    first, ahead, start, limit = chunk_facts(chunk, rows, prompt_chunks, cont_chunks, info_ref)
     key_place = lax.broadcasted_iota(jnp.int32, (rows, rows), 0)
     query_place = lax.broadcasted_iota(jnp.int32, (rows, rows), 1)
 
@@ -508,7 +559,7 @@
         return new_top, total, mixed
 
     def prompt_visit(key_chunk, state):
-        bias = jnp.where(key_chunk * rows + key_place < prompt_size, 0.0, masked_out)
+        bias = jnp.where(key_chunk * rows + key_place < info_ref[0], 0.0, masked_out)
         return visit(key_chunk, bias, state)
 
     def own_visit(key_chunk, state):
@@ -522,16 +573,8 @@
     state = visit(chunk, jnp.where(key_place <= query_place, 0.0, masked_out), state)
     state = lax.fori_loop(0, ahead, prompt_visit, state)
     top, total, mixed = lax.fori_loop(first, chunk, own_visit, state)
-    slot = jnp.maximum(chunk - prompt_chunks, 0) // cont_chunks
-    start = jnp.where(
-        chunk < prompt_chunks,
-        chunk,
-        jnp.maximum(chunk - prompt_chunks, 0) % cont_chunks,
-    )
-    limit = jnp.where(chunk < prompt_chunks, prompt_size, info_ref[1 + slot])
-    valid = start * rows + lax.broadcasted_iota(jnp.int32, (1, rows), 1) < limit
-    mixed = jnp.where(valid, mixed / total, 0.0)
-    settled = mixed.T
+    valid = start + lax.broadcasted_iota(jnp.int32, (1, rows), 1) < limit
+    settled = jnp.where(valid, mixed / total, 0.0).T
     out_ref[chunk] = settled.astype(bf16)
     exact_ref[chunk] = settled
     lse_ref[chunk] = top + jnp.log2(total)
@@ -556,18 +599,10 @@
     rows = qkv_ref.shape[2]
     scale = LOG2E / math.sqrt(HEAD)
     query = qkv_ref[chunk, 0]
-    prompt_size = info_ref[0]
-    first, ahead = key_span(chunk, prompt_chunks, cont_chunks)
+    first, ahead, start, limit = chunk_facts(chunk, rows, prompt_chunks, cont_chunks, info_ref)
     key_place = lax.broadcasted_iota(jnp.int32, (rows, rows), 0)
     query_place = lax.broadcasted_iota(jnp.int32, (rows, rows), 1)
-    slot = jnp.maximum(chunk - prompt_chunks, 0) // cont_chunks
-    start = jnp.where(
-        chunk < prompt_chunks,
-        chunk,
-        jnp.maximum(chunk - prompt_chunks, 0) % cont_chunks,
-    )
-    limit = jnp.where(chunk < prompt_chunks, prompt_size, info_ref[1 + slot])
-    valid = start * rows + lax.broadcasted_iota(jnp.int32, (rows, 1), 0) < limit
+    valid = start + lax.broadcasted_iota(jnp.int32, (rows, 1), 0) < limit
     grad_full = jnp.where(valid, grad_ref[chunk].astype(f32), 0.0)
     grad = grad_full.astype(bf16)
     delta = jnp.sum((grad_full * exact_ref[chunk]).T, axis=0, keepdims=True)
@@ -589,7 +624,7 @@
         return query_sum + dot_tn(key, score_grad)
 
     def prompt_visit(key_chunk, query_sum):
-        bias = jnp.where(key_chunk * rows + key_place < prompt_size, 0.0, masked_out)
+        bias = jnp.where(key_chunk * rows + key_place < info_ref[0], 0.0, masked_out)
         return visit(key_chunk, bias, query_sum)
 
     def own_visit(key_chunk, query_sum):
@@ -615,36 +650,75 @@
             out_ref[key_chunk, 2] = value_sum[key_chunk].astype(bf16)
 
 
-def mix_out_kernel(heads_ref, w_ref, keep_ref, send_ref):
+def mix_out_kernel(near_ref, far_ref, w_near_ref, w_far_ref, keep_ref, send_ref):
+    heads = near_ref.shape[0] // PLACES
+    part = heads * HEAD
+    for step in range(2):
+        total = 0.0
+        for ref, w_ref in ((near_ref, w_near_ref), (far_ref, w_far_ref)):
+            both = jnp.concatenate([ref[step * heads + j] for j in range(heads)], axis=1)
+            total = total + dot_nn(both, w_ref[...])
+        if step == 0:
+            keep_ref[...] = total
+        else:
+            send_ref[...] = total.astype(bf16)
+
+
+def heads_back_kernel(own_ref, beside_ref, w_near_ref, w_far_ref, near_ref, far_ref):
+    heads = near_ref.shape[0] // 2
+    for step, ref in enumerate((own_ref, beside_ref)):
+        for w_ref, out_ref in ((w_near_ref, near_ref), (w_far_ref, far_ref)):
+            both = dot_nt(ref[...], w_ref[...]).astype(bf16)
+            for head in range(heads):
+                out_ref[step * heads + head] = both[:, head * HEAD : (head + 1) * HEAD]
+
+
+def project_back_kernel(me_ref, pieces_ref, w0, w1, w2, w3, keep_ref, send_ref):
     step = pl.program_id(0)
-    both = jnp.concatenate([heads_ref[j] for j in range(heads_ref.shape[0])], axis=1)
-    put_partial(step, dot_nn(both, w_ref[...]), keep_ref, send_ref)
-
-
-def middle_kernel(
-    keep_ref, received_ref, across_ref, x_ref, two_ref, three_ref, branch_ref, middle_ref, input_ref
-):
-    branch = (
-        keep_ref[0].astype(f32) + received_ref[0].astype(f32) + across_ref[...].astype(f32)
-    )
+    heads = pieces_ref.shape[0]
+    pieces = jnp.concatenate(
+        [pieces_ref[head, kind] for kind in range(3) for head in range(heads)], axis=1
+    )
+    rows = w0.shape[0]
+    for target, parity in ((keep_ref, 0), (send_ref, 1)):
+
+        @pl.when(step % 2 == parity)
+        def _(target=target):
+            for place, w in enumerate((w0, w1, w2, w3)):
+                target[0, :, columns_of(me_ref, place, rows)] = dot_nt(pieces, w[...]).astype(bf16)
+
+
+def project_grad_kernel(me_ref, pieces_ref, own_ref, other_ref, gain_ref, out_ref, total):
+    step = pl.program_id(0)
+    side = me_ref[1] % 2
+
+    def add(ref, chunk):
+        x = ref[...].astype(f32)
+        normed = (x * inverse_rms(x) * gain_ref[...]).astype(bf16)
+        pieces = jnp.concatenate([pieces_ref[chunk, kind] for kind in range(3)], axis=1)
+        return dot_tn(normed, pieces)
+
+    term = add(own_ref.at[step], 2 * step + side) + add(other_ref.at[step], 2 * step + 1 - side)
+
+    @pl.when(step == 0)
+    def _():
+        total[...] = term
+
+    @pl.when(step > 0)
+    def _():
+        total[...] += term
+
+    @pl.when(step == pl.num_programs(0) - 1)
+    def _():
+        spread_rows(me_ref, total, [out_ref])
+
+
+def middle_kernel(keep_ref, received_ref, x_ref, two_ref, three_ref, branch_ref, middle_ref, input_ref):
+    branch = keep_ref[...] + received_ref[...].astype(f32)
     middle = x_ref[...].astype(f32) + branch * inverse_rms(branch) * two_ref[...]
     branch_ref[...] = branch
     middle_ref[...] = middle
     input_ref[...] = (middle * inverse_rms(middle) * three_ref[...]).astype(bf16)
-
-
-def ff_kernel(x_ref, gate_ref, up_ref, down_ref, keep_ref, send_ref, slope_ref, swish_ref, hidden_ref):
-    step = pl.program_id(0)
-    x = x_ref[0]
-    gate = dot_nn(x, gate_ref[...])
-    upward = dot_nn(x, up_ref[...])
-    sigma = 1.0 / (1.0 + jnp.exp(-gate))
-    swish = gate * sigma
-    hidden = (swish * upward).astype(bf16)
-    slope_ref[0] = (upward * sigma * (1.0 + gate * (1.0 - sigma))).astype(bf16)
-    swish_ref[0] = swish.astype(bf16)
-    hidden_ref[0] = hidden
-    put_partial(step, dot_nn(hidden, down_ref[...]), keep_ref, send_ref)
 
 
 def norm_back_parts(values, gain, upstream):
@@ -656,32 +730,18 @@
 
 
 def turnaround_kernel(
-    keep_ref, received_ref, across_ref, middle_ref, grad_ref, four_ref, out_ref, back_ref, gain_ref
+    keep_ref, received_ref, middle_ref, grad_ref, four_ref, out_ref, back_ref, gain_ref
 ):
-    ff_out = keep_ref[0].astype(f32) + received_ref[0].astype(f32) + across_ref[...].astype(f32)
+    ff_out = keep_ref[...] + received_ref[...].astype(f32)
     out_ref[...] = (middle_ref[...] + ff_out * inverse_rms(ff_out) * four_ref[...]).astype(bf16)
     value_grad, gain = norm_back_parts(ff_out, four_ref[...], grad_ref[...].astype(f32))
     back_ref[...] = value_grad.astype(bf16)
     gain_ref[...] = gain
 
 
-def ff_back_kernel(
-    grad_ref, gate_ref, up_ref, down_ref, slope_ref, swish_ref, keep_ref, send_ref, gate_grad_ref, up_grad_ref
-):
-    step = pl.program_id(0)
-    hidden_grad = dot_nt(grad_ref[0], down_ref[...])
-    gate_grad = (hidden_grad * slope_ref[0].astype(f32)).astype(bf16)
-    up_grad = (hidden_grad * swish_ref[0].astype(f32)).astype(bf16)
-    gate_grad_ref[0] = gate_grad
-    up_grad_ref[0] = up_grad
-    partial = dot_nt(gate_grad, gate_ref[...]) + dot_nt(up_grad, up_ref[...])
-    put_partial(step, partial, keep_ref, send_ref)
-
-
 def branch_back_kernel(
     keep_ref,
     received_ref,
-    across_ref,
     middle_ref,
     branch_ref,
     grad_ref,
@@ -692,44 +752,12 @@
     gain_two_ref,
     gain_three_ref,
 ):
-    input_grad = keep_ref[0].astype(f32) + received_ref[0].astype(f32) + across_ref[...].astype(f32)
+    input_grad = keep_ref[...] + received_ref[...].astype(f32)
     middle_part, gain_three_ref[...] = norm_back_parts(middle_ref[...], three_ref[...], input_grad)
     middle_grad = grad_ref[...].astype(f32) + middle_part
     middle_grad_ref[...] = middle_grad
     branch_grad, gain_two_ref[...] = norm_back_parts(branch_ref[...], two_ref[...], middle_grad)
     branch_grad_ref[...] = branch_grad.astype(bf16)
-
-
-def heads_back_kernel(grad_ref, w_ref, out_ref):
-    both = dot_nt(grad_ref[0], w_ref[...]).astype(bf16)
-    for head in range(out_ref.shape[0]):
-        out_ref[head] = both[:, head * HEAD : (head + 1) * HEAD]
-
-
-def project_back_kernel(
-    pieces_ref, x_ref, gain_ref, w_ref, keep_ref, send_ref, grad_ref, total
-):
-    step = pl.program_id(0)
-    heads = pieces_ref.shape[0]
-    pieces = jnp.concatenate(
-        [pieces_ref[head, kind] for kind in range(3) for head in range(heads)], axis=1
-    )
-    put_partial(step, dot_nt(pieces, w_ref[...]), keep_ref, send_ref)
-    x = x_ref[0].astype(f32)
-    normed = (x * inverse_rms(x) * gain_ref[...]).astype(bf16)
-    term = dot_tn(normed, pieces)
-
-    @pl.when(step == 0)
-    def _():
-        total[...] = term
-
-    @pl.when(step > 0)
-    def _():
-        total[...] += term
-
-    @pl.when(step == pl.num_programs(0) - 1)
-    def _():
-        grad_ref[...] = total[...].astype(bf16)
 
 
 def input_back_kernel(
@@ -738,6 +766,405 @@
     normed_grad = keep_ref[0].astype(f32) + received_ref[0].astype(f32) + across_ref[...].astype(f32)
     part, gain_ref[...] = norm_back_parts(x_ref[...].astype(f32), one_ref[...], normed_grad)
     out_ref[...] = middle_grad_ref[...] + part
+
+
+def far_columns(side, width, first, second):
+    half = width // 2
+    for place, ref in ((side, first), (1 - side, second)):
+        yield pl.ds(pl.multiple_of(place * half, half), half), ref
+
+
+def put_rows(scr, place_major, me_ref, *refs):
+    rows, width = refs[0].shape
+    size = width // PLACES
+    for index, ref in enumerate(refs):
+        where = slice(index * rows, (index + 1) * rows)
+        if place_major:
+            for place in range(PLACES):
+                scr[where, place * size : (place + 1) * size] = ref[:, columns_of(me_ref, place, size)]
+        else:
+            scr[where, :] = ref[...]
+
+
+def pair_product(x_scr, weights):
+    size = x_scr.shape[1] // PLACES
+    return sum(
+        dot_nn(x_scr[:, place * size : (place + 1) * size], w)
+        for place, w in enumerate(weights)
+    )
+
+
+def gate_parts(pair, half):
+    def parts(gate, upward):
+        sigma = 1.0 / (1.0 + jnp.exp(-gate))
+        swish = gate * sigma
+        slope = upward * sigma * (1.0 + gate * (1.0 - sigma))
+        return swish, slope, (swish * upward).astype(bf16)
+
+    main = half // HEAD * HEAD
+    rest = half - main
+    body = parts(pair[:, :main], pair[:, main : 2 * main])
+    edge = pair[:, 2 * main :]
+    edge_swish, edge_slope, edge_hidden = parts(edge, pltpu.roll(edge, rest, 1))
+    lane = lax.broadcasted_iota(jnp.int32, edge.shape, 1)
+    edge_factor = jnp.where(lane < rest, edge_slope, pltpu.roll(edge_swish, rest, 1))
+    return body, edge_factor, edge_hidden
+
+
+def put_hidden(ref, body, edge, main):
+    rows = ref.shape[1]
+    for row in range(2):
+        where = slice(row * rows, (row + 1) * rows)
+        ref[row, :, :main] = body[where]
+        ref[row, :, main:] = edge[where]
+
+
+def ff_kernel(
+    me_ref,
+    own_ref,
+    beside_ref,
+    w0,
+    w1,
+    w2y,
+    w2x,
+    w3y,
+    w3x,
+    down_near,
+    down_y,
+    down_x,
+    keep_ref,
+    send_ref,
+    saved_ref,
+    hidden_ref,
+    x_scr,
+    pair_scr,
+    hidden_scr,
+    total,
+):
+    turn_index = pl.program_id(0)
+    side = me_ref[1] % 2
+    block = turn_index ^ side
+    width = x_scr.shape[1]
+    half = down_near.shape[0]
+    main = half // HEAD * HEAD
+
+    @pl.when(turn_index == 0)
+    def _():
+        put_rows(x_scr, True, me_ref, own_ref, beside_ref)
+        pair_scr[...] = pair_product(x_scr, (w0[0], w1[0], w2y[...], w3y[...]))
+
+    @pl.when(turn_index == 1)
+    def _():
+        pair_scr[...] = pair_product(x_scr, (w0[0], w1[0], w2x[...], w3x[...]))
+
+    (swish, slope, hidden), edge_factor, edge_hidden = gate_parts(pair_scr[...], half)
+    saved_ref[0, :, :main] = slope.astype(bf16)
+    saved_ref[0, :, main : 2 * main] = swish.astype(bf16)
+    saved_ref[0, :, 2 * main :] = edge_factor.astype(bf16)
+    hidden_scr[:, :main] = hidden
+    hidden_scr[:, main:] = edge_hidden
+
+    def add_term(columns, term):
+        @pl.when(turn_index == 0)
+        def _():
+            total[:, columns] = term
+
+        @pl.when(turn_index == 1)
+        def _():
+            total[:, columns] += term
+
+    @pl.when(block == 0)
+    def _():
+        put_hidden(hidden_ref, hidden, edge_hidden, main)
+        add_term(slice(None), dot_nn(hidden_scr[:, :half], down_near[...]))
+
+    @pl.when(block == 1)
+    def _():
+        for columns, down in far_columns(side, width, down_y, down_x):
+            add_term(columns, dot_nn(hidden_scr[:, :half], down[...]))
+
+    @pl.when(turn_index == 1)
+    def _():
+        rows = keep_ref.shape[0]
+        keep_ref[...] = total[:rows]
+        send_ref[...] = total[rows:].astype(bf16)
+
+
+def put_pair_grad(target, hidden_grad, factors, half):
+    main = half // HEAD * HEAD
+    edge = hidden_grad[:, main:]
+    edge = jnp.concatenate([edge, edge], axis=1)
+    for values, start in ((hidden_grad[:, :main], 0), (hidden_grad[:, :main], main), (edge, 2 * main)):
+        columns = slice(start, start + values.shape[1])
+        target[:, columns] = (values * factors[:, columns].astype(f32)).astype(bf16)
+
+
+def ff_back_kernel(
+    me_ref,
+    own_ref,
+    beside_ref,
+    w0,
+    w1,
+    w2y,
+    w2x,
+    w3y,
+    w3x,
+    down_near,
+    down_y,
+    down_x,
+    saved_ref,
+    keep_ref,
+    send_ref,
+    pair_ref,
+    grad_scr,
+    hidden_scr,
+    pair_scr,
+    total,
+):
+    turn_index = pl.program_id(0)
+    side = me_ref[1] % 2
+    block = turn_index ^ side
+    width = grad_scr.shape[1]
+    half = down_near.shape[0]
+    rows = keep_ref.shape[0]
+
+    @pl.when(turn_index == 0)
+    def _():
+        put_rows(grad_scr, False, me_ref, own_ref, beside_ref)
+
+    @pl.when(block == 0)
+    def _():
+        hidden_scr[...] = dot_nt(grad_scr[...], down_near[...])
+
+    @pl.when(block == 1)
+    def _():
+        hidden_scr[...] = sum(
+            dot_nt(grad_scr[:, columns], down[...])
+            for columns, down in far_columns(side, width, down_y, down_x)
+        )
+
+    put_pair_grad(pair_scr, hidden_scr[...], saved_ref.at[0], half)
+
+    @pl.when(block == 0)
+    def _():
+        for row in range(2):
+            pair_ref[row] = pair_scr[row * rows : (row + 1) * rows]
+
+    size = width // PLACES
+    for index, far in enumerate(((w2y, w3y), (w2x, w3x))):
+
+        @pl.when(turn_index == index)
+        def _(index=index, far=far):
+            for place, w in enumerate((w0[0], w1[0], far[0][...], far[1][...])):
+                term = dot_nt(pair_scr[...], w)
+                columns = columns_of(me_ref, place, size)
+                if index == 0:
+                    total[:, place * size : (place + 1) * size] = term
+                else:
+                    term = term + total[:, place * size : (place + 1) * size]
+                    keep_ref[:, columns] = term[:rows]
+                    send_ref[:, columns] = term[rows:].astype(bf16)
+
+
+def ff_far_kernel(
+    me_ref,
+    x2_ref,
+    x3_ref,
+    grad2_ref,
+    grad3_ref,
+    w0,
+    w1,
+    w2y,
+    w2x,
+    w3y,
+    w3x,
+    down_near,
+    hidden_ref,
+    pair_ref,
+    x_scr,
+    pair_scr,
+    factor_scr,
+):
+    side = me_ref[1] % 2
+    half = down_near.shape[0]
+    main = half // HEAD * HEAD
+    rows = x2_ref.shape[0]
+    put_rows(x_scr, True, me_ref, x2_ref, x3_ref)
+    for index, far in enumerate(((w2y, w3y), (w2x, w3x))):
+
+        @pl.when(side == index)
+        def _(far=far):
+            pair_scr[...] = pair_product(x_scr, (w0[0], w1[0], far[0][...], far[1][...]))
+
+    (swish, slope, hidden), edge_factor, edge_hidden = gate_parts(pair_scr[...], half)
+    put_hidden(hidden_ref, hidden, edge_hidden, main)
+    factor_scr[:, :main] = slope.astype(bf16)
+    factor_scr[:, main : 2 * main] = swish.astype(bf16)
+    factor_scr[:, 2 * main :] = edge_factor.astype(bf16)
+    put_rows(x_scr, False, me_ref, grad2_ref, grad3_ref)
+    hidden_grad = dot_nt(x_scr[...], down_near[...])
+    for row in range(2):
+        where = slice(row * rows, (row + 1) * rows)
+        put_pair_grad(pair_ref.at[row], hidden_grad[where], factor_scr.at[where], half)
+
+
+def piece_height(me_ref, ahead):
+    size = 4
+    return (me_ref[1] // 2 + ahead) % size
+
+
+def piece_owner(me_ref, other_x, ahead):
+    return (me_ref[1] % 2 ^ other_x) + 2 * piece_height(me_ref, ahead)
+
+
+def spread_rows(me_ref, total, refs, columns=slice(None), contiguous=False):
+    across = len(refs)
+    for other_x, ref in enumerate(refs):
+        shards, piece_rows = ref.shape[1:3]
+        for ahead in range(4):
+            owner = (
+                piece_owner(me_ref, other_x, ahead) if across == 2 else piece_height(me_ref, ahead)
+            )
+            for shard in range(shards):
+                block = owner * shards + shard if contiguous else shard * 4 * across + owner
+                start = pl.multiple_of(block * piece_rows, 8)
+                ref[ahead, shard, :, columns] = total[pl.ds(start, piece_rows), :].astype(bf16)
+
+
+def weight_grads_kernel(sources, me_ref, *refs):
+    lefts, rights = [], []
+    for heads_layout, _ in sources:
+        lefts.append(refs[:4])
+        count = 1 if heads_layout else 2
+        rights.append(refs[4 : 4 + count])
+        refs = refs[4 + count :]
+    outs, (left_scr, head_scr), totals = refs[:2], refs[2:4], refs[4:]
+    step = pl.program_id(0)
+    for (heads_layout, _), left, right, total in zip(sources, lefts, rights, totals, strict=True):
+        choose(step, left, left_scr)
+        columns = total.shape[1]
+        if heads_layout:
+            heads = right[0].shape[0] // PLACES
+            for head in range(heads):
+                head_scr[:, head * HEAD : (head + 1) * HEAD] = right[0][step * heads + head]
+        for index in range(PLACES):
+
+            @pl.when(step == index)
+            def _(index=index, right=right, total=total, columns=columns, heads_layout=heads_layout):
+                if heads_layout:
+                    operand = head_scr[...]
+                else:
+                    operand = right[index // 2][index % 2, :, :columns]
+                term = dot_tn(left_scr[...], operand)
+                if index == 0:
+                    total[...] = term
+                else:
+                    total[...] += term
+
+    @pl.when(step == PLACES - 1)
+    def _():
+        first = 0
+        for (_, contiguous), total in zip(sources, totals, strict=True):
+            columns = slice(first, first + total.shape[1])
+            spread_rows(me_ref, total, outs, columns, contiguous)
+            first += total.shape[1]
+
+
+def weight_grads(me, name, expected, sources):
+    rows, width = sources[0][0][0].shape
+    specs, operands, kinds, columns = [SMEM], [me], [], []
+    for lefts, rights, count, contiguous in sources:
+        operands += [*lefts, *rights]
+        specs += [whole(value.shape) for value in (*lefts, *rights)]
+        kinds.append((len(rights) == 1, contiguous))
+        columns.append(count)
+    piece = (4, PLACES, width // PLACES // 8, sum(columns))
+    return pl.pallas_call(
+        functools.partial(weight_grads_kernel, tuple(kinds)),
+        name=name,
+        cost_estimate=cost(expected),
+        grid=(PLACES,),
+        in_specs=specs,
+        out_specs=[whole(piece)] * 2,
+        out_shape=[shaped(*piece)] * 2,
+        scratch_shapes=[pltpu.VMEM((rows, width), bf16), pltpu.VMEM((rows, 2 * HEAD), bf16)]
+        + [pltpu.VMEM((width, count), f32) for count in columns],
+        compiler_params=params(48, "arbitrary"),
+    )(*operands)
+
+
+def low_sum(*terms):
+    return sum(term.astype(f32) for term in terms).astype(bf16)
+
+
+def over_z(terms):
+    running = low_sum(*terms[3])
+    for ahead in (2, 1, 0):
+        running = low_sum(*terms[ahead], z_shift(running))
+    return running
+
+
+def spread_piece(piece):
+    near, far = [piece], []
+    for step in range(3):
+        ready = near[-1] if step == 0 else after(near[-1], far[-1])
+        far.append(ctx_swap(near[-1], 1))
+        near.append(z_shift(ready))
+    return near + far + [ctx_swap(after(near[-1], far[-1]), 1)]
+
+
+def settle_qkv_kernel(me_ref, *refs):
+    pieces, outs = refs[:8], refs[8:]
+    shards, rows = pieces[0].shape[:2]
+    part = outs[0].shape[1] // shards
+    for index, ref in enumerate(pieces):
+        height = piece_height(me_ref, -(index % 4))
+        head = me_ref[1] % 2 ^ (index // 4)
+        where = pl.ds(pl.multiple_of(height * rows, rows), rows)
+        for shard in range(shards):
+            columns = pl.ds(pl.multiple_of(shard * part + head * HEAD, HEAD), HEAD)
+            for kind, out in enumerate(outs):
+                out[where, columns] = ref[shard, :, kind * HEAD : (kind + 1) * HEAD].astype(f32)
+
+
+def settle_pair_kernel(me_ref, *refs):
+    pieces, outs = refs[:8], refs[8:]
+    shards, rows, columns = pieces[0].shape
+    half = columns // 2
+    for index, ref in enumerate(pieces):
+        owner = piece_owner(me_ref, index // 4, -(index % 4))
+        where = pl.ds(pl.multiple_of(owner * rows, rows), rows)
+        for kind, start, source, size in pair_columns(half):
+            for shard in range(shards):
+                first = shard * half + start
+                outs[kind][where, first : first + size] = ref[
+                    shard, :, source : source + size
+                ].astype(f32)
+
+
+def settle_turned_kernel(me_ref, *refs):
+    pieces, (down_ref, out_ref) = refs[:8], refs[8:]
+    shards, rows = pieces[0].shape[:2]
+    half = down_ref.shape[0]
+    for index, ref in enumerate(pieces):
+        owner = piece_owner(me_ref, index // 4, -(index % 4))
+        stretch = jnp.concatenate([ref[shard].astype(f32) for shard in range(shards)], axis=0)
+        columns = pl.ds(pl.multiple_of(owner * shards * rows, shards * rows), shards * rows)
+        down_ref[:, columns] = stretch[:, :half].T
+        out_ref[:, columns] = stretch[:, half:].T
+
+
+def settle(kernel, name, me, pieces, outs):
+    return pl.pallas_call(
+        kernel,
+        name=name,
+        grid=(1,),
+        in_specs=[SMEM] + [whole(pieces[0].shape)] * 8,
+        out_specs=[whole(out) for out in outs],
+        out_shape=[shaped(*out, kind=f32) for out in outs],
+        cost_estimate=cost(4),
+        compiler_params=params(40),
+    )(me, *pieces)
 
 
 def shaped(*shape, kind=bf16):
@@ -753,12 +1180,6 @@
         jnp.concatenate([cosine, cosine], axis=-1),
         jnp.concatenate([-sine, sine], axis=-1),
     )
-
-
-def cross_dot_low(operand, partner):
-    return lax.dot_general(
-        operand, partner, (((0,), (0,)), ((), ())), preferred_element_type=f32
-    ).astype(bf16)
 
 
 def pair_shards(
@@ -782,16 +1203,47 @@
 ):
     rows, width = block_in.shape[1:]
     ctx_size = lax.axis_size("ctx")
-    heads = width // HEAD // 4
+    heads = width // HEAD // PLACES
+    part = heads * HEAD
     prompt = P_DEV * ctx_size
     prompt_chunks, cont_chunks = prompt // rows, CONT // rows
     ff_part = w_down.shape[0]
-    ff_width = w_gate.shape[1]
     my_row = lax.axis_index("fsdp")
     my_chunk = lax.axis_index("ctx")
+    me = jnp.stack([my_row, my_chunk]).astype(jnp.int32)
     groups, slots = cont_ids.shape
-
-    row_of = my_row ^ jnp.array(REL, jnp.int32)
+    gain_one, gain_two, gain_three, gain_four = (
+        gain[None, :] for gain in (norm_one, norm_two, norm_three, norm_four)
+    )
+    x_own, grad_own = block_in[0], out_grad[0]
+    row_spec, gain_spec = whole((rows, width)), whole((1, width))
+    full_row, low_row, gain_row = (
+        shaped(rows, width, kind=f32),
+        shaped(rows, width),
+        shaped(1, width, kind=f32),
+    )
+
+    x_across = y_swap(x_own)
+    qkv_split = pl.pallas_call(
+        split_qkv_kernel,
+        name="split_qkv",
+        cost_estimate=cost(2),
+        grid=(1,),
+        in_specs=[SMEM] + [whole((rows, width))] * 3,
+        out_specs=[whole((rows, 3 * part))] * 4,
+        out_shape=[shaped(rows, 3 * part)] * 4,
+        compiler_params=params(16),
+    )(me, w_query, w_key, w_value)
+    w_qkv = [
+        qkv_split[0],
+        core_swap(qkv_split[1]),
+        y_swap(qkv_split[2]),
+        y_swap(core_swap(qkv_split[3])),
+    ]
+    x_beside = core_swap(x_own)
+    x_all = [x_own, x_beside, x_across, core_swap(x_across)]
+
+    row_of = my_row ^ jnp.arange(PLACES, dtype=jnp.int32)
     group_range = jnp.arange(groups, dtype=jnp.int32)
     slot_range = jnp.arange(slots, dtype=jnp.int32)
     pick_row = row_of[:, None] == group_range[None, :]
@@ -803,7 +1255,7 @@
     slot_lens = jnp.sum(
         jnp.where(ids_of[:, :, None] == slot_range, lens_of[:, None, :], 0), axis=2
     )
-    pick_pair = jnp.arange(4, dtype=jnp.int32) == my_chunk // heads
+    pick_pair = jnp.arange(PLACES, dtype=jnp.int32) == my_chunk // heads
     pair_prompt = jnp.sum(jnp.where(pick_pair, prompt_of, 0))
     pair_lens = jnp.sum(jnp.where(pick_pair[:, None], slot_lens, 0), axis=0)
     info = jnp.concatenate([pair_prompt[None], pair_lens])
@@ -816,54 +1268,58 @@
     all_slots = jnp.arange(rows * ctx_size, dtype=jnp.int32).reshape(ctx_size, rows)
     cos_all, sin_all = rope_tables(positions(all_slots, pair_prompt))
 
-    gain_one, gain_two, gain_three, gain_four = (
-        gain[None, :] for gain in (norm_one, norm_two, norm_three, norm_four)
-    )
-    x_own, grad_own = block_in[0], out_grad[0]
-
-    x_all = gather_rows(x_own)
-    part = heads * HEAD
-    wide = jnp.stack(
-        [w.reshape(rows, 4, part) for w in (w_query, w_key, w_value)], axis=2
-    ).transpose(1, 0, 2, 3)
-    w_qkv = lax.all_to_all(
-        wide.reshape(4, rows, 3 * part), "fsdp", 0, 0, tiled=True
-    ).reshape(width, 3 * part)
-    w_pair = lax.all_to_all(
-        jnp.stack([w.reshape(w.shape[0], 4, ff_part).transpose(1, 0, 2) for w in (w_gate, w_up)], axis=1),
-        "fsdp",
-        0,
-        0,
-        tiled=True,
-    )
-    gate_part = w_pair[:, 0].reshape(width, ff_part)
-    up_part = w_pair[:, 1].reshape(width, ff_part)
+    w_qkv = after(w_qkv, cos_own, sin_own, cos_all, sin_all)
+
+    ff_blocks, ff_block = (2, rows, 2 * ff_part), (rows, 2 * ff_part)
+    split_shapes = [ff_blocks, ff_block, ff_blocks, ff_block, (ff_part, width // 2)]
+    ff_own, ff_own_sent, ff_beside, ff_beside_sent, down_sent = pl.pallas_call(
+        split_ff_kernel,
+        name="split_ff",
+        cost_estimate=cost(3),
+        grid=(1,),
+        in_specs=[SMEM] + [whole(w_gate.shape)] * 2 + [whole((ff_part, width))],
+        out_specs=[whole(shape) for shape in split_shapes],
+        out_shape=[shaped(*shape) for shape in split_shapes],
+        compiler_params=params(32),
+    )(me, w_gate, w_up, w_down)
+    w_qkv, x_all, ff_own_sent, ff_beside_sent = tie(w_qkv, x_all, ff_own_sent, ff_beside_sent)
+    w_ff_beside = core_swap(ff_beside)
+    ff_beside_sent = core_swap(ff_beside_sent)
+    far_y = y_swap(ff_own_sent)
+    far_x = ctx_swap(far_y, 1)
+    corner_y = y_swap(after(ff_beside_sent, far_y))
+    corner_x = ctx_swap(corner_y, 1)
+    down_y = y_swap(after(down_sent, corner_y))
+    down_x = ctx_swap(down_y, 1)
+    w_out_far = y_swap(after(w_out, down_y))
 
     piece = (heads, 3, rows, HEAD)
     qkv = pl.pallas_call(
         project_kernel,
         name="project",
-        grid=(4,),
-        in_specs=[
-            place((rows, width)),
-            whole((1, width)),
-            whole((width, 3 * part)),
-            place((rows, HEAD)),
-            place((rows, HEAD)),
-        ],
+        cost_estimate=cost(4),
+        grid=(PLACES,),
+        in_specs=[SMEM]
+        + [row_spec] * 4
+        + [gain_spec]
+        + [whole((rows, 3 * part))] * 4
+        + [pl.BlockSpec((1, rows, HEAD), lambda t: (t, 0, 0))] * 2,
         out_specs=pl.BlockSpec(piece, lambda t: (t, 0, 0, 0)),
-        out_shape=shaped(4 * heads, 3, rows, HEAD),
+        out_shape=shaped(PLACES * heads, 3, rows, HEAD),
+        scratch_shapes=[pltpu.VMEM((rows, width), bf16)] * 2,
         compiler_params=params(24, "arbitrary"),
-    )(x_all, gain_one, w_qkv, cos_own, sin_own)
+    )(me, *x_all, gain_one, *w_qkv, cos_own, sin_own)
     qkv = lax.all_to_all(qkv, "ctx", 0, 0, tiled=True)
-
-    smem = pl.BlockSpec(memory_space=pltpu.SMEM)
+    x_stack = jnp.stack(x_all)
+    qkv = after(qkv, far_y, x_stack)
+
     qkv_shape, head_shape = (ctx_size, 3, rows, HEAD), (ctx_size, rows, HEAD)
     mixed, exact, log_total = pl.pallas_call(
         functools.partial(attend_kernel, prompt_chunks, cont_chunks),
         name="attend",
+        cost_estimate=cost(15),
         grid=(ctx_size,),
-        in_specs=[smem, whole(qkv_shape)],
+        in_specs=[SMEM, whole(qkv_shape)],
         out_specs=[whole(head_shape), whole(head_shape), whole((ctx_size, 1, rows))],
         out_shape=[
             shaped(*head_shape),
@@ -872,129 +1328,218 @@
         ],
         compiler_params=params(32, "arbitrary"),
     )(info, qkv)
+    mixed = after(mixed, far_x, corner_x, down_y)
     attended = lax.all_to_all(mixed, "ctx", 0, 0, tiled=True)
-
-    pair_spec = pl.BlockSpec((heads, rows, HEAD), lambda t: (t, 0, 0))
-    two = shaped(2, rows, width)
+    attended = after(attended, down_x, w_out_far)
+    attended_far = y_swap(attended[2 * heads :])
+
+    two_heads = (2 * heads, rows, HEAD)
     keep, send = pl.pallas_call(
         mix_out_kernel,
         name="mix_out",
-        grid=(4,),
-        in_specs=[pair_spec, whole((part, width))],
-        out_specs=[kept((rows, width)), sent((rows, width))],
-        out_shape=[two, two],
-        compiler_params=params(16, "arbitrary"),
-    )(attended, w_out)
-
-    row_spec, gain_spec = whole((rows, width)), whole((1, width))
-    sum_specs = [first_place((rows, width)), first_place((rows, width)), row_spec]
-    full_row, low_row, gain_row = (
-        shaped(rows, width, kind=f32),
-        shaped(rows, width),
-        shaped(1, width, kind=f32),
-    )
+        cost_estimate=cost(2),
+        grid=(1,),
+        in_specs=[whole((PLACES * heads, rows, HEAD)), whole(two_heads)] + [whole((part, width))] * 2,
+        out_specs=[row_spec] * 2,
+        out_shape=[full_row, low_row],
+        compiler_params=params(16),
+    )(attended, attended_far, w_out, w_out_far)
+
     branch, middle, ff_input = pl.pallas_call(
         middle_kernel,
         name="middle",
+        cost_estimate=cost(2),
         grid=(1,),
-        in_specs=sum_specs + [row_spec, gain_spec, gain_spec],
+        in_specs=[row_spec] * 3 + [gain_spec] * 2,
         out_specs=[row_spec] * 3,
         out_shape=[full_row, full_row, low_row],
         compiler_params=params(24),
-    )(*exchange_sums(keep, send), x_own, gain_two, gain_three)
-    ff_all = gather_rows(ff_input)
-
-    ff_rows = shaped(4, rows, ff_part)
-    keep, send, slope, swish, hidden = pl.pallas_call(
+    )(keep, core_swap(send), x_own, gain_two, gain_three)
+    ff_input_beside = core_swap(ff_input)
+    ff_input_far = far_rows(ff_input)
+    x_pair = lax.all_to_all(
+        after(x_stack, attended),
+        "ctx",
+        0,
+        0,
+        tiled=True,
+        axis_index_groups=[[x + 2 * z for z in range(ctx_size // 2)] for x in range(2)],
+    )
+
+    padded = pl.cdiv(ff_part, HEAD) * HEAD
+    far_pairs = [far_y, far_x, corner_y, corner_x]
+    far_weights = far_pairs + [w_down, down_y, down_x]
+
+    def turned(index, me_ref):
+        return index ^ (me_ref[1] % 2)
+
+    def grid_whole(shape):
+        return pl.BlockSpec(shape, lambda b, me_ref: (0,) * len(shape))
+
+    def ff_call(kernel, name, expected, more_in, outs, scratch):
+        specs = (
+            [grid_whole((rows, width))] * 2
+            + [pl.BlockSpec((1,) + ff_block, lambda b, me_ref: (turned(b, me_ref), 0, 0))] * 2
+            + [grid_whole(weight.shape) for weight in far_weights]
+            + more_in
+        )
+        return pl.pallas_call(
+            kernel,
+            name=name,
+            cost_estimate=cost(expected),
+            grid_spec=pltpu.PrefetchScalarGridSpec(
+                num_scalar_prefetch=1,
+                grid=(2,),
+                in_specs=specs,
+                out_specs=[spec for spec, _ in outs],
+                scratch_shapes=scratch,
+            ),
+            out_shape=[shape for _, shape in outs],
+            compiler_params=params(56, "arbitrary"),
+        )
+
+    both = 2 * rows
+    padded = pl.cdiv(ff_part, HEAD) * HEAD
+    saved = pl.BlockSpec((1, both, 2 * ff_part), lambda b, me_ref: (b, 0, 0))
+    grid_row = grid_whole((rows, width))
+    hidden_shape, pair_shape = (2, rows, padded), (2, rows, 2 * ff_part)
+    keep, send, ff_saved, hidden = ff_call(
         ff_kernel,
-        name="ff",
-        grid=(4,),
-        in_specs=[
-            place((rows, width)),
-            whole((width, ff_part)),
-            whole((width, ff_part)),
-            whole((ff_part, width)),
+        "ff",
+        9,
+        [],
+        [
+            (grid_row, full_row),
+            (grid_row, low_row),
+            (saved, shaped(2, both, 2 * ff_part)),
+            (grid_whole(hidden_shape), shaped(*hidden_shape)),
         ],
-        out_specs=[kept((rows, width)), sent((rows, width))] + [place((rows, ff_part))] * 3,
-        out_shape=[two, two, ff_rows, ff_rows, ff_rows],
-        compiler_params=params(40, "arbitrary"),
-    )(ff_all, gate_part, up_part, w_down)
-
+        [
+            pltpu.VMEM((both, width), bf16),
+            pltpu.VMEM((both, 2 * ff_part), f32),
+            pltpu.VMEM((both, padded), bf16),
+            pltpu.VMEM((both, width), f32),
+        ],
+    )(me, ff_input, ff_input_beside, ff_own, w_ff_beside, *far_weights)
+
+    send = after(send, ff_input_far[0])
     block_out, ff_grad, part_four = pl.pallas_call(
         turnaround_kernel,
         name="turnaround",
+        cost_estimate=cost(2),
         grid=(1,),
-        in_specs=sum_specs + [row_spec, row_spec, gain_spec],
+        in_specs=[row_spec] * 4 + [gain_spec],
         out_specs=[row_spec, row_spec, gain_spec],
         out_shape=[low_row, low_row, gain_row],
         compiler_params=params(24),
-    )(*exchange_sums(keep, send), middle, grad_own, gain_four)
-
-    ff_grad_all = gather_rows(ff_grad)
-    keep, send, gate_grad, up_grad = pl.pallas_call(
+    )(keep, core_swap(send), middle, grad_own, gain_four)
+
+    ff_grad_beside = core_swap(ff_grad)
+    ff_grad_far = far_rows(ff_grad)
+    keep, send, pair_grad = ff_call(
         ff_back_kernel,
-        name="ff_back",
-        grid=(4,),
-        in_specs=[
-            place((rows, width)),
-            whole((width, ff_part)),
-            whole((width, ff_part)),
-            whole((ff_part, width)),
-            place((rows, ff_part)),
-            place((rows, ff_part)),
+        "ff_back",
+        9,
+        [saved],
+        [
+            (grid_row, full_row),
+            (grid_row, low_row),
+            (grid_whole(pair_shape), shaped(*pair_shape)),
         ],
-        out_specs=[kept((rows, width)), sent((rows, width))] + [place((rows, ff_part))] * 2,
-        out_shape=[two, two, ff_rows, ff_rows],
-        compiler_params=params(40, "arbitrary"),
-    )(ff_grad_all, gate_part, up_part, w_down, slope, swish)
-
-    tokens = 4 * rows
-    flat_input = ff_all.reshape(tokens, width)
-    down_term = cross_dot_low(
-        hidden.reshape(tokens, ff_part), ff_grad_all.reshape(tokens, width)
-    )
-    pair_term = jnp.stack(
         [
-            cross_dot_low(flat_input, grad.reshape(tokens, ff_part)).reshape(4, rows, ff_part)
-            for grad in (gate_grad, up_grad)
+            pltpu.VMEM((both, width), bf16),
+            pltpu.VMEM((both, ff_part), f32),
+            pltpu.VMEM((both, 2 * ff_part), bf16),
+            pltpu.VMEM((both, width), f32),
         ],
-        axis=1,
-    )
-    pair_term = lax.all_to_all(pair_term, "fsdp", 0, 0, tiled=True)
-    pair_term = pair_term.transpose(1, 2, 0, 3).reshape(2, rows, ff_width)
+    )(me, ff_grad, ff_grad_beside, ff_own, w_ff_beside, *far_weights, ff_saved)
+    x_pair_other = ctx_swap(x_pair, 1)
+    send = after(send, ff_grad_far[0])
 
     middle_grad, branch_grad, part_two, part_three = pl.pallas_call(
         branch_back_kernel,
         name="branch_back",
+        cost_estimate=cost(2),
         grid=(1,),
-        in_specs=sum_specs + [row_spec, row_spec, row_spec, gain_spec, gain_spec],
+        in_specs=[row_spec] * 5 + [gain_spec] * 2,
         out_specs=[row_spec, row_spec, gain_spec, gain_spec],
         out_shape=[full_row, low_row, gain_row, gain_row],
         compiler_params=params(24),
-    )(*exchange_sums(keep, send), middle, branch, grad_own, gain_two, gain_three)
-    branch_grad_all = gather_rows(branch_grad)
-
-    attended_grad = pl.pallas_call(
+    )(keep, core_swap(send), middle, branch, grad_own, gain_two, gain_three)
+    branch_grad_beside = core_swap(branch_grad)
+
+    heads_near, heads_far = pl.pallas_call(
         heads_back_kernel,
         name="heads_back",
-        grid=(4,),
-        in_specs=[place((rows, width)), whole((part, width))],
-        out_specs=pair_spec,
-        out_shape=shaped(4 * heads, rows, HEAD),
-        compiler_params=params(16, "arbitrary"),
-    )(branch_grad_all, w_out)
-    attended_grad = lax.all_to_all(attended_grad, "ctx", 0, 0, tiled=True)
-    out_term = cross_dot_low(
-        attended.reshape(4, heads, rows, HEAD).transpose(0, 2, 1, 3).reshape(tokens, part),
-        branch_grad_all.reshape(tokens, width),
-    )
+        cost_estimate=cost(2),
+        grid=(1,),
+        in_specs=[row_spec] * 2 + [whole((part, width))] * 2,
+        out_specs=[whole(two_heads)] * 2,
+        out_shape=[shaped(*two_heads)] * 2,
+        compiler_params=params(16),
+    )(branch_grad, branch_grad_beside, w_out, w_out_far)
+    heads_far = y_swap(heads_far)
+    ff_input_far, ff_grad_far = after((ff_input_far, ff_grad_far), heads_near)
+    branch_grad_across = y_swap(branch_grad)
+
+    near_share = pl.BlockSpec((1,) + ff_block, lambda *_: (0, 0, 0))
+    hidden_far, pair_far = pl.pallas_call(
+        ff_far_kernel,
+        name="ff_far",
+        cost_estimate=cost(6),
+        grid=(1,),
+        in_specs=[SMEM]
+        + [row_spec] * 4
+        + [near_share] * 2
+        + [whole(ff_block)] * 4
+        + [whole((ff_part, width))],
+        out_specs=[whole(hidden_shape), whole(pair_shape)],
+        out_shape=[shaped(*hidden_shape), shaped(*pair_shape)],
+        scratch_shapes=[
+            pltpu.VMEM((both, width), bf16),
+            pltpu.VMEM((both, 2 * ff_part), f32),
+            pltpu.VMEM((both, 2 * ff_part), bf16),
+        ],
+        compiler_params=params(40),
+    )(me, *ff_input_far, *ff_grad_far, ff_own, w_ff_beside, *far_pairs, w_down)
+    pair_keep, pair_send = weight_grads(
+        me,
+        "pair_grads",
+        7,
+        [
+            (
+                [ff_input, ff_input_beside, *ff_input_far],
+                [pair_grad, pair_far],
+                2 * ff_part,
+                False,
+            )
+        ],
+    )
+    pair_over = ctx_swap(pair_send, 1)
+    heads_far = after(heads_far, x_pair, pair_send)
+    attended_grad = lax.all_to_all(
+        jnp.concatenate([heads_near, heads_far]), "ctx", 0, 0, tiled=True
+    )
+    branch_grad_far = [branch_grad_across, core_swap(branch_grad_across)]
+    down_keep, down_send = weight_grads(
+        me,
+        "down_grads",
+        8,
+        [
+            ([ff_grad, ff_grad_beside, *ff_grad_far], [hidden, hidden_far], ff_part, True),
+            ([branch_grad, branch_grad_beside, *branch_grad_far], [attended], part, True),
+        ],
+    )
+    down_over = ctx_swap(down_send, 1)
+    attended_grad = after(attended_grad, down_send, x_pair_other)
 
     pieces = pl.pallas_call(
         functools.partial(attend_back_kernel, prompt_chunks, cont_chunks),
         name="attend_back",
+        cost_estimate=cost(18),
         grid=(ctx_size,),
         in_specs=[
-            smem,
+            SMEM,
             whole(qkv_shape),
             whole(head_shape),
             whole(head_shape),
@@ -1007,57 +1552,100 @@
         scratch_shapes=[pltpu.VMEM(head_shape, f32), pltpu.VMEM(head_shape, f32)],
         compiler_params=params(40, "arbitrary"),
     )(info, qkv, attended_grad, exact, log_total, cos_all, sin_all)
+    qkv_piece = (4, PLACES, rows // 4, 3 * HEAD)
+    qkv_keep = pl.pallas_call(
+        project_grad_kernel,
+        name="project_grad",
+        cost_estimate=cost(6),
+        grid=(4,),
+        in_specs=[SMEM, whole(qkv_shape)] + [whole((4, rows, width))] * 2 + [gain_spec],
+        out_specs=whole(qkv_piece),
+        out_shape=shaped(*qkv_piece),
+        scratch_shapes=[pltpu.VMEM((width, 3 * HEAD), f32)],
+        compiler_params=params(32, "arbitrary"),
+    )(me, pieces, x_pair, x_pair_other, gain_one)
+    pair_over, down_over = after((pair_over, down_over), pieces)
+    pair_came = z_shift(low_sum(pair_keep[3], pair_over[3]))
+    pair_came = z_shift(low_sum(pair_keep[2], pair_over[2], pair_came))
+    qkv_came = z_shift(qkv_keep[3])
     pieces = lax.all_to_all(pieces, "ctx", 0, 0, tiled=True)
-
-    keep, send, qkv_term = pl.pallas_call(
+    pieces = after(pieces, qkv_keep)
+
+    piece_spec = pl.BlockSpec(piece, lambda t: (t, 0, 0, 0))
+    pair_rows = pl.BlockSpec((1, rows, width), lambda t: (t // 2, 0, 0))
+    keep, send = pl.pallas_call(
         project_back_kernel,
         name="project_back",
-        grid=(4,),
-        in_specs=[
-            pl.BlockSpec(piece, lambda t: (t, 0, 0, 0)),
-            place((rows, width)),
-            gain_spec,
-            whole((width, 3 * part)),
-        ],
-        out_specs=[kept((rows, width)), sent((rows, width)), whole((width, 3 * part))],
-        out_shape=[two, two, shaped(width, 3 * part)],
-        scratch_shapes=[pltpu.VMEM((width, 3 * part), f32)],
-        compiler_params=params(32, "arbitrary"),
-    )(pieces, x_all, gain_one, w_qkv)
-
+        cost_estimate=cost(5),
+        grid=(PLACES,),
+        in_specs=[SMEM, piece_spec] + [whole((rows, 3 * part))] * 4,
+        out_specs=[pair_rows, pair_rows],
+        out_shape=[shaped(2, rows, width)] * 2,
+        compiler_params=params(24, "arbitrary"),
+    )(me, pieces, *w_qkv)
+
+    received = core_swap(send)
+    onward = (keep[1].astype(f32) + received[1].astype(f32)).astype(bf16)
     in_grad, part_one = pl.pallas_call(
         input_back_kernel,
         name="input_back",
+        cost_estimate=cost(2),
         grid=(1,),
-        in_specs=sum_specs + [row_spec, row_spec, gain_spec],
+        in_specs=[pl.BlockSpec((1, rows, width), lambda *_: (0, 0, 0))] * 2
+        + [row_spec] * 3
+        + [gain_spec],
         out_specs=[row_spec, gain_spec],
         out_shape=[full_row, gain_row],
         compiler_params=params(24),
-    )(*exchange_sums(keep, send), x_own, middle_grad, gain_one)
-
-    qkv_term = lax.all_to_all(qkv_term.reshape(4, rows, 3 * part), "fsdp", 0, 0, tiled=True)
-    ff_sums = lax.psum((pair_term, down_term, out_term), "ctx")
-    qkv_sum = lax.psum(qkv_term, "ctx")
-    qkv_sum = (
-        qkv_sum.reshape(4, rows, 3, part).transpose(2, 1, 0, 3).reshape(3, rows, width).astype(f32)
-    )
-    gain_sums = lax.psum(
-        jnp.concatenate([part_one, part_two, part_three, part_four]), ("ctx", "fsdp")
-    )
+    )(keep, received, y_swap(onward), x_own, middle_grad, gain_one)
+
+    def shared_rows(piece):
+        return lax.all_to_all(piece, "fsdp", 0, 0, tiled=True)
+
+    pair_came, qkv_came, down_over = after((pair_came, qkv_came, down_over), send)
+    qkv_came = z_shift(low_sum(qkv_keep[2], qkv_came))
+    pair_came = z_shift(low_sum(pair_keep[1], pair_over[1], pair_came))
+    qkv_came = z_shift(low_sum(qkv_keep[1], qkv_came))
+    pair_piece = shared_rows(low_sum(pair_keep[0], pair_over[0], pair_came))
+    qkv_piece = shared_rows(low_sum(qkv_keep[0], qkv_came))
+    down_piece = over_z([[down_keep[ahead], down_over[ahead]] for ahead in range(4)])
+    query_sum, key_sum, value_sum = settle(
+        settle_qkv_kernel, "settle_qkv", me, spread_piece(qkv_piece), [(rows, width)] * 3
+    )
+    gate_sum, up_sum = settle(
+        settle_pair_kernel, "settle_pair", me, spread_piece(pair_piece), [w_gate.shape] * 2
+    )
+    down_sum, out_sum = settle(
+        settle_turned_kernel,
+        "settle_turned",
+        me,
+        spread_piece(down_piece),
+        [(ff_part, width), (part, width)],
+    )
+
+    gains = jnp.concatenate([part_one, part_two, part_three, part_four])
+    for swap in (
+        core_swap,
+        y_swap,
+        functools.partial(ctx_swap, bit=1),
+        functools.partial(ctx_swap, bit=2),
+        functools.partial(ctx_swap, bit=4),
+    ):
+        gains = gains + swap(gains)
     return (
         block_out[None],
         in_grad[None],
-        qkv_sum[0],
-        qkv_sum[1],
-        qkv_sum[2],
-        ff_sums[2].astype(f32),
-        gain_sums[0],
-        gain_sums[1],
-        ff_sums[0][0].astype(f32),
-        ff_sums[0][1].astype(f32),
-        ff_sums[1].astype(f32),
-        gain_sums[2],
-        gain_sums[3],
+        query_sum,
+        key_sum,
+        value_sum,
+        out_sum,
+        gains[0],
+        gains[1],
+        gate_sum,
+        up_sum,
+        down_sum,
+        gains[2],
+        gains[3],
     )
 
 

time: 701 us -> 495 us (0.71)
  waiting for transfers between devices: 388 us -> 200 us
  blocking collectives: 58.6 us -> 0 us
  Pallas kernels: 71.8 us -> 126 us
  starting transfers between devices: 43.8 us -> 74.5 us
  local copies, waits for them, and re-layouts: 70 us -> 49.9 us
  matrix products: 15.4 us -> 0 us
  between operations: 14.9 us -> 1.92 us
    psum x1 -> x0, waiting for transfers between devices: 157 us -> none  [pair_shards(): qkv_sum = lax.psum(qkv_term, 'ctx')]
    ppermute x0 -> x39, waiting for transfers between devices: none -> 136 us  [the longest x18 68.1 us: z_shift(): lax.ppermute(values, 'ctx', [(i, (i + 2) % size) for i in range(size)])]
    ppermute x8 -> x14, waiting for transfers between devices: 124 us -> 47.8 us  [y_swap(): return lax.ppermute(values, 'fsdp', [(i, i ^ 2) for i in range(4)])]
    pallas_call x10 -> x19, Pallas kernels: 38.1 us -> 90.6 us  [the longest x2 15.5 us: weight_grads(): pl.pallas_call(functools.partial(weight_grads_kernel, tuple(kinds)), name...]
    psum x1 -> x0, blocking collectives: 40.5 us -> none  [pair_shards(): lax.psum(jnp.concatenate([part_one, part_two, part_three, part_four]), ('...]
    all_to_all x5, waiting for transfers between devices: 47.1 us -> 11 us  [the longest x2 6 us: shared_rows(): return lax.all_to_all(piece, 'fsdp', 0, 0, tiled=True)]
    all_to_all x1, waiting for transfers between devices: 34.9 us -> 0.01 us  [pair_shards(): qkv = lax.all_to_all(qkv, 'ctx', 0, 0, tiled=True)]
    ppermute x0 -> x39, starting transfers between devices: none -> 22.6 us  [the longest x21 19 us: ctx_swap(): return lax.ppermute(values, 'ctx', [(i, i ^ bit) for i in range(size)])]
  transfers between devices with their start and end apart: 28 -> 77, of which waited for: 20 -> 35; matrix products, arithmetic and copies ran while one was open for 10% -> 7% of each run, Pallas kernels for 2% -> 24%
where the time goes in v2:
time: 495 us; the launch traced here: 486 us
  waiting for transfers between devices  200 us (40%)
  Pallas kernels  126 us (25%)
  starting transfers between devices  74.5 us (15%)
  local copies, waits for them, and re-layouts  49.9 us (10%)
  other arithmetic  33.4 us (7%)
    ppermute x18, waiting for transfers between devices, z_shift(): lax.ppermute(values, 'ctx', [(i, (i + 2) % size) for i in range(size)])  68.1 us
    ppermute x21, waiting for transfers between devices, ctx_swap(): return lax.ppermute(values, 'ctx', [(i, i ^ bit) for i in range(size)])  67.5 us
    ppermute x14, waiting for transfers between devices, y_swap(): return lax.ppermute(values, 'fsdp', [(i, i ^ 2) for i in range(4)])  47.8 us
    unnamed x204, local copies, waits for them, and re-layouts  47.6 us
    ppermute x21, starting transfers between devices, ctx_swap(): return lax.ppermute(values, 'ctx', [(i, i ^ bit) for i in range(size)])  19 us
    pallas_call x1, Pallas kernels, pair_shards(): pl.pallas_call(functools.partial(attend_back_kernel, prompt_chunks, cont_...  18.7 us
    ppermute x14, starting transfers between devices, y_swap(): return lax.ppermute(values, 'fsdp', [(i, i ^ 2) for i in range(4)])  17 us
    pallas_call x1, Pallas kernels, pair_shards(): pl.pallas_call(functools.partial(attend_kernel, prompt_chunks, cont_chunk...  16.5 us
  transfers between devices with their start and end apart: 77, of which 35 were waited for; matrix products, arithmetic and copies ran while one was open for 7% of the time, Pallas kernels for 24%

profile of v2, /device:TPU:0, one launch (start us, length us, event | category | flops | bytes accessed | tf_op | source)
XLA Modules:
  0.0 485.7 jit_solution(194252578029302382)
XLA Ops:
  0.7 3.0 collective-permute-start.5
  9.7 3.0 fusion.13
  25.7 3.7 fusion.11
  29.5 1.9 pad_maximum_fusion.1
  31.4 4.1 collective-permute-done.3.w3
  35.5 5.7 %project.1 = bf16[8,3,256,128]{3,2,1,0:T(8,128)(2,1)} custom-call(s32[2]{0:T(128)S(1)} %pad_add_fusion.me_ref, bf16[256,1024]{1,0:T(8,128)(2,1)S(1)} %bitcast.68, bf16[256,1024]{1,0:T(8,128)(2,1)S(1)} %collective-permute-done.4.x1, bf16[256,1024]{1,0:T(8,128)(2,1)S(1)} %collective-permute-done.5.x2, bf16[256,1024]{1,0:T(8,128)(2,1)S(1)} %collective-permute-done.6.x3, ...), custom_call_target="tpu_custom_call" | custom-call | flops 1200000000 | tf_op jit(solution)/shard_map/project/pallas_call | solution.py:1297
  42.8 6.7 %all-to-all-start = ((bf16[8,3,256,128]{3,2,1,0:T(8,128)(2,1)}), bf16[8,3,256,128]{3,2,1,0:T(8,128)(2,1)}, u32[]{:S(2)}, u32[]{:S(2)}) async-start(bf16[8,3,256,128]{3,2,1,0:T(8,128)(2,1)} %project.1), calls=%async_computation | async-start | bytes 3145728 | tf_op jit(solution)/shard_map/all_to_all | solution.py:1312
  51.1 15.9 %collective-permute-done.7.w2y = bf16[256,1408]{1,0:T(8,128)(2,1)S(1)} collective-permute-done((bf16[256,1408]{1,0:T(8,128)(2,1)}, bf16[256,1408]{1,0:T(8,128)(2,1)S(1)}, u32[]{:S(2)}, u32[]{:S(2)}) %collective-permute-start.7) | collective-permute-done | bytes 720928 | tf_op jit(solution)/shard_map/ppermute | solution.py:392
  69.0 1.8 collective-permute-start.8
  70.8 12.7 %collective-permute-done.10.w3y = bf16[256,1408]{1,0:T(8,128)(2,1)S(1)} collective-permute-done((bf16[256,1408]{1,0:T(8,128)(2,1)S(1)}, bf16[256,1408]{1,0:T(8,128)(2,1)S(1)}, u32[]{:S(2)}, u32[]{:S(2)}) %collective-permute-start.10) | collective-permute-done | bytes 720928 | tf_op jit(solution)/shard_map/ppermute | solution.py:392
  87.2 2.9 pad_maximum_fusion
  90.1 16.5 %attend.1 = (bf16[8,256,128]{2,1,0:T(8,128)(2,1)S(1)}, f32[8,256,128]{2,1,0:T(8,128)S(1)}, f32[8,1,256]{2,1,0:T(1,128)S(1)}) custom-call(s32[3]{0:T(128)S(1)} %pad_add_fusion.1.info_ref, bf16[8,3,256,128]{3,2,1,0:T(8,128)(2,1)} %all-to-all-done.qkv_ref), custom_call_target="tpu_custom_call" | custom-call | flops 4499999744 | tf_op jit(solution)/shard_map/attend/pallas_call | solution.py:1317
  109.0 4.5 all-to-all-start.1
  113.5 2.0 collective-permute-start.13
  116.1 9.4 %collective-permute-done.14.w_far_ref = bf16[256,1024]{1,0:T(8,128)(2,1)S(1)} collective-permute-done((bf16[256,1024]{1,0:T(8,128)(2,1)}, bf16[256,1024]{1,0:T(8,128)(2,1)S(1)}, u32[]{:S(2)}, u32[]{:S(2)}) %collective-permute-start.14) | collective-permute-done | bytes 524320 | tf_op jit(solution)/shard_map/ppermute | solution.py:392
  126.2 7.7 %collective-permute-done.13.down_x = bf16[704,512]{1,0:T(8,128)(2,1)} collective-permute-done((bf16[704,512]{1,0:T(8,128)(2,1)}, bf16[704,512]{1,0:T(8,128)(2,1)}, u32[]{:S(2)}, u32[]{:S(2)}) %collective-permute-start.13) | collective-permute-done | bytes 720928 | tf_op jit(solution)/shard_map/ppermute | solution.py:397
  135.5 5.8 %collective-permute-done.15.far_ref = bf16[4,256,128]{2,1,0:T(8,128)(2,1)S(1)} collective-permute-done((bf16[4,256,128]{2,1,0:T(8,128)(2,1)S(1)}, bf16[4,256,128]{2,1,0:T(8,128)(2,1)S(1)}, u32[]{:S(2)}, u32[]{:S(2)}) %collective-permute-start.15) | collective-permute-done | bytes 262176 | tf_op jit(solution)/shard_map/ppermute | solution.py:392
  143.4 2.5 mix_out.1
  146.9 4.7 all-to-all-start.2
  158.8 15.1 %ff.1 = (f32[256,1024]{1,0:T(8,128)}, bf16[256,1024]{1,0:T(8,128)(2,1)}, bf16[2,512,1408]{2,1,0:T(8,128)(2,1)}, bf16[2,256,768]{2,1,0:T(8,128)(2,1)}) custom-call(s32[2]{0:T(128)} %copy-done.53, bf16[256,1024]{1,0:T(8,128)(2,1)} %copy-done.77, bf16[256,1024]{1,0:T(8,128)(2,1)} %copy-done.79, bf16[2,256,1408]{2,1,0:T(8,128)(2,1)} %copy-done.2, ...), custom_call_target="tpu_custom_call" | custom-call | flops 2700000000 | tf_op jit(solution)/shard_map/ff/pallas_call | solution.py:1406
  174.4 1.8 collective-permute-done.20.received_ref
  181.5 13.8 %ff_back.1 = (f32[256,1024]{1,0:T(8,128)}, bf16[256,1024]{1,0:T(8,128)(2,1)}, bf16[2,256,1408]{2,1,0:T(8,128)(2,1)}) custom-call(s32[2]{0:T(128)} %copy-done.53, bf16[256,1024]{1,0:T(8,128)(2,1)} %copy-done.35, bf16[256,1024]{1,0:T(8,128)(2,1)} %copy-done.37, bf16[2,256,1408]{2,1,0:T(8,128)(2,1)} %copy-done.2, bf16[2,256,1408]{2,1,0:T(8,128)(2,1)} %copy-done.4, ...), custom_call_target="tpu_custom_call" | custom-call | flops 2700000000 | tf_op jit(solution)/shard_map/ff_back/pallas_call | solution.py:1439
  196.4 4.2 all-to-all-done.2.own_ref
  205.4 3.0 branch_back.1
  213.6 2.0 heads_back.1
  217.5 4.1 ff_far.1
  223.6 7.8 %pair_grads.1 = (bf16[4,4,32,1408]{3,2,1,0:T(8,128)(2,1)S(1)}, bf16[4,4,32,1408]{3,2,1,0:T(8,128)(2,1)}) custom-call(s32[2]{0:T(128)S(1)} %copy-done.54, bf16[256,1024]{1,0:T(8,128)(2,1)S(1)} %copy-done.78, bf16[256,1024]{1,0:T(8,128)(2,1)S(1)} %copy-done.80, bf16[256,1024]{1,0:T(8,128)(2,1)S(1)} %copy-done.44, ...), custom_call_target="tpu_custom_call" | custom-call | flops 2100000000 | tf_op jit(solution)/shard_map/pair_grads/pallas_call | solution.py:1082
  233.3 4.1 all-to-all-start.3
  238.4 1.8 collective-permute-start.33
  246.6 7.8 %down_grads.1 = (bf16[4,4,32,960]{3,2,1,0:T(8,128)(2,1)}, bf16[4,4,32,960]{3,2,1,0:T(8,128)(2,1)}) custom-call(s32[2]{0:T(128)S(1)} %copy-done.54, bf16[256,1024]{1,0:T(8,128)(2,1)S(1)} %copy-done.36, bf16[256,1024]{1,0:T(8,128)(2,1)S(1)} %copy-done.38, bf16[256,1024]{1,0:T(8,128)(2,1)S(1)} %copy-done.41, bf16[256,1024]{1,0:T(8,128)(2,1)S(1)} %copy-done.46, ...), custom_call_target="tpu_custom_call" | custom-call | flops 2400000000 | tf_op jit(solution)/shard_map/down_grads/pallas_call | solution.py:1082
  256.4 18.7 %attend_back.1.pieces_ref = bf16[8,3,256,128]{3,2,1,0:T(8,128)(2,1)S(1)} custom-call(s32[3]{0:T(128)S(1)} %copy-done.88, bf16[8,3,256,128]{3,2,1,0:T(8,128)(2,1)} %all-to-all-done.qkv_ref, bf16[8,256,128]{2,1,0:T(8,128)(2,1)} %all-to-all-done.3.grad_ref, f32[8,256,128]{2,1,0:T(8,128)S(1)} %copy-done.93, f32[8,1,256]{2,1,0:T(1,128)S(1)} %copy-done.95, ...), custom_call_target="tpu_custom_call" | custom-call | flops 5400000000 | tf_op jit(solution)/shard_map/attend_back/pallas_call | solution.py:1536
  276.2 4.5 all-to-all-start.4
  280.7 2.0 collective-permute-start.34
  282.7 6.8 %collective-permute-done.33 = bf16[4,4,32,1408]{3,2,1,0:T(8,128)(2,1)} collective-permute-done((bf16[4,4,32,1408]{3,2,1,0:T(8,128)(2,1)}, bf16[4,4,32,1408]{3,2,1,0:T(8,128)(2,1)}, u32[]{:S(2)}, u32[]{:S(2)}) %collective-permute-start.33) | collective-permute-done | bytes 1441824 | tf_op jit(solution)/shard_map/ppermute | solution.py:397
  289.5 34.3 %collective-permute-done.34 = bf16[4,4,32,960]{3,2,1,0:T(8,128)(2,1)} collective-permute-done((bf16[4,4,32,960]{3,2,1,0:T(8,128)(2,1)S(1)}, bf16[4,4,32,960]{3,2,1,0:T(8,128)(2,1)}, u32[]{:S(2)}, u32[]{:S(2)}) %collective-permute-start.34) | collective-permute-done | bytes 983072 | tf_op jit(solution)/shard_map/ppermute | solution.py:397
  326.9 6.7 %project_grad.1 = bf16[4,4,64,384]{3,2,1,0:T(8,128)(2,1)S(1)} custom-call(s32[2]{0:T(128)S(1)} %copy-done.54, bf16[8,3,256,128]{3,2,1,0:T(8,128)(2,1)S(1)} %copy-done.21, bf16[4,256,1024]{2,1,0:T(8,128)(2,1)} %all-to-all-done.2.own_ref, bf16[4,256,1024]{2,1,0:T(8,128)(2,1)} %collective-permute-done.30.other_ref, f32[1,1024]{1,0:T(1,128)S(1)} %bitcast.77), custom_call_target="tpu_custom_call" | custom-call | flops 1800000000 | tf_op jit(solution)/shard_map/project_grad/pallas_call | solution.py:1556
  333.6 2.7 collective-permute-done.35
  336.3 2.0 fusion.2
  341.8 4.9 %project_back.1 = (bf16[2,256,1024]{2,1,0:T(8,128)(2,1)S(1)}, bf16[2,256,1024]{2,1,0:T(8,128)(2,1)}) custom-call(s32[2]{0:T(128)S(1)} %copy-done.55, bf16[8,3,256,128]{3,2,1,0:T(8,128)(2,1)S(1)} %all-to-all-done.4.pieces_ref, bf16[256,768]{1,0:T(8,128)(2,1)S(1)} %copy-done.49, bf16[256,768]{1,0:T(8,128)(2,1)} %collective-permute-done.w1, ...), custom_call_target="tpu_custom_call" | custom-call | flops 1500000000 | tf_op jit(solution)/shard_map/project_back/pallas_call | solution.py:1576
  346.7 6.4 %collective-permute-done.37 = bf16[4,64,384]{2,1,0:T(8,128)(2,1)} collective-permute-done((bf16[4,64,384]{2,1,0:T(8,128)(2,1)}, bf16[4,64,384]{2,1,0:T(8,128)(2,1)}, u32[]{:S(2)}, u32[]{:S(2)}) %collective-permute-start.37) | collective-permute-done | bytes 196640 | tf_op jit(solution)/shard_map/ppermute | solution.py:402
  357.6 11.9 %collective-permute-done.38 = bf16[4,64,384]{2,1,0:T(8,128)(2,1)S(1)} collective-permute-done((bf16[4,64,384]{2,1,0:T(8,128)(2,1)S(1)}, bf16[4,64,384]{2,1,0:T(8,128)(2,1)S(1)}, u32[]{:S(2)}, u32[]{:S(2)}) %collective-permute-start.38) | collective-permute-done | bytes 196640 | tf_op jit(solution)/shard_map/ppermute | solution.py:402
  371.4 9.1 %collective-permute-done.39 = bf16[4,64,384]{2,1,0:T(8,128)(2,1)S(1)} collective-permute-done((bf16[4,64,384]{2,1,0:T(8,128)(2,1)S(1)}, bf16[4,64,384]{2,1,0:T(8,128)(2,1)S(1)}, u32[]{:S(2)}, u32[]{:S(2)}) %collective-permute-start.39) | collective-permute-done | bytes 196640 | tf_op jit(solution)/shard_map/ppermute | solution.py:402
  381.3 4.0 all-to-all-start.5
  385.3 2.0 fusion.1
  387.2 3.4 all-to-all-done.5.refs_0_
  390.7 3.5 all-to-all-start.6
  394.1 1.9 fusion.5
  397.1 2.0 collective-permute-start.32
  399.1 2.6 all-to-all-done.6.refs_0_
  401.7 5.6 %collective-permute-done.49 = bf16[4,32,960]{2,1,0:T(8,128)(2,1)} collective-permute-done((bf16[4,32,960]{2,1,0:T(8,128)(2,1)}, bf16[4,32,960]{2,1,0:T(8,128)(2,1)}, u32[]{:S(2)}, u32[]{:S(2)}) %collective-permute-start.49) | collective-permute-done | bytes 245792 | tf_op jit(solution)/shard_map/ppermute | solution.py:402
  408.6 3.0 collective-permute-done.40.refs_1_
  411.5 12.8 %collective-permute-done.50.refs_1_ = bf16[4,32,960]{2,1,0:T(8,128)(2,1)S(1)} collective-permute-done((bf16[4,32,960]{2,1,0:T(8,128)(2,1)S(1)}, bf16[4,32,960]{2,1,0:T(8,128)(2,1)S(1)}, u32[]{:S(2)}, u32[]{:S(2)}) %collective-permute-start.50) | collective-permute-done | bytes 245792 | tf_op jit(solution)/shard_map/ppermute | solution.py:402
  425.1 2.0 collective-permute-start.66
  428.7 5.4 %collective-permute-done.42.refs_2_ = bf16[4,64,384]{2,1,0:T(8,128)(2,1)S(1)} collective-permute-done((bf16[4,64,384]{2,1,0:T(8,128)(2,1)}, bf16[4,64,384]{2,1,0:T(8,128)(2,1)S(1)}, u32[]{:S(2)}, u32[]{:S(2)}) %collective-permute-start.42) | collective-permute-done | bytes 196640 | tf_op jit(solution)/shard_map/ppermute | solution.py:402
  435.3 4.4 collective-permute-done.52.refs_2_
  441.4 2.9 collective-permute-done.53.refs_5_
  444.7 2.8 collective-permute-done.65.refs_2_
  447.5 3.8 collective-permute-done.44.refs_3_
  453.5 10.2 %collective-permute-done.59 = f32[4,1024]{1,0:T(4,128)S(1)} collective-permute-done((f32[4,1024]{1,0:T(4,128)S(1)}, f32[4,1024]{1,0:T(4,128)S(1)}, u32[]{:S(2)}, u32[]{:S(2)}) %collective-permute-start.59) | collective-permute-done | bytes 16416 | tf_op jit(solution)/shard_map/ppermute | solution.py:397
  465.8 2.3 collective-permute-done.60
  471.5 3.1 settle_qkv.1
  475.2 1.9 collective-permute-done.56.refs_7_
  477.1 4.0 settle_turned.1
  481.6 3.6 settle_pair.1
  (360 shorter events, 106.7 us)
Async XLA Ops:
  0.7 16.1 %collective-permute-start.5 = (bf16[256,1024]{1,0:T(8,128)(2,1)}, bf16[256,1024]{1,0:T(8,128)(2,1)S(1)}, u32[]{:S(2)}, u32[]{:S(2)}) collective-permute-start(bf16[256,1024]{1,0:T(8,128)(2,1)} %bitcast.66), channel_id=1, source_target_pairs={{0,2},{1,3},{2,0},{3,1},{4,6},{5,7},{6,4},{7,5},{8,10},{9,11},{10,... | collective-permute-start | bytes 1572872 | tf_op jit(solution)/shard_map/ppermute | solution.py:392
  3.7 31.8 %collective-permute-start.4 = (bf16[256,1024]{1,0:T(8,128)(2,1)}, bf16[256,1024]{1,0:T(8,128)(2,1)S(1)}, u32[]{:S(2)}, u32[]{:S(2)}) collective-permute-start(bf16[256,1024]{1,0:T(8,128)(2,1)} %bitcast.67), channel_id=1, source_target_pairs={{0,1},{1,0},{2,3},{3,2},{4,5},{5,4},{6,7},{7,6},{8,9},{9,8},{10,11... | collective-permute-start | bytes 1572872 | tf_op jit(solution)/shard_map/ppermute | solution.py:388
  8.6 15.4 %collective-permute-start.2 = (bf16[256,768]{1,0:T(8,128)(2,1)}, bf16[256,768]{1,0:T(8,128)(2,1)}, u32[]{:S(2)}, u32[]{:S(2)}) collective-permute-start(bf16[256,768]{1,0:T(8,128)(2,1)} %get-tuple-element.110), channel_id=1, source_target_pairs={{0,1},{1,0},{2,3},{3,2},{4,5},{5,4},{6,7},{7,6},{8,9},{9,8},{10,11... | collective-permute-start | bytes 1179656 | tf_op jit(solution)/shard_map/ppermute | solution.py:388
  9.1 22.3 %collective-permute-start = (bf16[256,768]{1,0:T(8,128)(2,1)}, bf16[256,768]{1,0:T(8,128)(2,1)}, u32[]{:S(2)}, u32[]{:S(2)}) collective-permute-start(bf16[256,768]{1,0:T(8,128)(2,1)} %get-tuple-element.108), channel_id=1, source_target_pairs={{0,1},{1,0},{2,3},{3,2},{4,5},{5,4},{6,7},{7,6},{8,9},{9,8},{10,11... | collective-permute-start | bytes 1179656 | tf_op jit(solution)/shard_map/ppermute | solution.py:388
  9.1 22.3 %collective-permute-start.1 = (bf16[256,768]{1,0:T(8,128)(2,1)}, bf16[256,768]{1,0:T(8,128)(2,1)}, u32[]{:S(2)}, u32[]{:S(2)}) collective-permute-start(bf16[256,768]{1,0:T(8,128)(2,1)} %get-tuple-element.109), channel_id=1, source_target_pairs={{0,2},{1,3},{2,0},{3,1},{4,6},{5,7},{6,4},{7,5},{8,10},{9,11},{10,... | collective-permute-start | bytes 1179656 | tf_op jit(solution)/shard_map/ppermute | solution.py:392
  16.8 18.7 %collective-permute-start.6 = (bf16[256,1024]{1,0:T(8,128)(2,1)S(1)}, bf16[256,1024]{1,0:T(8,128)(2,1)S(1)}, u32[]{:S(2)}, u32[]{:S(2)}) collective-permute-start(bf16[256,1024]{1,0:T(8,128)(2,1)S(1)} %collective-permute-done.5.x2), channel_id=1, source_target_pairs={{0,1},{1,0},{2,3},{3,2},{4,5},{5,4},{6,7},{7,6},{8,9},{9,8},{10,11... | collective-permute-start | bytes 1572872 | tf_op jit(solution)/shard_map/ppermute | solution.py:388
  24.0 11.5 %collective-permute-start.3 = (bf16[256,768]{1,0:T(8,128)(2,1)}, bf16[256,768]{1,0:T(8,128)(2,1)S(1)}, u32[]{:S(2)}, u32[]{:S(2)}) collective-permute-start(bf16[256,768]{1,0:T(8,128)(2,1)} %collective-permute-done.2), channel_id=1, source_target_pairs={{0,2},{1,3},{2,0},{3,1},{4,6},{5,7},{6,4},{7,5},{8,10},{9,11},{10,... | collective-permute-start | bytes 1179656 | tf_op jit(solution)/shard_map/ppermute | solution.py:392
  42.8 47.3 %all-to-all-start = ((bf16[8,3,256,128]{3,2,1,0:T(8,128)(2,1)}), bf16[8,3,256,128]{3,2,1,0:T(8,128)(2,1)}, u32[]{:S(2)}, u32[]{:S(2)}) async-start(bf16[8,3,256,128]{3,2,1,0:T(8,128)(2,1)} %project.1), calls=%async_computation | async-start | bytes 3145728 | tf_op jit(solution)/shard_map/all_to_all | solution.py:1312
  49.5 17.5 %collective-permute-start.7 = (bf16[256,1408]{1,0:T(8,128)(2,1)}, bf16[256,1408]{1,0:T(8,128)(2,1)S(1)}, u32[]{:S(2)}, u32[]{:S(2)}) collective-permute-start(bf16[256,1408]{1,0:T(8,128)(2,1)} %copy-done.68), channel_id=1, source_target_pairs={{0,2},{1,3},{2,0},{3,1},{4,6},{5,7},{6,4},{7,5},{8,10},{9,11},{10,... | collective-permute-start | bytes 2162696 | tf_op jit(solution)/shard_map/ppermute | solution.py:392
  51.1 15.9 %collective-permute-start.9 = (bf16[256,1408]{1,0:T(8,128)(2,1)S(1)}, bf16[256,1408]{1,0:T(8,128)(2,1)S(1)}, u32[]{:S(2)}, u32[]{:S(2)}) collective-permute-start(bf16[256,1408]{1,0:T(8,128)(2,1)S(1)} %copy-done.67), channel_id=1, source_target_pairs={{0,1},{1,0},{2,3},{3,2},{4,5},{5,4},{6,7},{7,6},{8,9},{9,8},{10,11... | collective-permute-start | bytes 2162696 | tf_op jit(solution)/shard_map/ppermute | solution.py:388
  67.1 16.4 %collective-permute-start.10 = (bf16[256,1408]{1,0:T(8,128)(2,1)S(1)}, bf16[256,1408]{1,0:T(8,128)(2,1)S(1)}, u32[]{:S(2)}, u32[]{:S(2)}) collective-permute-start(bf16[256,1408]{1,0:T(8,128)(2,1)S(1)} %collective-permute-done.9), channel_id=1, source_target_pairs={{0,2},{1,3},{2,0},{3,1},{4,6},{5,7},{6,4},{7,5},{8,10},{9,11},{10,... | collective-permute-start | bytes 2162696 | tf_op jit(solution)/shard_map/ppermute | solution.py:392
  69.0 39.9 %collective-permute-start.8 = (bf16[256,1408]{1,0:T(8,128)(2,1)S(1)}, bf16[256,1408]{1,0:T(8,128)(2,1)S(1)}, u32[]{:S(2)}, u32[]{:S(2)}) collective-permute-start(bf16[256,1408]{1,0:T(8,128)(2,1)S(1)} %collective-permute-done.7.w2y), channel_id=1, source_target_pairs={{0,4},{4,0},{8,12},{12,8},{16,20},{20,16},{24,28},{28,24},{1,5},{5... | collective-permute-start | bytes 2162696 | tf_op jit(solution)/shard_map/ppermute | solution.py:397
  83.5 25.5 %collective-permute-start.12 = (bf16[704,512]{1,0:T(8,128)(2,1)}, bf16[704,512]{1,0:T(8,128)(2,1)}, u32[]{:S(2)}, u32[]{:S(2)}) collective-permute-start(bf16[704,512]{1,0:T(8,128)(2,1)} %copy-done.65), channel_id=1, source_target_pairs={{0,2},{1,3},{2,0},{3,1},{4,6},{5,7},{6,4},{7,5},{8,10},{9,11},{10,... | collective-permute-start | bytes 2162696 | tf_op jit(solution)/shard_map/ppermute | solution.py:392
  85.0 24.0 %collective-permute-start.11 = (bf16[256,1408]{1,0:T(8,128)(2,1)S(1)}, bf16[256,1408]{1,0:T(8,128)(2,1)S(1)}, u32[]{:S(2)}, u32[]{:S(2)}) collective-permute-start(bf16[256,1408]{1,0:T(8,128)(2,1)S(1)} %collective-permute-done.10.w3y), channel_id=1, source_target_pairs={{0,4},{4,0},{8,12},{12,8},{16,20},{20,16},{24,28},{28,24},{1,5},{5... | collective-permute-start | bytes 2162696 | tf_op jit(solution)/shard_map/ppermute | solution.py:397
  109.0 24.9 %all-to-all-start.1 = ((bf16[8,256,128]{2,1,0:T(8,128)(2,1)}), bf16[8,256,128]{2,1,0:T(8,128)(2,1)}, u32[]{:S(2)}, u32[]{:S(2)}) async-start(bf16[8,256,128]{2,1,0:T(8,128)(2,1)} %copy-done.47), calls=%async_computation.1 | async-start | bytes 1048576 | tf_op jit(solution)/shard_map/all_to_all | solution.py:1332
  113.5 20.4 %collective-permute-start.13 = (bf16[704,512]{1,0:T(8,128)(2,1)}, bf16[704,512]{1,0:T(8,128)(2,1)}, u32[]{:S(2)}, u32[]{:S(2)}) collective-permute-start(bf16[704,512]{1,0:T(8,128)(2,1)} %collective-permute-done.12.down_y), channel_id=1, source_target_pairs={{0,4},{4,0},{8,12},{12,8},{16,20},{20,16},{24,28},{28,24},{1,5},{5... | collective-permute-start | bytes 2162696 | tf_op jit(solution)/shard_map/ppermute | solution.py:397
  115.5 9.9 %collective-permute-start.14 = (bf16[256,1024]{1,0:T(8,128)(2,1)}, bf16[256,1024]{1,0:T(8,128)(2,1)S(1)}, u32[]{:S(2)}, u32[]{:S(2)}) collective-permute-start(bf16[256,1024]{1,0:T(8,128)(2,1)} %w_near_ref.3), channel_id=1, source_target_pairs={{0,2},{1,3},{2,0},{3,1},{4,6},{5,7},{6,4},{7,5},{8,10},{9,11},{10,... | collective-permute-start | bytes 1572872 | tf_op jit(solution)/shard_map/ppermute | solution.py:392
  116.1 40.9 %collective-permute-start.18 = (bf16[2,256,1408]{2,1,0:T(8,128)(2,1)}, bf16[2,256,1408]{2,1,0:T(8,128)(2,1)S(1)}, u32[]{:S(2)}, u32[]{:S(2)}) collective-permute-start(bf16[2,256,1408]{2,1,0:T(8,128)(2,1)} %copy-done.62), channel_id=1, source_target_pairs={{0,1},{1,0},{2,3},{3,2},{4,5},{5,4},{6,7},{7,6},{8,9},{9,8},{10,11... | collective-permute-start | bytes 4325384 | tf_op jit(solution)/shard_map/ppermute | solution.py:388
  146.9 53.7 %all-to-all-start.2 = ((bf16[4,256,1024]{2,1,0:T(8,128)(2,1)}), bf16[4,256,1024]{2,1,0:T(8,128)(2,1)}, u32[]{:S(2)}, u32[]{:S(2)}) async-start(bf16[4,256,1024]{2,1,0:T(8,128)(2,1)} %pad_maximum_fusion), calls=%async_computation.2 | async-start | bytes 4194304 | tf_op jit(solution)/shard_map/all_to_all | solution.py:1360
  156.4 17.6 %collective-permute-start.19 = (bf16[256,1024]{1,0:T(8,128)(2,1)S(1)}, bf16[256,1024]{1,0:T(8,128)(2,1)S(1)}, u32[]{:S(2)}, u32[]{:S(2)}) collective-permute-start(bf16[256,1024]{1,0:T(8,128)(2,1)S(1)} %get-tuple-element.137.own_ref.refs_0_), channel_id=1, source_target_pairs={{0,2},{1,3},{2,0},{3,1},{4,6},{5,7},{6,4},{7,5},{8,10},{9,11},{10,... | collective-permute-start | bytes 1572872 | tf_op jit(solution)/shard_map/ppermute | solution.py:392
  179.1 16.2 %collective-permute-start.22 = (bf16[256,1024]{1,0:T(8,128)(2,1)S(1)}, bf16[256,1024]{1,0:T(8,128)(2,1)S(1)}, u32[]{:S(2)}, u32[]{:S(2)}) collective-permute-start(bf16[256,1024]{1,0:T(8,128)(2,1)S(1)} %get-tuple-element.145.own_ref.refs_0_), channel_id=1, source_target_pairs={{0,2},{1,3},{2,0},{3,1},{4,6},{5,7},{6,4},{7,5},{8,10},{9,11},{10,... | collective-permute-start | bytes 1572872 | tf_op jit(solution)/shard_map/ppermute | solution.py:392
  200.6 54.5 %collective-permute-start.30 = (bf16[4,256,1024]{2,1,0:T(8,128)(2,1)}, bf16[4,256,1024]{2,1,0:T(8,128)(2,1)}, u32[]{:S(2)}, u32[]{:S(2)}) collective-permute-start(bf16[4,256,1024]{2,1,0:T(8,128)(2,1)} %all-to-all-done.2.own_ref), channel_id=1, source_target_pairs={{0,4},{4,0},{8,12},{12,8},{16,20},{20,16},{24,28},{28,24},{1,5},{5... | collective-permute-start | bytes 6291464 | tf_op jit(solution)/shard_map/ppermute | solution.py:397
  210.0 27.5 %collective-permute-start.28 = (bf16[256,1024]{1,0:T(8,128)(2,1)}, bf16[256,1024]{1,0:T(8,128)(2,1)S(1)}, u32[]{:S(2)}, u32[]{:S(2)}) collective-permute-start(bf16[256,1024]{1,0:T(8,128)(2,1)} %get-tuple-element.151.own_ref.refs_6_), channel_id=1, source_target_pairs={{0,2},{1,3},{2,0},{3,1},{4,6},{5,7},{6,4},{7,5},{8,10},{9,11},{10,... | collective-permute-start | bytes 1572872 | tf_op jit(solution)/shard_map/ppermute | solution.py:392
  215.6 16.9 %collective-permute-start.25 = (bf16[4,256,128]{2,1,0:T(8,128)(2,1)S(1)}, bf16[4,256,128]{2,1,0:T(8,128)(2,1)S(1)}, u32[]{:S(2)}, u32[]{:S(2)}) collective-permute-start(bf16[4,256,128]{2,1,0:T(8,128)(2,1)S(1)} %get-tuple-element.153), channel_id=1, source_target_pairs={{0,2},{1,3},{2,0},{3,1},{4,6},{5,7},{6,4},{7,5},{8,10},{9,11},{10,... | collective-permute-start | bytes 786440 | tf_op jit(solution)/shard_map/ppermute | solution.py:392
  233.3 21.8 %all-to-all-start.3 = ((bf16[8,256,128]{2,1,0:T(8,128)(2,1)}), bf16[8,256,128]{2,1,0:T(8,128)(2,1)}, u32[]{:S(2)}, u32[]{:S(2)}) async-start(bf16[8,256,128]{2,1,0:T(8,128)(2,1)} %pad_maximum_fusion.5), calls=%async_computation.3 | async-start | bytes 1048576 | tf_op jit(solution)/shard_map/all_to_all | solution.py:1520
  238.4 51.1 %collective-permute-start.33 = (bf16[4,4,32,1408]{3,2,1,0:T(8,128)(2,1)}, bf16[4,4,32,1408]{3,2,1,0:T(8,128)(2,1)}, u32[]{:S(2)}, u32[]{:S(2)}) collective-permute-start(bf16[4,4,32,1408]{3,2,1,0:T(8,128)(2,1)} %get-tuple-element.161), channel_id=1, source_target_pairs={{0,4},{4,0},{8,12},{12,8},{16,20},{20,16},{24,28},{28,24},{1,5},{5... | collective-permute-start | bytes 4325384 | tf_op jit(solution)/shard_map/ppermute | solution.py:397
  276.2 64.0 %all-to-all-start.4 = ((bf16[8,3,256,128]{3,2,1,0:T(8,128)(2,1)}), bf16[8,3,256,128]{3,2,1,0:T(8,128)(2,1)S(1)}, u32[]{:S(2)}, u32[]{:S(2)}) async-start(bf16[8,3,256,128]{3,2,1,0:T(8,128)(2,1)} %copy-done.20), calls=%async_computation.4 | async-start | bytes 3145728 | tf_op jit(solution)/shard_map/all_to_all | solution.py:1571
  280.7 43.1 %collective-permute-start.34 = (bf16[4,4,32,960]{3,2,1,0:T(8,128)(2,1)S(1)}, bf16[4,4,32,960]{3,2,1,0:T(8,128)(2,1)}, u32[]{:S(2)}, u32[]{:S(2)}) collective-permute-start(bf16[4,4,32,960]{3,2,1,0:T(8,128)(2,1)S(1)} %copy-done.99), channel_id=1, source_target_pairs={{0,4},{4,0},{8,12},{12,8},{16,20},{20,16},{24,28},{28,24},{1,5},{5... | collective-permute-start | bytes 2949128 | tf_op jit(solution)/shard_map/ppermute | solution.py:397
  324.9 11.4 %collective-permute-start.35 = (bf16[4,32,1408]{2,1,0:T(8,128)(2,1)S(1)}, bf16[4,32,1408]{2,1,0:T(8,128)(2,1)S(1)}, u32[]{:S(2)}, u32[]{:S(2)}) collective-permute-start(bf16[4,32,1408]{2,1,0:T(8,128)(2,1)S(1)} %fusion.10), channel_id=1, source_target_pairs={{0,8},{4,12},{8,16},{12,20},{16,24},{20,28},{24,0},{28,4},{1,9},{5... | collective-permute-start | bytes 1081352 | tf_op jit(solution)/shard_map/ppermute | solution.py:402
  338.2 14.9 %collective-permute-start.36 = (bf16[4,32,1408]{2,1,0:T(8,128)(2,1)}, bf16[4,32,1408]{2,1,0:T(8,128)(2,1)}, u32[]{:S(2)}, u32[]{:S(2)}) collective-permute-start(bf16[4,32,1408]{2,1,0:T(8,128)(2,1)} %fusion.2), channel_id=1, source_target_pairs={{0,8},{4,12},{8,16},{12,20},{16,24},{20,28},{24,0},{28,4},{1,9},{5... | collective-permute-start | bytes 1081352 | tf_op jit(solution)/shard_map/ppermute | solution.py:402
  338.9 14.2 %collective-permute-start.37 = (bf16[4,64,384]{2,1,0:T(8,128)(2,1)}, bf16[4,64,384]{2,1,0:T(8,128)(2,1)}, u32[]{:S(2)}, u32[]{:S(2)}) collective-permute-start(bf16[4,64,384]{2,1,0:T(8,128)(2,1)} %slice_bitcast_fusion), channel_id=1, source_target_pairs={{0,8},{4,12},{8,16},{12,20},{16,24},{20,28},{24,0},{28,4},{1,9},{5... | collective-permute-start | bytes 589832 | tf_op jit(solution)/shard_map/ppermute | solution.py:402
  346.7 49.4 %collective-permute-start.31 = (bf16[2,256,1024]{2,1,0:T(8,128)(2,1)}, bf16[2,256,1024]{2,1,0:T(8,128)(2,1)S(1)}, u32[]{:S(2)}, u32[]{:S(2)}) collective-permute-start(bf16[2,256,1024]{2,1,0:T(8,128)(2,1)} %get-tuple-element.171), channel_id=1, source_target_pairs={{0,1},{1,0},{2,3},{3,2},{4,5},{5,4},{6,7},{7,6},{8,9},{9,8},{10,11... | collective-permute-start | bytes 3145736 | tf_op jit(solution)/shard_map/ppermute | solution.py:388
  354.2 15.4 %collective-permute-start.47 = (bf16[4,32,960]{2,1,0:T(8,128)(2,1)S(1)}, bf16[4,32,960]{2,1,0:T(8,128)(2,1)S(1)}, u32[]{:S(2)}, u32[]{:S(2)}) collective-permute-start(bf16[4,32,960]{2,1,0:T(8,128)(2,1)S(1)} %fusion.12), channel_id=1, source_target_pairs={{0,8},{4,12},{8,16},{12,20},{16,24},{20,28},{24,0},{28,4},{1,9},{5... | collective-permute-start | bytes 737288 | tf_op jit(solution)/shard_map/ppermute | solution.py:402
  355.2 14.2 %collective-permute-start.38 = (bf16[4,64,384]{2,1,0:T(8,128)(2,1)S(1)}, bf16[4,64,384]{2,1,0:T(8,128)(2,1)S(1)}, u32[]{:S(2)}, u32[]{:S(2)}) collective-permute-start(bf16[4,64,384]{2,1,0:T(8,128)(2,1)S(1)} %fusion.7), channel_id=1, source_target_pairs={{0,8},{4,12},{8,16},{12,20},{16,24},{20,28},{24,0},{28,4},{1,9},{5... | collective-permute-start | bytes 589832 | tf_op jit(solution)/shard_map/ppermute | solution.py:402
  356.7 28.6 %collective-permute-start.62 = (bf16[4,32,1408]{2,1,0:T(8,128)(2,1)S(1)}, bf16[4,32,1408]{2,1,0:T(8,128)(2,1)S(1)}, u32[]{:S(2)}, u32[]{:S(2)}) collective-permute-start(bf16[4,32,1408]{2,1,0:T(8,128)(2,1)S(1)} %fusion), channel_id=1, source_target_pairs={{0,8},{4,12},{8,16},{12,20},{16,24},{20,28},{24,0},{28,4},{1,9},{5... | collective-permute-start | bytes 1081352 | tf_op jit(solution)/shard_map/ppermute | solution.py:402
  369.5 11.0 %collective-permute-start.39 = (bf16[4,64,384]{2,1,0:T(8,128)(2,1)S(1)}, bf16[4,64,384]{2,1,0:T(8,128)(2,1)S(1)}, u32[]{:S(2)}, u32[]{:S(2)}) collective-permute-start(bf16[4,64,384]{2,1,0:T(8,128)(2,1)S(1)} %fusion.8), channel_id=1, source_target_pairs={{0,8},{4,12},{8,16},{12,20},{16,24},{20,28},{24,0},{28,4},{1,9},{5... | collective-permute-start | bytes 589832 | tf_op jit(solution)/shard_map/ppermute | solution.py:402
  371.4 22.7 %collective-permute-start.48 = (bf16[4,32,960]{2,1,0:T(8,128)(2,1)}, bf16[4,32,960]{2,1,0:T(8,128)(2,1)}, u32[]{:S(2)}, u32[]{:S(2)}) collective-permute-start(bf16[4,32,960]{2,1,0:T(8,128)(2,1)} %fusion.4), channel_id=1, source_target_pairs={{0,8},{4,12},{8,16},{12,20},{16,24},{20,28},{24,0},{28,4},{1,9},{5... | collective-permute-start | bytes 737288 | tf_op jit(solution)/shard_map/ppermute | solution.py:402
  381.3 9.4 %all-to-all-start.5 = ((bf16[4,64,384]{2,1,0:T(8,128)(2,1)}), bf16[4,64,384]{2,1,0:T(8,128)(2,1)}, u32[]{:S(2)}, u32[]{:S(2)}) async-start(bf16[4,64,384]{2,1,0:T(8,128)(2,1)} %fusion.9), calls=%async_computation.5 | async-start | bytes 393216 | tf_op jit(solution)/shard_map/all_to_all | solution.py:1603
  390.7 11.0 %all-to-all-start.6 = ((bf16[4,32,1408]{2,1,0:T(8,128)(2,1)}), bf16[4,32,1408]{2,1,0:T(8,128)(2,1)S(1)}, u32[]{:S(2)}, u32[]{:S(2)}) async-start(bf16[4,32,1408]{2,1,0:T(8,128)(2,1)} %fusion.1), calls=%async_computation.6 | async-start | bytes 720896 | tf_op jit(solution)/shard_map/all_to_all | solution.py:1603
  396.1 11.2 %collective-permute-start.49 = (bf16[4,32,960]{2,1,0:T(8,128)(2,1)}, bf16[4,32,960]{2,1,0:T(8,128)(2,1)}, u32[]{:S(2)}, u32[]{:S(2)}) collective-permute-start(bf16[4,32,960]{2,1,0:T(8,128)(2,1)} %fusion.5), channel_id=1, source_target_pairs={{0,8},{4,12},{8,16},{12,20},{16,24},{20,28},{24,0},{28,4},{1,9},{5... | collective-permute-start | bytes 737288 | tf_op jit(solution)/shard_map/ppermute | solution.py:402
  396.1 15.4 %collective-permute-start.40 = (bf16[4,64,384]{2,1,0:T(8,128)(2,1)}, bf16[4,64,384]{2,1,0:T(8,128)(2,1)}, u32[]{:S(2)}, u32[]{:S(2)}) collective-permute-start(bf16[4,64,384]{2,1,0:T(8,128)(2,1)} %all-to-all-done.5.refs_0_), channel_id=1, source_target_pairs={{0,8},{4,12},{8,16},{12,20},{16,24},{20,28},{24,0},{28,4},{1,9},{5... | collective-permute-start | bytes 589832 | tf_op jit(solution)/shard_map/ppermute | solution.py:402
  396.1 15.4 %collective-permute-start.41 = (bf16[4,64,384]{2,1,0:T(8,128)(2,1)}, bf16[4,64,384]{2,1,0:T(8,128)(2,1)}, u32[]{:S(2)}, u32[]{:S(2)}) collective-permute-start(bf16[4,64,384]{2,1,0:T(8,128)(2,1)} %all-to-all-done.5.refs_0_), channel_id=1, source_target_pairs={{0,4},{4,0},{8,12},{12,8},{16,20},{20,16},{24,28},{28,24},{1,5},{5... | collective-permute-start | bytes 589832 | tf_op jit(solution)/shard_map/ppermute | solution.py:397
  397.1 28.0 %collective-permute-start.32 = (bf16[256,1024]{1,0:T(8,128)(2,1)}, bf16[256,1024]{1,0:T(8,128)(2,1)S(1)}, u32[]{:S(2)}, u32[]{:S(2)}) collective-permute-start(bf16[256,1024]{1,0:T(8,128)(2,1)} %fusion.3), channel_id=1, source_target_pairs={{0,2},{1,3},{2,0},{3,1},{4,6},{5,7},{6,4},{7,5},{8,10},{9,11},{10,... | collective-permute-start | bytes 1572872 | tf_op jit(solution)/shard_map/ppermute | solution.py:392
  401.7 22.7 %collective-permute-start.63 = (bf16[4,32,1408]{2,1,0:T(8,128)(2,1)S(1)}, bf16[4,32,1408]{2,1,0:T(8,128)(2,1)S(1)}, u32[]{:S(2)}, u32[]{:S(2)}) collective-permute-start(bf16[4,32,1408]{2,1,0:T(8,128)(2,1)S(1)} %all-to-all-done.6.refs_0_), channel_id=1, source_target_pairs={{0,8},{4,12},{8,16},{12,20},{16,24},{20,28},{24,0},{28,4},{1,9},{5... | collective-permute-start | bytes 1081352 | tf_op jit(solution)/shard_map/ppermute | solution.py:402
  407.3 17.1 %collective-permute-start.64 = (bf16[4,32,1408]{2,1,0:T(8,128)(2,1)S(1)}, bf16[4,32,1408]{2,1,0:T(8,128)(2,1)S(1)}, u32[]{:S(2)}, u32[]{:S(2)}) collective-permute-start(bf16[4,32,1408]{2,1,0:T(8,128)(2,1)S(1)} %all-to-all-done.6.refs_0_), channel_id=1, source_target_pairs={{0,4},{4,0},{8,12},{12,8},{16,20},{20,16},{24,28},{28,24},{1,5},{5... | collective-permute-start | bytes 1081352 | tf_op jit(solution)/shard_map/ppermute | solution.py:397
  411.5 12.8 %collective-permute-start.50 = (bf16[4,32,960]{2,1,0:T(8,128)(2,1)S(1)}, bf16[4,32,960]{2,1,0:T(8,128)(2,1)S(1)}, u32[]{:S(2)}, u32[]{:S(2)}) collective-permute-start(bf16[4,32,960]{2,1,0:T(8,128)(2,1)S(1)} %fusion.6.refs_0_), channel_id=1, source_target_pairs={{0,8},{4,12},{8,16},{12,20},{16,24},{20,28},{24,0},{28,4},{1,9},{5... | collective-permute-start | bytes 737288 | tf_op jit(solution)/shard_map/ppermute | solution.py:402
  411.5 12.8 %collective-permute-start.51 = (bf16[4,32,960]{2,1,0:T(8,128)(2,1)S(1)}, bf16[4,32,960]{2,1,0:T(8,128)(2,1)S(1)}, u32[]{:S(2)}, u32[]{:S(2)}) collective-permute-start(bf16[4,32,960]{2,1,0:T(8,128)(2,1)S(1)} %fusion.6.refs_0_), channel_id=1, source_target_pairs={{0,4},{4,0},{8,12},{12,8},{16,20},{20,16},{24,28},{28,24},{1,5},{5... | collective-permute-start | bytes 737288 | tf_op jit(solution)/shard_map/ppermute | solution.py:397
  424.3 9.8 %collective-permute-start.42 = (bf16[4,64,384]{2,1,0:T(8,128)(2,1)}, bf16[4,64,384]{2,1,0:T(8,128)(2,1)S(1)}, u32[]{:S(2)}, u32[]{:S(2)}) collective-permute-start(bf16[4,64,384]{2,1,0:T(8,128)(2,1)} %collective-permute-done.40.refs_1_), channel_id=1, source_target_pairs={{0,8},{4,12},{8,16},{12,20},{16,24},{20,28},{24,0},{28,4},{1,9},{5... | collective-permute-start | bytes 589832 | tf_op jit(solution)/shard_map/ppermute | solution.py:402
  424.3 9.8 %collective-permute-start.43 = (bf16[4,64,384]{2,1,0:T(8,128)(2,1)}, bf16[4,64,384]{2,1,0:T(8,128)(2,1)S(1)}, u32[]{:S(2)}, u32[]{:S(2)}) collective-permute-start(bf16[4,64,384]{2,1,0:T(8,128)(2,1)} %collective-permute-done.40.refs_1_), channel_id=1, source_target_pairs={{0,4},{4,0},{8,12},{12,8},{16,20},{20,16},{24,28},{28,24},{1,5},{5... | collective-permute-start | bytes 589832 | tf_op jit(solution)/shard_map/ppermute | solution.py:397
  424.3 15.4 %collective-permute-start.52 = (bf16[4,32,960]{2,1,0:T(8,128)(2,1)S(1)}, bf16[4,32,960]{2,1,0:T(8,128)(2,1)S(1)}, u32[]{:S(2)}, u32[]{:S(2)}) collective-permute-start(bf16[4,32,960]{2,1,0:T(8,128)(2,1)S(1)} %collective-permute-done.50.refs_1_), channel_id=1, source_target_pairs={{0,8},{4,12},{8,16},{12,20},{16,24},{20,28},{24,0},{28,4},{1,9},{5... | collective-permute-start | bytes 737288 | tf_op jit(solution)/shard_map/ppermute | solution.py:402
  424.4 23.1 %collective-permute-start.65 = (bf16[4,32,1408]{2,1,0:T(8,128)(2,1)S(1)}, bf16[4,32,1408]{2,1,0:T(8,128)(2,1)S(1)}, u32[]{:S(2)}, u32[]{:S(2)}) collective-permute-start(bf16[4,32,1408]{2,1,0:T(8,128)(2,1)S(1)} %collective-permute-done.63.refs_1_), channel_id=1, source_target_pairs={{0,8},{4,12},{8,16},{12,20},{16,24},{20,28},{24,0},{28,4},{1,9},{5... | collective-permute-start | bytes 1081352 | tf_op jit(solution)/shard_map/ppermute | solution.py:402
  425.1 22.4 %collective-permute-start.66 = (bf16[4,32,1408]{2,1,0:T(8,128)(2,1)S(1)}, bf16[4,32,1408]{2,1,0:T(8,128)(2,1)S(1)}, u32[]{:S(2)}, u32[]{:S(2)}) collective-permute-start(bf16[4,32,1408]{2,1,0:T(8,128)(2,1)S(1)} %collective-permute-done.63.refs_1_), channel_id=1, source_target_pairs={{0,4},{4,0},{8,12},{12,8},{16,20},{20,16},{24,28},{28,24},{1,5},{5... | collective-permute-start | bytes 1081352 | tf_op jit(solution)/shard_map/ppermute | solution.py:397
  434.1 10.2 %collective-permute-start.53 = (bf16[4,32,960]{2,1,0:T(8,128)(2,1)S(1)}, bf16[4,32,960]{2,1,0:T(8,128)(2,1)S(1)}, u32[]{:S(2)}, u32[]{:S(2)}) collective-permute-start(bf16[4,32,960]{2,1,0:T(8,128)(2,1)S(1)} %collective-permute-done.50.refs_1_), channel_id=1, source_target_pairs={{0,4},{4,0},{8,12},{12,8},{16,20},{20,16},{24,28},{28,24},{1,5},{5... | collective-permute-start | bytes 737288 | tf_op jit(solution)/shard_map/ppermute | solution.py:397
  435.3 16.0 %collective-permute-start.44 = (bf16[4,64,384]{2,1,0:T(8,128)(2,1)S(1)}, bf16[4,64,384]{2,1,0:T(8,128)(2,1)S(1)}, u32[]{:S(2)}, u32[]{:S(2)}) collective-permute-start(bf16[4,64,384]{2,1,0:T(8,128)(2,1)S(1)} %collective-permute-done.42.refs_2_), channel_id=1, source_target_pairs={{0,8},{4,12},{8,16},{12,20},{16,24},{20,28},{24,0},{28,4},{1,9},{5... | collective-permute-start | bytes 589832 | tf_op jit(solution)/shard_map/ppermute | solution.py:402
  439.8 11.6 %collective-permute-start.58 = (f32[4,1024]{1,0:T(4,128)S(1)}, f32[4,1024]{1,0:T(4,128)S(1)}, u32[]{:S(2)}, u32[]{:S(2)}) collective-permute-start(f32[4,1024]{1,0:T(4,128)S(1)} %fusion.20), channel_id=1, source_target_pairs={{0,2},{1,3},{2,0},{3,1},{4,6},{5,7},{6,4},{7,5},{8,10},{9,11},{10,... | collective-permute-start | bytes 49160 | tf_op jit(solution)/shard_map/ppermute | solution.py:392
  444.4 7.8 %collective-permute-start.45 = (bf16[4,64,384]{2,1,0:T(8,128)(2,1)S(1)}, bf16[4,64,384]{2,1,0:T(8,128)(2,1)S(1)}, u32[]{:S(2)}, u32[]{:S(2)}) collective-permute-start(bf16[4,64,384]{2,1,0:T(8,128)(2,1)S(1)} %collective-permute-done.42.refs_2_), channel_id=1, source_target_pairs={{0,4},{4,0},{8,12},{12,8},{16,20},{20,16},{24,28},{28,24},{1,5},{5... | collective-permute-start | bytes 589832 | tf_op jit(solution)/shard_map/ppermute | solution.py:397
  447.5 16.8 %collective-permute-start.54 = (bf16[4,32,960]{2,1,0:T(8,128)(2,1)S(1)}, bf16[4,32,960]{2,1,0:T(8,128)(2,1)S(1)}, u32[]{:S(2)}, u32[]{:S(2)}) collective-permute-start(bf16[4,32,960]{2,1,0:T(8,128)(2,1)S(1)} %collective-permute-done.52.refs_2_), channel_id=1, source_target_pairs={{0,8},{4,12},{8,16},{12,20},{16,24},{20,28},{24,0},{28,4},{1,9},{5... | collective-permute-start | bytes 737288 | tf_op jit(solution)/shard_map/ppermute | solution.py:402
  447.5 17.2 %collective-permute-start.55 = (bf16[4,32,960]{2,1,0:T(8,128)(2,1)S(1)}, bf16[4,32,960]{2,1,0:T(8,128)(2,1)S(1)}, u32[]{:S(2)}, u32[]{:S(2)}) collective-permute-start(bf16[4,32,960]{2,1,0:T(8,128)(2,1)S(1)} %collective-permute-done.52.refs_2_), channel_id=1, source_target_pairs={{0,4},{4,0},{8,12},{12,8},{16,20},{20,16},{24,28},{28,24},{1,5},{5... | collective-permute-start | bytes 737288 | tf_op jit(solution)/shard_map/ppermute | solution.py:397
  451.3 18.5 %collective-permute-start.67 = (bf16[4,32,1408]{2,1,0:T(8,128)(2,1)S(1)}, bf16[4,32,1408]{2,1,0:T(8,128)(2,1)S(1)}, u32[]{:S(2)}, u32[]{:S(2)}) collective-permute-start(bf16[4,32,1408]{2,1,0:T(8,128)(2,1)S(1)} %collective-permute-done.65.refs_2_), channel_id=1, source_target_pairs={{0,8},{4,12},{8,16},{12,20},{16,24},{20,28},{24,0},{28,4},{1,9},{5... | collective-permute-start | bytes 1081352 | tf_op jit(solution)/shard_map/ppermute | solution.py:402
  451.3 18.5 %collective-permute-start.68 = (bf16[4,32,1408]{2,1,0:T(8,128)(2,1)S(1)}, bf16[4,32,1408]{2,1,0:T(8,128)(2,1)S(1)}, u32[]{:S(2)}, u32[]{:S(2)}) collective-permute-start(bf16[4,32,1408]{2,1,0:T(8,128)(2,1)S(1)} %collective-permute-done.65.refs_2_), channel_id=1, source_target_pairs={{0,4},{4,0},{8,12},{12,8},{16,20},{20,16},{24,28},{28,24},{1,5},{5... | collective-permute-start | bytes 1081352 | tf_op jit(solution)/shard_map/ppermute | solution.py:397
  452.2 11.4 %collective-permute-start.59 = (f32[4,1024]{1,0:T(4,128)S(1)}, f32[4,1024]{1,0:T(4,128)S(1)}, u32[]{:S(2)}, u32[]{:S(2)}) collective-permute-start(f32[4,1024]{1,0:T(4,128)S(1)} %fusion.22), channel_id=1, source_target_pairs={{0,4},{4,0},{8,12},{12,8},{16,20},{20,16},{24,28},{28,24},{1,5},{5... | collective-permute-start | bytes 49160 | tf_op jit(solution)/shard_map/ppermute | solution.py:397
  463.6 7.8 %collective-permute-start.46 = (bf16[4,64,384]{2,1,0:T(8,128)(2,1)S(1)}, bf16[4,64,384]{2,1,0:T(8,128)(2,1)S(1)}, u32[]{:S(2)}, u32[]{:S(2)}) collective-permute-start(bf16[4,64,384]{2,1,0:T(8,128)(2,1)S(1)} %collective-permute-done.44.refs_3_), channel_id=1, source_target_pairs={{0,4},{4,0},{8,12},{12,8},{16,20},{20,16},{24,28},{28,24},{1,5},{5... | collective-permute-start | bytes 589832 | tf_op jit(solution)/shard_map/ppermute | solution.py:397
  464.6 12.4 %collective-permute-start.56 = (bf16[4,32,960]{2,1,0:T(8,128)(2,1)S(1)}, bf16[4,32,960]{2,1,0:T(8,128)(2,1)S(1)}, u32[]{:S(2)}, u32[]{:S(2)}) collective-permute-start(bf16[4,32,960]{2,1,0:T(8,128)(2,1)S(1)} %collective-permute-done.54.refs_3_), channel_id=1, source_target_pairs={{0,4},{4,0},{8,12},{12,8},{16,20},{20,16},{24,28},{28,24},{1,5},{5... | collective-permute-start | bytes 737288 | tf_op jit(solution)/shard_map/ppermute | solution.py:397
  469.9 11.8 %collective-permute-start.69 = (bf16[4,32,1408]{2,1,0:T(8,128)(2,1)S(1)}, bf16[4,32,1408]{2,1,0:T(8,128)(2,1)S(1)}, u32[]{:S(2)}, u32[]{:S(2)}) collective-permute-start(bf16[4,32,1408]{2,1,0:T(8,128)(2,1)S(1)} %collective-permute-done.67.refs_3_), channel_id=1, source_target_pairs={{0,4},{4,0},{8,12},{12,8},{16,20},{20,16},{24,28},{28,24},{1,5},{5... | collective-permute-start | bytes 1081352 | tf_op jit(solution)/shard_map/ppermute | solution.py:397
  (115 other events, 775.3 us)

commit v3 on v2

--- a/solution.py
+++ b/solution.py
@@ -422,7 +422,7 @@
 
 
 def cost(microseconds):
-    return pl.CostEstimate(flops=int(microseconds * 3e8), bytes_accessed=0, transcendentals=0)
+    return pl.CostEstimate(flops=int(microseconds * 1e6), bytes_accessed=0, transcendentals=0)
 
 
 def whole(shape):
@@ -483,7 +483,7 @@
 
 
 def split_ff_kernel(
-    me_ref, gate_ref, up_ref, down_ref, own_ref, own_sent, beside_ref, beside_sent, down_sent
+    me_ref, gate_ref, up_ref, own_ref, own_sent, beside_ref, beside_sent
 ):
     half = own_ref.shape[-1] // 2
     for me in range(PLACES):
@@ -501,8 +501,6 @@
     side = me_ref[1] % 2
     own_sent[...] = own_ref[1 - side]
     beside_sent[...] = beside_ref[1 - side]
-    columns = down_sent.shape[1]
-    down_sent[...] = down_ref[:, pl.ds(pl.multiple_of(side * columns, columns), columns)]
 
 
 def project_kernel(
@@ -526,63 +524,72 @@
             out_ref[head, kind] = part.astype(bf16)
 
 
-def chunk_facts(chunk, rows, prompt_chunks, cont_chunks, info_ref):
-    beyond = jnp.maximum(chunk - prompt_chunks, 0)
-    in_cont = chunk >= prompt_chunks
-    slot = beyond // cont_chunks
-    first = jnp.where(in_cont, prompt_chunks + slot * cont_chunks, 0)
-    ahead = jnp.where(in_cont, prompt_chunks, 0)
-    start = jnp.where(in_cont, beyond % cont_chunks, chunk) * rows
+def block_facts(block, rows, prompt_blocks, cont_blocks, info_ref):
+    beyond = jnp.maximum(block - prompt_blocks, 0)
+    in_cont = block >= prompt_blocks
+    slot = beyond // cont_blocks
+    first = jnp.where(in_cont, prompt_blocks + slot * cont_blocks, 0)
+    ahead = jnp.where(in_cont, prompt_blocks, 0)
+    start = jnp.where(in_cont, beyond % cont_blocks, block) * rows
     limit = jnp.where(in_cont, info_ref[1 + slot], info_ref[0])
     return first, ahead, start, limit
 
 
-def attend_kernel(
-    prompt_chunks, cont_chunks, info_ref, qkv_ref, out_ref, exact_ref, lse_ref
-):
-    chunk = pl.program_id(0)
-    rows = qkv_ref.shape[2]
-    scale = LOG2E / math.sqrt(HEAD)
-    query = qkv_ref[chunk, 0]
-    first, ahead, start, limit = chunk_facts(chunk, rows, prompt_chunks, cont_chunks, info_ref)
+def visit_blocks(visit, block, rows, first, ahead, info_ref, state):
     key_place = lax.broadcasted_iota(jnp.int32, (rows, rows), 0)
     query_place = lax.broadcasted_iota(jnp.int32, (rows, rows), 1)
-
-    def visit(key_chunk, bias, state):
+    key_row = lax.broadcasted_iota(jnp.int32, (rows, 1), 0)
+
+    def prompt_visit(key_block, state):
+        bias = jnp.where(key_block * rows + key_row < info_ref[0], 0.0, masked_out)
+        return visit(key_block, bias, False, state)
+
+    state = visit(block, jnp.where(key_place <= query_place, 0.0, masked_out), True, state)
+    state = lax.fori_loop(0, ahead, prompt_visit, state)
+    return lax.fori_loop(
+        first, block, lambda key_block, state: visit(key_block, 0.0, False, state), state
+    )
+
+
+def attend_kernel(span, prompt_blocks, cont_blocks, info_ref, qkv_ref, out_ref, exact_ref, lse_ref):
+    block = pl.program_id(0)
+    small = qkv_ref.shape[2]
+    rows = small * span
+    scale = LOG2E / math.sqrt(HEAD)
+
+    def take(block, kind):
+        return qkv_ref[pl.ds(block * span, span), kind].reshape(rows, HEAD)
+
+    query = take(block, 0)
+    first, ahead, start, limit = block_facts(block, rows, prompt_blocks, cont_blocks, info_ref)
+
+    def visit(key_block, bias, _, state):
         top, total, mixed = state
-        scores = dot_nt(qkv_ref[key_chunk, 1], query) * scale + bias
+        scores = dot_nt(take(key_block, 1), query) * scale + bias
         new_top = jnp.maximum(top, jnp.max(scores, axis=0, keepdims=True))
         weights = jnp.exp2(scores - new_top)
         shrink = jnp.exp2(top - new_top)
         total = total * shrink + jnp.sum(weights, axis=0, keepdims=True)
-        mixed = mixed * shrink + dot_tn(qkv_ref[key_chunk, 2], weights.astype(bf16))
+        mixed = mixed * shrink + dot_tn(take(key_block, 2), weights.astype(bf16))
         return new_top, total, mixed
-
-    def prompt_visit(key_chunk, state):
-        bias = jnp.where(key_chunk * rows + key_place < info_ref[0], 0.0, masked_out)
-        return visit(key_chunk, bias, state)
-
-    def own_visit(key_chunk, state):
-        return visit(key_chunk, 0.0, state)
 
     state = (
         jnp.full((1, rows), -1e38, f32),
         jnp.zeros((1, rows), f32),
         jnp.zeros((HEAD, rows), f32),
     )
-    state = visit(chunk, jnp.where(key_place <= query_place, 0.0, masked_out), state)
-    state = lax.fori_loop(0, ahead, prompt_visit, state)
-    top, total, mixed = lax.fori_loop(first, chunk, own_visit, state)
+    top, total, mixed = visit_blocks(visit, block, rows, first, ahead, info_ref, state)
     valid = start + lax.broadcasted_iota(jnp.int32, (1, rows), 1) < limit
-    settled = jnp.where(valid, mixed / total, 0.0).T
-    out_ref[chunk] = settled.astype(bf16)
-    exact_ref[chunk] = settled
-    lse_ref[chunk] = top + jnp.log2(total)
+    settled = jnp.where(valid, mixed / total, 0.0).T.reshape(span, small, HEAD)
+    out_ref[pl.ds(block * span, span)] = settled.astype(bf16)
+    exact_ref[pl.ds(block * span, span)] = settled
+    lse_ref[block] = top + jnp.log2(total)
 
 
 def attend_back_kernel(
-    prompt_chunks,
-    cont_chunks,
+    span,
+    prompt_blocks,
+    cont_blocks,
     info_ref,
     qkv_ref,
     grad_ref,
@@ -594,74 +601,71 @@
     key_sum,
     value_sum,
 ):
-    chunk = pl.program_id(0)
-    chunks = pl.num_programs(0)
-    rows = qkv_ref.shape[2]
+    block = pl.program_id(0)
+    blocks = pl.num_programs(0)
+    small = qkv_ref.shape[2]
+    rows = small * span
     scale = LOG2E / math.sqrt(HEAD)
-    query = qkv_ref[chunk, 0]
-    first, ahead, start, limit = chunk_facts(chunk, rows, prompt_chunks, cont_chunks, info_ref)
-    key_place = lax.broadcasted_iota(jnp.int32, (rows, rows), 0)
-    query_place = lax.broadcasted_iota(jnp.int32, (rows, rows), 1)
+
+    def at(block):
+        return pl.ds(block * span, span)
+
+    def flat(values):
+        return values.reshape(rows, HEAD)
+
+    def split(values):
+        return values.reshape(span, small, HEAD)
+
+    query = flat(qkv_ref[at(block), 0])
+    first, ahead, start, limit = block_facts(block, rows, prompt_blocks, cont_blocks, info_ref)
     valid = start + lax.broadcasted_iota(jnp.int32, (rows, 1), 0) < limit
-    grad_full = jnp.where(valid, grad_ref[chunk].astype(f32), 0.0)
+    grad_full = jnp.where(valid, flat(grad_ref[at(block)]).astype(f32), 0.0)
     grad = grad_full.astype(bf16)
-    delta = jnp.sum((grad_full * exact_ref[chunk]).T, axis=0, keepdims=True)
-    log_total = lse_ref[chunk]
-
-    @pl.when(chunk == 0)
-    def _():
-        key_sum[...] = jnp.zeros_like(key_sum)
-        value_sum[...] = jnp.zeros_like(value_sum)
-
-    def visit(key_chunk, bias, query_sum):
-        key = qkv_ref[key_chunk, 1]
+    delta = jnp.sum((grad_full * flat(exact_ref[at(block)])).T, axis=0, keepdims=True)
+    log_total = lse_ref[block]
+
+    def visit(key_block, bias, fresh, query_sum):
+        key = flat(qkv_ref[at(key_block), 1])
         scores = dot_nt(key, query) * scale + bias
         weights = jnp.exp2(scores - log_total)
-        weight_grad = dot_nt(qkv_ref[key_chunk, 2], grad)
+        weight_grad = dot_nt(flat(qkv_ref[at(key_block), 2]), grad)
         score_grad = (weights * (weight_grad - delta)).astype(bf16)
-        value_sum[key_chunk] += dot_nn(weights.astype(bf16), grad)
-        key_sum[key_chunk] += dot_nn(score_grad, query)
+        value_term = dot_nn(weights.astype(bf16), grad)
+        key_term = dot_nn(score_grad, query)
+        if fresh:
+            value_sum[key_block] = value_term
+            key_sum[key_block] = key_term
+        else:
+            value_sum[key_block] += value_term
+            key_sum[key_block] += key_term
         return query_sum + dot_tn(key, score_grad)
 
-    def prompt_visit(key_chunk, query_sum):
-        bias = jnp.where(key_chunk * rows + key_place < info_ref[0], 0.0, masked_out)
-        return visit(key_chunk, bias, query_sum)
-
-    def own_visit(key_chunk, query_sum):
-        return visit(key_chunk, 0.0, query_sum)
-
-    query_sum = visit(
-        chunk,
-        jnp.where(key_place <= query_place, 0.0, masked_out),
-        jnp.zeros((HEAD, rows), f32),
-    )
-    query_sum = lax.fori_loop(0, ahead, prompt_visit, query_sum)
-    query_sum = lax.fori_loop(first, chunk, own_visit, query_sum)
+    query_sum = visit_blocks(
+        visit, block, rows, first, ahead, info_ref, jnp.zeros((HEAD, rows), f32)
+    )
     back = 1.0 / math.sqrt(HEAD)
-    out_ref[chunk, 0] = turn(query_sum.T * back, cos_ref[chunk], -sin_ref[chunk]).astype(bf16)
-
-    @pl.when(chunk == chunks - 1)
+
+    def unturn(values, block):
+        return split(turn(values * back, flat(cos_ref[at(block)]), -flat(sin_ref[at(block)])).astype(bf16))
+
+    out_ref[at(block), 0] = unturn(query_sum.T, block)
+
+    @pl.when(block == blocks - 1)
     def _():
-        @pl.loop(0, chunks)
-        def _(key_chunk):
-            out_ref[key_chunk, 1] = turn(
-                key_sum[key_chunk] * back, cos_ref[key_chunk], -sin_ref[key_chunk]
-            ).astype(bf16)
-            out_ref[key_chunk, 2] = value_sum[key_chunk].astype(bf16)
+        @pl.loop(0, blocks)
+        def _(key_block):
+            out_ref[at(key_block), 1] = unturn(key_sum[key_block], key_block)
+            out_ref[at(key_block), 2] = split(value_sum[key_block].astype(bf16))
 
 
 def mix_out_kernel(near_ref, far_ref, w_near_ref, w_far_ref, keep_ref, send_ref):
     heads = near_ref.shape[0] // PLACES
-    part = heads * HEAD
-    for step in range(2):
+    for step, out_ref in enumerate((keep_ref, send_ref)):
         total = 0.0
         for ref, w_ref in ((near_ref, w_near_ref), (far_ref, w_far_ref)):
             both = jnp.concatenate([ref[step * heads + j] for j in range(heads)], axis=1)
             total = total + dot_nn(both, w_ref[...])
-        if step == 0:
-            keep_ref[...] = total
-        else:
-            send_ref[...] = total.astype(bf16)
+        out_ref[...] = total.astype(out_ref.dtype)
 
 
 def heads_back_kernel(own_ref, beside_ref, w_near_ref, w_far_ref, near_ref, far_ref):
@@ -688,17 +692,38 @@
                 target[0, :, columns_of(me_ref, place, rows)] = dot_nt(pieces, w[...]).astype(bf16)
 
 
-def project_grad_kernel(me_ref, pieces_ref, own_ref, other_ref, gain_ref, out_ref, total):
+def project_grad_kernel(
+    me_ref,
+    pieces_ref,
+    x0,
+    x1,
+    x2,
+    x3,
+    gain_ref,
+    w0,
+    w1,
+    w2,
+    w3,
+    two_ref,
+    three_ref,
+    four_ref,
+    keep_ref,
+    late_ref,
+    early_ref,
+    x_scr,
+    total,
+    lanes_scr,
+    gains_scr,
+):
     step = pl.program_id(0)
-    side = me_ref[1] % 2
-
-    def add(ref, chunk):
-        x = ref[...].astype(f32)
-        normed = (x * inverse_rms(x) * gain_ref[...]).astype(bf16)
-        pieces = jnp.concatenate([pieces_ref[chunk, kind] for kind in range(3)], axis=1)
-        return dot_tn(normed, pieces)
-
-    term = add(own_ref.at[step], 2 * step + side) + add(other_ref.at[step], 2 * step + 1 - side)
+    heads = pieces_ref.shape[0]
+    choose(step, (x0, x1, x2, x3), x_scr)
+    pieces = jnp.concatenate(
+        [pieces_ref[head, kind] for kind in range(3) for head in range(heads)], axis=1
+    )
+    x = x_scr[...].astype(f32)
+    normed = (x * inverse_rms(x) * gain_ref[...]).astype(bf16)
+    term = dot_tn(normed, pieces)
 
     @pl.when(step == 0)
     def _():
@@ -710,7 +735,26 @@
 
     @pl.when(step == pl.num_programs(0) - 1)
     def _():
-        spread_rows(me_ref, total, [out_ref])
+        rows, columns = w0.shape
+        refs = (keep_ref, late_ref, early_ref)
+        spread_rows(me_ref, total, refs, slice(0, columns))
+        for place, w in enumerate((w0, w1, w2, w3)):
+            where = columns_of(me_ref, place, rows)
+            product = total[where, :] * w[...].astype(f32)
+            lanes_scr[where, :] = sum(
+                product[:, first : first + HEAD] for first in range(0, columns, HEAD)
+            )
+        one = jnp.sum(lanes_scr[...].T, axis=0, keepdims=True) / gain_ref[...]
+        gains = jnp.concatenate([one, two_ref[...], three_ref[...], four_ref[...]], axis=0)
+        high = gains.astype(bf16).astype(f32)
+        gains_scr[...] = jnp.concatenate([high, gains - high], axis=0)
+        shards, piece_rows = keep_ref.shape[1:3]
+        for ref, owner in piece_views(me_ref, refs):
+            part = gains_scr[:, pl.ds(pl.multiple_of(owner * HEAD, HEAD), HEAD)]
+            rest = jnp.zeros((piece_rows - part.shape[0], HEAD), f32)
+            block = jnp.concatenate([part, rest], axis=0).astype(bf16)
+            for shard in range(shards):
+                ref[shard, :, columns:] = block
 
 
 def middle_kernel(keep_ref, received_ref, x_ref, two_ref, three_ref, branch_ref, middle_ref, input_ref):
@@ -761,17 +805,55 @@
 
 
 def input_back_kernel(
-    keep_ref, received_ref, across_ref, x_ref, middle_grad_ref, one_ref, out_ref, gain_ref
+    keep_ref, received_ref, across_ref, x_ref, middle_grad_ref, one_ref, out_ref
 ):
     normed_grad = keep_ref[0].astype(f32) + received_ref[0].astype(f32) + across_ref[...].astype(f32)
-    part, gain_ref[...] = norm_back_parts(x_ref[...].astype(f32), one_ref[...], normed_grad)
+    part, _ = norm_back_parts(x_ref[...].astype(f32), one_ref[...], normed_grad)
     out_ref[...] = middle_grad_ref[...] + part
 
 
-def far_columns(side, width, first, second):
-    half = width // 2
-    for place, ref in ((side, first), (1 - side, second)):
-        yield pl.ds(pl.multiple_of(place * half, half), half), ref
+class Weights:
+    def __init__(self, me_ref, refs, pair_scr, down_scr, sems):
+        own, beside, far_y, far_x, corner_y, corner_x, down_near, *down_far = refs
+        side = me_ref[1] % 2
+        rows = far_y.shape[0]
+        half = down_far[0].shape[1]
+        moves = []
+        for turn_index, far, corner in ((0, far_y, corner_y), (1, far_x, corner_x)):
+            block = turn_index ^ side
+            for place, source in enumerate((own.at[block], beside.at[block], far, corner)):
+                target = pair_scr.at[turn_index, place * rows : (place + 1) * rows]
+                moves.append((source, target))
+        moves.append((down_near, down_scr.at[0]))
+        for index, source in enumerate(down_far):
+            moves.append((source, down_scr.at[1, :, index * half : (index + 1) * half]))
+        self.copies = [
+            pltpu.make_async_copy(source, target, sems.at[index])
+            for index, (source, target) in enumerate(moves)
+        ]
+        self.pair_scr, self.down_scr = pair_scr, down_scr
+
+    COUNT = 11
+    DOWN = range(8, 11)
+
+    def start(self, order):
+        for index in order:
+            self.copies[index].start()
+
+    def wait(self, order):
+        for index in order:
+            self.copies[index].wait()
+
+    def wait_turn(self, turn_index):
+        for index in range(2):
+
+            @pl.when(turn_index == index)
+            def _(index=index):
+                self.wait(self.turn(index))
+
+    @staticmethod
+    def turn(turn_index):
+        return range(4 * turn_index, 4 * turn_index + 4)
 
 
 def put_rows(scr, place_major, me_ref, *refs):
@@ -786,14 +868,6 @@
             scr[where, :] = ref[...]
 
 
-def pair_product(x_scr, weights):
-    size = x_scr.shape[1] // PLACES
-    return sum(
-        dot_nn(x_scr[:, place * size : (place + 1) * size], w)
-        for place, w in enumerate(weights)
-    )
-
-
 def gate_parts(pair, half):
     def parts(gate, upward):
         sigma = 1.0 / (1.0 + jnp.exp(-gate))
@@ -819,75 +893,49 @@
         ref[row, :, main:] = edge[where]
 
 
-def ff_kernel(
-    me_ref,
-    own_ref,
-    beside_ref,
-    w0,
-    w1,
-    w2y,
-    w2x,
-    w3y,
-    w3x,
-    down_near,
-    down_y,
-    down_x,
-    keep_ref,
-    send_ref,
-    saved_ref,
-    hidden_ref,
-    x_scr,
-    pair_scr,
-    hidden_scr,
-    total,
-):
-    turn_index = pl.program_id(0)
-    side = me_ref[1] % 2
-    block = turn_index ^ side
-    width = x_scr.shape[1]
-    half = down_near.shape[0]
+def ff_kernel(me_ref, own_ref, beside_ref, *refs):
+    weight_refs, (keep_ref, send_ref, saved_ref, hidden_ref) = refs[:9], refs[9:13]
+    x_scr, hidden_scr, saved_scr, total, pair_w, down_w, sems, saved_sems = refs[13:]
+    weights = Weights(me_ref, weight_refs, pair_w, down_w, sems)
+    weights.start([*weights.turn(0), *weights.DOWN, *weights.turn(1)])
+    put_rows(x_scr, True, me_ref, own_ref, beside_ref)
+    half = down_w.shape[1]
     main = half // HEAD * HEAD
-
-    @pl.when(turn_index == 0)
-    def _():
-        put_rows(x_scr, True, me_ref, own_ref, beside_ref)
-        pair_scr[...] = pair_product(x_scr, (w0[0], w1[0], w2y[...], w3y[...]))
-
-    @pl.when(turn_index == 1)
-    def _():
-        pair_scr[...] = pair_product(x_scr, (w0[0], w1[0], w2x[...], w3x[...]))
-
-    (swish, slope, hidden), edge_factor, edge_hidden = gate_parts(pair_scr[...], half)
-    saved_ref[0, :, :main] = slope.astype(bf16)
-    saved_ref[0, :, main : 2 * main] = swish.astype(bf16)
-    saved_ref[0, :, 2 * main :] = edge_factor.astype(bf16)
-    hidden_scr[:, :main] = hidden
-    hidden_scr[:, main:] = edge_hidden
-
-    def add_term(columns, term):
+    total[...] = jnp.zeros_like(total)
+
+    def save(turn_index):
+        return pltpu.make_async_copy(
+            saved_scr.at[turn_index], saved_ref.at[turn_index], saved_sems.at[turn_index]
+        )
+
+    @pl.loop(0, 2)
+    def _(turn_index):
+        block = turn_index ^ (me_ref[1] % 2)
+        weights.wait_turn(turn_index)
+        pair = dot_nn(x_scr[...], pair_w[turn_index])
+        (swish, slope, hidden), edge_factor, edge_hidden = gate_parts(pair, half)
+        saved_scr[turn_index, :, :main] = slope.astype(bf16)
+        saved_scr[turn_index, :, main : 2 * main] = swish.astype(bf16)
+        saved_scr[turn_index, :, 2 * main :] = edge_factor.astype(bf16)
+        save(turn_index).start()
+        hidden_scr[:, :main] = hidden
+        hidden_scr[:, main:] = edge_hidden
+
+        @pl.when(block == 0)
+        def _():
+            put_hidden(hidden_ref, hidden, edge_hidden, main)
+
         @pl.when(turn_index == 0)
         def _():
-            total[:, columns] = term
-
-        @pl.when(turn_index == 1)
-        def _():
-            total[:, columns] += term
-
-    @pl.when(block == 0)
-    def _():
-        put_hidden(hidden_ref, hidden, edge_hidden, main)
-        add_term(slice(None), dot_nn(hidden_scr[:, :half], down_near[...]))
-
-    @pl.when(block == 1)
-    def _():
-        for columns, down in far_columns(side, width, down_y, down_x):
-            add_term(columns, dot_nn(hidden_scr[:, :half], down[...]))
-
-    @pl.when(turn_index == 1)
-    def _():
-        rows = keep_ref.shape[0]
-        keep_ref[...] = total[:rows]
-        send_ref[...] = total[rows:].astype(bf16)
+            weights.wait(weights.DOWN)
+
+        total[...] += dot_nn(hidden_scr[:, :half], down_w[block])
+
+    rows = keep_ref.shape[0]
+    keep_ref[...] = total[:rows]
+    send_ref[...] = total[rows:].astype(bf16)
+    for turn_index in range(2):
+        save(turn_index).wait()
 
 
 def put_pair_grad(target, hidden_grad, factors, half):
@@ -899,104 +947,58 @@
         target[:, columns] = (values * factors[:, columns].astype(f32)).astype(bf16)
 
 
-def ff_back_kernel(
-    me_ref,
-    own_ref,
-    beside_ref,
-    w0,
-    w1,
-    w2y,
-    w2x,
-    w3y,
-    w3x,
-    down_near,
-    down_y,
-    down_x,
-    saved_ref,
-    keep_ref,
-    send_ref,
-    pair_ref,
-    grad_scr,
-    hidden_scr,
-    pair_scr,
-    total,
+def ff_back_kernel(me_ref, own_ref, beside_ref, *refs):
+    weight_refs, saved_ref, (keep_ref, send_ref, pair_ref) = refs[:9], refs[9], refs[10:13]
+    grad_scr, pair_scr, total, pair_w, down_w, sems = refs[13:]
+    weights = Weights(me_ref, weight_refs, pair_w, down_w, sems)
+    weights.start([*weights.DOWN, *weights.turn(0), *weights.turn(1)])
+    put_rows(grad_scr, False, me_ref, own_ref, beside_ref)
+    half, width = down_w.shape[1:]
+    rows = keep_ref.shape[0]
+    size = width // PLACES
+    weights.wait(weights.DOWN)
+    total[...] = jnp.zeros_like(total)
+
+    @pl.loop(0, 2)
+    def _(turn_index):
+        block = turn_index ^ (me_ref[1] % 2)
+        hidden_grad = dot_nt(grad_scr[...], down_w[block])
+        put_pair_grad(pair_scr, hidden_grad, saved_ref.at[turn_index], half)
+
+        @pl.when(block == 0)
+        def _():
+            for row in range(2):
+                pair_ref[row] = pair_scr[row * rows : (row + 1) * rows]
+
+        weights.wait_turn(turn_index)
+        total[...] += dot_nt(pair_scr[...], pair_w[turn_index])
+
+    for place in range(PLACES):
+        where = slice(place * size, (place + 1) * size)
+        columns = columns_of(me_ref, place, size)
+        keep_ref[:, columns] = total[:rows, where]
+        send_ref[:, columns] = total[rows:, where].astype(bf16)
+
+
+def ff_far_kernel(
+    me_ref, x2_ref, x3_ref, grad2_ref, grad3_ref, *refs
 ):
-    turn_index = pl.program_id(0)
-    side = me_ref[1] % 2
-    block = turn_index ^ side
-    width = grad_scr.shape[1]
-    half = down_near.shape[0]
-    rows = keep_ref.shape[0]
-
-    @pl.when(turn_index == 0)
-    def _():
-        put_rows(grad_scr, False, me_ref, own_ref, beside_ref)
-
-    @pl.when(block == 0)
-    def _():
-        hidden_scr[...] = dot_nt(grad_scr[...], down_near[...])
-
-    @pl.when(block == 1)
-    def _():
-        hidden_scr[...] = sum(
-            dot_nt(grad_scr[:, columns], down[...])
-            for columns, down in far_columns(side, width, down_y, down_x)
-        )
-
-    put_pair_grad(pair_scr, hidden_scr[...], saved_ref.at[0], half)
-
-    @pl.when(block == 0)
-    def _():
-        for row in range(2):
-            pair_ref[row] = pair_scr[row * rows : (row + 1) * rows]
-
-    size = width // PLACES
-    for index, far in enumerate(((w2y, w3y), (w2x, w3x))):
-
-        @pl.when(turn_index == index)
-        def _(index=index, far=far):
-            for place, w in enumerate((w0[0], w1[0], far[0][...], far[1][...])):
-                term = dot_nt(pair_scr[...], w)
-                columns = columns_of(me_ref, place, size)
-                if index == 0:
-                    total[:, place * size : (place + 1) * size] = term
-                else:
-                    term = term + total[:, place * size : (place + 1) * size]
-                    keep_ref[:, columns] = term[:rows]
-                    send_ref[:, columns] = term[rows:].astype(bf16)
-
-
-def ff_far_kernel(
-    me_ref,
-    x2_ref,
-    x3_ref,
-    grad2_ref,
-    grad3_ref,
-    w0,
-    w1,
-    w2y,
-    w2x,
-    w3y,
-    w3x,
-    down_near,
-    hidden_ref,
-    pair_ref,
-    x_scr,
-    pair_scr,
-    factor_scr,
-):
-    side = me_ref[1] % 2
+    own, beside, far_y, far_x, corner_y, corner_x, down_near, hidden_ref, pair_ref = refs[:9]
+    x_scr, factor_scr, pair_w = refs[9:]
     half = down_near.shape[0]
     main = half // HEAD * HEAD
     rows = x2_ref.shape[0]
+    pair_w[:rows] = own[0]
+    pair_w[rows : 2 * rows] = beside[0]
+    for index, far in enumerate(((far_y, corner_y), (far_x, corner_x))):
+
+        @pl.when(me_ref[1] % 2 == index)
+        def _(far=far):
+            pair_w[2 * rows : 3 * rows] = far[0][...]
+            pair_w[3 * rows :] = far[1][...]
+
     put_rows(x_scr, True, me_ref, x2_ref, x3_ref)
-    for index, far in enumerate(((w2y, w3y), (w2x, w3x))):
-
-        @pl.when(side == index)
-        def _(far=far):
-            pair_scr[...] = pair_product(x_scr, (w0[0], w1[0], far[0][...], far[1][...]))
-
-    (swish, slope, hidden), edge_factor, edge_hidden = gate_parts(pair_scr[...], half)
+    (swish, slope, hidden), edge_factor, edge_hidden = gate_parts(dot_nn(x_scr[...], pair_w[...]), half)
     put_hidden(hidden_ref, hidden, edge_hidden, main)
     factor_scr[:, :main] = slope.astype(bf16)
     factor_scr[:, main : 2 * main] = swish.astype(bf16)
@@ -1017,79 +1019,99 @@
     return (me_ref[1] % 2 ^ other_x) + 2 * piece_height(me_ref, ahead)
 
 
+def piece_views(me_ref, refs):
+    keep, late, early = refs
+    for ahead in range(4):
+        yield keep.at[ahead], piece_owner(me_ref, 0, ahead)
+        yield (late, early)[ahead // 2].at[ahead % 2], piece_owner(me_ref, 1, ahead)
+
+
 def spread_rows(me_ref, total, refs, columns=slice(None), contiguous=False):
-    across = len(refs)
-    for other_x, ref in enumerate(refs):
-        shards, piece_rows = ref.shape[1:3]
-        for ahead in range(4):
-            owner = (
-                piece_owner(me_ref, other_x, ahead) if across == 2 else piece_height(me_ref, ahead)
-            )
-            for shard in range(shards):
-                block = owner * shards + shard if contiguous else shard * 4 * across + owner
-                start = pl.multiple_of(block * piece_rows, 8)
-                ref[ahead, shard, :, columns] = total[pl.ds(start, piece_rows), :].astype(bf16)
+    shards, piece_rows = refs[0].shape[1:3]
+    for ref, owner in piece_views(me_ref, refs):
+        for shard in range(shards):
+            block = owner * shards + shard if contiguous else shard * 8 + owner
+            start = pl.multiple_of(block * piece_rows, 8)
+            ref[shard, :, columns] = total[pl.ds(start, piece_rows), :].astype(bf16)
+
+
+def piece_shapes(shape):
+    return [(count,) + shape for count in (4, 2, 2)]
+
+
+def over_x(late, early):
+    early = ctx_swap(early, 1)
+    late = ctx_swap(after(late, early), 1)
+    return [late[0], late[1], early[0], early[1]], early
 
 
 def weight_grads_kernel(sources, me_ref, *refs):
-    lefts, rights = [], []
-    for heads_layout, _ in sources:
-        lefts.append(refs[:4])
-        count = 1 if heads_layout else 2
-        rights.append(refs[4 : 4 + count])
-        refs = refs[4 + count :]
-    outs, (left_scr, head_scr), totals = refs[:2], refs[2:4], refs[4:]
-    step = pl.program_id(0)
-    for (heads_layout, _), left, right, total in zip(sources, lefts, rights, totals, strict=True):
-        choose(step, left, left_scr)
+    operands, refs = refs[: sum(4 + count for count, _ in sources)], refs[len(sources) * 4 + sum(count for count, _ in sources) :]
+    outs, scratch, sems = refs[:3], refs[3:-1], refs[-1]
+    lefts, rights, totals = scratch[0::3], scratch[1::3], scratch[2::3]
+    copies, groups = [], []
+
+    def fetch(source, target):
+        copies.append(pltpu.make_async_copy(source, target, sems.at[len(copies)]))
+
+    for (count, _), left, right in zip(sources, lefts, rights, strict=True):
+        first = len(copies)
+        columns = right.shape[2]
+        for place in range(PLACES):
+            fetch(operands[place], left.at[place])
+            if count == 2:
+                fetch(operands[4 + place // 2].at[place % 2], right.at[place])
+            else:
+                heads = operands[4].shape[0] // PLACES
+                for head in range(heads):
+                    where = slice(head * HEAD, (head + 1) * HEAD)
+                    fetch(operands[4].at[place * heads + head], right.at[place, :, where])
+        operands = operands[4 + count :]
+        groups.append(range(first, len(copies)))
+    for copy in copies:
+        copy.start()
+    first = 0
+    for (_, contiguous), group, left, right, total in zip(
+        sources, groups, lefts, rights, totals, strict=True
+    ):
+        for index in group:
+            copies[index].wait()
         columns = total.shape[1]
-        if heads_layout:
-            heads = right[0].shape[0] // PLACES
-            for head in range(heads):
-                head_scr[:, head * HEAD : (head + 1) * HEAD] = right[0][step * heads + head]
-        for index in range(PLACES):
-
-            @pl.when(step == index)
-            def _(index=index, right=right, total=total, columns=columns, heads_layout=heads_layout):
-                if heads_layout:
-                    operand = head_scr[...]
-                else:
-                    operand = right[index // 2][index % 2, :, :columns]
-                term = dot_tn(left_scr[...], operand)
-                if index == 0:
-                    total[...] = term
-                else:
-                    total[...] += term
-
-    @pl.when(step == PLACES - 1)
-    def _():
-        first = 0
-        for (_, contiguous), total in zip(sources, totals, strict=True):
-            columns = slice(first, first + total.shape[1])
-            spread_rows(me_ref, total, outs, columns, contiguous)
-            first += total.shape[1]
+        total[...] = jnp.zeros_like(total)
+
+        @pl.loop(0, PLACES)
+        def _(place, left=left, right=right, total=total, columns=columns):
+            total[...] += dot_tn(left[place], right[place, :, :columns])
+
+        spread_rows(me_ref, total, outs, slice(first, first + columns), contiguous)
+        first += columns
 
 
 def weight_grads(me, name, expected, sources):
     rows, width = sources[0][0][0].shape
-    specs, operands, kinds, columns = [SMEM], [me], [], []
+    operands, kinds, columns, scratch, moves = [me], [], [], [], 0
     for lefts, rights, count, contiguous in sources:
         operands += [*lefts, *rights]
-        specs += [whole(value.shape) for value in (*lefts, *rights)]
-        kinds.append((len(rights) == 1, contiguous))
+        kinds.append((len(rights), contiguous))
         columns.append(count)
-    piece = (4, PLACES, width // PLACES // 8, sum(columns))
+        held = count if len(rights) == 1 else rights[0].shape[2]
+        scratch += [
+            pltpu.VMEM((PLACES, rows, width), bf16),
+            pltpu.VMEM((PLACES, rows, held), bf16),
+            pltpu.VMEM((width, count), f32),
+        ]
+        moves += 2 * PLACES if len(rights) == 2 else PLACES + rights[0].shape[0]
+    pieces = piece_shapes((PLACES, width // PLACES // 8, sum(columns)))
     return pl.pallas_call(
         functools.partial(weight_grads_kernel, tuple(kinds)),
         name=name,
         cost_estimate=cost(expected),
-        grid=(PLACES,),
-        in_specs=specs,
-        out_specs=[whole(piece)] * 2,
-        out_shape=[shaped(*piece)] * 2,
-        scratch_shapes=[pltpu.VMEM((rows, width), bf16), pltpu.VMEM((rows, 2 * HEAD), bf16)]
-        + [pltpu.VMEM((width, count), f32) for count in columns],
-        compiler_params=params(48, "arbitrary"),
+        grid=(1,),
+        in_specs=[SMEM] + [pl.BlockSpec(memory_space=pl.ANY)] * (len(operands) - 1),
+        out_specs=[whole(piece) for piece in pieces],
+        out_shape=[shaped(*piece) for piece in pieces],
+        scratch_shapes=scratch + [pltpu.SemaphoreType.DMA((moves,))],
+        compiler_params=params(32, "arbitrary"),
     )(*operands)
 
 
@@ -1114,17 +1136,22 @@
 
 
 def settle_qkv_kernel(me_ref, *refs):
-    pieces, outs = refs[:8], refs[8:]
-    shards, rows = pieces[0].shape[:2]
-    part = outs[0].shape[1] // shards
+    pieces, outs, gains_ref = refs[:8], refs[8:11], refs[11]
+    shards, rows, columns = pieces[0].shape
+    part = columns // 3 // HEAD * HEAD
+    count = gains_ref.shape[0]
     for index, ref in enumerate(pieces):
-        height = piece_height(me_ref, -(index % 4))
-        head = me_ref[1] % 2 ^ (index // 4)
-        where = pl.ds(pl.multiple_of(height * rows, rows), rows)
+        owner = piece_owner(me_ref, index // 4, -(index % 4))
+        where = pl.ds(pl.multiple_of(owner * rows, rows), rows)
+        gains = 0.0
         for shard in range(shards):
-            columns = pl.ds(pl.multiple_of(shard * part + head * HEAD, HEAD), HEAD)
             for kind, out in enumerate(outs):
-                out[where, columns] = ref[shard, :, kind * HEAD : (kind + 1) * HEAD].astype(f32)
+                out[where, shard * part : (shard + 1) * part] = ref[
+                    shard, :, kind * part : (kind + 1) * part
+                ].astype(f32)
+            gains = gains + ref[shard, :16, 3 * part :].astype(f32)
+        stretch = pl.ds(pl.multiple_of(owner * HEAD, HEAD), HEAD)
+        gains_ref[:, stretch] = gains[:count] + gains[count : 2 * count]
 
 
 def settle_pair_kernel(me_ref, *refs):
@@ -1171,14 +1198,20 @@
     return jax.ShapeDtypeStruct(shape, kind)
 
 
-def rope_tables(position):
+def rope_tables(base, count):
     half = HEAD // 2
     frequencies = rope_base ** (-2.0 * jnp.arange(half, dtype=f32) / HEAD)
-    angles = position.astype(f32)[..., None] * frequencies
+    frequencies = jnp.concatenate([frequencies, frequencies])
+    sign = jnp.where(jnp.arange(HEAD) < half, -1.0, 1.0)
+    blocks = base.shape[0]
+    places = jnp.concatenate([base, jnp.arange(count, dtype=base.dtype)])
+    angles = places.astype(f32)[:, None] * frequencies
     cosine, sine = jnp.cos(angles), jnp.sin(angles)
+    cos_base, sin_base = cosine[:blocks, None], sine[:blocks, None]
+    cos_step, sin_step = cosine[None, blocks:], sine[None, blocks:]
     return (
-        jnp.concatenate([cosine, cosine], axis=-1),
-        jnp.concatenate([-sine, sine], axis=-1),
+        cos_base * cos_step - sin_base * sin_step,
+        (sin_base * cos_step + cos_base * sin_step) * sign,
     )
 
 
@@ -1260,38 +1293,41 @@
     pair_lens = jnp.sum(jnp.where(pick_pair[:, None], slot_lens, 0), axis=0)
     info = jnp.concatenate([pair_prompt[None], pair_lens])
 
-    def positions(slot, prompt_size):
+    def first_position(slot, prompt_size):
         return jnp.where(slot >= prompt, prompt_size + (slot - prompt) % CONT, slot)
 
-    own_slots = my_chunk * rows + jnp.arange(rows, dtype=jnp.int32)
-    cos_own, sin_own = rope_tables(positions(own_slots[None, :], prompt_of[:, None]))
-    all_slots = jnp.arange(rows * ctx_size, dtype=jnp.int32).reshape(ctx_size, rows)
-    cos_all, sin_all = rope_tables(positions(all_slots, pair_prompt))
-
+    starts = jnp.arange(ctx_size, dtype=jnp.int32) * rows
+    bases = jnp.concatenate(
+        [first_position(my_chunk * rows, prompt_of), first_position(starts, pair_prompt)]
+    )
+    cos_tables, sin_tables = rope_tables(bases, rows)
+    cos_own, sin_own = cos_tables[:PLACES], sin_tables[:PLACES]
+    cos_all, sin_all = cos_tables[PLACES:], sin_tables[PLACES:]
     w_qkv = after(w_qkv, cos_own, sin_own, cos_all, sin_all)
 
     ff_blocks, ff_block = (2, rows, 2 * ff_part), (rows, 2 * ff_part)
-    split_shapes = [ff_blocks, ff_block, ff_blocks, ff_block, (ff_part, width // 2)]
-    ff_own, ff_own_sent, ff_beside, ff_beside_sent, down_sent = pl.pallas_call(
+    split_shapes = [ff_blocks, ff_block, ff_blocks, ff_block]
+    ff_own, ff_own_sent, ff_beside, ff_beside_sent = pl.pallas_call(
         split_ff_kernel,
         name="split_ff",
         cost_estimate=cost(3),
         grid=(1,),
-        in_specs=[SMEM] + [whole(w_gate.shape)] * 2 + [whole((ff_part, width))],
+        in_specs=[SMEM] + [whole(w_gate.shape)] * 2,
         out_specs=[whole(shape) for shape in split_shapes],
         out_shape=[shaped(*shape) for shape in split_shapes],
-        compiler_params=params(32),
-    )(me, w_gate, w_up, w_down)
-    w_qkv, x_all, ff_own_sent, ff_beside_sent = tie(w_qkv, x_all, ff_own_sent, ff_beside_sent)
+        compiler_params=params(20),
+    )(me, w_gate, w_up)
+    half = width // 2
+    w_qkv, x_all, w_out_sent, ff_beside_sent = tie(w_qkv, x_all, w_out, ff_beside_sent)
     w_ff_beside = core_swap(ff_beside)
     ff_beside_sent = core_swap(ff_beside_sent)
-    far_y = y_swap(ff_own_sent)
+    w_out_far = y_swap(w_out_sent)
+    far_y = y_swap(after(ff_own_sent, w_out_far))
     far_x = ctx_swap(far_y, 1)
     corner_y = y_swap(after(ff_beside_sent, far_y))
     corner_x = ctx_swap(corner_y, 1)
-    down_y = y_swap(after(down_sent, corner_y))
-    down_x = ctx_swap(down_y, 1)
-    w_out_far = y_swap(after(w_out, down_y))
+    down_left = y_swap(after(w_down, corner_y)[:, :half])
+    down_right = y_swap(after(w_down, down_left)[:, half:])
 
     piece = (heads, 3, rows, HEAD)
     qkv = pl.pallas_call(
@@ -1307,42 +1343,46 @@
         out_specs=pl.BlockSpec(piece, lambda t: (t, 0, 0, 0)),
         out_shape=shaped(PLACES * heads, 3, rows, HEAD),
         scratch_shapes=[pltpu.VMEM((rows, width), bf16)] * 2,
-        compiler_params=params(24, "arbitrary"),
+        compiler_params=params(16, "arbitrary"),
     )(me, *x_all, gain_one, *w_qkv, cos_own, sin_own)
-    qkv = lax.all_to_all(qkv, "ctx", 0, 0, tiled=True)
-    x_stack = jnp.stack(x_all)
-    qkv = after(qkv, far_y, x_stack)
+    qkv = lax.all_to_all(after(qkv, w_out_far), "ctx", 0, 0, tiled=True)
+    qkv = after(qkv, far_x, corner_y)
 
     qkv_shape, head_shape = (ctx_size, 3, rows, HEAD), (ctx_size, rows, HEAD)
+    span = math.gcd(prompt_chunks, cont_chunks)
+    blocks = ctx_size // span
+    block_shape, lse_shape = (blocks, span * rows, HEAD), (blocks, 1, span * rows)
+    block_counts = (span, prompt_chunks // span, cont_chunks // span)
     mixed, exact, log_total = pl.pallas_call(
-        functools.partial(attend_kernel, prompt_chunks, cont_chunks),
+        functools.partial(attend_kernel, *block_counts),
         name="attend",
-        cost_estimate=cost(15),
-        grid=(ctx_size,),
+        cost_estimate=cost(9),
+        grid=(blocks,),
         in_specs=[SMEM, whole(qkv_shape)],
-        out_specs=[whole(head_shape), whole(head_shape), whole((ctx_size, 1, rows))],
+        out_specs=[whole(head_shape), whole(head_shape), whole(lse_shape)],
         out_shape=[
             shaped(*head_shape),
             shaped(*head_shape, kind=f32),
-            shaped(ctx_size, 1, rows, kind=f32),
+            shaped(*lse_shape, kind=f32),
         ],
-        compiler_params=params(32, "arbitrary"),
+        compiler_params=params(16, "arbitrary"),
     )(info, qkv)
-    mixed = after(mixed, far_x, corner_x, down_y)
+    mixed = after(mixed, corner_x, down_left)
     attended = lax.all_to_all(mixed, "ctx", 0, 0, tiled=True)
-    attended = after(attended, down_x, w_out_far)
+    attended = after(attended, down_right)
     attended_far = y_swap(attended[2 * heads :])
 
     two_heads = (2 * heads, rows, HEAD)
+    mix_specs = [whole((part, width))] * 2
     keep, send = pl.pallas_call(
         mix_out_kernel,
         name="mix_out",
         cost_estimate=cost(2),
         grid=(1,),
-        in_specs=[whole((PLACES * heads, rows, HEAD)), whole(two_heads)] + [whole((part, width))] * 2,
+        in_specs=[whole((PLACES * heads, rows, HEAD)), whole(two_heads)] + mix_specs,
         out_specs=[row_spec] * 2,
         out_shape=[full_row, low_row],
-        compiler_params=params(16),
+        compiler_params=params(10),
     )(attended, attended_far, w_out, w_out_far)
 
     branch, middle, ff_input = pl.pallas_call(
@@ -1353,75 +1393,58 @@
         in_specs=[row_spec] * 3 + [gain_spec] * 2,
         out_specs=[row_spec] * 3,
         out_shape=[full_row, full_row, low_row],
-        compiler_params=params(24),
+        compiler_params=params(10),
     )(keep, core_swap(send), x_own, gain_two, gain_three)
     ff_input_beside = core_swap(ff_input)
     ff_input_far = far_rows(ff_input)
-    x_pair = lax.all_to_all(
-        after(x_stack, attended),
-        "ctx",
-        0,
-        0,
-        tiled=True,
-        axis_index_groups=[[x + 2 * z for z in range(ctx_size // 2)] for x in range(2)],
-    )
-
+
+    far_pairs = [far_y, far_x, corner_y, corner_x]
+    far_weights = far_pairs + [w_down, down_left, down_right]
+
+    both = 2 * rows
     padded = pl.cdiv(ff_part, HEAD) * HEAD
-    far_pairs = [far_y, far_x, corner_y, corner_x]
-    far_weights = far_pairs + [w_down, down_y, down_x]
-
-    def turned(index, me_ref):
-        return index ^ (me_ref[1] % 2)
-
-    def grid_whole(shape):
-        return pl.BlockSpec(shape, lambda b, me_ref: (0,) * len(shape))
-
-    def ff_call(kernel, name, expected, more_in, outs, scratch):
-        specs = (
-            [grid_whole((rows, width))] * 2
-            + [pl.BlockSpec((1,) + ff_block, lambda b, me_ref: (turned(b, me_ref), 0, 0))] * 2
-            + [grid_whole(weight.shape) for weight in far_weights]
-            + more_in
-        )
+    saved_shape = (2, both, 2 * ff_part)
+    hidden_shape, pair_shape = (2, rows, padded), (2, rows, 2 * ff_part)
+    anywhere = pl.BlockSpec(memory_space=pl.ANY)
+
+    def ff_call(kernel, name, expected, more_in, outs, scratch, last=()):
         return pl.pallas_call(
             kernel,
             name=name,
             cost_estimate=cost(expected),
-            grid_spec=pltpu.PrefetchScalarGridSpec(
-                num_scalar_prefetch=1,
-                grid=(2,),
-                in_specs=specs,
-                out_specs=[spec for spec, _ in outs],
-                scratch_shapes=scratch,
-            ),
+            grid=(1,),
+            in_specs=[SMEM] + [row_spec] * 2 + [anywhere] * 9 + more_in,
+            out_specs=[spec for spec, _ in outs],
             out_shape=[shape for _, shape in outs],
-            compiler_params=params(56, "arbitrary"),
+            scratch_shapes=scratch
+            + [
+                pltpu.VMEM((both, width), f32),
+                pltpu.VMEM((2, width, 2 * ff_part), bf16),
+                pltpu.VMEM((2, ff_part, width), bf16),
+                pltpu.SemaphoreType.DMA((Weights.COUNT,)),
+                *last,
+            ],
+            compiler_params=params(40, "arbitrary"),
         )
 
-    both = 2 * rows
-    padded = pl.cdiv(ff_part, HEAD) * HEAD
-    saved = pl.BlockSpec((1, both, 2 * ff_part), lambda b, me_ref: (b, 0, 0))
-    grid_row = grid_whole((rows, width))
-    hidden_shape, pair_shape = (2, rows, padded), (2, rows, 2 * ff_part)
     keep, send, ff_saved, hidden = ff_call(
         ff_kernel,
         "ff",
         9,
         [],
         [
-            (grid_row, full_row),
-            (grid_row, low_row),
-            (saved, shaped(2, both, 2 * ff_part)),
-            (grid_whole(hidden_shape), shaped(*hidden_shape)),
+            (row_spec, full_row),
+            (row_spec, low_row),
+            (anywhere, shaped(*saved_shape)),
+            (whole(hidden_shape), shaped(*hidden_shape)),
         ],
         [
             pltpu.VMEM((both, width), bf16),
-            pltpu.VMEM((both, 2 * ff_part), f32),
             pltpu.VMEM((both, padded), bf16),
-            pltpu.VMEM((both, width), f32),
+            pltpu.VMEM(saved_shape, bf16),
         ],
+        [pltpu.SemaphoreType.DMA((2,))],
     )(me, ff_input, ff_input_beside, ff_own, w_ff_beside, *far_weights)
-
     send = after(send, ff_input_far[0])
     block_out, ff_grad, part_four = pl.pallas_call(
         turnaround_kernel,
@@ -1431,7 +1454,7 @@
         in_specs=[row_spec] * 4 + [gain_spec],
         out_specs=[row_spec, row_spec, gain_spec],
         out_shape=[low_row, low_row, gain_row],
-        compiler_params=params(24),
+        compiler_params=params(10),
     )(keep, core_swap(send), middle, grad_own, gain_four)
 
     ff_grad_beside = core_swap(ff_grad)
@@ -1440,20 +1463,10 @@
         ff_back_kernel,
         "ff_back",
         9,
-        [saved],
-        [
-            (grid_row, full_row),
-            (grid_row, low_row),
-            (grid_whole(pair_shape), shaped(*pair_shape)),
-        ],
-        [
-            pltpu.VMEM((both, width), bf16),
-            pltpu.VMEM((both, ff_part), f32),
-            pltpu.VMEM((both, 2 * ff_part), bf16),
-            pltpu.VMEM((both, width), f32),
-        ],
+        [whole(saved_shape)],
+        [(row_spec, full_row), (row_spec, low_row), (whole(pair_shape), shaped(*pair_shape))],
+        [pltpu.VMEM((both, width), bf16), pltpu.VMEM((both, 2 * ff_part), bf16)],
     )(me, ff_grad, ff_grad_beside, ff_own, w_ff_beside, *far_weights, ff_saved)
-    x_pair_other = ctx_swap(x_pair, 1)
     send = after(send, ff_grad_far[0])
 
     middle_grad, branch_grad, part_two, part_three = pl.pallas_call(
@@ -1464,7 +1477,7 @@
         in_specs=[row_spec] * 5 + [gain_spec] * 2,
         out_specs=[row_spec, row_spec, gain_spec, gain_spec],
         out_shape=[full_row, low_row, gain_row, gain_row],
-        compiler_params=params(24),
+        compiler_params=params(10),
     )(keep, core_swap(send), middle, branch, grad_own, gain_two, gain_three)
     branch_grad_beside = core_swap(branch_grad)
 
@@ -1473,10 +1486,10 @@
         name="heads_back",
         cost_estimate=cost(2),
         grid=(1,),
-        in_specs=[row_spec] * 2 + [whole((part, width))] * 2,
+        in_specs=[row_spec] * 2 + mix_specs,
         out_specs=[whole(two_heads)] * 2,
         out_shape=[shaped(*two_heads)] * 2,
-        compiler_params=params(16),
+        compiler_params=params(10),
     )(branch_grad, branch_grad_beside, w_out, w_out_far)
     heads_far = y_swap(heads_far)
     ff_input_far, ff_grad_far = after((ff_input_far, ff_grad_far), heads_near)
@@ -1497,12 +1510,13 @@
         out_shape=[shaped(*hidden_shape), shaped(*pair_shape)],
         scratch_shapes=[
             pltpu.VMEM((both, width), bf16),
-            pltpu.VMEM((both, 2 * ff_part), f32),
             pltpu.VMEM((both, 2 * ff_part), bf16),
+            pltpu.VMEM((width, 2 * ff_part), bf16),
         ],
-        compiler_params=params(40),
+        compiler_params=params(26),
     )(me, *ff_input_far, *ff_grad_far, ff_own, w_ff_beside, *far_pairs, w_down)
-    pair_keep, pair_send = weight_grads(
+    pair_far = after(pair_far, heads_far)
+    pair_keep, pair_late, pair_early = weight_grads(
         me,
         "pair_grads",
         7,
@@ -1515,13 +1529,34 @@
             )
         ],
     )
-    pair_over = ctx_swap(pair_send, 1)
-    heads_far = after(heads_far, x_pair, pair_send)
     attended_grad = lax.all_to_all(
         jnp.concatenate([heads_near, heads_far]), "ctx", 0, 0, tiled=True
     )
     branch_grad_far = [branch_grad_across, core_swap(branch_grad_across)]
-    down_keep, down_send = weight_grads(
+    pair_over, pair_first = over_x(pair_late, pair_early)
+    attended_grad = after(attended_grad, pair_keep)
+
+    pieces = pl.pallas_call(
+        functools.partial(attend_back_kernel, *block_counts),
+        name="attend_back",
+        cost_estimate=cost(11),
+        grid=(blocks,),
+        in_specs=[
+            SMEM,
+            whole(qkv_shape),
+            whole(head_shape),
+            whole(head_shape),
+            whole(lse_shape),
+            whole(head_shape),
+            whole(head_shape),
+        ],
+        out_specs=whole(qkv_shape),
+        out_shape=shaped(*qkv_shape),
+        scratch_shapes=[pltpu.VMEM(block_shape, f32)] * 2,
+        compiler_params=params(20, "arbitrary"),
+    )(info, qkv, attended_grad, exact, log_total, cos_all, sin_all)
+    hidden, hidden_far = after((hidden, hidden_far), pieces)
+    down_keep, down_late, down_early = weight_grads(
         me,
         "down_grads",
         8,
@@ -1530,48 +1565,34 @@
             ([branch_grad, branch_grad_beside, *branch_grad_far], [attended], part, True),
         ],
     )
-    down_over = ctx_swap(down_send, 1)
-    attended_grad = after(attended_grad, down_send, x_pair_other)
-
-    pieces = pl.pallas_call(
-        functools.partial(attend_back_kernel, prompt_chunks, cont_chunks),
-        name="attend_back",
-        cost_estimate=cost(18),
-        grid=(ctx_size,),
-        in_specs=[
-            SMEM,
-            whole(qkv_shape),
-            whole(head_shape),
-            whole(head_shape),
-            whole((ctx_size, 1, rows)),
-            whole(head_shape),
-            whole(head_shape),
-        ],
-        out_specs=whole(qkv_shape),
-        out_shape=shaped(*qkv_shape),
-        scratch_shapes=[pltpu.VMEM(head_shape, f32), pltpu.VMEM(head_shape, f32)],
-        compiler_params=params(40, "arbitrary"),
-    )(info, qkv, attended_grad, exact, log_total, cos_all, sin_all)
-    qkv_piece = (4, PLACES, rows // 4, 3 * HEAD)
-    qkv_keep = pl.pallas_call(
+    pieces = lax.all_to_all(after(pieces, pair_first), "ctx", 0, 0, tiled=True)
+    pieces = after(pieces, down_keep)
+
+    piece_spec = pl.BlockSpec(piece, lambda t: (t, 0, 0, 0))
+    qkv_pieces = piece_shapes((PLACES, rows // 8, 3 * part + HEAD))
+    qkv_keep, qkv_late, qkv_early = pl.pallas_call(
         project_grad_kernel,
         name="project_grad",
-        cost_estimate=cost(6),
-        grid=(4,),
-        in_specs=[SMEM, whole(qkv_shape)] + [whole((4, rows, width))] * 2 + [gain_spec],
-        out_specs=whole(qkv_piece),
-        out_shape=shaped(*qkv_piece),
-        scratch_shapes=[pltpu.VMEM((width, 3 * HEAD), f32)],
-        compiler_params=params(32, "arbitrary"),
-    )(me, pieces, x_pair, x_pair_other, gain_one)
-    pair_over, down_over = after((pair_over, down_over), pieces)
-    pair_came = z_shift(low_sum(pair_keep[3], pair_over[3]))
-    pair_came = z_shift(low_sum(pair_keep[2], pair_over[2], pair_came))
-    qkv_came = z_shift(qkv_keep[3])
-    pieces = lax.all_to_all(pieces, "ctx", 0, 0, tiled=True)
+        cost_estimate=cost(5),
+        grid=(PLACES,),
+        in_specs=[SMEM, piece_spec]
+        + [row_spec] * 4
+        + [gain_spec]
+        + [whole((rows, 3 * part))] * 4
+        + [gain_spec] * 3,
+        out_specs=[whole(shape) for shape in qkv_pieces],
+        out_shape=[shaped(*shape) for shape in qkv_pieces],
+        scratch_shapes=[
+            pltpu.VMEM((rows, width), bf16),
+            pltpu.VMEM((width, 3 * part), f32),
+            pltpu.VMEM((width, HEAD), f32),
+            pltpu.VMEM((8, width), f32),
+        ],
+        compiler_params=params(20, "arbitrary"),
+    )(me, pieces, *x_all, gain_one, *w_qkv, part_two, part_three, part_four)
+    qkv_over, _ = over_x(qkv_late, qkv_early)
     pieces = after(pieces, qkv_keep)
 
-    piece_spec = pl.BlockSpec(piece, lambda t: (t, 0, 0, 0))
     pair_rows = pl.BlockSpec((1, rows, width), lambda t: (t // 2, 0, 0))
     keep, send = pl.pallas_call(
         project_back_kernel,
@@ -1581,12 +1602,12 @@
         in_specs=[SMEM, piece_spec] + [whole((rows, 3 * part))] * 4,
         out_specs=[pair_rows, pair_rows],
         out_shape=[shaped(2, rows, width)] * 2,
-        compiler_params=params(24, "arbitrary"),
+        compiler_params=params(12, "arbitrary"),
     )(me, pieces, *w_qkv)
 
     received = core_swap(send)
     onward = (keep[1].astype(f32) + received[1].astype(f32)).astype(bf16)
-    in_grad, part_one = pl.pallas_call(
+    in_grad = pl.pallas_call(
         input_back_kernel,
         name="input_back",
         cost_estimate=cost(2),
@@ -1594,23 +1615,26 @@
         in_specs=[pl.BlockSpec((1, rows, width), lambda *_: (0, 0, 0))] * 2
         + [row_spec] * 3
         + [gain_spec],
-        out_specs=[row_spec, gain_spec],
-        out_shape=[full_row, gain_row],
-        compiler_params=params(24),
+        out_specs=row_spec,
+        out_shape=full_row,
+        compiler_params=params(10),
     )(keep, received, y_swap(onward), x_own, middle_grad, gain_one)
 
     def shared_rows(piece):
         return lax.all_to_all(piece, "fsdp", 0, 0, tiled=True)
 
-    pair_came, qkv_came, down_over = after((pair_came, qkv_came, down_over), send)
-    qkv_came = z_shift(low_sum(qkv_keep[2], qkv_came))
+    pair_over = after(pair_over, pieces)
+    pair_came = z_shift(low_sum(pair_keep[3], pair_over[3]))
+    pair_came = z_shift(low_sum(pair_keep[2], pair_over[2], pair_came))
     pair_came = z_shift(low_sum(pair_keep[1], pair_over[1], pair_came))
-    qkv_came = z_shift(low_sum(qkv_keep[1], qkv_came))
     pair_piece = shared_rows(low_sum(pair_keep[0], pair_over[0], pair_came))
-    qkv_piece = shared_rows(low_sum(qkv_keep[0], qkv_came))
+    down_over, _ = over_x(down_late, after(down_early, pair_over))
+    qkv_piece = shared_rows(
+        over_z([[qkv_keep[ahead], qkv_over[ahead]] for ahead in range(4)])
+    )
     down_piece = over_z([[down_keep[ahead], down_over[ahead]] for ahead in range(4)])
-    query_sum, key_sum, value_sum = settle(
-        settle_qkv_kernel, "settle_qkv", me, spread_piece(qkv_piece), [(rows, width)] * 3
+    query_sum, key_sum, value_sum, gains = settle(
+        settle_qkv_kernel, "settle_qkv", me, spread_piece(qkv_piece), [(rows, width)] * 3 + [(4, width)]
     )
     gate_sum, up_sum = settle(
         settle_pair_kernel, "settle_pair", me, spread_piece(pair_piece), [w_gate.shape] * 2
@@ -1623,15 +1647,6 @@
         [(ff_part, width), (part, width)],
     )
 
-    gains = jnp.concatenate([part_one, part_two, part_three, part_four])
-    for swap in (
-        core_swap,
-        y_swap,
-        functools.partial(ctx_swap, bit=1),
-        functools.partial(ctx_swap, bit=2),
-        functools.partial(ctx_swap, bit=4),
-    ):
-        gains = gains + swap(gains)
     return (
         block_out[None],
         in_grad[None],

time: 495 us -> 454 us (0.917)
  Pallas kernels: 126 us -> 93.4 us
  other arithmetic: 33.4 us -> 14.9 us
  waiting for transfers between devices: 200 us -> 209 us
  starting transfers between devices: 74.5 us -> 79.8 us
    ppermute x14, waiting for transfers between devices: 47.8 us -> 90.6 us  [y_swap(): return lax.ppermute(values, 'fsdp', [(i, i ^ 2) for i in range(4)])]
    pallas_call x4, Pallas kernels: 64 us -> 36.4 us  [the longest x1 10.2 us: pair_shards(): pl.pallas_call(functools.partial(attend_back_kernel, *block_counts), name...]
    ppermute x21 -> x20, waiting for transfers between devices: 67.5 us -> 41 us  [ctx_swap(): return lax.ppermute(values, 'ctx', [(i, i ^ bit) for i in range(size)])]
    unnamed x204 -> x212, local copies, waits for them, and re-layouts: 47.6 us -> 39.8 us
    neg x2 -> x0, other arithmetic: 6.75 us -> none  [rope_tables(): -sine]
    ppermute x18, waiting for transfers between devices: 68.1 us -> 61.7 us  [z_shift(): lax.ppermute(values, 'ctx', [(i, (i + 2) % size) for i in range(size)])]
    convert_element_type x11 -> x12, other arithmetic: 14.2 us -> 8.47 us  [low_sum(): return sum((term.astype(f32) for term in terms)).astype(bf16)]
    ppermute x17 -> x16, waiting for transfers between devices: 5.81 us -> 11 us  [core_swap(): return lax.ppermute(values, 'fsdp', [(i, i ^ 1) for i in range(4)])]
  transfers between devices with their start and end apart: 77 -> 74, of which waited for: 35 -> 45; matrix products, arithmetic and copies ran while one was open for 7% -> 5% of each run, Pallas kernels for 24% -> 18%
where the time goes in v3:
time: 454 us; the launch traced here: 446 us
  waiting for transfers between devices  209 us (46%)
  Pallas kernels  93.4 us (21%)
  starting transfers between devices  79.8 us (18%)
  local copies, waits for them, and re-layouts  47.5 us (10%)
  other arithmetic  14.9 us (3%)
    ppermute x14, waiting for transfers between devices, y_swap(): return lax.ppermute(values, 'fsdp', [(i, i ^ 2) for i in range(4)])  90.6 us
    ppermute x18, waiting for transfers between devices, z_shift(): lax.ppermute(values, 'ctx', [(i, (i + 2) % size) for i in range(size)])  61.7 us
    ppermute x20, waiting for transfers between devices, ctx_swap(): return lax.ppermute(values, 'ctx', [(i, i ^ bit) for i in range(size)])  41 us
    unnamed x212, local copies, waits for them, and re-layouts  39.8 us
    ppermute x20, starting transfers between devices, ctx_swap(): return lax.ppermute(values, 'ctx', [(i, i ^ bit) for i in range(size)])  21.9 us
    ppermute x14, starting transfers between devices, y_swap(): return lax.ppermute(values, 'fsdp', [(i, i ^ 2) for i in range(4)])  16.3 us
    pallas_call x2, Pallas kernels, weight_grads(): pl.pallas_call(functools.partial(weight_grads_kernel, tuple(kinds)), name...  15.3 us
    pallas_call x3, Pallas kernels, settle(): pl.pallas_call(kernel, name=name, grid=(1,), in_specs=[SMEM] + [whole(pie...  11.1 us
  transfers between devices with their start and end apart: 74, of which 45 were waited for; matrix products, arithmetic and copies ran while one was open for 5% of the time, Pallas kernels for 18%

profile of v3, /device:TPU:0, one launch (start us, length us, event | category | flops | bytes accessed | tf_op | source)
XLA Modules:
  0.0 446.2 jit_solution(1458229599711572761)
XLA Ops:
  0.7 3.0 collective-permute-start.5
  11.0 5.6 %collective-permute-done.5.x2 = bf16[256,1024]{1,0:T(8,128)(2,1)S(1)} collective-permute-done((bf16[256,1024]{1,0:T(8,128)(2,1)}, bf16[256,1024]{1,0:T(8,128)(2,1)S(1)}, u32[]{:S(2)}, u32[]{:S(2)}) %collective-permute-start.5) | collective-permute-done | bytes 524320 | tf_op jit(solution)/shard_map/ppermute | solution.py:392
  17.3 2.1 collective-permute-start.3
  25.4 7.3 %collective-permute-done.3.w3 = bf16[256,768]{1,0:T(8,128)(2,1)S(1)} collective-permute-done((bf16[256,768]{1,0:T(8,128)(2,1)}, bf16[256,768]{1,0:T(8,128)(2,1)S(1)}, u32[]{:S(2)}, u32[]{:S(2)}) %collective-permute-start.3) | collective-permute-done | bytes 393248 | tf_op jit(solution)/shard_map/ppermute | solution.py:392
  34.5 4.3 project.1
  42.3 3.6 collective-permute-done.7.w_far_ref
  46.7 5.7 %all-to-all-start = ((bf16[8,3,256,128]{3,2,1,0:T(8,128)(2,1)}), bf16[8,3,256,128]{3,2,1,0:T(8,128)(2,1)S(1)}, u32[]{:S(2)}, u32[]{:S(2)}) async-start(bf16[8,3,256,128]{3,2,1,0:T(8,128)(2,1)} %copy-done.11), calls=%async_computation | async-start | bytes 3145728 | tf_op jit(solution)/shard_map/all_to_all | solution.py:1348
  54.8 16.4 %collective-permute-done.8.refs_2_ = bf16[256,1408]{1,0:T(8,128)(2,1)S(1)} collective-permute-done((bf16[256,1408]{1,0:T(8,128)(2,1)}, bf16[256,1408]{1,0:T(8,128)(2,1)S(1)}, u32[]{:S(2)}, u32[]{:S(2)}) %collective-permute-start.8) | collective-permute-done | bytes 720928 | tf_op jit(solution)/shard_map/ppermute | solution.py:392
  73.5 2.0 collective-permute-start.9
  75.5 13.5 %collective-permute-done.11.refs_4_ = bf16[256,1408]{1,0:T(8,128)(2,1)} collective-permute-done((bf16[256,1408]{1,0:T(8,128)(2,1)S(1)}, bf16[256,1408]{1,0:T(8,128)(2,1)}, u32[]{:S(2)}, u32[]{:S(2)}) %collective-permute-start.11) | collective-permute-done | bytes 720928 | tf_op jit(solution)/shard_map/ppermute | solution.py:392
  91.4 2.1 collective-permute-start.12
  96.2 7.3 %attend.1 = (bf16[8,256,128]{2,1,0:T(8,128)(2,1)S(1)}, f32[8,256,128]{2,1,0:T(8,128)S(1)}, f32[4,1,512]{2,1,0:T(1,128)S(1)}) custom-call(s32[3]{0:T(128)S(1)} %pad_add_fusion.1.info_ref, bf16[8,3,256,128]{3,2,1,0:T(8,128)(2,1)S(1)} %all-to-all-done.qkv_ref), custom_call_target="tpu_custom_call" | custom-call | flops 9000000 | tf_op jit(solution)/shard_map/attend/pallas_call | solution.py:1356
  107.0 1.9 collective-permute-done.12.refs_5_
  108.9 7.4 %all-to-all-start.1 = ((bf16[8,256,128]{2,1,0:T(8,128)(2,1)}), bf16[8,256,128]{2,1,0:T(8,128)(2,1)}, u32[]{:S(2)}, u32[]{:S(2)}) async-start(bf16[8,256,128]{2,1,0:T(8,128)(2,1)} %copy-done.72), calls=%async_computation.1 | async-start | bytes 1048576 | tf_op jit(solution)/shard_map/all_to_all | solution.py:1371
  117.0 15.9 %collective-permute-done.14.refs_8_ = bf16[704,512]{1,0:T(8,128)(2,1)S(1)} collective-permute-done((bf16[704,512]{1,0:T(8,128)(2,1)S(1)}, bf16[704,512]{1,0:T(8,128)(2,1)S(1)}, u32[]{:S(2)}, u32[]{:S(2)}) %collective-permute-start.14) | collective-permute-done | bytes 720928 | tf_op jit(solution)/shard_map/ppermute | solution.py:392
  135.2 6.0 %collective-permute-done.15.far_ref = bf16[4,256,128]{2,1,0:T(8,128)(2,1)S(1)} collective-permute-done((bf16[4,256,128]{2,1,0:T(8,128)(2,1)S(1)}, bf16[4,256,128]{2,1,0:T(8,128)(2,1)S(1)}, u32[]{:S(2)}, u32[]{:S(2)}) %collective-permute-start.15) | collective-permute-done | bytes 262176 | tf_op jit(solution)/shard_map/ppermute | solution.py:392
  145.1 1.9 collective-permute-done.16.received_ref
  149.5 8.9 %ff.1 = (f32[256,1024]{1,0:T(8,128)S(1)}, bf16[256,1024]{1,0:T(8,128)(2,1)S(1)}, bf16[2,512,1408]{2,1,0:T(8,128)(2,1)}, bf16[2,256,768]{2,1,0:T(8,128)(2,1)S(1)}) custom-call(s32[2]{0:T(128)S(1)} %pad_add_fusion.me_ref, bf16[256,1024]{1,0:T(8,128)(2,1)S(1)} %get-tuple-element.149.own_ref.refs_0_, ...), custom_call_target="tpu_custom_call" | custom-call | flops 9000000 | tf_op jit(solution)/shard_map/ff/pallas_call | solution.py:1430
  158.5 3.6 collective-permute-done.19.x2_ref.refs_2_
  162.0 1.9 collective-permute-done.20.received_ref
  167.8 10.0 %ff_back.1 = (f32[256,1024]{1,0:T(8,128)S(1)}, bf16[256,1024]{1,0:T(8,128)(2,1)S(1)}, bf16[2,256,1408]{2,1,0:T(8,128)(2,1)S(1)}) custom-call(s32[2]{0:T(128)S(1)} %pad_add_fusion.me_ref, bf16[256,1024]{1,0:T(8,128)(2,1)S(1)} %get-tuple-element.157.own_ref.refs_0_, bf16[256,1024]{1,0:T(8,128)(2,1)S(1)} %collective-permute-done.21.beside_ref.refs_1_, ...), custom_call_target="tpu_custom_call" | custom-call | flops 9000000 | tf_op jit(solution)/shard_map/ff_back/pallas_call | solution.py:1462
  180.4 1.9 collective-permute-done.23.received_ref
  188.2 7.4 %collective-permute-done.25 = bf16[4,256,128]{2,1,0:T(8,128)(2,1)S(1)} collective-permute-done((bf16[4,256,128]{2,1,0:T(8,128)(2,1)S(1)}, bf16[4,256,128]{2,1,0:T(8,128)(2,1)S(1)}, u32[]{:S(2)}, u32[]{:S(2)}) %collective-permute-start.25) | collective-permute-done | bytes 262176 | tf_op jit(solution)/shard_map/ppermute | solution.py:392
  196.5 5.7 %all-to-all-start.2 = ((bf16[8,256,128]{2,1,0:T(8,128)(2,1)}), bf16[8,256,128]{2,1,0:T(8,128)(2,1)}, u32[]{:S(2)}, u32[]{:S(2)}) async-start(bf16[8,256,128]{2,1,0:T(8,128)(2,1)} %pad_maximum_fusion), calls=%async_computation.2 | async-start | bytes 1048576 | tf_op jit(solution)/shard_map/all_to_all | solution.py:1532
  205.9 5.7 %ff_far.1 = (bf16[2,256,768]{2,1,0:T(8,128)(2,1)S(1)}, bf16[2,256,1408]{2,1,0:T(8,128)(2,1)S(1)}) custom-call(s32[2]{0:T(128)S(1)} %pad_add_fusion.me_ref, bf16[256,1024]{1,0:T(8,128)(2,1)} %collective-permute-done.19.x2_ref.refs_2_, bf16[256,1024]{1,0:T(8,128)(2,1)} %collective-permute-done.26.x3_ref.refs_3_, ...), custom_call_target="tpu_custom_call" | custom-call | flops 6000000 | tf_op jit(solution)/shard_map/ff_far/pallas_call | solution.py:1499
  212.5 8.3 %pair_grads.1 = (bf16[4,4,32,1408]{3,2,1,0:T(8,128)(2,1)S(1)}, bf16[2,4,32,1408]{3,2,1,0:T(8,128)(2,1)S(1)}, bf16[2,4,32,1408]{3,2,1,0:T(8,128)(2,1)}) custom-call(s32[2]{0:T(128)S(1)} %pad_add_fusion.me_ref, bf16[256,1024]{1,0:T(8,128)(2,1)S(1)} %copy-done.32, bf16[256,1024]{1,0:T(8,128)(2,1)S(1)} %copy-done.34, ...), custom_call_target="tpu_custom_call" | custom-call | flops 7000000 | tf_op jit(solution)/shard_map/pair_grads/pallas_call | solution.py:1105
  222.7 2.0 collective-permute-start.28
  227.2 10.2 %attend_back.1 = bf16[8,3,256,128]{3,2,1,0:T(8,128)(2,1)S(1)} custom-call(s32[3]{0:T(128)S(1)} %copy-done.86, bf16[8,3,256,128]{3,2,1,0:T(8,128)(2,1)S(1)} %all-to-all-done.qkv_ref, bf16[8,256,128]{2,1,0:T(8,128)(2,1)} %all-to-all-done.2.grad_ref, f32[8,256,128]{2,1,0:T(8,128)S(1)} %copy-done.63, f32[4,1,512]{2,1,0:T(1,128)S(1)} %copy-done.77, ...), custom_call_target="tpu_custom_call" | custom-call | flops 11000000 | tf_op jit(solution)/shard_map/attend_back/pallas_call | solution.py:1539
  240.1 5.7 %all-to-all-start.3 = ((bf16[8,3,256,128]{3,2,1,0:T(8,128)(2,1)}), bf16[8,3,256,128]{3,2,1,0:T(8,128)(2,1)S(1)}, u32[]{:S(2)}, u32[]{:S(2)}) async-start(bf16[8,3,256,128]{3,2,1,0:T(8,128)(2,1)} %copy-done.12), calls=%async_computation.3 | async-start | bytes 3145728 | tf_op jit(solution)/shard_map/all_to_all | solution.py:1568
  246.3 1.9 collective-permute-start.45
  248.2 9.3 %collective-permute-done.29.refs_8_ = bf16[256,1024]{1,0:T(8,128)(2,1)S(1)} collective-permute-done((bf16[256,1024]{1,0:T(8,128)(2,1)}, bf16[256,1024]{1,0:T(8,128)(2,1)S(1)}, u32[]{:S(2)}, u32[]{:S(2)}) %collective-permute-start.29) | collective-permute-done | bytes 524320 | tf_op jit(solution)/shard_map/ppermute | solution.py:392
  257.5 2.0 slice_bitcast_fusion
  261.8 7.0 %down_grads.1 = (bf16[4,4,32,960]{3,2,1,0:T(8,128)(2,1)S(1)}, bf16[2,4,32,960]{3,2,1,0:T(8,128)(2,1)S(1)}, bf16[2,4,32,960]{3,2,1,0:T(8,128)(2,1)S(1)}) custom-call(s32[2]{0:T(128)S(1)} %pad_add_fusion.me_ref, bf16[256,1024]{1,0:T(8,128)(2,1)S(1)} %copy-done.28, bf16[256,1024]{1,0:T(8,128)(2,1)S(1)} %copy-done.30, ...), custom_call_target="tpu_custom_call" | custom-call | flops 8000000 | tf_op jit(solution)/shard_map/down_grads/pallas_call | solution.py:1105
  271.4 7.1 %collective-permute-done.45 = bf16[2,4,32,1408]{3,2,1,0:T(8,128)(2,1)S(1)} collective-permute-done((bf16[2,4,32,1408]{3,2,1,0:T(8,128)(2,1)}, bf16[2,4,32,1408]{3,2,1,0:T(8,128)(2,1)S(1)}, u32[]{:S(2)}, u32[]{:S(2)}) %collective-permute-start.45) | collective-permute-done | bytes 720928 | tf_op jit(solution)/shard_map/ppermute | solution.py:397
  285.2 6.6 %project_grad.1 = (bf16[4,4,32,896]{3,2,1,0:T(8,128)(2,1)S(1)}, bf16[2,4,32,896]{3,2,1,0:T(8,128)(2,1)}, bf16[2,4,32,896]{3,2,1,0:T(8,128)(2,1)S(1)}) custom-call(s32[2]{0:T(128)S(1)} %pad_add_fusion.me_ref, bf16[8,3,256,128]{3,2,1,0:T(8,128)(2,1)S(1)} %all-to-all-done.3.pieces_ref, bf16[256,1024]{1,0:T(8,128)(2,1)S(1)} %bitcast.69, ...), custom_call_target="tpu_custom_call" | custom-call | flops 5000000 | tf_op jit(solution)/shard_map/project_grad/pallas_call | solution.py:1573
  294.4 4.1 project_back.1
  299.5 2.0 collective-permute-done.58
  301.7 12.6 %collective-permute-done.33 = bf16[2,4,32,896]{3,2,1,0:T(8,128)(2,1)S(1)} collective-permute-done((bf16[2,4,32,896]{3,2,1,0:T(8,128)(2,1)S(1)}, bf16[2,4,32,896]{3,2,1,0:T(8,128)(2,1)S(1)}, u32[]{:S(2)}, u32[]{:S(2)}) %collective-permute-start.33) | collective-permute-done | bytes 458784 | tf_op jit(solution)/shard_map/ppermute | solution.py:397
  317.9 2.2 collective-permute-start.48
  320.2 6.3 %collective-permute-done.35 = bf16[4,32,896]{2,1,0:T(8,128)(2,1)S(1)} collective-permute-done((bf16[4,32,896]{2,1,0:T(8,128)(2,1)S(1)}, bf16[4,32,896]{2,1,0:T(8,128)(2,1)S(1)}, u32[]{:S(2)}, u32[]{:S(2)}) %collective-permute-start.35) | collective-permute-done | bytes 229408 | tf_op jit(solution)/shard_map/ppermute | solution.py:402
  326.6 5.5 %collective-permute-done.48 = bf16[4,32,960]{2,1,0:T(8,128)(2,1)S(1)} collective-permute-done((bf16[4,32,960]{2,1,0:T(8,128)(2,1)S(1)}, bf16[4,32,960]{2,1,0:T(8,128)(2,1)S(1)}, u32[]{:S(2)}, u32[]{:S(2)}) %collective-permute-start.48) | collective-permute-done | bytes 245792 | tf_op jit(solution)/shard_map/ppermute | solution.py:402
  332.9 6.9 %collective-permute-done.60 = bf16[4,32,1408]{2,1,0:T(8,128)(2,1)S(1)} collective-permute-done((bf16[4,32,1408]{2,1,0:T(8,128)(2,1)S(1)}, bf16[4,32,1408]{2,1,0:T(8,128)(2,1)S(1)}, u32[]{:S(2)}, u32[]{:S(2)}) %collective-permute-start.60) | collective-permute-done | bytes 360480 | tf_op jit(solution)/shard_map/ppermute | solution.py:402
  340.7 3.5 all-to-all-start.5
  345.0 1.8 fusion.12
  353.0 4.3 collective-permute-done.37
  357.4 1.9 fusion.13
  359.3 3.4 all-to-all-start.4
  366.2 2.2 all-to-all-done.4.refs_0_
  368.4 2.4 collective-permute-done.61.refs_1_
  370.7 3.4 collective-permute-done.62.refs_4_
  374.1 2.2 collective-permute-done.51.refs_1_
  377.1 2.6 collective-permute-done.52.refs_4_
  381.9 2.5 collective-permute-done.39.refs_4_
  384.7 9.5 %collective-permute-done.53.refs_2_ = bf16[4,32,960]{2,1,0:T(8,128)(2,1)S(1)} collective-permute-done((bf16[4,32,960]{2,1,0:T(8,128)(2,1)}, bf16[4,32,960]{2,1,0:T(8,128)(2,1)S(1)}, u32[]{:S(2)}, u32[]{:S(2)}) %collective-permute-start.53) | collective-permute-done | bytes 245792 | tf_op jit(solution)/shard_map/ppermute | solution.py:402
  398.0 1.9 collective-permute-start.32
  399.8 4.7 %collective-permute-done.40.refs_2_ = bf16[4,32,896]{2,1,0:T(8,128)(2,1)S(1)} collective-permute-done((bf16[4,32,896]{2,1,0:T(8,128)(2,1)S(1)}, bf16[4,32,896]{2,1,0:T(8,128)(2,1)S(1)}, u32[]{:S(2)}, u32[]{:S(2)}) %collective-permute-start.40) | collective-permute-done | bytes 229408 | tf_op jit(solution)/shard_map/ppermute | solution.py:402
  404.9 5.3 %collective-permute-done.55.refs_3_ = bf16[4,32,960]{2,1,0:T(8,128)(2,1)S(1)} collective-permute-done((bf16[4,32,960]{2,1,0:T(8,128)(2,1)S(1)}, bf16[4,32,960]{2,1,0:T(8,128)(2,1)S(1)}, u32[]{:S(2)}, u32[]{:S(2)}) %collective-permute-start.55) | collective-permute-done | bytes 245792 | tf_op jit(solution)/shard_map/ppermute | solution.py:402
  410.5 11.2 %collective-permute-done.42.refs_3_ = bf16[4,32,896]{2,1,0:T(8,128)(2,1)S(1)} collective-permute-done((bf16[4,32,896]{2,1,0:T(8,128)(2,1)S(1)}, bf16[4,32,896]{2,1,0:T(8,128)(2,1)S(1)}, u32[]{:S(2)}, u32[]{:S(2)}) %collective-permute-start.42) | collective-permute-done | bytes 229408 | tf_op jit(solution)/shard_map/ppermute | solution.py:402
  421.7 2.0 collective-permute-start.44
  425.3 5.6 %collective-permute-done.57.refs_7_ = bf16[4,32,960]{2,1,0:T(8,128)(2,1)S(1)} collective-permute-done((bf16[4,32,960]{2,1,0:T(8,128)(2,1)S(1)}, bf16[4,32,960]{2,1,0:T(8,128)(2,1)S(1)}, u32[]{:S(2)}, u32[]{:S(2)}) %collective-permute-start.57) | collective-permute-done | bytes 245792 | tf_op jit(solution)/shard_map/ppermute | solution.py:397
  430.9 4.5 settle_turned.1
  435.9 2.4 settle_qkv.1
  438.9 2.7 collective-permute-done.67.refs_7_
  441.6 4.2 settle_pair.1
  (365 shorter events, 109.3 us)
Async XLA Ops:
  0.7 16.0 %collective-permute-start.5 = (bf16[256,1024]{1,0:T(8,128)(2,1)}, bf16[256,1024]{1,0:T(8,128)(2,1)S(1)}, u32[]{:S(2)}, u32[]{:S(2)}) collective-permute-start(bf16[256,1024]{1,0:T(8,128)(2,1)} %bitcast.65), channel_id=1, source_target_pairs={{0,2},{1,3},{2,0},{3,1},{4,6},{5,7},{6,4},{7,5},{8,10},{9,11},{10,... | collective-permute-start | bytes 1572872 | tf_op jit(solution)/shard_map/ppermute | solution.py:392
  3.7 29.0 %collective-permute-start.4 = (bf16[256,1024]{1,0:T(8,128)(2,1)}, bf16[256,1024]{1,0:T(8,128)(2,1)S(1)}, u32[]{:S(2)}, u32[]{:S(2)}) collective-permute-start(bf16[256,1024]{1,0:T(8,128)(2,1)} %bitcast.66), channel_id=1, source_target_pairs={{0,1},{1,0},{2,3},{3,2},{4,5},{5,4},{6,7},{7,6},{8,9},{9,8},{10,11... | collective-permute-start | bytes 1572872 | tf_op jit(solution)/shard_map/ppermute | solution.py:388
  8.5 8.8 %collective-permute-start.2 = (bf16[256,768]{1,0:T(8,128)(2,1)S(1)}, bf16[256,768]{1,0:T(8,128)(2,1)}, u32[]{:S(2)}, u32[]{:S(2)}) collective-permute-start(bf16[256,768]{1,0:T(8,128)(2,1)S(1)} %get-tuple-element.121), channel_id=1, source_target_pairs={{0,1},{1,0},{2,3},{3,2},{4,5},{5,4},{6,7},{7,6},{8,9},{9,8},{10,11... | collective-permute-start | bytes 1179656 | tf_op jit(solution)/shard_map/ppermute | solution.py:388
  9.0 16.3 %collective-permute-start = (bf16[256,768]{1,0:T(8,128)(2,1)}, bf16[256,768]{1,0:T(8,128)(2,1)S(1)}, u32[]{:S(2)}, u32[]{:S(2)}) collective-permute-start(bf16[256,768]{1,0:T(8,128)(2,1)} %get-tuple-element.119), channel_id=1, source_target_pairs={{0,1},{1,0},{2,3},{3,2},{4,5},{5,4},{6,7},{7,6},{8,9},{9,8},{10,11... | collective-permute-start | bytes 1179656 | tf_op jit(solution)/shard_map/ppermute | solution.py:388
  9.0 16.3 %collective-permute-start.1 = (bf16[256,768]{1,0:T(8,128)(2,1)}, bf16[256,768]{1,0:T(8,128)(2,1)S(1)}, u32[]{:S(2)}, u32[]{:S(2)}) collective-permute-start(bf16[256,768]{1,0:T(8,128)(2,1)} %get-tuple-element.120), channel_id=1, source_target_pairs={{0,2},{1,3},{2,0},{3,1},{4,6},{5,7},{6,4},{7,5},{8,10},{9,11},{10,... | collective-permute-start | bytes 1179656 | tf_op jit(solution)/shard_map/ppermute | solution.py:392
  16.7 16.0 %collective-permute-start.6 = (bf16[256,1024]{1,0:T(8,128)(2,1)S(1)}, bf16[256,1024]{1,0:T(8,128)(2,1)S(1)}, u32[]{:S(2)}, u32[]{:S(2)}) collective-permute-start(bf16[256,1024]{1,0:T(8,128)(2,1)S(1)} %collective-permute-done.5.x2), channel_id=1, source_target_pairs={{0,1},{1,0},{2,3},{3,2},{4,5},{5,4},{6,7},{7,6},{8,9},{9,8},{10,11... | collective-permute-start | bytes 1572872 | tf_op jit(solution)/shard_map/ppermute | solution.py:388
  17.3 15.4 %collective-permute-start.3 = (bf16[256,768]{1,0:T(8,128)(2,1)}, bf16[256,768]{1,0:T(8,128)(2,1)S(1)}, u32[]{:S(2)}, u32[]{:S(2)}) collective-permute-start(bf16[256,768]{1,0:T(8,128)(2,1)} %collective-permute-done.2), channel_id=1, source_target_pairs={{0,2},{1,3},{2,0},{3,1},{4,6},{5,7},{6,4},{7,5},{8,10},{9,11},{10,... | collective-permute-start | bytes 1179656 | tf_op jit(solution)/shard_map/ppermute | solution.py:392
  32.7 13.2 %collective-permute-start.7 = (bf16[256,1024]{1,0:T(8,128)(2,1)S(1)}, bf16[256,1024]{1,0:T(8,128)(2,1)S(1)}, u32[]{:S(2)}, u32[]{:S(2)}) collective-permute-start(bf16[256,1024]{1,0:T(8,128)(2,1)S(1)} %copy-done.35), channel_id=1, source_target_pairs={{0,2},{1,3},{2,0},{3,1},{4,6},{5,7},{6,4},{7,5},{8,10},{9,11},{10,... | collective-permute-start | bytes 1572872 | tf_op jit(solution)/shard_map/ppermute | solution.py:392
  46.7 49.4 %all-to-all-start = ((bf16[8,3,256,128]{3,2,1,0:T(8,128)(2,1)}), bf16[8,3,256,128]{3,2,1,0:T(8,128)(2,1)S(1)}, u32[]{:S(2)}, u32[]{:S(2)}) async-start(bf16[8,3,256,128]{3,2,1,0:T(8,128)(2,1)} %copy-done.11), calls=%async_computation | async-start | bytes 3145728 | tf_op jit(solution)/shard_map/all_to_all | solution.py:1348
  52.5 18.8 %collective-permute-start.8 = (bf16[256,1408]{1,0:T(8,128)(2,1)}, bf16[256,1408]{1,0:T(8,128)(2,1)S(1)}, u32[]{:S(2)}, u32[]{:S(2)}) collective-permute-start(bf16[256,1408]{1,0:T(8,128)(2,1)} %copy-done.89), channel_id=1, source_target_pairs={{0,2},{1,3},{2,0},{3,1},{4,6},{5,7},{6,4},{7,5},{8,10},{9,11},{10,... | collective-permute-start | bytes 2162696 | tf_op jit(solution)/shard_map/ppermute | solution.py:392
  71.2 17.8 %collective-permute-start.11 = (bf16[256,1408]{1,0:T(8,128)(2,1)S(1)}, bf16[256,1408]{1,0:T(8,128)(2,1)}, u32[]{:S(2)}, u32[]{:S(2)}) collective-permute-start(bf16[256,1408]{1,0:T(8,128)(2,1)S(1)} %collective-permute-done.10), channel_id=1, source_target_pairs={{0,2},{1,3},{2,0},{3,1},{4,6},{5,7},{6,4},{7,5},{8,10},{9,11},{10,... | collective-permute-start | bytes 2162696 | tf_op jit(solution)/shard_map/ppermute | solution.py:392
  73.5 21.8 %collective-permute-start.9 = (bf16[256,1408]{1,0:T(8,128)(2,1)S(1)}, bf16[256,1408]{1,0:T(8,128)(2,1)S(1)}, u32[]{:S(2)}, u32[]{:S(2)}) collective-permute-start(bf16[256,1408]{1,0:T(8,128)(2,1)S(1)} %collective-permute-done.8.refs_2_), channel_id=1, source_target_pairs={{0,4},{4,0},{8,12},{12,8},{16,20},{20,16},{24,28},{28,24},{1,5},{5... | collective-permute-start | bytes 2162696 | tf_op jit(solution)/shard_map/ppermute | solution.py:397
  89.9 17.1 %collective-permute-start.13 = (bf16[704,512]{1,0:T(8,128)(2,1)}, bf16[704,512]{1,0:T(8,128)(2,1)}, u32[]{:S(2)}, u32[]{:S(2)}) collective-permute-start(bf16[704,512]{1,0:T(8,128)(2,1)} %slice.131), channel_id=1, source_target_pairs={{0,2},{1,3},{2,0},{3,1},{4,6},{5,7},{6,4},{7,5},{8,10},{9,11},{10,... | collective-permute-start | bytes 2162696 | tf_op jit(solution)/shard_map/ppermute | solution.py:392
  91.4 17.4 %collective-permute-start.12 = (bf16[256,1408]{1,0:T(8,128)(2,1)}, bf16[256,1408]{1,0:T(8,128)(2,1)}, u32[]{:S(2)}, u32[]{:S(2)}) collective-permute-start(bf16[256,1408]{1,0:T(8,128)(2,1)} %collective-permute-done.11.refs_4_), channel_id=1, source_target_pairs={{0,4},{4,0},{8,12},{12,8},{16,20},{20,16},{24,28},{28,24},{1,5},{5... | collective-permute-start | bytes 2162696 | tf_op jit(solution)/shard_map/ppermute | solution.py:397
  108.9 24.9 %all-to-all-start.1 = ((bf16[8,256,128]{2,1,0:T(8,128)(2,1)}), bf16[8,256,128]{2,1,0:T(8,128)(2,1)}, u32[]{:S(2)}, u32[]{:S(2)}) async-start(bf16[8,256,128]{2,1,0:T(8,128)(2,1)} %copy-done.72), calls=%async_computation.1 | async-start | bytes 1048576 | tf_op jit(solution)/shard_map/all_to_all | solution.py:1371
  116.4 16.5 %collective-permute-start.14 = (bf16[704,512]{1,0:T(8,128)(2,1)S(1)}, bf16[704,512]{1,0:T(8,128)(2,1)S(1)}, u32[]{:S(2)}, u32[]{:S(2)}) collective-permute-start(bf16[704,512]{1,0:T(8,128)(2,1)S(1)} %slice.132), channel_id=1, source_target_pairs={{0,2},{1,3},{2,0},{3,1},{4,6},{5,7},{6,4},{7,5},{8,10},{9,11},{10,... | collective-permute-start | bytes 2162696 | tf_op jit(solution)/shard_map/ppermute | solution.py:392
  117.0 31.2 %collective-permute-start.18 = (bf16[2,256,1408]{2,1,0:T(8,128)(2,1)}, bf16[2,256,1408]{2,1,0:T(8,128)(2,1)}, u32[]{:S(2)}, u32[]{:S(2)}) collective-permute-start(bf16[2,256,1408]{2,1,0:T(8,128)(2,1)} %copy-done.87), channel_id=1, source_target_pairs={{0,1},{1,0},{2,3},{3,2},{4,5},{5,4},{6,7},{7,6},{8,9},{9,8},{10,11... | collective-permute-start | bytes 4325384 | tf_op jit(solution)/shard_map/ppermute | solution.py:388
  147.7 14.3 %collective-permute-start.19 = (bf16[256,1024]{1,0:T(8,128)(2,1)S(1)}, bf16[256,1024]{1,0:T(8,128)(2,1)}, u32[]{:S(2)}, u32[]{:S(2)}) collective-permute-start(bf16[256,1024]{1,0:T(8,128)(2,1)S(1)} %get-tuple-element.149.own_ref.refs_0_), channel_id=1, source_target_pairs={{0,2},{1,3},{2,0},{3,1},{4,6},{5,7},{6,4},{7,5},{8,10},{9,11},{10,... | collective-permute-start | bytes 1572872 | tf_op jit(solution)/shard_map/ppermute | solution.py:392
  166.1 14.3 %collective-permute-start.22 = (bf16[256,1024]{1,0:T(8,128)(2,1)S(1)}, bf16[256,1024]{1,0:T(8,128)(2,1)}, u32[]{:S(2)}, u32[]{:S(2)}) collective-permute-start(bf16[256,1024]{1,0:T(8,128)(2,1)S(1)} %get-tuple-element.157.own_ref.refs_0_), channel_id=1, source_target_pairs={{0,2},{1,3},{2,0},{3,1},{4,6},{5,7},{6,4},{7,5},{8,10},{9,11},{10,... | collective-permute-start | bytes 1572872 | tf_op jit(solution)/shard_map/ppermute | solution.py:392
  187.3 8.4 %collective-permute-start.25 = (bf16[4,256,128]{2,1,0:T(8,128)(2,1)S(1)}, bf16[4,256,128]{2,1,0:T(8,128)(2,1)S(1)}, u32[]{:S(2)}, u32[]{:S(2)}) collective-permute-start(bf16[4,256,128]{2,1,0:T(8,128)(2,1)S(1)} %get-tuple-element.165), channel_id=1, source_target_pairs={{0,2},{1,3},{2,0},{3,1},{4,6},{5,7},{6,4},{7,5},{8,10},{9,11},{10,... | collective-permute-start | bytes 786440 | tf_op jit(solution)/shard_map/ppermute | solution.py:392
  187.7 14.5 %collective-permute-start.26 = (bf16[256,1024]{1,0:T(8,128)(2,1)}, bf16[256,1024]{1,0:T(8,128)(2,1)}, u32[]{:S(2)}, u32[]{:S(2)}) collective-permute-start(bf16[256,1024]{1,0:T(8,128)(2,1)} %collective-permute-done.19.x2_ref.refs_2_), channel_id=1, source_target_pairs={{0,1},{1,0},{2,3},{3,2},{4,5},{5,4},{6,7},{7,6},{8,9},{9,8},{10,11... | collective-permute-start | bytes 1572872 | tf_op jit(solution)/shard_map/ppermute | solution.py:388
  187.7 14.5 %collective-permute-start.27 = (bf16[256,1024]{1,0:T(8,128)(2,1)}, bf16[256,1024]{1,0:T(8,128)(2,1)}, u32[]{:S(2)}, u32[]{:S(2)}) collective-permute-start(bf16[256,1024]{1,0:T(8,128)(2,1)} %collective-permute-done.22.grad2_ref.refs_2_), channel_id=1, source_target_pairs={{0,1},{1,0},{2,3},{3,2},{4,5},{5,4},{6,7},{7,6},{8,9},{9,8},{10,11... | collective-permute-start | bytes 1572872 | tf_op jit(solution)/shard_map/ppermute | solution.py:388
  196.5 28.2 %all-to-all-start.2 = ((bf16[8,256,128]{2,1,0:T(8,128)(2,1)}), bf16[8,256,128]{2,1,0:T(8,128)(2,1)}, u32[]{:S(2)}, u32[]{:S(2)}) async-start(bf16[8,256,128]{2,1,0:T(8,128)(2,1)} %pad_maximum_fusion), calls=%async_computation.2 | async-start | bytes 1048576 | tf_op jit(solution)/shard_map/all_to_all | solution.py:1532
  222.7 17.4 %collective-permute-start.28 = (bf16[2,4,32,1408]{3,2,1,0:T(8,128)(2,1)}, bf16[2,4,32,1408]{3,2,1,0:T(8,128)(2,1)}, u32[]{:S(2)}, u32[]{:S(2)}) collective-permute-start(bf16[2,4,32,1408]{3,2,1,0:T(8,128)(2,1)} %get-tuple-element.177), channel_id=1, source_target_pairs={{0,4},{4,0},{8,12},{12,8},{16,20},{20,16},{24,28},{28,24},{1,5},{5... | collective-permute-start | bytes 2162696 | tf_op jit(solution)/shard_map/ppermute | solution.py:397
  240.1 40.9 %all-to-all-start.3 = ((bf16[8,3,256,128]{3,2,1,0:T(8,128)(2,1)}), bf16[8,3,256,128]{3,2,1,0:T(8,128)(2,1)S(1)}, u32[]{:S(2)}, u32[]{:S(2)}) async-start(bf16[8,3,256,128]{3,2,1,0:T(8,128)(2,1)} %copy-done.12), calls=%async_computation.3 | async-start | bytes 3145728 | tf_op jit(solution)/shard_map/all_to_all | solution.py:1568
  245.8 11.7 %collective-permute-start.29 = (bf16[256,1024]{1,0:T(8,128)(2,1)}, bf16[256,1024]{1,0:T(8,128)(2,1)S(1)}, u32[]{:S(2)}, u32[]{:S(2)}) collective-permute-start(bf16[256,1024]{1,0:T(8,128)(2,1)} %copy-done.41), channel_id=1, source_target_pairs={{0,2},{1,3},{2,0},{3,1},{4,6},{5,7},{6,4},{7,5},{8,10},{9,11},{10,... | collective-permute-start | bytes 1572872 | tf_op jit(solution)/shard_map/ppermute | solution.py:392
  246.3 32.2 %collective-permute-start.45 = (bf16[2,4,32,1408]{3,2,1,0:T(8,128)(2,1)}, bf16[2,4,32,1408]{3,2,1,0:T(8,128)(2,1)S(1)}, u32[]{:S(2)}, u32[]{:S(2)}) collective-permute-start(bf16[2,4,32,1408]{3,2,1,0:T(8,128)(2,1)} %copy-done.88), channel_id=1, source_target_pairs={{0,4},{4,0},{8,12},{12,8},{16,20},{20,16},{24,28},{28,24},{1,5},{5... | collective-permute-start | bytes 2162696 | tf_op jit(solution)/shard_map/ppermute | solution.py:397
  292.0 9.5 %collective-permute-start.58 = (bf16[4,32,1408]{2,1,0:T(8,128)(2,1)S(1)}, bf16[4,32,1408]{2,1,0:T(8,128)(2,1)S(1)}, u32[]{:S(2)}, u32[]{:S(2)}) collective-permute-start(bf16[4,32,1408]{2,1,0:T(8,128)(2,1)S(1)} %fusion), channel_id=1, source_target_pairs={{0,8},{4,12},{8,16},{12,20},{16,24},{20,28},{24,0},{28,4},{1,9},{5... | collective-permute-start | bytes 1081352 | tf_op jit(solution)/shard_map/ppermute | solution.py:402
  292.3 24.5 %collective-permute-start.46 = (bf16[2,4,32,960]{3,2,1,0:T(8,128)(2,1)S(1)}, bf16[2,4,32,960]{3,2,1,0:T(8,128)(2,1)S(1)}, u32[]{:S(2)}, u32[]{:S(2)}) collective-permute-start(bf16[2,4,32,960]{3,2,1,0:T(8,128)(2,1)S(1)} %copy-done.94), channel_id=1, source_target_pairs={{0,4},{4,0},{8,12},{12,8},{16,20},{20,16},{24,28},{28,24},{1,5},{5... | collective-permute-start | bytes 1474568 | tf_op jit(solution)/shard_map/ppermute | solution.py:397
  293.7 20.6 %collective-permute-start.33 = (bf16[2,4,32,896]{3,2,1,0:T(8,128)(2,1)S(1)}, bf16[2,4,32,896]{3,2,1,0:T(8,128)(2,1)S(1)}, u32[]{:S(2)}, u32[]{:S(2)}) collective-permute-start(bf16[2,4,32,896]{3,2,1,0:T(8,128)(2,1)S(1)} %get-tuple-element.194), channel_id=1, source_target_pairs={{0,4},{4,0},{8,12},{12,8},{16,20},{20,16},{24,28},{28,24},{1,5},{5... | collective-permute-start | bytes 1376264 | tf_op jit(solution)/shard_map/ppermute | solution.py:397
  299.5 95.0 %collective-permute-start.31 = (bf16[2,256,1024]{2,1,0:T(8,128)(2,1)}, bf16[2,256,1024]{2,1,0:T(8,128)(2,1)S(1)}, u32[]{:S(2)}, u32[]{:S(2)}) collective-permute-start(bf16[2,256,1024]{2,1,0:T(8,128)(2,1)} %get-tuple-element.191), channel_id=1, source_target_pairs={{0,1},{1,0},{2,3},{3,2},{4,5},{5,4},{6,7},{7,6},{8,9},{9,8},{10,11... | collective-permute-start | bytes 3145736 | tf_op jit(solution)/shard_map/ppermute | solution.py:388
  301.6 16.3 %collective-permute-start.59 = (bf16[4,32,1408]{2,1,0:T(8,128)(2,1)S(1)}, bf16[4,32,1408]{2,1,0:T(8,128)(2,1)S(1)}, u32[]{:S(2)}, u32[]{:S(2)}) collective-permute-start(bf16[4,32,1408]{2,1,0:T(8,128)(2,1)S(1)} %fusion.2), channel_id=1, source_target_pairs={{0,8},{4,12},{8,16},{12,20},{16,24},{20,28},{24,0},{28,4},{1,9},{5... | collective-permute-start | bytes 1081352 | tf_op jit(solution)/shard_map/ppermute | solution.py:402
  314.3 29.9 %collective-permute-start.34 = (bf16[2,4,32,896]{3,2,1,0:T(8,128)(2,1)}, bf16[2,4,32,896]{3,2,1,0:T(8,128)(2,1)S(1)}, u32[]{:S(2)}, u32[]{:S(2)}) collective-permute-start(bf16[2,4,32,896]{3,2,1,0:T(8,128)(2,1)} %get-tuple-element.195), channel_id=1, source_target_pairs={{0,4},{4,0},{8,12},{12,8},{16,20},{20,16},{24,28},{28,24},{1,5},{5... | collective-permute-start | bytes 1376264 | tf_op jit(solution)/shard_map/ppermute | solution.py:397
  316.1 10.4 %collective-permute-start.35 = (bf16[4,32,896]{2,1,0:T(8,128)(2,1)S(1)}, bf16[4,32,896]{2,1,0:T(8,128)(2,1)S(1)}, u32[]{:S(2)}, u32[]{:S(2)}) collective-permute-start(bf16[4,32,896]{2,1,0:T(8,128)(2,1)S(1)} %fusion.15), channel_id=1, source_target_pairs={{0,8},{4,12},{8,16},{12,20},{16,24},{20,28},{24,0},{28,4},{1,9},{5... | collective-permute-start | bytes 688136 | tf_op jit(solution)/shard_map/ppermute | solution.py:402
  316.8 31.7 %collective-permute-start.47 = (bf16[2,4,32,960]{3,2,1,0:T(8,128)(2,1)S(1)}, bf16[2,4,32,960]{3,2,1,0:T(8,128)(2,1)}, u32[]{:S(2)}, u32[]{:S(2)}) collective-permute-start(bf16[2,4,32,960]{3,2,1,0:T(8,128)(2,1)S(1)} %copy-done.92), channel_id=1, source_target_pairs={{0,4},{4,0},{8,12},{12,8},{16,20},{20,16},{24,28},{28,24},{1,5},{5... | collective-permute-start | bytes 1474568 | tf_op jit(solution)/shard_map/ppermute | solution.py:397
  317.9 14.2 %collective-permute-start.48 = (bf16[4,32,960]{2,1,0:T(8,128)(2,1)S(1)}, bf16[4,32,960]{2,1,0:T(8,128)(2,1)S(1)}, u32[]{:S(2)}, u32[]{:S(2)}) collective-permute-start(bf16[4,32,960]{2,1,0:T(8,128)(2,1)S(1)} %fusion.14), channel_id=1, source_target_pairs={{0,8},{4,12},{8,16},{12,20},{16,24},{20,28},{24,0},{28,4},{1,9},{5... | collective-permute-start | bytes 737288 | tf_op jit(solution)/shard_map/ppermute | solution.py:402
  326.5 13.3 %collective-permute-start.60 = (bf16[4,32,1408]{2,1,0:T(8,128)(2,1)S(1)}, bf16[4,32,1408]{2,1,0:T(8,128)(2,1)S(1)}, u32[]{:S(2)}, u32[]{:S(2)}) collective-permute-start(bf16[4,32,1408]{2,1,0:T(8,128)(2,1)S(1)} %fusion.4), channel_id=1, source_target_pairs={{0,8},{4,12},{8,16},{12,20},{16,24},{20,28},{24,0},{28,4},{1,9},{5... | collective-permute-start | bytes 1081352 | tf_op jit(solution)/shard_map/ppermute | solution.py:402
  332.1 12.1 %collective-permute-start.36 = (bf16[4,32,896]{2,1,0:T(8,128)(2,1)S(1)}, bf16[4,32,896]{2,1,0:T(8,128)(2,1)}, u32[]{:S(2)}, u32[]{:S(2)}) collective-permute-start(bf16[4,32,896]{2,1,0:T(8,128)(2,1)S(1)} %fusion.11), channel_id=1, source_target_pairs={{0,8},{4,12},{8,16},{12,20},{16,24},{20,28},{24,0},{28,4},{1,9},{5... | collective-permute-start | bytes 688136 | tf_op jit(solution)/shard_map/ppermute | solution.py:402
  339.8 8.7 %collective-permute-start.49 = (bf16[4,32,960]{2,1,0:T(8,128)(2,1)}, bf16[4,32,960]{2,1,0:T(8,128)(2,1)}, u32[]{:S(2)}, u32[]{:S(2)}) collective-permute-start(bf16[4,32,960]{2,1,0:T(8,128)(2,1)} %fusion.8), channel_id=1, source_target_pairs={{0,8},{4,12},{8,16},{12,20},{16,24},{20,28},{24,0},{28,4},{1,9},{5... | collective-permute-start | bytes 737288 | tf_op jit(solution)/shard_map/ppermute | solution.py:402
  340.7 10.5 %all-to-all-start.5 = ((bf16[4,32,1408]{2,1,0:T(8,128)(2,1)}), bf16[4,32,1408]{2,1,0:T(8,128)(2,1)S(1)}, u32[]{:S(2)}, u32[]{:S(2)}) async-start(bf16[4,32,1408]{2,1,0:T(8,128)(2,1)} %fusion.6), calls=%async_computation.5 | async-start | bytes 720896 | tf_op jit(solution)/shard_map/all_to_all | solution.py:1624
  346.8 10.6 %collective-permute-start.37 = (bf16[4,32,896]{2,1,0:T(8,128)(2,1)}, bf16[4,32,896]{2,1,0:T(8,128)(2,1)}, u32[]{:S(2)}, u32[]{:S(2)}) collective-permute-start(bf16[4,32,896]{2,1,0:T(8,128)(2,1)} %fusion.12), channel_id=1, source_target_pairs={{0,8},{4,12},{8,16},{12,20},{16,24},{20,28},{24,0},{28,4},{1,9},{5... | collective-permute-start | bytes 688136 | tf_op jit(solution)/shard_map/ppermute | solution.py:402
  349.7 13.3 %collective-permute-start.50 = (bf16[4,32,960]{2,1,0:T(8,128)(2,1)S(1)}, bf16[4,32,960]{2,1,0:T(8,128)(2,1)}, u32[]{:S(2)}, u32[]{:S(2)}) collective-permute-start(bf16[4,32,960]{2,1,0:T(8,128)(2,1)S(1)} %fusion.9), channel_id=1, source_target_pairs={{0,8},{4,12},{8,16},{12,20},{16,24},{20,28},{24,0},{28,4},{1,9},{5... | collective-permute-start | bytes 737288 | tf_op jit(solution)/shard_map/ppermute | solution.py:402
  351.2 19.5 %collective-permute-start.61 = (bf16[4,32,1408]{2,1,0:T(8,128)(2,1)S(1)}, bf16[4,32,1408]{2,1,0:T(8,128)(2,1)}, u32[]{:S(2)}, u32[]{:S(2)}) collective-permute-start(bf16[4,32,1408]{2,1,0:T(8,128)(2,1)S(1)} %all-to-all-done.5.refs_0_), channel_id=1, source_target_pairs={{0,8},{4,12},{8,16},{12,20},{16,24},{20,28},{24,0},{28,4},{1,9},{5... | collective-permute-start | bytes 1081352 | tf_op jit(solution)/shard_map/ppermute | solution.py:402
  359.3 9.0 %all-to-all-start.4 = ((bf16[4,32,896]{2,1,0:T(8,128)(2,1)}), bf16[4,32,896]{2,1,0:T(8,128)(2,1)S(1)}, u32[]{:S(2)}, u32[]{:S(2)}) async-start(bf16[4,32,896]{2,1,0:T(8,128)(2,1)} %fusion.13), calls=%async_computation.4 | async-start | bytes 458752 | tf_op jit(solution)/shard_map/all_to_all | solution.py:1624
  362.7 11.4 %collective-permute-start.62 = (bf16[4,32,1408]{2,1,0:T(8,128)(2,1)S(1)}, bf16[4,32,1408]{2,1,0:T(8,128)(2,1)}, u32[]{:S(2)}, u32[]{:S(2)}) collective-permute-start(bf16[4,32,1408]{2,1,0:T(8,128)(2,1)S(1)} %all-to-all-done.5.refs_0_), channel_id=1, source_target_pairs={{0,4},{4,0},{8,12},{12,8},{16,20},{20,16},{24,28},{28,24},{1,5},{5... | collective-permute-start | bytes 1081352 | tf_op jit(solution)/shard_map/ppermute | solution.py:397
  364.3 12.0 %collective-permute-start.51 = (bf16[4,32,960]{2,1,0:T(8,128)(2,1)S(1)}, bf16[4,32,960]{2,1,0:T(8,128)(2,1)}, u32[]{:S(2)}, u32[]{:S(2)}) collective-permute-start(bf16[4,32,960]{2,1,0:T(8,128)(2,1)S(1)} %fusion.10.refs_0_), channel_id=1, source_target_pairs={{0,8},{4,12},{8,16},{12,20},{16,24},{20,28},{24,0},{28,4},{1,9},{5... | collective-permute-start | bytes 737288 | tf_op jit(solution)/shard_map/ppermute | solution.py:402
  364.4 15.3 %collective-permute-start.52 = (bf16[4,32,960]{2,1,0:T(8,128)(2,1)S(1)}, bf16[4,32,960]{2,1,0:T(8,128)(2,1)}, u32[]{:S(2)}, u32[]{:S(2)}) collective-permute-start(bf16[4,32,960]{2,1,0:T(8,128)(2,1)S(1)} %fusion.10.refs_0_), channel_id=1, source_target_pairs={{0,4},{4,0},{8,12},{12,8},{16,20},{20,16},{24,28},{28,24},{1,5},{5... | collective-permute-start | bytes 737288 | tf_op jit(solution)/shard_map/ppermute | solution.py:397
  370.7 10.4 %collective-permute-start.38 = (bf16[4,32,896]{2,1,0:T(8,128)(2,1)S(1)}, bf16[4,32,896]{2,1,0:T(8,128)(2,1)S(1)}, u32[]{:S(2)}, u32[]{:S(2)}) collective-permute-start(bf16[4,32,896]{2,1,0:T(8,128)(2,1)S(1)} %all-to-all-done.4.refs_0_), channel_id=1, source_target_pairs={{0,8},{4,12},{8,16},{12,20},{16,24},{20,28},{24,0},{28,4},{1,9},{5... | collective-permute-start | bytes 688136 | tf_op jit(solution)/shard_map/ppermute | solution.py:402
  374.1 21.2 %collective-permute-start.63 = (bf16[4,32,1408]{2,1,0:T(8,128)(2,1)}, bf16[4,32,1408]{2,1,0:T(8,128)(2,1)S(1)}, u32[]{:S(2)}, u32[]{:S(2)}) collective-permute-start(bf16[4,32,1408]{2,1,0:T(8,128)(2,1)} %collective-permute-done.61.refs_1_), channel_id=1, source_target_pairs={{0,8},{4,12},{8,16},{12,20},{16,24},{20,28},{24,0},{28,4},{1,9},{5... | collective-permute-start | bytes 1081352 | tf_op jit(solution)/shard_map/ppermute | solution.py:402
  379.7 14.5 %collective-permute-start.53 = (bf16[4,32,960]{2,1,0:T(8,128)(2,1)}, bf16[4,32,960]{2,1,0:T(8,128)(2,1)S(1)}, u32[]{:S(2)}, u32[]{:S(2)}) collective-permute-start(bf16[4,32,960]{2,1,0:T(8,128)(2,1)} %collective-permute-done.51.refs_1_), channel_id=1, source_target_pairs={{0,8},{4,12},{8,16},{12,20},{16,24},{20,28},{24,0},{28,4},{1,9},{5... | collective-permute-start | bytes 737288 | tf_op jit(solution)/shard_map/ppermute | solution.py:402
  381.1 13.1 %collective-permute-start.54 = (bf16[4,32,960]{2,1,0:T(8,128)(2,1)}, bf16[4,32,960]{2,1,0:T(8,128)(2,1)S(1)}, u32[]{:S(2)}, u32[]{:S(2)}) collective-permute-start(bf16[4,32,960]{2,1,0:T(8,128)(2,1)} %collective-permute-done.51.refs_1_), channel_id=1, source_target_pairs={{0,4},{4,0},{8,12},{12,8},{16,20},{20,16},{24,28},{28,24},{1,5},{5... | collective-permute-start | bytes 737288 | tf_op jit(solution)/shard_map/ppermute | solution.py:397
  384.4 13.5 %collective-permute-start.64 = (bf16[4,32,1408]{2,1,0:T(8,128)(2,1)}, bf16[4,32,1408]{2,1,0:T(8,128)(2,1)S(1)}, u32[]{:S(2)}, u32[]{:S(2)}) collective-permute-start(bf16[4,32,1408]{2,1,0:T(8,128)(2,1)} %collective-permute-done.61.refs_1_), channel_id=1, source_target_pairs={{0,4},{4,0},{8,12},{12,8},{16,20},{20,16},{24,28},{28,24},{1,5},{5... | collective-permute-start | bytes 1081352 | tf_op jit(solution)/shard_map/ppermute | solution.py:397
  394.3 10.3 %collective-permute-start.40 = (bf16[4,32,896]{2,1,0:T(8,128)(2,1)S(1)}, bf16[4,32,896]{2,1,0:T(8,128)(2,1)S(1)}, u32[]{:S(2)}, u32[]{:S(2)}) collective-permute-start(bf16[4,32,896]{2,1,0:T(8,128)(2,1)S(1)} %collective-permute-done.38.refs_1_), channel_id=1, source_target_pairs={{0,8},{4,12},{8,16},{12,20},{16,24},{20,28},{24,0},{28,4},{1,9},{5... | collective-permute-start | bytes 688136 | tf_op jit(solution)/shard_map/ppermute | solution.py:402
  394.3 10.3 %collective-permute-start.41 = (bf16[4,32,896]{2,1,0:T(8,128)(2,1)S(1)}, bf16[4,32,896]{2,1,0:T(8,128)(2,1)S(1)}, u32[]{:S(2)}, u32[]{:S(2)}) collective-permute-start(bf16[4,32,896]{2,1,0:T(8,128)(2,1)S(1)} %collective-permute-done.38.refs_1_), channel_id=1, source_target_pairs={{0,4},{4,0},{8,12},{12,8},{16,20},{20,16},{24,28},{28,24},{1,5},{5... | collective-permute-start | bytes 688136 | tf_op jit(solution)/shard_map/ppermute | solution.py:397
  394.6 15.6 %collective-permute-start.55 = (bf16[4,32,960]{2,1,0:T(8,128)(2,1)S(1)}, bf16[4,32,960]{2,1,0:T(8,128)(2,1)S(1)}, u32[]{:S(2)}, u32[]{:S(2)}) collective-permute-start(bf16[4,32,960]{2,1,0:T(8,128)(2,1)S(1)} %collective-permute-done.53.refs_2_), channel_id=1, source_target_pairs={{0,8},{4,12},{8,16},{12,20},{16,24},{20,28},{24,0},{28,4},{1,9},{5... | collective-permute-start | bytes 737288 | tf_op jit(solution)/shard_map/ppermute | solution.py:402
  395.3 14.9 %collective-permute-start.56 = (bf16[4,32,960]{2,1,0:T(8,128)(2,1)S(1)}, bf16[4,32,960]{2,1,0:T(8,128)(2,1)S(1)}, u32[]{:S(2)}, u32[]{:S(2)}) collective-permute-start(bf16[4,32,960]{2,1,0:T(8,128)(2,1)S(1)} %collective-permute-done.53.refs_2_), channel_id=1, source_target_pairs={{0,4},{4,0},{8,12},{12,8},{16,20},{20,16},{24,28},{28,24},{1,5},{5... | collective-permute-start | bytes 737288 | tf_op jit(solution)/shard_map/ppermute | solution.py:397
  398.0 25.8 %collective-permute-start.32 = (bf16[256,1024]{1,0:T(8,128)(2,1)S(1)}, bf16[256,1024]{1,0:T(8,128)(2,1)S(1)}, u32[]{:S(2)}, u32[]{:S(2)}) collective-permute-start(bf16[256,1024]{1,0:T(8,128)(2,1)S(1)} %fusion.7), channel_id=1, source_target_pairs={{0,2},{1,3},{2,0},{3,1},{4,6},{5,7},{6,4},{7,5},{8,10},{9,11},{10,... | collective-permute-start | bytes 1572872 | tf_op jit(solution)/shard_map/ppermute | solution.py:392
  404.5 19.2 %collective-permute-start.65 = (bf16[4,32,1408]{2,1,0:T(8,128)(2,1)S(1)}, bf16[4,32,1408]{2,1,0:T(8,128)(2,1)S(1)}, u32[]{:S(2)}, u32[]{:S(2)}) collective-permute-start(bf16[4,32,1408]{2,1,0:T(8,128)(2,1)S(1)} %collective-permute-done.63.refs_2_), channel_id=1, source_target_pairs={{0,8},{4,12},{8,16},{12,20},{16,24},{20,28},{24,0},{28,4},{1,9},{5... | collective-permute-start | bytes 1081352 | tf_op jit(solution)/shard_map/ppermute | solution.py:402
  404.5 19.2 %collective-permute-start.66 = (bf16[4,32,1408]{2,1,0:T(8,128)(2,1)S(1)}, bf16[4,32,1408]{2,1,0:T(8,128)(2,1)S(1)}, u32[]{:S(2)}, u32[]{:S(2)}) collective-permute-start(bf16[4,32,1408]{2,1,0:T(8,128)(2,1)S(1)} %collective-permute-done.63.refs_2_), channel_id=1, source_target_pairs={{0,4},{4,0},{8,12},{12,8},{16,20},{20,16},{24,28},{28,24},{1,5},{5... | collective-permute-start | bytes 1081352 | tf_op jit(solution)/shard_map/ppermute | solution.py:397
  410.2 11.5 %collective-permute-start.42 = (bf16[4,32,896]{2,1,0:T(8,128)(2,1)S(1)}, bf16[4,32,896]{2,1,0:T(8,128)(2,1)S(1)}, u32[]{:S(2)}, u32[]{:S(2)}) collective-permute-start(bf16[4,32,896]{2,1,0:T(8,128)(2,1)S(1)} %collective-permute-done.40.refs_2_), channel_id=1, source_target_pairs={{0,8},{4,12},{8,16},{12,20},{16,24},{20,28},{24,0},{28,4},{1,9},{5... | collective-permute-start | bytes 688136 | tf_op jit(solution)/shard_map/ppermute | solution.py:402
  410.2 11.5 %collective-permute-start.43 = (bf16[4,32,896]{2,1,0:T(8,128)(2,1)S(1)}, bf16[4,32,896]{2,1,0:T(8,128)(2,1)S(1)}, u32[]{:S(2)}, u32[]{:S(2)}) collective-permute-start(bf16[4,32,896]{2,1,0:T(8,128)(2,1)S(1)} %collective-permute-done.40.refs_2_), channel_id=1, source_target_pairs={{0,4},{4,0},{8,12},{12,8},{16,20},{20,16},{24,28},{28,24},{1,5},{5... | collective-permute-start | bytes 688136 | tf_op jit(solution)/shard_map/ppermute | solution.py:397
  421.7 9.2 %collective-permute-start.57 = (bf16[4,32,960]{2,1,0:T(8,128)(2,1)S(1)}, bf16[4,32,960]{2,1,0:T(8,128)(2,1)S(1)}, u32[]{:S(2)}, u32[]{:S(2)}) collective-permute-start(bf16[4,32,960]{2,1,0:T(8,128)(2,1)S(1)} %collective-permute-done.55.refs_3_), channel_id=1, source_target_pairs={{0,4},{4,0},{8,12},{12,8},{16,20},{20,16},{24,28},{28,24},{1,5},{5... | collective-permute-start | bytes 737288 | tf_op jit(solution)/shard_map/ppermute | solution.py:397
  421.7 14.2 %collective-permute-start.44 = (bf16[4,32,896]{2,1,0:T(8,128)(2,1)S(1)}, bf16[4,32,896]{2,1,0:T(8,128)(2,1)S(1)}, u32[]{:S(2)}, u32[]{:S(2)}) collective-permute-start(bf16[4,32,896]{2,1,0:T(8,128)(2,1)S(1)} %collective-permute-done.42.refs_3_), channel_id=1, source_target_pairs={{0,4},{4,0},{8,12},{12,8},{16,20},{20,16},{24,28},{28,24},{1,5},{5... | collective-permute-start | bytes 688136 | tf_op jit(solution)/shard_map/ppermute | solution.py:397
  423.7 17.8 %collective-permute-start.67 = (bf16[4,32,1408]{2,1,0:T(8,128)(2,1)S(1)}, bf16[4,32,1408]{2,1,0:T(8,128)(2,1)S(1)}, u32[]{:S(2)}, u32[]{:S(2)}) collective-permute-start(bf16[4,32,1408]{2,1,0:T(8,128)(2,1)S(1)} %collective-permute-done.65.refs_3_), channel_id=1, source_target_pairs={{0,4},{4,0},{8,12},{12,8},{16,20},{20,16},{24,28},{28,24},{1,5},{5... | collective-permute-start | bytes 1081352 | tf_op jit(solution)/shard_map/ppermute | solution.py:397
  (116 other events, 1069.2 us)

commit v4 on v3

--- a/solution.py
+++ b/solution.py
@@ -464,11 +464,27 @@
     return pl.ds(pl.multiple_of((me_ref[0] ^ place) * rows, rows), rows)
 
 
-def split_qkv_kernel(me_ref, q_ref, k_ref, v_ref, *out_refs):
-    part = out_refs[0].shape[1] // 3
-    for place, out_ref in enumerate(out_refs):
+def half_columns(which, ref):
+    columns = ref.shape[1]
+    return pl.ds(pl.multiple_of(which * columns, HEAD), columns)
+
+
+def split_qkv_kernel(
+    me_ref, q_ref, k_ref, v_ref, mix_ref, own_ref, beside_ref, far_sent, corner_sent, mix_sent, block_scr
+):
+    part = own_ref.shape[1] // 3
+    side = me_ref[1] % 2
+
+    def put(target, place):
         for kind, ref in enumerate((q_ref, k_ref, v_ref)):
-            out_ref[:, kind * part : (kind + 1) * part] = ref[:, columns_of(me_ref, place, part)]
+            target[:, kind * part : (kind + 1) * part] = ref[:, columns_of(me_ref, place, part)]
+
+    put(own_ref, 0)
+    put(beside_ref, 1)
+    for place, target in ((2, far_sent), (3, corner_sent)):
+        put(block_scr, place)
+        target[...] = block_scr[:, half_columns(side, target)]
+    mix_sent[...] = mix_ref[:, half_columns(side, mix_sent)]
 
 
 def pair_columns(half):
@@ -483,7 +499,7 @@
 
 
 def split_ff_kernel(
-    me_ref, gate_ref, up_ref, own_ref, own_sent, beside_ref, beside_sent
+    me_ref, gate_ref, up_ref, down_ref, own_ref, own_sent, beside_ref, beside_sent, left_ref, right_ref
 ):
     half = own_ref.shape[-1] // 2
     for me in range(PLACES):
@@ -499,20 +515,51 @@
                     ]
 
     side = me_ref[1] % 2
+    middle = left_ref.shape[1]
+    left_ref[...] = down_ref[:, :middle]
+    right_ref[...] = down_ref[:, middle:]
     own_sent[...] = own_ref[1 - side]
     beside_sent[...] = beside_ref[1 - side]
 
 
 def project_kernel(
-    me_ref, x0, x1, x2, x3, gain_ref, w0, w1, w2, w3, cos_ref, sin_ref, out_ref, x_scr, normed_scr
+    me_ref,
+    x0,
+    x1,
+    x2,
+    x3,
+    gain_ref,
+    w0,
+    w1,
+    far_y,
+    far_x,
+    corner_y,
+    corner_x,
+    cos_ref,
+    sin_ref,
+    out_ref,
+    w_ref,
+    x_scr,
+    normed_scr,
 ):
-    choose(pl.program_id(0), (x0, x1, x2, x3), x_scr)
+    step = pl.program_id(0)
+
+    @pl.when(step == 0)
+    def _():
+        side = me_ref[1] % 2
+        w_ref[0] = w0[...]
+        w_ref[1] = w1[...]
+        for place, first, second in ((2, far_y, far_x), (3, corner_y, corner_x)):
+            w_ref[place, :, half_columns(side, first)] = first[...]
+            w_ref[place, :, half_columns(1 - side, second)] = second[...]
+
+    choose(step, (x0, x1, x2, x3), x_scr)
     x = x_scr[...].astype(f32)
     normed_scr[...] = (x * inverse_rms(x) * gain_ref[...]).astype(bf16)
     rows = w0.shape[0]
     product = sum(
-        dot_nn(normed_scr[:, columns_of(me_ref, place, rows)], w[...])
-        for place, w in enumerate((w0, w1, w2, w3))
+        dot_nn(normed_scr[:, columns_of(me_ref, place, rows)], w_ref[place])
+        for place in range(PLACES)
     )
     heads = out_ref.shape[0]
     for kind in range(3):
@@ -645,8 +692,11 @@
     )
     back = 1.0 / math.sqrt(HEAD)
 
+    ahead_tables = cos_ref.shape[0] - qkv_ref.shape[0]
+
     def unturn(values, block):
-        return split(turn(values * back, flat(cos_ref[at(block)]), -flat(sin_ref[at(block)])).astype(bf16))
+        where = pl.ds(ahead_tables + block * span, span)
+        return split(turn(values * back, flat(cos_ref[where]), -flat(sin_ref[where])).astype(bf16))
 
     out_ref[at(block), 0] = unturn(query_sum.T, block)
 
@@ -658,38 +708,49 @@
             out_ref[at(key_block), 2] = split(value_sum[key_block].astype(bf16))
 
 
-def mix_out_kernel(near_ref, far_ref, w_near_ref, w_far_ref, keep_ref, send_ref):
+def mix_out_kernel(me_ref, near_ref, far_ref, w_near_ref, w_y_ref, w_x_ref, keep_ref, send_ref):
     heads = near_ref.shape[0] // PLACES
+    side = me_ref[1] % 2
     for step, out_ref in enumerate((keep_ref, send_ref)):
-        total = 0.0
-        for ref, w_ref in ((near_ref, w_near_ref), (far_ref, w_far_ref)):
-            both = jnp.concatenate([ref[step * heads + j] for j in range(heads)], axis=1)
-            total = total + dot_nn(both, w_ref[...])
-        out_ref[...] = total.astype(out_ref.dtype)
-
-
-def heads_back_kernel(own_ref, beside_ref, w_near_ref, w_far_ref, near_ref, far_ref):
+        near, far = (
+            jnp.concatenate([ref[step * heads + j] for j in range(heads)], axis=1)
+            for ref in (near_ref, far_ref)
+        )
+        for which, w_ref in ((side, w_y_ref), (1 - side, w_x_ref)):
+            columns = half_columns(which, w_ref)
+            term = dot_nn(near, w_near_ref[:, columns]) + dot_nn(far, w_ref[...])
+            out_ref[:, columns] = term.astype(out_ref.dtype)
+
+
+def heads_back_kernel(me_ref, own_ref, beside_ref, w_near_ref, w_y_ref, w_x_ref, near_ref, far_ref):
     heads = near_ref.shape[0] // 2
+    side = me_ref[1] % 2
     for step, ref in enumerate((own_ref, beside_ref)):
-        for w_ref, out_ref in ((w_near_ref, near_ref), (w_far_ref, far_ref)):
-            both = dot_nt(ref[...], w_ref[...]).astype(bf16)
+        near = dot_nt(ref[...], w_near_ref[...])
+        far = sum(
+            dot_nt(ref[:, half_columns(which, w_ref)], w_ref[...])
+            for which, w_ref in ((side, w_y_ref), (1 - side, w_x_ref))
+        )
+        for value, out_ref in ((near, near_ref), (far, far_ref)):
+            low = value.astype(bf16)
             for head in range(heads):
-                out_ref[step * heads + head] = both[:, head * HEAD : (head + 1) * HEAD]
-
-
-def project_back_kernel(me_ref, pieces_ref, w0, w1, w2, w3, keep_ref, send_ref):
+                out_ref[step * heads + head] = low[:, head * HEAD : (head + 1) * HEAD]
+
+
+def project_back_kernel(me_ref, pieces_ref, w_ref, keep_ref, send_ref):
     step = pl.program_id(0)
     heads = pieces_ref.shape[0]
     pieces = jnp.concatenate(
         [pieces_ref[head, kind] for kind in range(3) for head in range(heads)], axis=1
     )
-    rows = w0.shape[0]
+    rows = w_ref.shape[1]
     for target, parity in ((keep_ref, 0), (send_ref, 1)):
 
         @pl.when(step % 2 == parity)
         def _(target=target):
-            for place, w in enumerate((w0, w1, w2, w3)):
-                target[0, :, columns_of(me_ref, place, rows)] = dot_nt(pieces, w[...]).astype(bf16)
+            for place in range(PLACES):
+                term = dot_nt(pieces, w_ref[place])
+                target[0, :, columns_of(me_ref, place, rows)] = term.astype(bf16)
 
 
 def project_grad_kernel(
@@ -700,10 +761,7 @@
     x2,
     x3,
     gain_ref,
-    w0,
-    w1,
-    w2,
-    w3,
+    w_ref,
     two_ref,
     three_ref,
     four_ref,
@@ -735,12 +793,12 @@
 
     @pl.when(step == pl.num_programs(0) - 1)
     def _():
-        rows, columns = w0.shape
+        rows, columns = w_ref.shape[1:]
         refs = (keep_ref, late_ref, early_ref)
         spread_rows(me_ref, total, refs, slice(0, columns))
-        for place, w in enumerate((w0, w1, w2, w3)):
+        for place in range(PLACES):
             where = columns_of(me_ref, place, rows)
-            product = total[where, :] * w[...].astype(f32)
+            product = total[where, :] * w_ref[place].astype(f32)
             lanes_scr[where, :] = sum(
                 product[:, first : first + HEAD] for first in range(0, columns, HEAD)
             )
@@ -1257,21 +1315,28 @@
     )
 
     x_across = y_swap(x_own)
-    qkv_split = pl.pallas_call(
+    qkv_block, qkv_half, mix_half = (rows, 3 * part), (rows, 3 * part // 2), (part, width // 2)
+    split_shapes = [qkv_block, qkv_block, qkv_half, qkv_half, mix_half]
+    qkv_own, qkv_beside, qkv_far, qkv_corner, w_out_sent = pl.pallas_call(
         split_qkv_kernel,
         name="split_qkv",
         cost_estimate=cost(2),
         grid=(1,),
-        in_specs=[SMEM] + [whole((rows, width))] * 3,
-        out_specs=[whole((rows, 3 * part))] * 4,
-        out_shape=[shaped(rows, 3 * part)] * 4,
-        compiler_params=params(16),
-    )(me, w_query, w_key, w_value)
+        in_specs=[SMEM] + [whole((rows, width))] * 3 + [whole((part, width))],
+        out_specs=[whole(shape) for shape in split_shapes],
+        out_shape=[shaped(*shape) for shape in split_shapes],
+        scratch_shapes=[pltpu.VMEM(qkv_block, bf16)],
+        compiler_params=params(58),
+    )(me, w_query, w_key, w_value, w_out)
+    qkv_far = y_swap(qkv_far)
+    qkv_corner = lax.ppermute(qkv_corner, "fsdp", [(i, i ^ 3) for i in range(4)])
     w_qkv = [
-        qkv_split[0],
-        core_swap(qkv_split[1]),
-        y_swap(qkv_split[2]),
-        y_swap(core_swap(qkv_split[3])),
+        qkv_own,
+        core_swap(qkv_beside),
+        qkv_far,
+        ctx_swap(qkv_far, 1),
+        qkv_corner,
+        ctx_swap(qkv_corner, 1),
     ]
     x_beside = core_swap(x_own)
     x_all = [x_own, x_beside, x_across, core_swap(x_across)]
@@ -1301,36 +1366,34 @@
         [first_position(my_chunk * rows, prompt_of), first_position(starts, pair_prompt)]
     )
     cos_tables, sin_tables = rope_tables(bases, rows)
-    cos_own, sin_own = cos_tables[:PLACES], sin_tables[:PLACES]
-    cos_all, sin_all = cos_tables[PLACES:], sin_tables[PLACES:]
-    w_qkv = after(w_qkv, cos_own, sin_own, cos_all, sin_all)
+    w_qkv = after(w_qkv, cos_tables, sin_tables, info)
 
     ff_blocks, ff_block = (2, rows, 2 * ff_part), (rows, 2 * ff_part)
-    split_shapes = [ff_blocks, ff_block, ff_blocks, ff_block]
-    ff_own, ff_own_sent, ff_beside, ff_beside_sent = pl.pallas_call(
+    split_shapes = [ff_blocks, ff_block, ff_blocks, ff_block] + [(ff_part, width // 2)] * 2
+    ff_own, ff_own_sent, ff_beside, ff_beside_sent, left_sent, right_sent = pl.pallas_call(
         split_ff_kernel,
         name="split_ff",
         cost_estimate=cost(3),
         grid=(1,),
-        in_specs=[SMEM] + [whole(w_gate.shape)] * 2,
+        in_specs=[SMEM] + [whole(w_gate.shape)] * 2 + [whole(w_down.shape)],
         out_specs=[whole(shape) for shape in split_shapes],
         out_shape=[shaped(*shape) for shape in split_shapes],
-        compiler_params=params(20),
-    )(me, w_gate, w_up)
-    half = width // 2
-    w_qkv, x_all, w_out_sent, ff_beside_sent = tie(w_qkv, x_all, w_out, ff_beside_sent)
+        compiler_params=params(58),
+    )(me, w_gate, w_up, w_down)
+    w_qkv, x_all, w_out_sent, ff_beside_sent = tie(w_qkv, x_all, w_out_sent, ff_beside_sent)
     w_ff_beside = core_swap(ff_beside)
     ff_beside_sent = core_swap(ff_beside_sent)
-    w_out_far = y_swap(w_out_sent)
-    far_y = y_swap(after(ff_own_sent, w_out_far))
+    w_out_y = y_swap(w_out_sent)
+    w_out_x = ctx_swap(w_out_y, 1)
+    far_y = y_swap(after(ff_own_sent, w_out_y))
     far_x = ctx_swap(far_y, 1)
     corner_y = y_swap(after(ff_beside_sent, far_y))
     corner_x = ctx_swap(corner_y, 1)
-    down_left = y_swap(after(w_down, corner_y)[:, :half])
-    down_right = y_swap(after(w_down, down_left)[:, half:])
+    down_left = y_swap(after(left_sent, corner_y))
+    down_right = y_swap(after(right_sent, down_left))
 
     piece = (heads, 3, rows, HEAD)
-    qkv = pl.pallas_call(
+    qkv, w_qkv = pl.pallas_call(
         project_kernel,
         name="project",
         cost_estimate=cost(4),
@@ -1338,14 +1401,15 @@
         in_specs=[SMEM]
         + [row_spec] * 4
         + [gain_spec]
-        + [whole((rows, 3 * part))] * 4
+        + [whole(qkv_block)] * 2
+        + [whole(qkv_half)] * 4
         + [pl.BlockSpec((1, rows, HEAD), lambda t: (t, 0, 0))] * 2,
-        out_specs=pl.BlockSpec(piece, lambda t: (t, 0, 0, 0)),
-        out_shape=shaped(PLACES * heads, 3, rows, HEAD),
+        out_specs=[pl.BlockSpec(piece, lambda t: (t, 0, 0, 0)), whole((PLACES,) + qkv_block)],
+        out_shape=[shaped(PLACES * heads, 3, rows, HEAD), shaped(PLACES, *qkv_block)],
         scratch_shapes=[pltpu.VMEM((rows, width), bf16)] * 2,
-        compiler_params=params(16, "arbitrary"),
-    )(me, *x_all, gain_one, *w_qkv, cos_own, sin_own)
-    qkv = lax.all_to_all(after(qkv, w_out_far), "ctx", 0, 0, tiled=True)
+        compiler_params=params(58, "arbitrary"),
+    )(me, *x_all, gain_one, *w_qkv, cos_tables, sin_tables)
+    qkv = lax.all_to_all(after(qkv, w_out_y), "ctx", 0, 0, tiled=True)
     qkv = after(qkv, far_x, corner_y)
 
     qkv_shape, head_shape = (ctx_size, 3, rows, HEAD), (ctx_size, rows, HEAD)
@@ -1365,25 +1429,25 @@
             shaped(*head_shape, kind=f32),
             shaped(*lse_shape, kind=f32),
         ],
-        compiler_params=params(16, "arbitrary"),
+        compiler_params=params(58, "arbitrary"),
     )(info, qkv)
     mixed = after(mixed, corner_x, down_left)
     attended = lax.all_to_all(mixed, "ctx", 0, 0, tiled=True)
-    attended = after(attended, down_right)
+    attended = after(attended, down_right, w_out_x)
     attended_far = y_swap(attended[2 * heads :])
 
     two_heads = (2 * heads, rows, HEAD)
-    mix_specs = [whole((part, width))] * 2
+    mix_specs = [whole((part, width))] + [whole(mix_half)] * 2
     keep, send = pl.pallas_call(
         mix_out_kernel,
         name="mix_out",
         cost_estimate=cost(2),
         grid=(1,),
-        in_specs=[whole((PLACES * heads, rows, HEAD)), whole(two_heads)] + mix_specs,
+        in_specs=[SMEM, whole((PLACES * heads, rows, HEAD)), whole(two_heads)] + mix_specs,
         out_specs=[row_spec] * 2,
         out_shape=[full_row, low_row],
         compiler_params=params(10),
-    )(attended, attended_far, w_out, w_out_far)
+    )(me, attended, attended_far, w_out, w_out_y, w_out_x)
 
     branch, middle, ff_input = pl.pallas_call(
         middle_kernel,
@@ -1486,11 +1550,11 @@
         name="heads_back",
         cost_estimate=cost(2),
         grid=(1,),
-        in_specs=[row_spec] * 2 + mix_specs,
+        in_specs=[SMEM] + [row_spec] * 2 + mix_specs,
         out_specs=[whole(two_heads)] * 2,
         out_shape=[shaped(*two_heads)] * 2,
         compiler_params=params(10),
-    )(branch_grad, branch_grad_beside, w_out, w_out_far)
+    )(me, branch_grad, branch_grad_beside, w_out, w_out_y, w_out_x)
     heads_far = y_swap(heads_far)
     ff_input_far, ff_grad_far = after((ff_input_far, ff_grad_far), heads_near)
     branch_grad_across = y_swap(branch_grad)
@@ -1529,12 +1593,15 @@
             )
         ],
     )
+    heads_far = after(heads_far, pair_keep)
     attended_grad = lax.all_to_all(
         jnp.concatenate([heads_near, heads_far]), "ctx", 0, 0, tiled=True
     )
     branch_grad_far = [branch_grad_across, core_swap(branch_grad_across)]
     pair_over, pair_first = over_x(pair_late, pair_early)
-    attended_grad = after(attended_grad, pair_keep)
+    pair_run = low_sum(pair_keep[3], pair_over[3])
+    pair_came = z_shift(pair_run)
+    attended_grad = after(attended_grad, pair_run)
 
     pieces = pl.pallas_call(
         functools.partial(attend_back_kernel, *block_counts),
@@ -1547,14 +1614,14 @@
             whole(head_shape),
             whole(head_shape),
             whole(lse_shape),
-            whole(head_shape),
-            whole(head_shape),
+            whole(cos_tables.shape),
+            whole(sin_tables.shape),
         ],
         out_specs=whole(qkv_shape),
         out_shape=shaped(*qkv_shape),
         scratch_shapes=[pltpu.VMEM(block_shape, f32)] * 2,
-        compiler_params=params(20, "arbitrary"),
-    )(info, qkv, attended_grad, exact, log_total, cos_all, sin_all)
+        compiler_params=params(58, "arbitrary"),
+    )(info, qkv, attended_grad, exact, log_total, cos_tables, sin_tables)
     hidden, hidden_far = after((hidden, hidden_far), pieces)
     down_keep, down_late, down_early = weight_grads(
         me,
@@ -1565,7 +1632,7 @@
             ([branch_grad, branch_grad_beside, *branch_grad_far], [attended], part, True),
         ],
     )
-    pieces = lax.all_to_all(after(pieces, pair_first), "ctx", 0, 0, tiled=True)
+    pieces = lax.all_to_all(after(pieces, pair_came), "ctx", 0, 0, tiled=True)
     pieces = after(pieces, down_keep)
 
     piece_spec = pl.BlockSpec(piece, lambda t: (t, 0, 0, 0))
@@ -1577,8 +1644,7 @@
         grid=(PLACES,),
         in_specs=[SMEM, piece_spec]
         + [row_spec] * 4
-        + [gain_spec]
-        + [whole((rows, 3 * part))] * 4
+        + [gain_spec, whole((PLACES,) + qkv_block)]
         + [gain_spec] * 3,
         out_specs=[whole(shape) for shape in qkv_pieces],
         out_shape=[shaped(*shape) for shape in qkv_pieces],
@@ -1589,7 +1655,7 @@
             pltpu.VMEM((8, width), f32),
         ],
         compiler_params=params(20, "arbitrary"),
-    )(me, pieces, *x_all, gain_one, *w_qkv, part_two, part_three, part_four)
+    )(me, pieces, *x_all, gain_one, w_qkv, part_two, part_three, part_four)
     qkv_over, _ = over_x(qkv_late, qkv_early)
     pieces = after(pieces, qkv_keep)
 
@@ -1599,11 +1665,11 @@
         name="project_back",
         cost_estimate=cost(5),
         grid=(PLACES,),
-        in_specs=[SMEM, piece_spec] + [whole((rows, 3 * part))] * 4,
+        in_specs=[SMEM, piece_spec, whole((PLACES,) + qkv_block)],
         out_specs=[pair_rows, pair_rows],
         out_shape=[shaped(2, rows, width)] * 2,
         compiler_params=params(12, "arbitrary"),
-    )(me, pieces, *w_qkv)
+    )(me, pieces, w_qkv)
 
     received = core_swap(send)
     onward = (keep[1].astype(f32) + received[1].astype(f32)).astype(bf16)
@@ -1623,9 +1689,9 @@
     def shared_rows(piece):
         return lax.all_to_all(piece, "fsdp", 0, 0, tiled=True)
 
+    pair_came = after(pair_came, pieces)
+    pair_came = z_shift(low_sum(pair_keep[2], pair_over[2], pair_came))
     pair_over = after(pair_over, pieces)
-    pair_came = z_shift(low_sum(pair_keep[3], pair_over[3]))
-    pair_came = z_shift(low_sum(pair_keep[2], pair_over[2], pair_came))
     pair_came = z_shift(low_sum(pair_keep[1], pair_over[1], pair_came))
     pair_piece = shared_rows(low_sum(pair_keep[0], pair_over[0], pair_came))
     down_over, _ = over_x(down_late, after(down_early, pair_over))

time: 454 us -> 439 us (0.967)
  local copies, waits for them, and re-layouts: 47.5 us -> 27.4 us
  waiting for transfers between devices: 209 us -> 193 us
  Pallas kernels: 93.4 us -> 107 us
  other arithmetic: 14.9 us -> 21.8 us
    ppermute x14 -> x13, waiting for transfers between devices: 90.6 us -> 57.4 us  [y_swap(): return lax.ppermute(values, 'fsdp', [(i, i ^ 2) for i in range(4)])]
    ppermute x20 -> x23, waiting for transfers between devices: 41 us -> 58.3 us  [ctx_swap(): return lax.ppermute(values, 'ctx', [(i, i ^ bit) for i in range(size)])]
    unnamed x212 -> x140, local copies, waits for them, and re-layouts: 39.8 us -> 24.5 us
    convert_element_type x12, other arithmetic: 8.47 us -> 14.1 us  [low_sum(): return sum((term.astype(f32) for term in terms)).astype(bf16)]
    all_to_all x2, waiting for transfers between devices: 1.65 us -> 6.35 us  [the longest x1 6.35 us: pair_shards(): pieces = lax.all_to_all(after(pieces, pair_came), 'ctx', 0, 0, tiled=True)]
    ppermute x16 -> x15, waiting for transfers between devices: 11 us -> 9.8 us  [core_swap(): return lax.ppermute(values, 'fsdp', [(i, i ^ 1) for i in range(4)])]
    ppermute x20 -> x23, starting transfers between devices: 21.9 us -> 22.9 us  [ctx_swap(): return lax.ppermute(values, 'ctx', [(i, i ^ bit) for i in range(size)])]
    ppermute x14 -> x13, starting transfers between devices: 16.3 us -> 16.3 us  [y_swap(): return lax.ppermute(values, 'fsdp', [(i, i ^ 2) for i in range(4)])]
  transfers between devices with their start and end apart: 74 -> 76, of which waited for: 45 -> 47; matrix products, arithmetic and copies ran while one was open for 5% -> 6% of each run, Pallas kernels for 18% -> 22%
where the time goes in v4:
time: 439 us; the launch traced here: 431 us
  waiting for transfers between devices  193 us (44%)
  Pallas kernels  107 us (24%)
  starting transfers between devices  80.1 us (18%)
  local copies, waits for them, and re-layouts  27.4 us (6%)
  other arithmetic  21.8 us (5%)
    ppermute x18, waiting for transfers between devices, z_shift(): lax.ppermute(values, 'ctx', [(i, (i + 2) % size) for i in range(size)])  60.1 us
    ppermute x23, waiting for transfers between devices, ctx_swap(): return lax.ppermute(values, 'ctx', [(i, i ^ bit) for i in range(size)])  58.3 us
    ppermute x13, waiting for transfers between devices, y_swap(): return lax.ppermute(values, 'fsdp', [(i, i ^ 2) for i in range(4)])  57.4 us
    unnamed x140, local copies, waits for them, and re-layouts  24.5 us
    ppermute x23, starting transfers between devices, ctx_swap(): return lax.ppermute(values, 'ctx', [(i, i ^ bit) for i in range(size)])  22.9 us
    ppermute x13, starting transfers between devices, y_swap(): return lax.ppermute(values, 'fsdp', [(i, i ^ 2) for i in range(4)])  16.3 us
    convert_element_type x12, other arithmetic, low_sum(): return sum((term.astype(f32) for term in terms)).astype(bf16)  14.1 us
    pallas_call x2, Pallas kernels, weight_grads(): pl.pallas_call(functools.partial(weight_grads_kernel, tuple(kinds)), name...  13.8 us
  transfers between devices with their start and end apart: 76, of which 47 were waited for; matrix products, arithmetic and copies ran while one was open for 6% of the time, Pallas kernels for 22%

profile of v4, /device:TPU:0, one launch (start us, length us, event | category | flops | bytes accessed | tf_op | source)
XLA Modules:
  0.0 430.9 jit_solution(14930682106041393009)
XLA Ops:
  0.7 3.0 collective-permute-start.6
  4.3 2.7 split_qkv.1
  11.7 5.4 %split_ff.1 = (bf16[2,256,1408]{2,1,0:T(8,128)(2,1)}, bf16[256,1408]{1,0:T(8,128)(2,1)}, bf16[2,256,1408]{2,1,0:T(8,128)(2,1)}, bf16[256,1408]{1,0:T(8,128)(2,1)...) custom-call(s32[2]{0:T(128)} %pad_add_fusion.me_ref, bf16[256,2816]{1,0:T(8,128)(2,1)} %gate_ref.1, ...), custom_call_target="tpu_custom_call" | custom-call | flops 3000000 | tf_op jit(solution)/shard_map/split_ff/pallas_call | solution.py:1373
  17.2 2.1 add_multiply_fusion
  20.9 2.0 collective-permute-start.2
  27.0 4.1 collective-permute-done.4.corner_x
  33.0 7.0 %project.1 = (bf16[8,3,256,128]{3,2,1,0:T(8,128)(2,1)}, bf16[4,256,768]{2,1,0:T(8,128)(2,1)}) custom-call(s32[2]{0:T(128)} %pad_add_fusion.me_ref, bf16[256,1024]{1,0:T(8,128)(2,1)} %bitcast.71, bf16[256,1024]{1,0:T(8,128)(2,1)} %copy-done.28, bf16[256,1024]{1,0:T(8,128)(2,1)} %copy-done.26, bf16[256,1024]{1,0:T(8,128)(2,1)} %copy-done.30, ...), custom_call_target="tpu_custom_call" | custom-call | flops 4000000 | tf_op jit(solution)/shard_map/project/pallas_call | solution.py:1396
  40.0 6.0 %all-to-all-start = ((bf16[8,3,256,128]{3,2,1,0:T(8,128)(2,1)}), bf16[8,3,256,128]{3,2,1,0:T(8,128)(2,1)}, u32[]{:S(2)}, u32[]{:S(2)}) async-start(bf16[8,3,256,128]{3,2,1,0:T(8,128)(2,1)} %get-tuple-element.151), calls=%async_computation | async-start | bytes 3145728 | tf_op jit(solution)/shard_map/all_to_all | solution.py:1412
  48.2 16.4 %collective-permute-done.9.refs_2_ = bf16[256,1408]{1,0:T(8,128)(2,1)S(1)} collective-permute-done((bf16[256,1408]{1,0:T(8,128)(2,1)S(1)}, bf16[256,1408]{1,0:T(8,128)(2,1)S(1)}, u32[]{:S(2)}, u32[]{:S(2)}) %collective-permute-start.9) | collective-permute-done | bytes 720928 | tf_op jit(solution)/shard_map/ppermute | solution.py:392
  65.8 2.0 collective-permute-start.10
  67.8 14.6 %collective-permute-done.12.refs_4_ = bf16[256,1408]{1,0:T(8,128)(2,1)S(1)} collective-permute-done((bf16[256,1408]{1,0:T(8,128)(2,1)S(1)}, bf16[256,1408]{1,0:T(8,128)(2,1)S(1)}, u32[]{:S(2)}, u32[]{:S(2)}) %collective-permute-start.12) | collective-permute-done | bytes 720928 | tf_op jit(solution)/shard_map/ppermute | solution.py:392
  83.6 1.9 collective-permute-start.13
  85.5 2.1 collective-permute-done.10.refs_3_
  88.4 9.3 %attend.1 = (bf16[8,256,128]{2,1,0:T(8,128)(2,1)}, f32[8,256,128]{2,1,0:T(8,128)}, f32[4,1,512]{2,1,0:T(1,128)}) custom-call(s32[3]{0:T(128)} %pad_add_fusion.1.info_ref, bf16[8,3,256,128]{3,2,1,0:T(8,128)(2,1)} %all-to-all-done.qkv_ref), custom_call_target="tpu_custom_call" | custom-call | flops 9000000 | tf_op jit(solution)/shard_map/attend/pallas_call | solution.py:1420
  97.8 1.9 collective-permute-done.14.refs_7_
  102.3 7.0 %all-to-all-start.1 = ((bf16[8,256,128]{2,1,0:T(8,128)(2,1)}), bf16[8,256,128]{2,1,0:T(8,128)(2,1)}, u32[]{:S(2)}, u32[]{:S(2)}) async-start(bf16[8,256,128]{2,1,0:T(8,128)(2,1)} %get-tuple-element.160), calls=%async_computation.1 | async-start | bytes 1048576 | tf_op jit(solution)/shard_map/all_to_all | solution.py:1435
  110.2 2.0 collective-permute-start.16
  112.2 9.3 %collective-permute-done.16.w_x_ref = bf16[256,512]{1,0:T(8,128)(2,1)S(1)} collective-permute-done((bf16[256,512]{1,0:T(8,128)(2,1)}, bf16[256,512]{1,0:T(8,128)(2,1)S(1)}, u32[]{:S(2)}, u32[]{:S(2)}) %collective-permute-start.16) | collective-permute-done | bytes 262176 | tf_op jit(solution)/shard_map/ppermute | solution.py:397
  122.2 3.7 collective-permute-done.15.refs_8_
  128.7 5.5 %collective-permute-done.17.far_ref = bf16[4,256,128]{2,1,0:T(8,128)(2,1)S(1)} collective-permute-done((bf16[4,256,128]{2,1,0:T(8,128)(2,1)S(1)}, bf16[4,256,128]{2,1,0:T(8,128)(2,1)S(1)}, u32[]{:S(2)}, u32[]{:S(2)}) %collective-permute-start.17) | collective-permute-done | bytes 262176 | tf_op jit(solution)/shard_map/ppermute | solution.py:392
  136.3 1.8 mix_out.1
  138.2 1.9 collective-permute-done.18.received_ref
  144.8 10.1 %ff.1 = (f32[256,1024]{1,0:T(8,128)S(1)}, bf16[256,1024]{1,0:T(8,128)(2,1)S(1)}, bf16[2,512,1408]{2,1,0:T(8,128)(2,1)}, bf16[2,256,768]{2,1,0:T(8,128)(2,1)S(1)}) custom-call(s32[2]{0:T(128)S(1)} %copy-done.46, bf16[256,1024]{1,0:T(8,128)(2,1)S(1)} %get-tuple-element.166.own_ref.refs_0_, bf16[256,1024]{1,0:T(8,128)(2,1)S(1)} %collective-permute-done.19.beside_ref.refs_1_, ...), custom_call_target="tpu_custom_call" | custom-call | flops 9000000 | tf_op jit(solution)/shard_map/ff/pallas_call | solution.py:1494
  161.0 11.3 %ff_back.1 = (f32[256,1024]{1,0:T(8,128)S(1)}, bf16[256,1024]{1,0:T(8,128)(2,1)S(1)}, bf16[2,256,1408]{2,1,0:T(8,128)(2,1)S(1)}) custom-call(s32[2]{0:T(128)S(1)} %copy-done.46, bf16[256,1024]{1,0:T(8,128)(2,1)S(1)} %get-tuple-element.174.own_ref.refs_0_, bf16[256,1024]{1,0:T(8,128)(2,1)S(1)} %collective-permute-done.23.beside_ref.refs_1_, ...), custom_call_target="tpu_custom_call" | custom-call | flops 9000000 | tf_op jit(solution)/shard_map/ff_back/pallas_call | solution.py:1526
  173.4 1.9 collective-permute-done.25.received_ref
  178.4 1.9 heads_back.1
  181.2 3.9 ff_far.1
  186.0 2.7 collective-permute-done.27
  188.7 6.7 %pair_grads.1 = (bf16[4,4,32,1408]{3,2,1,0:T(8,128)(2,1)S(1)}, bf16[2,4,32,1408]{3,2,1,0:T(8,128)(2,1)S(1)}, bf16[2,4,32,1408]{3,2,1,0:T(8,128)(2,1)S(1)}) custom-call(s32[2]{0:T(128)S(1)} %copy-done.46, bf16[256,1024]{1,0:T(8,128)(2,1)S(1)} %get-tuple-element.166.own_ref.refs_0_, bf16[256,1024]{1,0:T(8,128)(2,1)S(1)} %collective-permute-done.19.beside_ref.refs_1_, ...), custom_call_target="tpu_custom_call" | custom-call | flops 7000000 | tf_op jit(solution)/shard_map/pair_grads/pallas_call | solution.py:1163
  198.8 4.5 %all-to-all-start.2 = ((bf16[8,256,128]{2,1,0:T(8,128)(2,1)}), bf16[8,256,128]{2,1,0:T(8,128)(2,1)S(1)}, u32[]{:S(2)}, u32[]{:S(2)}) async-start(bf16[8,256,128]{2,1,0:T(8,128)(2,1)} %pad_maximum_fusion), calls=%async_computation.2 | async-start | bytes 1048576 | tf_op jit(solution)/shard_map/all_to_all | solution.py:1597
  203.4 15.2 %collective-permute-done.30 = bf16[2,4,32,1408]{3,2,1,0:T(8,128)(2,1)} collective-permute-done((bf16[2,4,32,1408]{3,2,1,0:T(8,128)(2,1)S(1)}, bf16[2,4,32,1408]{3,2,1,0:T(8,128)(2,1)}, u32[]{:S(2)}, u32[]{:S(2)}) %collective-permute-start.30) | collective-permute-done | bytes 720928 | tf_op jit(solution)/shard_map/ppermute | solution.py:397
  222.3 13.2 %attend_back.1 = bf16[8,3,256,128]{3,2,1,0:T(8,128)(2,1)} custom-call(s32[3]{0:T(128)} %pad_add_fusion.1.info_ref, bf16[8,3,256,128]{3,2,1,0:T(8,128)(2,1)} %all-to-all-done.qkv_ref, bf16[8,256,128]{2,1,0:T(8,128)(2,1)} %copy-done.54, f32[8,256,128]{2,1,0:T(8,128)} %get-tuple-element.194.exact_ref, f32[4,1,512]{2,1,0:T(1,128)} %get-tuple-element.195.lse_ref, ...), custom_call_target="tpu_custom_call" | custom-call | flops 11000000 | tf_op jit(solution)/shard_map/attend_back/pallas_call | solution.py:1606
  236.3 4.8 %all-to-all-start.3 = ((bf16[8,3,256,128]{3,2,1,0:T(8,128)(2,1)}), bf16[8,3,256,128]{3,2,1,0:T(8,128)(2,1)S(1)}, u32[]{:S(2)}, u32[]{:S(2)}) async-start(bf16[8,3,256,128]{3,2,1,0:T(8,128)(2,1)} %attend_back.1), calls=%async_computation.3 | async-start | bytes 3145728 | tf_op jit(solution)/shard_map/all_to_all | solution.py:1635
  242.0 10.3 %collective-permute-done.32.refs_8_ = bf16[256,1024]{1,0:T(8,128)(2,1)S(1)} collective-permute-done((bf16[256,1024]{1,0:T(8,128)(2,1)}, bf16[256,1024]{1,0:T(8,128)(2,1)S(1)}, u32[]{:S(2)}, u32[]{:S(2)}) %collective-permute-start.32) | collective-permute-done | bytes 524320 | tf_op jit(solution)/shard_map/ppermute | solution.py:392
  260.7 7.1 %down_grads.1 = (bf16[4,4,32,960]{3,2,1,0:T(8,128)(2,1)S(1)}, bf16[2,4,32,960]{3,2,1,0:T(8,128)(2,1)}, bf16[2,4,32,960]{3,2,1,0:T(8,128)(2,1)S(1)}) custom-call(s32[2]{0:T(128)S(1)} %copy-done.46, bf16[256,1024]{1,0:T(8,128)(2,1)S(1)} %copy-done.15, bf16[256,1024]{1,0:T(8,128)(2,1)S(1)} %copy-done.17, bf16[256,1024]{1,0:T(8,128)(2,1)S(1)} %copy-done.19, ...), custom_call_target="tpu_custom_call" | custom-call | flops 8000000 | tf_op jit(solution)/shard_map/down_grads/pallas_call | solution.py:1163
  269.6 6.3 %all-to-all-done.3.pieces_ref = bf16[8,3,256,128]{3,2,1,0:T(8,128)(2,1)S(1)} async-done(((bf16[8,3,256,128]{3,2,1,0:T(8,128)(2,1)}), bf16[8,3,256,128]{3,2,1,0:T(8,128)(2,1)S(1)}, u32[]{:S(2)}, u32[]{:S(2)}) %all-to-all-start.3) | async-done | bytes 1572896 | tf_op jit(solution)/shard_map/all_to_all | solution.py:1635
  280.4 6.6 %project_grad.1 = (bf16[4,4,32,896]{3,2,1,0:T(8,128)(2,1)S(1)}, bf16[2,4,32,896]{3,2,1,0:T(8,128)(2,1)}, bf16[2,4,32,896]{3,2,1,0:T(8,128)(2,1)S(1)}) custom-call(s32[2]{0:T(128)S(1)} %copy-done.46, bf16[8,3,256,128]{3,2,1,0:T(8,128)(2,1)S(1)} %all-to-all-done.3.pieces_ref, bf16[256,1024]{1,0:T(8,128)(2,1)S(1)} %bitcast.73, ...), custom_call_target="tpu_custom_call" | custom-call | flops 5000000 | tf_op jit(solution)/shard_map/project_grad/pallas_call | solution.py:1640
  291.9 4.1 project_back.1
  298.0 13.4 %collective-permute-done.36 = bf16[2,4,32,896]{3,2,1,0:T(8,128)(2,1)S(1)} collective-permute-done((bf16[2,4,32,896]{3,2,1,0:T(8,128)(2,1)S(1)}, bf16[2,4,32,896]{3,2,1,0:T(8,128)(2,1)S(1)}, u32[]{:S(2)}, u32[]{:S(2)}) %collective-permute-start.36) | collective-permute-done | bytes 458784 | tf_op jit(solution)/shard_map/ppermute | solution.py:397
  315.7 5.5 %collective-permute-done.38 = bf16[4,32,896]{2,1,0:T(8,128)(2,1)S(1)} collective-permute-done((bf16[4,32,896]{2,1,0:T(8,128)(2,1)S(1)}, bf16[4,32,896]{2,1,0:T(8,128)(2,1)S(1)}, u32[]{:S(2)}, u32[]{:S(2)}) %collective-permute-start.38) | collective-permute-done | bytes 229408 | tf_op jit(solution)/shard_map/ppermute | solution.py:402
  321.9 2.1 collective-permute-start.39
  324.9 3.5 all-to-all-start.5
  332.5 1.8 fusion.12
  335.0 7.4 %collective-permute-done.52 = bf16[4,32,960]{2,1,0:T(8,128)(2,1)S(1)} collective-permute-done((bf16[4,32,960]{2,1,0:T(8,128)(2,1)S(1)}, bf16[4,32,960]{2,1,0:T(8,128)(2,1)S(1)}, u32[]{:S(2)}, u32[]{:S(2)}) %collective-permute-start.52) | collective-permute-done | bytes 245792 | tf_op jit(solution)/shard_map/ppermute | solution.py:402
  342.4 1.9 fusion.9
  345.7 1.8 fusion.13
  347.5 3.4 all-to-all-start.4
  350.9 3.7 collective-permute-done.53
  356.6 3.2 collective-permute-done.63.refs_1_
  360.4 6.7 %collective-permute-done.54.refs_1_ = bf16[4,32,960]{2,1,0:T(8,128)(2,1)} collective-permute-done((bf16[4,32,960]{2,1,0:T(8,128)(2,1)S(1)}, bf16[4,32,960]{2,1,0:T(8,128)(2,1)}, u32[]{:S(2)}, u32[]{:S(2)}) %collective-permute-start.54) | collective-permute-done | bytes 245792 | tf_op jit(solution)/shard_map/ppermute | solution.py:402
  367.3 4.7 %collective-permute-done.41.refs_1_ = bf16[4,32,896]{2,1,0:T(8,128)(2,1)S(1)} collective-permute-done((bf16[4,32,896]{2,1,0:T(8,128)(2,1)S(1)}, bf16[4,32,896]{2,1,0:T(8,128)(2,1)S(1)}, u32[]{:S(2)}, u32[]{:S(2)}) %collective-permute-start.41) | collective-permute-done | bytes 229408 | tf_op jit(solution)/shard_map/ppermute | solution.py:402
  372.1 3.6 collective-permute-done.42.refs_4_
  375.8 6.5 %collective-permute-done.56.refs_2_ = bf16[4,32,960]{2,1,0:T(8,128)(2,1)S(1)} collective-permute-done((bf16[4,32,960]{2,1,0:T(8,128)(2,1)}, bf16[4,32,960]{2,1,0:T(8,128)(2,1)S(1)}, u32[]{:S(2)}, u32[]{:S(2)}) %collective-permute-start.56) | collective-permute-done | bytes 245792 | tf_op jit(solution)/shard_map/ppermute | solution.py:402
  382.7 2.1 collective-permute-start.58
  386.4 2.5 collective-permute-start.35
  388.9 3.6 collective-permute-done.43.refs_2_
  393.0 5.1 %collective-permute-done.58.refs_3_ = bf16[4,32,960]{2,1,0:T(8,128)(2,1)S(1)} collective-permute-done((bf16[4,32,960]{2,1,0:T(8,128)(2,1)S(1)}, bf16[4,32,960]{2,1,0:T(8,128)(2,1)S(1)}, u32[]{:S(2)}, u32[]{:S(2)}) %collective-permute-start.58) | collective-permute-done | bytes 245792 | tf_op jit(solution)/shard_map/ppermute | solution.py:402
  399.0 8.0 %collective-permute-done.45.refs_3_ = bf16[4,32,896]{2,1,0:T(8,128)(2,1)S(1)} collective-permute-done((bf16[4,32,896]{2,1,0:T(8,128)(2,1)S(1)}, bf16[4,32,896]{2,1,0:T(8,128)(2,1)S(1)}, u32[]{:S(2)}, u32[]{:S(2)}) %collective-permute-start.45) | collective-permute-done | bytes 229408 | tf_op jit(solution)/shard_map/ppermute | solution.py:402
  409.6 2.0 collective-permute-start.69
  413.1 3.1 collective-permute-done.60.refs_7_
  416.2 4.5 %settle_turned.1 = (f32[704,1024]{1,0:T(8,128)}, f32[256,1024]{1,0:T(8,128)}) custom-call(s32[2]{0:T(128)S(1)} %copy-done.46, bf16[4,32,960]{2,1,0:T(8,128)(2,1)S(1)} %fusion.10.refs_0_, bf16[4,32,960]{2,1,0:T(8,128)(2,1)} %collective-permute-done.54.refs_1_, bf16[4,32,960]{2,1,0:T(8,128)(2,1)S(1)} %collective-permute-done.56.refs_2_, ...), custom_call_target="tpu_custom_call" | custom-call | flops 4000000 | tf_op jit(solution)/shard_map/settle_turned/pallas_call | solution.py:1243
  421.1 2.4 settle_qkv.1
  424.2 2.0 collective-permute-done.69.refs_7_
  426.2 4.2 settle_pair.1
  (290 shorter events, 97.8 us)
Async XLA Ops:
  0.7 18.6 %collective-permute-start.6 = (bf16[256,1024]{1,0:T(8,128)(2,1)}, bf16[256,1024]{1,0:T(8,128)(2,1)S(1)}, u32[]{:S(2)}, u32[]{:S(2)}) collective-permute-start(bf16[256,1024]{1,0:T(8,128)(2,1)} %bitcast.69), channel_id=1, source_target_pairs={{0,2},{1,3},{2,0},{3,1},{4,6},{5,7},{6,4},{7,5},{8,10},{9,11},{10,... | collective-permute-start | bytes 1572872 | tf_op jit(solution)/shard_map/ppermute | solution.py:392
  3.7 27.4 %collective-permute-start.5 = (bf16[256,1024]{1,0:T(8,128)(2,1)}, bf16[256,1024]{1,0:T(8,128)(2,1)S(1)}, u32[]{:S(2)}, u32[]{:S(2)}) collective-permute-start(bf16[256,1024]{1,0:T(8,128)(2,1)} %bitcast.70), channel_id=1, source_target_pairs={{0,1},{1,0},{2,3},{3,2},{4,5},{5,4},{6,7},{7,6},{8,9},{9,8},{10,11... | collective-permute-start | bytes 1572872 | tf_op jit(solution)/shard_map/ppermute | solution.py:388
  7.0 13.9 %collective-permute-start.1 = (bf16[256,384]{1,0:T(8,128)(2,1)}, bf16[256,384]{1,0:T(8,128)(2,1)S(1)}, u32[]{:S(2)}, u32[]{:S(2)}) collective-permute-start(bf16[256,384]{1,0:T(8,128)(2,1)} %get-tuple-element.129), channel_id=1, source_target_pairs={{0,2},{1,3},{2,0},{3,1},{4,6},{5,7},{6,4},{7,5},{8,10},{9,11},{10,... | collective-permute-start | bytes 589832 | tf_op jit(solution)/shard_map/ppermute | solution.py:392
  7.1 16.6 %collective-permute-start.3 = (bf16[256,384]{1,0:T(8,128)(2,1)}, bf16[256,384]{1,0:T(8,128)(2,1)S(1)}, u32[]{:S(2)}, u32[]{:S(2)}) collective-permute-start(bf16[256,384]{1,0:T(8,128)(2,1)} %get-tuple-element.130), channel_id=1, source_target_pairs={{0,3},{1,2},{2,1},{3,0},{4,7},{5,6},{6,5},{7,4},{8,11},{9,10},{10,... | collective-permute-start | bytes 589832 | tf_op jit(solution)/shard_map/ppermute | solution.py:1332
  8.8 22.3 %collective-permute-start = (bf16[256,768]{1,0:T(8,128)(2,1)}, bf16[256,768]{1,0:T(8,128)(2,1)S(1)}, u32[]{:S(2)}, u32[]{:S(2)}) collective-permute-start(bf16[256,768]{1,0:T(8,128)(2,1)} %get-tuple-element.128), channel_id=1, source_target_pairs={{0,1},{1,0},{2,3},{3,2},{4,5},{5,4},{6,7},{7,6},{8,9},{9,8},{10,11... | collective-permute-start | bytes 1179656 | tf_op jit(solution)/shard_map/ppermute | solution.py:388
  19.3 11.8 %collective-permute-start.7 = (bf16[256,1024]{1,0:T(8,128)(2,1)S(1)}, bf16[256,1024]{1,0:T(8,128)(2,1)S(1)}, u32[]{:S(2)}, u32[]{:S(2)}) collective-permute-start(bf16[256,1024]{1,0:T(8,128)(2,1)S(1)} %collective-permute-done.6.x2), channel_id=1, source_target_pairs={{0,1},{1,0},{2,3},{3,2},{4,5},{5,4},{6,7},{7,6},{8,9},{9,8},{10,11... | collective-permute-start | bytes 1572872 | tf_op jit(solution)/shard_map/ppermute | solution.py:388
  23.6 7.5 %collective-permute-start.4 = (bf16[256,384]{1,0:T(8,128)(2,1)S(1)}, bf16[256,384]{1,0:T(8,128)(2,1)S(1)}, u32[]{:S(2)}, u32[]{:S(2)}) collective-permute-start(bf16[256,384]{1,0:T(8,128)(2,1)S(1)} %collective-permute-done.3.corner_y), channel_id=1, source_target_pairs={{0,4},{4,0},{8,12},{12,8},{16,20},{20,16},{24,28},{28,24},{1,5},{5... | collective-permute-start | bytes 589832 | tf_op jit(solution)/shard_map/ppermute | solution.py:397
  31.1 8.9 %collective-permute-start.8 = (bf16[256,512]{1,0:T(8,128)(2,1)S(1)}, bf16[256,512]{1,0:T(8,128)(2,1)}, u32[]{:S(2)}, u32[]{:S(2)}) collective-permute-start(bf16[256,512]{1,0:T(8,128)(2,1)S(1)} %copy-done.67), channel_id=1, source_target_pairs={{0,2},{1,3},{2,0},{3,1},{4,6},{5,7},{6,4},{7,5},{8,10},{9,11},{10,... | collective-permute-start | bytes 786440 | tf_op jit(solution)/shard_map/ppermute | solution.py:392
  40.0 48.4 %all-to-all-start = ((bf16[8,3,256,128]{3,2,1,0:T(8,128)(2,1)}), bf16[8,3,256,128]{3,2,1,0:T(8,128)(2,1)}, u32[]{:S(2)}, u32[]{:S(2)}) async-start(bf16[8,3,256,128]{3,2,1,0:T(8,128)(2,1)} %get-tuple-element.151), calls=%async_computation | async-start | bytes 3145728 | tf_op jit(solution)/shard_map/all_to_all | solution.py:1412
  46.1 18.5 %collective-permute-start.9 = (bf16[256,1408]{1,0:T(8,128)(2,1)S(1)}, bf16[256,1408]{1,0:T(8,128)(2,1)S(1)}, u32[]{:S(2)}, u32[]{:S(2)}) collective-permute-start(bf16[256,1408]{1,0:T(8,128)(2,1)S(1)} %copy-done.65), channel_id=1, source_target_pairs={{0,2},{1,3},{2,0},{3,1},{4,6},{5,7},{6,4},{7,5},{8,10},{9,11},{10,... | collective-permute-start | bytes 2162696 | tf_op jit(solution)/shard_map/ppermute | solution.py:392
  64.6 17.8 %collective-permute-start.12 = (bf16[256,1408]{1,0:T(8,128)(2,1)S(1)}, bf16[256,1408]{1,0:T(8,128)(2,1)S(1)}, u32[]{:S(2)}, u32[]{:S(2)}) collective-permute-start(bf16[256,1408]{1,0:T(8,128)(2,1)S(1)} %collective-permute-done.11), channel_id=1, source_target_pairs={{0,2},{1,3},{2,0},{3,1},{4,6},{5,7},{6,4},{7,5},{8,10},{9,11},{10,... | collective-permute-start | bytes 2162696 | tf_op jit(solution)/shard_map/ppermute | solution.py:392
  65.8 21.7 %collective-permute-start.10 = (bf16[256,1408]{1,0:T(8,128)(2,1)S(1)}, bf16[256,1408]{1,0:T(8,128)(2,1)S(1)}, u32[]{:S(2)}, u32[]{:S(2)}) collective-permute-start(bf16[256,1408]{1,0:T(8,128)(2,1)S(1)} %collective-permute-done.9.refs_2_), channel_id=1, source_target_pairs={{0,4},{4,0},{8,12},{12,8},{16,20},{20,16},{24,28},{28,24},{1,5},{5... | collective-permute-start | bytes 2162696 | tf_op jit(solution)/shard_map/ppermute | solution.py:397
  82.4 17.2 %collective-permute-start.14 = (bf16[704,512]{1,0:T(8,128)(2,1)}, bf16[704,512]{1,0:T(8,128)(2,1)S(1)}, u32[]{:S(2)}, u32[]{:S(2)}) collective-permute-start(bf16[704,512]{1,0:T(8,128)(2,1)} %get-tuple-element.159), channel_id=1, source_target_pairs={{0,2},{1,3},{2,0},{3,1},{4,6},{5,7},{6,4},{7,5},{8,10},{9,11},{10,... | collective-permute-start | bytes 2162696 | tf_op jit(solution)/shard_map/ppermute | solution.py:392
  83.6 18.7 %collective-permute-start.13 = (bf16[256,1408]{1,0:T(8,128)(2,1)S(1)}, bf16[256,1408]{1,0:T(8,128)(2,1)S(1)}, u32[]{:S(2)}, u32[]{:S(2)}) collective-permute-start(bf16[256,1408]{1,0:T(8,128)(2,1)S(1)} %collective-permute-done.12.refs_4_), channel_id=1, source_target_pairs={{0,4},{4,0},{8,12},{12,8},{16,20},{20,16},{24,28},{28,24},{1,5},{5... | collective-permute-start | bytes 2162696 | tf_op jit(solution)/shard_map/ppermute | solution.py:397
  102.3 24.5 %all-to-all-start.1 = ((bf16[8,256,128]{2,1,0:T(8,128)(2,1)}), bf16[8,256,128]{2,1,0:T(8,128)(2,1)}, u32[]{:S(2)}, u32[]{:S(2)}) async-start(bf16[8,256,128]{2,1,0:T(8,128)(2,1)} %get-tuple-element.160), calls=%async_computation.1 | async-start | bytes 1048576 | tf_op jit(solution)/shard_map/all_to_all | solution.py:1435
  109.3 16.6 %collective-permute-start.15 = (bf16[704,512]{1,0:T(8,128)(2,1)}, bf16[704,512]{1,0:T(8,128)(2,1)S(1)}, u32[]{:S(2)}, u32[]{:S(2)}) collective-permute-start(bf16[704,512]{1,0:T(8,128)(2,1)} %get-tuple-element.162), channel_id=1, source_target_pairs={{0,2},{1,3},{2,0},{3,1},{4,6},{5,7},{6,4},{7,5},{8,10},{9,11},{10,... | collective-permute-start | bytes 2162696 | tf_op jit(solution)/shard_map/ppermute | solution.py:392
  110.2 11.3 %collective-permute-start.16 = (bf16[256,512]{1,0:T(8,128)(2,1)}, bf16[256,512]{1,0:T(8,128)(2,1)S(1)}, u32[]{:S(2)}, u32[]{:S(2)}) collective-permute-start(bf16[256,512]{1,0:T(8,128)(2,1)} %collective-permute-done.8.w_y_ref), channel_id=1, source_target_pairs={{0,4},{4,0},{8,12},{12,8},{16,20},{20,16},{24,28},{28,24},{1,5},{5... | collective-permute-start | bytes 786440 | tf_op jit(solution)/shard_map/ppermute | solution.py:397
  112.2 29.4 %collective-permute-start.20 = (bf16[2,256,1408]{2,1,0:T(8,128)(2,1)}, bf16[2,256,1408]{2,1,0:T(8,128)(2,1)S(1)}, u32[]{:S(2)}, u32[]{:S(2)}) collective-permute-start(bf16[2,256,1408]{2,1,0:T(8,128)(2,1)} %get-tuple-element.168), channel_id=1, source_target_pairs={{0,1},{1,0},{2,3},{3,2},{4,5},{5,4},{6,7},{7,6},{8,9},{9,8},{10,11... | collective-permute-start | bytes 4325384 | tf_op jit(solution)/shard_map/ppermute | solution.py:388
  140.8 15.1 %collective-permute-start.21 = (bf16[256,1024]{1,0:T(8,128)(2,1)S(1)}, bf16[256,1024]{1,0:T(8,128)(2,1)S(1)}, u32[]{:S(2)}, u32[]{:S(2)}) collective-permute-start(bf16[256,1024]{1,0:T(8,128)(2,1)S(1)} %get-tuple-element.166.own_ref.refs_0_), channel_id=1, source_target_pairs={{0,2},{1,3},{2,0},{3,1},{4,6},{5,7},{6,4},{7,5},{8,10},{9,11},{10,... | collective-permute-start | bytes 1572872 | tf_op jit(solution)/shard_map/ppermute | solution.py:392
  159.2 14.2 %collective-permute-start.24 = (bf16[256,1024]{1,0:T(8,128)(2,1)S(1)}, bf16[256,1024]{1,0:T(8,128)(2,1)S(1)}, u32[]{:S(2)}, u32[]{:S(2)}) collective-permute-start(bf16[256,1024]{1,0:T(8,128)(2,1)S(1)} %get-tuple-element.174.own_ref.refs_0_), channel_id=1, source_target_pairs={{0,2},{1,3},{2,0},{3,1},{4,6},{5,7},{6,4},{7,5},{8,10},{9,11},{10,... | collective-permute-start | bytes 1572872 | tf_op jit(solution)/shard_map/ppermute | solution.py:392
  180.3 8.4 %collective-permute-start.27 = (bf16[4,256,128]{2,1,0:T(8,128)(2,1)S(1)}, bf16[4,256,128]{2,1,0:T(8,128)(2,1)S(1)}, u32[]{:S(2)}, u32[]{:S(2)}) collective-permute-start(bf16[4,256,128]{2,1,0:T(8,128)(2,1)S(1)} %get-tuple-element.182), channel_id=1, source_target_pairs={{0,2},{1,3},{2,0},{3,1},{4,6},{5,7},{6,4},{7,5},{8,10},{9,11},{10,... | collective-permute-start | bytes 786440 | tf_op jit(solution)/shard_map/ppermute | solution.py:392
  196.2 22.4 %collective-permute-start.30 = (bf16[2,4,32,1408]{3,2,1,0:T(8,128)(2,1)S(1)}, bf16[2,4,32,1408]{3,2,1,0:T(8,128)(2,1)}, u32[]{:S(2)}, u32[]{:S(2)}) collective-permute-start(bf16[2,4,32,1408]{3,2,1,0:T(8,128)(2,1)S(1)} %get-tuple-element.192), channel_id=1, source_target_pairs={{0,4},{4,0},{8,12},{12,8},{16,20},{20,16},{24,28},{28,24},{1,5},{5... | collective-permute-start | bytes 2162696 | tf_op jit(solution)/shard_map/ppermute | solution.py:397
  198.8 22.7 %all-to-all-start.2 = ((bf16[8,256,128]{2,1,0:T(8,128)(2,1)}), bf16[8,256,128]{2,1,0:T(8,128)(2,1)S(1)}, u32[]{:S(2)}, u32[]{:S(2)}) async-start(bf16[8,256,128]{2,1,0:T(8,128)(2,1)} %pad_maximum_fusion), calls=%async_computation.2 | async-start | bytes 1048576 | tf_op jit(solution)/shard_map/all_to_all | solution.py:1597
  219.7 15.9 %collective-permute-start.31 = (bf16[4,32,1408]{2,1,0:T(8,128)(2,1)S(1)}, bf16[4,32,1408]{2,1,0:T(8,128)(2,1)S(1)}, u32[]{:S(2)}, u32[]{:S(2)}) collective-permute-start(bf16[4,32,1408]{2,1,0:T(8,128)(2,1)S(1)} %fusion.6), channel_id=1, source_target_pairs={{0,8},{4,12},{8,16},{12,20},{16,24},{20,28},{24,0},{28,4},{1,9},{5... | collective-permute-start | bytes 1081352 | tf_op jit(solution)/shard_map/ppermute | solution.py:402
  236.3 39.6 %all-to-all-start.3 = ((bf16[8,3,256,128]{3,2,1,0:T(8,128)(2,1)}), bf16[8,3,256,128]{3,2,1,0:T(8,128)(2,1)S(1)}, u32[]{:S(2)}, u32[]{:S(2)}) async-start(bf16[8,3,256,128]{3,2,1,0:T(8,128)(2,1)} %attend_back.1), calls=%async_computation.3 | async-start | bytes 3145728 | tf_op jit(solution)/shard_map/all_to_all | solution.py:1635
  241.1 11.2 %collective-permute-start.32 = (bf16[256,1024]{1,0:T(8,128)(2,1)}, bf16[256,1024]{1,0:T(8,128)(2,1)S(1)}, u32[]{:S(2)}, u32[]{:S(2)}) collective-permute-start(bf16[256,1024]{1,0:T(8,128)(2,1)} %copy-done.20), channel_id=1, source_target_pairs={{0,2},{1,3},{2,0},{3,1},{4,6},{5,7},{6,4},{7,5},{8,10},{9,11},{10,... | collective-permute-start | bytes 1572872 | tf_op jit(solution)/shard_map/ppermute | solution.py:392
  252.3 36.3 %collective-permute-start.48 = (bf16[2,4,32,1408]{3,2,1,0:T(8,128)(2,1)}, bf16[2,4,32,1408]{3,2,1,0:T(8,128)(2,1)}, u32[]{:S(2)}, u32[]{:S(2)}) collective-permute-start(bf16[2,4,32,1408]{3,2,1,0:T(8,128)(2,1)} %copy-done.51), channel_id=1, source_target_pairs={{0,4},{4,0},{8,12},{12,8},{16,20},{20,16},{24,28},{28,24},{1,5},{5... | collective-permute-start | bytes 2162696 | tf_op jit(solution)/shard_map/ppermute | solution.py:397
  288.5 9.3 %collective-permute-start.61 = (bf16[4,32,1408]{2,1,0:T(8,128)(2,1)S(1)}, bf16[4,32,1408]{2,1,0:T(8,128)(2,1)S(1)}, u32[]{:S(2)}, u32[]{:S(2)}) collective-permute-start(bf16[4,32,1408]{2,1,0:T(8,128)(2,1)S(1)} %fusion.1), channel_id=1, source_target_pairs={{0,8},{4,12},{8,16},{12,20},{16,24},{20,28},{24,0},{28,4},{1,9},{5... | collective-permute-start | bytes 1081352 | tf_op jit(solution)/shard_map/ppermute | solution.py:402
  289.8 23.8 %collective-permute-start.49 = (bf16[2,4,32,960]{3,2,1,0:T(8,128)(2,1)S(1)}, bf16[2,4,32,960]{3,2,1,0:T(8,128)(2,1)S(1)}, u32[]{:S(2)}, u32[]{:S(2)}) collective-permute-start(bf16[2,4,32,960]{3,2,1,0:T(8,128)(2,1)S(1)} %copy-done.53), channel_id=1, source_target_pairs={{0,4},{4,0},{8,12},{12,8},{16,20},{20,16},{24,28},{28,24},{1,5},{5... | collective-permute-start | bytes 1474568 | tf_op jit(solution)/shard_map/ppermute | solution.py:397
  291.0 20.4 %collective-permute-start.36 = (bf16[2,4,32,896]{3,2,1,0:T(8,128)(2,1)S(1)}, bf16[2,4,32,896]{3,2,1,0:T(8,128)(2,1)S(1)}, u32[]{:S(2)}, u32[]{:S(2)}) collective-permute-start(bf16[2,4,32,896]{3,2,1,0:T(8,128)(2,1)S(1)} %get-tuple-element.213), channel_id=1, source_target_pairs={{0,4},{4,0},{8,12},{12,8},{16,20},{20,16},{24,28},{28,24},{1,5},{5... | collective-permute-start | bytes 1376264 | tf_op jit(solution)/shard_map/ppermute | solution.py:397
  296.0 86.6 %collective-permute-start.34 = (bf16[2,256,1024]{2,1,0:T(8,128)(2,1)}, bf16[2,256,1024]{2,1,0:T(8,128)(2,1)S(1)}, u32[]{:S(2)}, u32[]{:S(2)}) collective-permute-start(bf16[2,256,1024]{2,1,0:T(8,128)(2,1)} %get-tuple-element.210), channel_id=1, source_target_pairs={{0,1},{1,0},{2,3},{3,2},{4,5},{5,4},{6,7},{7,6},{8,9},{9,8},{10,11... | collective-permute-start | bytes 3145736 | tf_op jit(solution)/shard_map/ppermute | solution.py:388
  298.0 24.0 %collective-permute-start.62 = (bf16[4,32,1408]{2,1,0:T(8,128)(2,1)S(1)}, bf16[4,32,1408]{2,1,0:T(8,128)(2,1)S(1)}, u32[]{:S(2)}, u32[]{:S(2)}) collective-permute-start(bf16[4,32,1408]{2,1,0:T(8,128)(2,1)S(1)} %fusion.3), channel_id=1, source_target_pairs={{0,8},{4,12},{8,16},{12,20},{16,24},{20,28},{24,0},{28,4},{1,9},{5... | collective-permute-start | bytes 1081352 | tf_op jit(solution)/shard_map/ppermute | solution.py:402
  311.5 19.9 %collective-permute-start.37 = (bf16[2,4,32,896]{3,2,1,0:T(8,128)(2,1)}, bf16[2,4,32,896]{3,2,1,0:T(8,128)(2,1)S(1)}, u32[]{:S(2)}, u32[]{:S(2)}) collective-permute-start(bf16[2,4,32,896]{3,2,1,0:T(8,128)(2,1)} %get-tuple-element.214), channel_id=1, source_target_pairs={{0,4},{4,0},{8,12},{12,8},{16,20},{20,16},{24,28},{28,24},{1,5},{5... | collective-permute-start | bytes 1376264 | tf_op jit(solution)/shard_map/ppermute | solution.py:397
  313.3 7.9 %collective-permute-start.38 = (bf16[4,32,896]{2,1,0:T(8,128)(2,1)S(1)}, bf16[4,32,896]{2,1,0:T(8,128)(2,1)S(1)}, u32[]{:S(2)}, u32[]{:S(2)}) collective-permute-start(bf16[4,32,896]{2,1,0:T(8,128)(2,1)S(1)} %fusion.15), channel_id=1, source_target_pairs={{0,8},{4,12},{8,16},{12,20},{16,24},{20,28},{24,0},{28,4},{1,9},{5... | collective-permute-start | bytes 688136 | tf_op jit(solution)/shard_map/ppermute | solution.py:402
  313.6 28.8 %collective-permute-start.50 = (bf16[2,4,32,960]{3,2,1,0:T(8,128)(2,1)}, bf16[2,4,32,960]{3,2,1,0:T(8,128)(2,1)}, u32[]{:S(2)}, u32[]{:S(2)}) collective-permute-start(bf16[2,4,32,960]{3,2,1,0:T(8,128)(2,1)} %get-tuple-element.228), channel_id=1, source_target_pairs={{0,4},{4,0},{8,12},{12,8},{16,20},{20,16},{24,28},{28,24},{1,5},{5... | collective-permute-start | bytes 1474568 | tf_op jit(solution)/shard_map/ppermute | solution.py:397
  321.1 8.9 %collective-permute-start.51 = (bf16[4,32,960]{2,1,0:T(8,128)(2,1)}, bf16[4,32,960]{2,1,0:T(8,128)(2,1)}, u32[]{:S(2)}, u32[]{:S(2)}) collective-permute-start(bf16[4,32,960]{2,1,0:T(8,128)(2,1)} %fusion.14), channel_id=1, source_target_pairs={{0,8},{4,12},{8,16},{12,20},{16,24},{20,28},{24,0},{28,4},{1,9},{5... | collective-permute-start | bytes 737288 | tf_op jit(solution)/shard_map/ppermute | solution.py:402
  321.9 10.6 %collective-permute-start.39 = (bf16[4,32,896]{2,1,0:T(8,128)(2,1)}, bf16[4,32,896]{2,1,0:T(8,128)(2,1)}, u32[]{:S(2)}, u32[]{:S(2)}) collective-permute-start(bf16[4,32,896]{2,1,0:T(8,128)(2,1)} %fusion.11), channel_id=1, source_target_pairs={{0,8},{4,12},{8,16},{12,20},{16,24},{20,28},{24,0},{28,4},{1,9},{5... | collective-permute-start | bytes 688136 | tf_op jit(solution)/shard_map/ppermute | solution.py:402
  324.9 19.4 %all-to-all-start.5 = ((bf16[4,32,1408]{2,1,0:T(8,128)(2,1)}), bf16[4,32,1408]{2,1,0:T(8,128)(2,1)S(1)}, u32[]{:S(2)}, u32[]{:S(2)}) async-start(bf16[4,32,1408]{2,1,0:T(8,128)(2,1)} %fusion.5), calls=%async_computation.5 | async-start | bytes 720896 | tf_op jit(solution)/shard_map/all_to_all | solution.py:1690
  331.3 11.1 %collective-permute-start.52 = (bf16[4,32,960]{2,1,0:T(8,128)(2,1)S(1)}, bf16[4,32,960]{2,1,0:T(8,128)(2,1)S(1)}, u32[]{:S(2)}, u32[]{:S(2)}) collective-permute-start(bf16[4,32,960]{2,1,0:T(8,128)(2,1)S(1)} %fusion.8), channel_id=1, source_target_pairs={{0,8},{4,12},{8,16},{12,20},{16,24},{20,28},{24,0},{28,4},{1,9},{5... | collective-permute-start | bytes 737288 | tf_op jit(solution)/shard_map/ppermute | solution.py:402
  334.4 11.3 %collective-permute-start.40 = (bf16[4,32,896]{2,1,0:T(8,128)(2,1)}, bf16[4,32,896]{2,1,0:T(8,128)(2,1)}, u32[]{:S(2)}, u32[]{:S(2)}) collective-permute-start(bf16[4,32,896]{2,1,0:T(8,128)(2,1)} %fusion.12), channel_id=1, source_target_pairs={{0,8},{4,12},{8,16},{12,20},{16,24},{20,28},{24,0},{28,4},{1,9},{5... | collective-permute-start | bytes 688136 | tf_op jit(solution)/shard_map/ppermute | solution.py:402
  344.3 10.4 %collective-permute-start.53 = (bf16[4,32,960]{2,1,0:T(8,128)(2,1)}, bf16[4,32,960]{2,1,0:T(8,128)(2,1)}, u32[]{:S(2)}, u32[]{:S(2)}) collective-permute-start(bf16[4,32,960]{2,1,0:T(8,128)(2,1)} %fusion.9), channel_id=1, source_target_pairs={{0,8},{4,12},{8,16},{12,20},{16,24},{20,28},{24,0},{28,4},{1,9},{5... | collective-permute-start | bytes 737288 | tf_op jit(solution)/shard_map/ppermute | solution.py:402
  344.3 15.5 %collective-permute-start.63 = (bf16[4,32,1408]{2,1,0:T(8,128)(2,1)S(1)}, bf16[4,32,1408]{2,1,0:T(8,128)(2,1)}, u32[]{:S(2)}, u32[]{:S(2)}) collective-permute-start(bf16[4,32,1408]{2,1,0:T(8,128)(2,1)S(1)} %all-to-all-done.5.refs_0_), channel_id=1, source_target_pairs={{0,8},{4,12},{8,16},{12,20},{16,24},{20,28},{24,0},{28,4},{1,9},{5... | collective-permute-start | bytes 1081352 | tf_op jit(solution)/shard_map/ppermute | solution.py:402
  344.3 15.5 %collective-permute-start.64 = (bf16[4,32,1408]{2,1,0:T(8,128)(2,1)S(1)}, bf16[4,32,1408]{2,1,0:T(8,128)(2,1)}, u32[]{:S(2)}, u32[]{:S(2)}) collective-permute-start(bf16[4,32,1408]{2,1,0:T(8,128)(2,1)S(1)} %all-to-all-done.5.refs_0_), channel_id=1, source_target_pairs={{0,4},{4,0},{8,12},{12,8},{16,20},{20,16},{24,28},{28,24},{1,5},{5... | collective-permute-start | bytes 1081352 | tf_op jit(solution)/shard_map/ppermute | solution.py:397
  347.5 9.0 %all-to-all-start.4 = ((bf16[4,32,896]{2,1,0:T(8,128)(2,1)}), bf16[4,32,896]{2,1,0:T(8,128)(2,1)S(1)}, u32[]{:S(2)}, u32[]{:S(2)}) async-start(bf16[4,32,896]{2,1,0:T(8,128)(2,1)} %fusion.13), calls=%async_computation.4 | async-start | bytes 458752 | tf_op jit(solution)/shard_map/all_to_all | solution.py:1690
  355.9 11.2 %collective-permute-start.54 = (bf16[4,32,960]{2,1,0:T(8,128)(2,1)S(1)}, bf16[4,32,960]{2,1,0:T(8,128)(2,1)}, u32[]{:S(2)}, u32[]{:S(2)}) collective-permute-start(bf16[4,32,960]{2,1,0:T(8,128)(2,1)S(1)} %fusion.10.refs_0_), channel_id=1, source_target_pairs={{0,8},{4,12},{8,16},{12,20},{16,24},{20,28},{24,0},{28,4},{1,9},{5... | collective-permute-start | bytes 737288 | tf_op jit(solution)/shard_map/ppermute | solution.py:402
  356.0 11.3 %collective-permute-start.55 = (bf16[4,32,960]{2,1,0:T(8,128)(2,1)S(1)}, bf16[4,32,960]{2,1,0:T(8,128)(2,1)}, u32[]{:S(2)}, u32[]{:S(2)}) collective-permute-start(bf16[4,32,960]{2,1,0:T(8,128)(2,1)S(1)} %fusion.10.refs_0_), channel_id=1, source_target_pairs={{0,4},{4,0},{8,12},{12,8},{16,20},{20,16},{24,28},{28,24},{1,5},{5... | collective-permute-start | bytes 737288 | tf_op jit(solution)/shard_map/ppermute | solution.py:397
  359.8 12.2 %collective-permute-start.41 = (bf16[4,32,896]{2,1,0:T(8,128)(2,1)S(1)}, bf16[4,32,896]{2,1,0:T(8,128)(2,1)S(1)}, u32[]{:S(2)}, u32[]{:S(2)}) collective-permute-start(bf16[4,32,896]{2,1,0:T(8,128)(2,1)S(1)} %all-to-all-done.4.refs_0_), channel_id=1, source_target_pairs={{0,8},{4,12},{8,16},{12,20},{16,24},{20,28},{24,0},{28,4},{1,9},{5... | collective-permute-start | bytes 688136 | tf_op jit(solution)/shard_map/ppermute | solution.py:402
  359.8 24.9 %collective-permute-start.65 = (bf16[4,32,1408]{2,1,0:T(8,128)(2,1)}, bf16[4,32,1408]{2,1,0:T(8,128)(2,1)S(1)}, u32[]{:S(2)}, u32[]{:S(2)}) collective-permute-start(bf16[4,32,1408]{2,1,0:T(8,128)(2,1)} %collective-permute-done.63.refs_1_), channel_id=1, source_target_pairs={{0,8},{4,12},{8,16},{12,20},{16,24},{20,28},{24,0},{28,4},{1,9},{5... | collective-permute-start | bytes 1081352 | tf_op jit(solution)/shard_map/ppermute | solution.py:402
  367.1 8.5 %collective-permute-start.42 = (bf16[4,32,896]{2,1,0:T(8,128)(2,1)S(1)}, bf16[4,32,896]{2,1,0:T(8,128)(2,1)S(1)}, u32[]{:S(2)}, u32[]{:S(2)}) collective-permute-start(bf16[4,32,896]{2,1,0:T(8,128)(2,1)S(1)} %all-to-all-done.4.refs_0_), channel_id=1, source_target_pairs={{0,4},{4,0},{8,12},{12,8},{16,20},{20,16},{24,28},{28,24},{1,5},{5... | collective-permute-start | bytes 688136 | tf_op jit(solution)/shard_map/ppermute | solution.py:397
  367.3 15.0 %collective-permute-start.56 = (bf16[4,32,960]{2,1,0:T(8,128)(2,1)}, bf16[4,32,960]{2,1,0:T(8,128)(2,1)S(1)}, u32[]{:S(2)}, u32[]{:S(2)}) collective-permute-start(bf16[4,32,960]{2,1,0:T(8,128)(2,1)} %collective-permute-done.54.refs_1_), channel_id=1, source_target_pairs={{0,8},{4,12},{8,16},{12,20},{16,24},{20,28},{24,0},{28,4},{1,9},{5... | collective-permute-start | bytes 737288 | tf_op jit(solution)/shard_map/ppermute | solution.py:402
  371.9 10.4 %collective-permute-start.57 = (bf16[4,32,960]{2,1,0:T(8,128)(2,1)}, bf16[4,32,960]{2,1,0:T(8,128)(2,1)S(1)}, u32[]{:S(2)}, u32[]{:S(2)}) collective-permute-start(bf16[4,32,960]{2,1,0:T(8,128)(2,1)} %collective-permute-done.54.refs_1_), channel_id=1, source_target_pairs={{0,4},{4,0},{8,12},{12,8},{16,20},{20,16},{24,28},{28,24},{1,5},{5... | collective-permute-start | bytes 737288 | tf_op jit(solution)/shard_map/ppermute | solution.py:397
  375.7 10.7 %collective-permute-start.66 = (bf16[4,32,1408]{2,1,0:T(8,128)(2,1)}, bf16[4,32,1408]{2,1,0:T(8,128)(2,1)S(1)}, u32[]{:S(2)}, u32[]{:S(2)}) collective-permute-start(bf16[4,32,1408]{2,1,0:T(8,128)(2,1)} %collective-permute-done.63.refs_1_), channel_id=1, source_target_pairs={{0,4},{4,0},{8,12},{12,8},{16,20},{20,16},{24,28},{28,24},{1,5},{5... | collective-permute-start | bytes 1081352 | tf_op jit(solution)/shard_map/ppermute | solution.py:397
  382.3 10.2 %collective-permute-start.43 = (bf16[4,32,896]{2,1,0:T(8,128)(2,1)S(1)}, bf16[4,32,896]{2,1,0:T(8,128)(2,1)S(1)}, u32[]{:S(2)}, u32[]{:S(2)}) collective-permute-start(bf16[4,32,896]{2,1,0:T(8,128)(2,1)S(1)} %collective-permute-done.41.refs_1_), channel_id=1, source_target_pairs={{0,8},{4,12},{8,16},{12,20},{16,24},{20,28},{24,0},{28,4},{1,9},{5... | collective-permute-start | bytes 688136 | tf_op jit(solution)/shard_map/ppermute | solution.py:402
  382.3 10.2 %collective-permute-start.44 = (bf16[4,32,896]{2,1,0:T(8,128)(2,1)S(1)}, bf16[4,32,896]{2,1,0:T(8,128)(2,1)S(1)}, u32[]{:S(2)}, u32[]{:S(2)}) collective-permute-start(bf16[4,32,896]{2,1,0:T(8,128)(2,1)S(1)} %collective-permute-done.41.refs_1_), channel_id=1, source_target_pairs={{0,4},{4,0},{8,12},{12,8},{16,20},{20,16},{24,28},{28,24},{1,5},{5... | collective-permute-start | bytes 688136 | tf_op jit(solution)/shard_map/ppermute | solution.py:397
  382.7 15.5 %collective-permute-start.58 = (bf16[4,32,960]{2,1,0:T(8,128)(2,1)S(1)}, bf16[4,32,960]{2,1,0:T(8,128)(2,1)S(1)}, u32[]{:S(2)}, u32[]{:S(2)}) collective-permute-start(bf16[4,32,960]{2,1,0:T(8,128)(2,1)S(1)} %collective-permute-done.56.refs_2_), channel_id=1, source_target_pairs={{0,8},{4,12},{8,16},{12,20},{16,24},{20,28},{24,0},{28,4},{1,9},{5... | collective-permute-start | bytes 737288 | tf_op jit(solution)/shard_map/ppermute | solution.py:402
  384.7 13.7 %collective-permute-start.59 = (bf16[4,32,960]{2,1,0:T(8,128)(2,1)S(1)}, bf16[4,32,960]{2,1,0:T(8,128)(2,1)S(1)}, u32[]{:S(2)}, u32[]{:S(2)}) collective-permute-start(bf16[4,32,960]{2,1,0:T(8,128)(2,1)S(1)} %collective-permute-done.56.refs_2_), channel_id=1, source_target_pairs={{0,4},{4,0},{8,12},{12,8},{16,20},{20,16},{24,28},{28,24},{1,5},{5... | collective-permute-start | bytes 737288 | tf_op jit(solution)/shard_map/ppermute | solution.py:397
  386.4 25.2 %collective-permute-start.35 = (bf16[256,1024]{1,0:T(8,128)(2,1)S(1)}, bf16[256,1024]{1,0:T(8,128)(2,1)S(1)}, u32[]{:S(2)}, u32[]{:S(2)}) collective-permute-start(bf16[256,1024]{1,0:T(8,128)(2,1)S(1)} %fusion.7), channel_id=1, source_target_pairs={{0,2},{1,3},{2,0},{3,1},{4,6},{5,7},{6,4},{7,5},{8,10},{9,11},{10,... | collective-permute-start | bytes 1572872 | tf_op jit(solution)/shard_map/ppermute | solution.py:392
  392.5 17.1 %collective-permute-start.67 = (bf16[4,32,1408]{2,1,0:T(8,128)(2,1)S(1)}, bf16[4,32,1408]{2,1,0:T(8,128)(2,1)S(1)}, u32[]{:S(2)}, u32[]{:S(2)}) collective-permute-start(bf16[4,32,1408]{2,1,0:T(8,128)(2,1)S(1)} %collective-permute-done.65.refs_2_), channel_id=1, source_target_pairs={{0,8},{4,12},{8,16},{12,20},{16,24},{20,28},{24,0},{28,4},{1,9},{5... | collective-permute-start | bytes 1081352 | tf_op jit(solution)/shard_map/ppermute | solution.py:402
  392.5 17.1 %collective-permute-start.68 = (bf16[4,32,1408]{2,1,0:T(8,128)(2,1)S(1)}, bf16[4,32,1408]{2,1,0:T(8,128)(2,1)S(1)}, u32[]{:S(2)}, u32[]{:S(2)}) collective-permute-start(bf16[4,32,1408]{2,1,0:T(8,128)(2,1)S(1)} %collective-permute-done.65.refs_2_), channel_id=1, source_target_pairs={{0,4},{4,0},{8,12},{12,8},{16,20},{20,16},{24,28},{28,24},{1,5},{5... | collective-permute-start | bytes 1081352 | tf_op jit(solution)/shard_map/ppermute | solution.py:397
  398.1 8.8 %collective-permute-start.45 = (bf16[4,32,896]{2,1,0:T(8,128)(2,1)S(1)}, bf16[4,32,896]{2,1,0:T(8,128)(2,1)S(1)}, u32[]{:S(2)}, u32[]{:S(2)}) collective-permute-start(bf16[4,32,896]{2,1,0:T(8,128)(2,1)S(1)} %collective-permute-done.43.refs_2_), channel_id=1, source_target_pairs={{0,8},{4,12},{8,16},{12,20},{16,24},{20,28},{24,0},{28,4},{1,9},{5... | collective-permute-start | bytes 688136 | tf_op jit(solution)/shard_map/ppermute | solution.py:402
  398.4 11.1 %collective-permute-start.46 = (bf16[4,32,896]{2,1,0:T(8,128)(2,1)S(1)}, bf16[4,32,896]{2,1,0:T(8,128)(2,1)S(1)}, u32[]{:S(2)}, u32[]{:S(2)}) collective-permute-start(bf16[4,32,896]{2,1,0:T(8,128)(2,1)S(1)} %collective-permute-done.43.refs_2_), channel_id=1, source_target_pairs={{0,4},{4,0},{8,12},{12,8},{16,20},{20,16},{24,28},{28,24},{1,5},{5... | collective-permute-start | bytes 688136 | tf_op jit(solution)/shard_map/ppermute | solution.py:397
  407.0 9.2 %collective-permute-start.60 = (bf16[4,32,960]{2,1,0:T(8,128)(2,1)S(1)}, bf16[4,32,960]{2,1,0:T(8,128)(2,1)S(1)}, u32[]{:S(2)}, u32[]{:S(2)}) collective-permute-start(bf16[4,32,960]{2,1,0:T(8,128)(2,1)S(1)} %collective-permute-done.58.refs_3_), channel_id=1, source_target_pairs={{0,4},{4,0},{8,12},{12,8},{16,20},{20,16},{24,28},{28,24},{1,5},{5... | collective-permute-start | bytes 737288 | tf_op jit(solution)/shard_map/ppermute | solution.py:397
  409.6 11.6 %collective-permute-start.47 = (bf16[4,32,896]{2,1,0:T(8,128)(2,1)S(1)}, bf16[4,32,896]{2,1,0:T(8,128)(2,1)S(1)}, u32[]{:S(2)}, u32[]{:S(2)}) collective-permute-start(bf16[4,32,896]{2,1,0:T(8,128)(2,1)S(1)} %collective-permute-done.45.refs_3_), channel_id=1, source_target_pairs={{0,4},{4,0},{8,12},{12,8},{16,20},{20,16},{24,28},{28,24},{1,5},{5... | collective-permute-start | bytes 688136 | tf_op jit(solution)/shard_map/ppermute | solution.py:397
  409.6 16.6 %collective-permute-start.69 = (bf16[4,32,1408]{2,1,0:T(8,128)(2,1)S(1)}, bf16[4,32,1408]{2,1,0:T(8,128)(2,1)S(1)}, u32[]{:S(2)}, u32[]{:S(2)}) collective-permute-start(bf16[4,32,1408]{2,1,0:T(8,128)(2,1)S(1)} %collective-permute-done.67.refs_3_), channel_id=1, source_target_pairs={{0,4},{4,0},{8,12},{12,8},{16,20},{20,16},{24,28},{28,24},{1,5},{5... | collective-permute-start | bytes 1081352 | tf_op jit(solution)/shard_map/ppermute | solution.py:397
  (82 other events, 670.8 us)
